TPU v7x, 256 devices: a whole 4x4x8 slice. The times are simulated.
256 devices in a mesh: dom: 64 (over z, x, core), tp: 4 (over y).
Axes of the slice: x: 4, y: 4, z: 8, core: 2. Of those that a mesh axis runs over, the one named last changes fastest.
Arguments:
- state: bfloat16 [2, 65536, 512], P(None, 'dom'), may hold values from -6 to 6
- norm_gain: float32 [2, 2, 512], replicated, may hold values from 0.1 to 1.9
- norm_shift: float32 [2, 2, 512], replicated, may hold values from -3 to 3
- qkv_weight: bfloat16 [512, 3, 512], P(None, None, 'tp'), may hold values from -0.5 to 0.5
- out_weight: bfloat16 [512, 512], P('tp'), may hold values from -0.25 to 0.25
- up_weight: bfloat16 [512, 2048], P(None, 'tp'), may hold values from -0.25 to 0.25
- down_weight: bfloat16 [2048, 512], P('tp'), may hold values from -0.125 to 0.125
- neighbours: int32 [512, 8], P('dom'), may hold values from 0 to 511, as said below
- counts: int32 [512], P('dom'), may hold values from 2 to 8, as said below
Outputs:
- layer_out: bfloat16 [2, 65536, 512], P(None, 'dom', 'tp')
Inputs may be any that keep to these rules, and one draw needn't show every extreme that they name: `neighbours`: entry 0 of row b is b itself; the other 7 entries are distinct blocks whose partition (block // 8) lies at most two partitions before or after b's on a closed chain of partitions, block numbers taken modulo 512. `counts`: every partition has a block whose count is 8.
All inputs are finite; a program needn't handle non-finite values.
Results may differ from a plain program's by a relative error of at most 0.017.
Values may be sent and summed in bfloat16 or wider, within the bound.
No kernel may reach another device: no remote copies, remote signals or barrier semaphores. Data moves between devices by JAX's collectives and lax.ppermute only.
A program may use at most 64 MiB of HBM per device.

v0:
```python
import math

import jax
import jax.numpy as jnp
from jax import lax
from jax.sharding import PartitionSpec as P

HEADS = 4
NODE_BLK = 128
KMAX = 8


def with_halo(value, sides, width):
    for axis, dim in sides:
        peers, length = (lax.axis_size(axis), value.shape[dim])
        up = [(i, (i + 1) % peers) for i in range(peers)]
        down = [(j, i) for i, j in up]
        last = lax.slice_in_dim(value, length - width, length, axis=dim)
        leading = lax.slice_in_dim(value, 0, width, axis=dim)
        before = lax.ppermute(last, axis, up)
        after = lax.ppermute(leading, axis, down)
        value = jnp.concatenate([before, value, after], axis=dim)
    return value


def shifted(block, axis, distance):
    devices = range(lax.axis_size(axis))
    route = [((i - distance) % len(devices), i) for i in devices]
    return lax.ppermute(block, axis, route)


def layer_norm(values, gain_row, shift_row):
    row_mean = jnp.mean(values, axis=-1, keepdims=True)
    centred = values - row_mean
    spread = jnp.mean(centred * centred, axis=-1, keepdims=True)
    return centred * lax.rsqrt(spread + 1e-05) * gain_row + shift_row


def local(
    state, norm_gain, norm_shift, qkv_weight, out_weight, up_weight, down_weight, neighbours, counts
):
    samples, row_count, feat_width = state.shape
    per_dev = row_count // NODE_BLK
    block_count = per_dev * lax.axis_size("dom")
    head_cols = qkv_weight.shape[2]
    head_size = feat_width // HEADS
    heads_here = head_cols // head_size
    tp_rank = lax.axis_index("tp")
    resid_in = state.astype(jnp.float32)
    normed = layer_norm(resid_in, norm_gain[0][:, None, :], norm_shift[0][:, None, :]).astype(
        jnp.bfloat16
    )
    normed = normed.reshape(samples, per_dev, NODE_BLK, feat_width)
    projected = jnp.einsum(
        "sbnd,dce->bsnce", normed, qkv_weight, preferred_element_type=jnp.float32
    ).astype(jnp.bfloat16)
    query_heads = projected[:, :, :, 0].reshape(per_dev, samples, NODE_BLK, heads_here, head_size)
    own_pairs = projected[:, :, :, 1:].reshape(per_dev, samples, NODE_BLK, 2 * head_cols)
    near_side = with_halo(own_pairs, (("dom", 0),), per_dev)
    far_side = [shifted(own_pairs, "dom", offset) for offset in (2, -2)]
    window = jnp.concatenate([far_side[0], near_side, far_side[1]], axis=0)
    first_block = lax.axis_index("dom") * per_dev - 2 * per_dev
    window_idx = jnp.mod(neighbours - first_block, block_count)
    chosen = window[window_idx]
    key_rows = chosen[..., :head_cols].reshape(
        per_dev, KMAX, samples, NODE_BLK, heads_here, head_size
    )
    value_rows = chosen[..., head_cols:].reshape(
        per_dev, KMAX, samples, NODE_BLK, heads_here, head_size
    )
    scores = jnp.einsum(
        "bsqhe,bjskhe->bshqjk", query_heads, key_rows, preferred_element_type=jnp.float32
    ) / math.sqrt(head_size)
    live_mask = jnp.arange(KMAX, dtype=jnp.int32)[None, :] < counts[:, None]
    masked = jnp.where(live_mask[:, None, None, None, :, None], scores, -1e30)
    row_top = jnp.max(masked, axis=(4, 5), keepdims=True)
    weights = jnp.exp(masked - row_top)
    weights = (weights / jnp.sum(weights, axis=(4, 5), keepdims=True)).astype(jnp.bfloat16)
    mixed_heads = jnp.einsum(
        "bshqjk,bjskhe->sbqhe", weights, value_rows, preferred_element_type=jnp.float32
    ).astype(jnp.bfloat16)
    mixed_heads = mixed_heads.reshape(samples, row_count, head_cols)
    partial_value = jnp.einsum(
        "sre,ed->srd", mixed_heads, out_weight, preferred_element_type=jnp.float32
    )
    attn_sum = lax.psum(partial_value.astype(jnp.bfloat16), "tp").astype(jnp.float32)
    residual = resid_in + attn_sum
    normed2 = layer_norm(residual, norm_gain[1][:, None, :], norm_shift[1][:, None, :]).astype(
        jnp.bfloat16
    )
    hidden = jax.nn.silu(
        jnp.einsum("srd,df->srf", normed2, up_weight, preferred_element_type=jnp.float32)
    ).astype(jnp.bfloat16)
    update = jnp.einsum("srf,fd->srd", hidden, down_weight, preferred_element_type=jnp.float32)
    update = lax.psum_scatter(
        update.astype(jnp.bfloat16), "tp", scatter_dimension=2, tiled=True
    ).astype(jnp.float32)
    col_share = update.shape[2]
    kept_cols = lax.dynamic_slice_in_dim(residual, tp_rank * col_share, col_share, 2)
    return (kept_cols + update).astype(jnp.bfloat16)


def solution(mesh):
    placed = (
        P(None, "dom", None),
        P(),
        P(),
        P(None, None, "tp"),
        P("tp", None),
        P(None, "tp"),
        P("tp", None),
        P("dom", None),
        P("dom"),
    )
    return jax.shard_map(
        local, mesh=mesh, in_specs=placed, out_specs=P(None, "dom", "tp"), check_vma=False
    )
```

profile of v0, /device:TPU:1, one launch (start us, length us, event | category | flops | bytes accessed | tf_op | source)
XLA Modules:
  0.0 212.9 jit_solution(13900519222820151107)
XLA Ops:
  6.6 2.1 convert_reduce_fusion
  8.7 2.4 %fusion.4 = f32[2,1024]{1,0:T(2,128)S(1)} fusion(bf16[2,1024,512]{2,1,0:T(8,128)(2,1)} %param.9, f32[2,1024]{1,0:T(2,128)S(1)} %broadcast_multiply_fusion.1), kind=kLoop, calls=%fused_computation.11 | loop fusion | flops 4192256 | bytes 2113536 | tf_op jit(solution)/shard_map/reduce_sum | solution.py:35
  15.5 2.3 %copy.30 = bf16[8,2,128,256]{3,2,1,0:T(8,128)(2,1)} copy(bf16[8,2,128,256]{2,3,0,1:T(8,128)(2,1)} %bitcast.55) | data formatting | bytes 2097152 | tf_op jit(solution)/shard_map/reshape | solution.py:58
  17.7 2.0 collective-permute-start
  19.8 2.1 collective-permute-start.1
  21.8 5.3 %collective-permute-start.3 = (bf16[8,2,128,256]{3,2,1,0:T(8,128)(2,1)}, bf16[8,2,128,256]{3,2,1,0:T(8,128)(2,1)}, u32[]{:S(2)}, u32[]{:S(2)}) collective-permute-start(bf16[8,2,128,256]{3,2,1,0:T(8,128)(2,1)} %copy.30), channel_id=1, source_target_pairs={{8,0},{12,4},{16,8},{20,12},{24,16},{28,20},{32,24},{36,28},{40,32... | collective-permute-start | bytes 3145736 | tf_op jit(solution)/shard_map/ppermute | solution.py:29
  27.3 22.3 %collective-permute-done = bf16[8,2,128,256]{3,2,1,0:T(8,128)(2,1)} collective-permute-done((bf16[8,2,128,256]{3,2,1,0:T(8,128)(2,1)}, bf16[8,2,128,256]{3,2,1,0:T(8,128)(2,1)}, u32[]{:S(2)}, u32[]{:S(2)}) %collective-permute-start) | collective-permute-done | bytes 1048608 | tf_op jit(solution)/shard_map/ppermute | solution.py:29
  49.5 2.4 %constant_dynamic-update-slice_fusion.4 = bf16[40,2,128,256]{3,2,1,0:T(8,128)(2,1)} fusion(bf16[8,2,128,256]{3,2,1,0:T(8,128)(2,1)} %collective-permute-done), kind=kLoop, calls=%fused_computation.47 | loop fusion | bytes 2097152
  51.9 2.4 %collective-permute-done.1 = bf16[8,2,128,256]{3,2,1,0:T(8,128)(2,1)} collective-permute-done((bf16[8,2,128,256]{3,2,1,0:T(8,128)(2,1)}, bf16[8,2,128,256]{3,2,1,0:T(8,128)(2,1)}, u32[]{:S(2)}, u32[]{:S(2)}) %collective-permute-start.1) | collective-permute-done | bytes 1048608 | tf_op jit(solution)/shard_map/ppermute | solution.py:20
  54.3 2.3 %constant_dynamic-update-slice_fusion.3 = bf16[40,2,128,256]{3,2,1,0:T(8,128)(2,1)} fusion(bf16[40,2,128,256]{3,2,1,0:T(8,128)(2,1)} %constant_dynamic-update-slice_fusion.4, bf16[8,2,128,256]{3,2,1,0:T(8,128)(2,1)} %collective-permute-done.1), kind=kLoop, calls=%fused_computation.46 | loop fusion | bytes 2097152
  57.6 2.3 %constant_dynamic-update-slice_fusion.1 = bf16[40,2,128,256]{3,2,1,0:T(8,128)(2,1)} fusion(bf16[40,2,128,256]{3,2,1,0:T(8,128)(2,1)} %constant_dynamic-update-slice_fusion.2, bf16[8,2,128,256]{3,2,1,0:T(8,128)(2,1)} %collective-permute-done.2), kind=kLoop, calls=%fused_computation.44 | loop fusion | bytes 2097152
  59.9 2.4 %constant_dynamic-update-slice_fusion = bf16[40,2,128,256]{3,2,1,0:T(8,128)(2,1)} fusion(bf16[40,2,128,256]{3,2,1,0:T(8,128)(2,1)} %constant_dynamic-update-slice_fusion.1, bf16[8,2,128,256]{3,2,1,0:T(8,128)(2,1)} %collective-permute-done.3), kind=kLoop, calls=%fused_computation.43 | loop fusion | bytes 2097152 | tf_op jit(solution)/shard_map/concatenate | solution.py:61
  62.3 8.0 %gather_fusion = bf16[64,2,128,256]{3,2,1,0:T(8,128)(2,1)} fusion(bf16[40,2,128,256]{3,2,1,0:T(8,128)(2,1)} %constant_dynamic-update-slice_fusion, s32[1024]{0:T(1024)S(1)} %pad_clamp_fusion), kind=kCustom, calls=%fused_computation | custom fusion | bytes 16777472 | tf_op jit(solution)/shard_map/gather | solution.py:64
  70.3 3.8 %fusion.40 = (bf16[8,8,2,128,128]{4,3,2,1,0:T(8,128)(2,1)S(1)}, bf16[8,8,2,128,128]{4,3,2,1,0:T(8,128)(2,1)S(1)}) fusion(bf16[8,8,2,128,256]{4,3,2,1,0:T(8,128)(2,1)} %bitcast.52), kind=kLoop, calls=%fused_computation.64 | loop fusion | bytes 16777216 | tf_op jit(solution)/shard_map/slice | solution.py:68
  74.1 2.4 %fusion = (f32[8,2,128]{2,1,0:T(2,128)S(1)}, f32[8,2,128,8,128]{2,4,3,1,0:T(8,128)S(1)}) fusion(pred[8,8]{1,0:T(8,128)(4,1)S(1)} %iota_compare_fusion, bf16[8,8,2,128,128]{4,3,2,1,0:T(8,128)(2,1)S(1)} %get-tuple-element.6, bf16[8,2,128,3,128]{2,4,3,0,1:T(8,128)(2,1)} %copy-done.4), kind=kOutput, calls=%fused_computation.4 | convolution fusion | flops 543160320 | bytes 13115456 | tf_op jit(solution)/shard_map/bsqhe,bjskhe->bshqjk/dot_general | solution.py:71
  76.5 2.0 fusion.1
  78.5 2.8 %fusion.26 = bf16[2,8,128,128]{2,3,1,0:T(8,128)(2,1)S(1)} fusion(bf16[8,8,2,128,128]{4,3,2,1,0:T(8,128)(2,1)S(1)} %get-tuple-element.5, f32[8,2,128,8,128]{2,4,3,1,0:T(8,128)S(1)} %get-tuple-element.14, f32[8,2,128]{2,1,0:T(2,128)S(1)} %fusion.1, f32[8,2,128]{2,1,0:T(2,128)S(1)} %get-tuple-element.13, pred[8,8]{1,0:T(8,128)(4,1)S(1)} %iota_compare_fusion), kind=kOutput, calls=%fused_computation.34 | convolution fusion | flops 547618816 | bytes 13123648 | tf_op jit(solution)/shard_map/bshqjk,bjskhe->sbqhe/dot_general | solution.py:79
  81.3 2.0 convolution_convert_fusion
  83.4 68.5 %all-reduce.2.cloned.1.call-done = bf16[2,1024,512]{2,1,0:T(8,128)(2,1)} async-done(((bf16[2,1024,512]{2,1,0:T(8,128)(2,1)}), bf16[2,1024,512]{2,1,0:T(8,128)(2,1)}) %all-reduce.2.cloned.1.call-update) | async-done | bytes 2097168 | tf_op jit(solution)/shard_map/psum | solution.py:86
  151.9 4.2 %convert_add_fusion = (f32[2,1024,512]{2,1,0:T(8,128)}, f32[2,1024]{1,0:T(2,128)S(1)}) fusion(bf16[2,1024,512]{2,1,0:T(8,128)(2,1)S(1)} %copy-done.1, bf16[2,1024,512]{2,1,0:T(8,128)(2,1)} %all-reduce.2.cloned.1.call-done), kind=kLoop, calls=%fused_computation.6 | loop fusion | flops 4192256 | bytes 8396800 | tf_op jit(solution)/shard_map/add | solution.py:87
  157.2 5.5 %fusion.19 = bf16[2,1024,512]{2,1,0:T(8,128)(2,1)} fusion(f32[2,512]{1,0:T(2,128)S(1)} %get-tuple-element.12, f32[2,512]{1,0:T(2,128)S(1)} %get-tuple-element.15, f32[2,1024]{1,0:T(2,128)S(1)} %add_rsqrt_fusion, f32[2,1024]{1,0:T(2,128)S(1)} %broadcast_multiply_fusion, bf16[512,512]{1,0:T(8,128)(2,1)S(1)} %copy-done, bf16[512,512]{1,0:T(8,128)(2,1)S(1)} %copy-done.9, ...), kind=kOutput, calls=%fused_computation.29 | convolution fusion | flops 2162163712 | bytes 7364608 | tf_op jit(solution)/shard_map/srf,fd->srd/dot_general | solution.py:94
  162.7 5.0 %copy.48 = bf16[2,1024,512]{1,0,2:T(2,128)(2,1)S(1)} copy(bf16[2,1024,512]{2,1,0:T(8,128)(2,1)} %fusion.19) | data formatting | bytes 4194304
  169.7 32.3 %reduce-scatter.4.cloned.1.call-done = bf16[128,2048]{1,0:T(8,128)(2,1)} async-done(((bf16[512,2048]{1,0:T(8,128)(2,1)}), bf16[128,2048]{1,0:T(8,128)(2,1)}) %reduce-scatter.4.cloned.1.call-update) | async-done | bytes 524304
  203.9 2.1 %add_convert_fusion.6 = bf16[2,1024,128]{2,1,0:T(8,128)(2,1)} fusion(bf16[2,1024,128]{2,1,0:T(8,128)(2,1)S(1)} %copy.49, f32[2,1024,512]{2,1,0:T(8,128)} %get-tuple-element.7, s32[]{:T(128)S(6)} %select_n.21), kind=kLoop, calls=%fused_computation.35 | loop fusion | flops 786432 | bytes 2097156 | tf_op jit(solution)/shard_map/convert_element_type | solution.py:100
  (48 shorter events, 10.5 us)
Async XLA Ops:
  6.5 150.6 %copy-start = (bf16[512,512]{1,0:T(8,128)(2,1)S(1)}, bf16[512,512]{1,0:T(8,128)(2,1)}, u32[]{:S(2)}) copy-start(bf16[512,512]{1,0:T(8,128)(2,1)} %param.15) | copy-start | bytes 1572868
  6.5 4.7 %copy-start.1 = (bf16[2,1024,512]{2,1,0:T(8,128)(2,1)S(1)}, bf16[2,1024,512]{2,1,0:T(8,128)(2,1)}, u32[]{:S(2)}) copy-start(bf16[2,1024,512]{2,1,0:T(8,128)(2,1)} %param.9) | copy-start | bytes 6291460
  6.5 4.6 %copy-start.6 = (f32[2,2,512]{2,1,0:T(2,128)S(1)}, f32[2,2,512]{2,1,0:T(2,128)}, u32[]{:S(2)}) copy-start(f32[2,2,512]{2,1,0:T(2,128)} %param.11) | copy-start | bytes 24580
  6.5 4.6 %copy-start.7 = (f32[2,2,512]{2,1,0:T(2,128)S(1)}, f32[2,2,512]{2,1,0:T(2,128)}, u32[]{:S(2)}) copy-start(f32[2,2,512]{2,1,0:T(2,128)} %param.10) | copy-start | bytes 24580
  6.5 5.6 %copy-start.10 = (bf16[512,3,128]{2,0,1:T(8,128)(2,1)S(1)}, bf16[512,3,128]{2,0,1:T(8,128)(2,1)}, u32[]{:S(2)}) copy-start(bf16[512,3,128]{2,0,1:T(8,128)(2,1)} %param.12) | copy-start | bytes 1179652
  6.5 145.4 %all-reduce.2.cloned.1.call-start = ((), (), s32[]{:S(2)}) async-start(), calls=%async_computation.1 | async-start | bytes 4194304 | tf_op jit(solution)/shard_map/psum | solution.py:86
  12.2 14.9 %copy-start.8 = (s32[8,8]{1,0:T(8,128)S(1)}, s32[8,8]{1,0:T(8,128)}, u32[]{:S(2)}) copy-start(s32[8,8]{1,0:T(8,128)} %param.16) | copy-start | bytes 772
  12.2 15.0 %copy-start.11 = (s32[8]{0:T(128)S(1)}, s32[8]{0:T(128)}, u32[]{:S(2)}) copy-start(s32[8]{0:T(128)} %param.17) | copy-start | bytes 100
  13.2 1.2 copy-start.4
  17.7 31.8 %collective-permute-start = (bf16[8,2,128,256]{3,2,1,0:T(8,128)(2,1)}, bf16[8,2,128,256]{3,2,1,0:T(8,128)(2,1)}, u32[]{:S(2)}, u32[]{:S(2)}) collective-permute-start(bf16[8,2,128,256]{3,2,1,0:T(8,128)(2,1)} %copy.30), channel_id=1, source_target_pairs={{248,0},{252,4},{0,8},{4,12},{8,16},{12,20},{16,24},{20,28},{24,32... | collective-permute-start | bytes 3145736 | tf_op jit(solution)/shard_map/ppermute | solution.py:29
  19.8 34.5 %collective-permute-start.1 = (bf16[8,2,128,256]{3,2,1,0:T(8,128)(2,1)}, bf16[8,2,128,256]{3,2,1,0:T(8,128)(2,1)}, u32[]{:S(2)}, u32[]{:S(2)}) collective-permute-start(bf16[8,2,128,256]{3,2,1,0:T(8,128)(2,1)} %copy.30), channel_id=1, source_target_pairs={{0,4},{4,8},{8,12},{12,16},{16,20},{20,24},{24,28},{28,32},{32,36}... | collective-permute-start | bytes 3145736 | tf_op jit(solution)/shard_map/ppermute | solution.py:20
  21.8 35.8 %collective-permute-start.2 = (bf16[8,2,128,256]{3,2,1,0:T(8,128)(2,1)}, bf16[8,2,128,256]{3,2,1,0:T(8,128)(2,1)}, u32[]{:S(2)}, u32[]{:S(2)}) collective-permute-start(bf16[8,2,128,256]{3,2,1,0:T(8,128)(2,1)} %copy.30), channel_id=1, source_target_pairs={{4,0},{8,4},{12,8},{16,12},{20,16},{24,20},{28,24},{32,28},{36,32}... | collective-permute-start | bytes 3145736 | tf_op jit(solution)/shard_map/ppermute | solution.py:21
  21.8 38.1 %collective-permute-start.3 = (bf16[8,2,128,256]{3,2,1,0:T(8,128)(2,1)}, bf16[8,2,128,256]{3,2,1,0:T(8,128)(2,1)}, u32[]{:S(2)}, u32[]{:S(2)}) collective-permute-start(bf16[8,2,128,256]{3,2,1,0:T(8,128)(2,1)} %copy.30), channel_id=1, source_target_pairs={{8,0},{12,4},{16,8},{20,12},{24,16},{28,20},{32,24},{36,28},{40,32... | collective-permute-start | bytes 3145736 | tf_op jit(solution)/shard_map/ppermute | solution.py:29
  27.2 29.4 %copy-start.3 = (bf16[8,2,128,256]{3,2,1,0:T(8,128)(2,1)S(1)}, bf16[8,2,128,256]{3,2,1,0:T(8,128)(2,1)}, u32[]{:S(2)}) copy-start(bf16[8,2,128,256]{3,2,1,0:T(8,128)(2,1)} %copy.30) | copy-start | bytes 3145732
  78.5 2.8 %copy-start.5 = (bf16[128,512]{1,0:T(8,128)(2,1)S(1)}, bf16[128,512]{1,0:T(8,128)(2,1)}, u32[]{:S(2)}) copy-start(bf16[128,512]{1,0:T(8,128)(2,1)} %param.13) | copy-start | bytes 393220
  83.3 118.6 %reduce-scatter.4.cloned.1.call-start = ((), (), s32[]{:S(2)}) async-start(), calls=%async_computation.2 | async-start | bytes 2621440
  151.9 4.2 %copy-start.2 = (bf16[2,1024,512]{2,1,0:T(8,128)(2,1)S(1)}, bf16[2,1024,512]{2,1,0:T(8,128)(2,1)}, u32[]{:S(2)}) copy-start(bf16[2,1024,512]{2,1,0:T(8,128)(2,1)} %all-reduce.2.cloned.1.call-done) | copy-start | bytes 6291460
  156.1 1.0 copy-start.9
Sparse Core Ops, SparseCore 0:
  83.5 68.4 all-reduce.1
  169.8 32.1 reduce-scatter.3
where the time goes:
time: 213 us
  waiting for transfers between devices  125 us (59%)
  local copies, waits for them, and re-layouts  35.7 us (17%)
  other arithmetic  14.9 us (7%)
  matrix products  13.7 us (6%)
  between operations  13.6 us (6%)
  starting transfers between devices  9.43 us (4%)
    psum x1, waiting for transfers between devices, local(): lax.psum(partial_value.astype(jnp.bfloat16), 'tp').astype(jnp.float32)  68.5 us
    unnamed x3, waiting for transfers between devices  32.3 us
    ppermute x2, waiting for transfers between devices, shifted(): return lax.ppermute(block, axis, route)  22.3 us
    unnamed x32, local copies, waits for them, and re-layouts  18.1 us
    gather x1, local copies, waits for them, and re-layouts, local(): chosen = window[window_idx]  8.01 us
    ppermute x2, starting transfers between devices, shifted(): return lax.ppermute(block, axis, route)  7.3 us
    dot_general x1, matrix products, local(): jnp.einsum('srf,fd->srd', hidden, down_weight, preferred_element_type=jnp...  5.49 us
  transfers between devices with their start and end apart: 6, of which 4 were waited for; matrix products, arithmetic and copies ran while one was open for 4% of the time, Pallas kernels for 0%

commit v1 on v0

v1 whole, which is shorter than its diff:
```python
import functools
import math

import jax
import jax.numpy as jnp
from jax import lax
from jax.experimental import pallas as pl
from jax.experimental.pallas import tpu as pltpu
from jax.sharding import PartitionSpec as P

HEADS = 4
NODE_BLK = 128
KMAX = 8
ROWS = 256
VMEM_LIMIT = 56 * 1024 * 1024


def bf(v):
    return v.astype(jnp.bfloat16)


def normalise(values, gain, shift):
    mean = jnp.mean(values, axis=-1, keepdims=True)
    centred = values - mean
    spread = jnp.mean(centred * centred, axis=-1, keepdims=True)
    return centred * lax.rsqrt(spread + 1e-05) * gain + shift


def matmul(a, b):
    return jnp.dot(a, b, preferred_element_type=jnp.float32)


def kv_kernel(x_ref, norm_ref, w0, w1, w2, w3a, w3b, *rest):
    kv_ref = rest[-1]
    normed = bf(normalise(x_ref[...].astype(jnp.float32), norm_ref[0:1], norm_ref[1:2]))
    cols = []
    for w in (w0, w1, w2):
        cols += [w[1], w[2]]
    for c in (1, 2):
        cols.append(jnp.concatenate([w3a[c], w3b[c]], axis=0))
    out = bf(matmul(normed, jnp.concatenate(cols, axis=1)))
    kv_ref[...] = out.reshape(kv_ref.shape)


def project_kv(x, norms, weights, kv, slot, per_dev, slots):
    rows, width = x.shape
    steps = rows // ROWS
    per_step = ROWS // NODE_BLK
    held = pl.BlockSpec(memory_space=pltpu.VMEM)
    specs = [pl.BlockSpec((ROWS, width), lambda i: (i, 0))] + [held] * (1 + len(weights))
    args = [x, norms, *weights]
    aliases = {}
    if kv is not None:
        specs.append(pl.BlockSpec(memory_space=pl.ANY))
        args.append(kv)
        aliases = {len(args) - 1: 0}
    kv_width = 2 * width
    return pl.pallas_call(
        kv_kernel,
        grid=(steps,),
        in_specs=specs,
        out_specs=pl.BlockSpec(
            (per_step, NODE_BLK, kv_width), lambda i: (slot * steps + i, 0, 0)
        ),
        out_shape=jax.ShapeDtypeStruct((slots * per_dev, NODE_BLK, kv_width), jnp.bfloat16),
        input_output_aliases=aliases,
        name="kv_rows",
        compiler_params=pltpu.CompilerParams(vmem_limit_bytes=24 * 1024 * 1024),
        cost_estimate=pl.CostEstimate(
            flops=2 * rows * width * kv_width, bytes_accessed=6 * rows * width, transcendentals=0
        ),
    )(*args)


def q_kernel(place_ref, x_ref, norm_ref, w0, w1, w2, w3a, w3b, q_ref):
    normed = bf(normalise(x_ref[0].astype(jnp.float32), norm_ref[0:1], norm_ref[1:2]))
    cols = [w0[0], w1[0], w2[0], jnp.concatenate([w3a[0], w3b[0]], axis=0)]
    q_ref[...] = bf(matmul(normed, jnp.concatenate(cols, axis=1)))


def project_q(place, state, norms, weights, rows):
    width = state.shape[2]
    held = pl.BlockSpec(memory_space=pltpu.VMEM)
    return pl.pallas_call(
        q_kernel,
        grid_spec=pltpu.PrefetchScalarGridSpec(
            num_scalar_prefetch=1,
            grid=(1,),
            in_specs=[pl.BlockSpec((1, rows, width), lambda i, p: (p[0], p[1], 0))]
            + [held] * (1 + len(weights)),
            out_specs=pl.BlockSpec((rows, width), lambda i, p: (0, 0)),
        ),
        out_shape=jax.ShapeDtypeStruct((rows, width), jnp.bfloat16),
        name="q_rows",
        compiler_params=pltpu.CompilerParams(vmem_limit_bytes=16 * 1024 * 1024),
        cost_estimate=pl.CostEstimate(
            flops=2 * rows * width * width, bytes_accessed=4 * rows * width, transcendentals=0
        ),
    )(place, state, norms, *weights)


def main_kernel(
    place_ref, near_ref, count_ref, x_ref, norm_ref, q_ref, *rest
):
    kv_refs = rest[:KMAX]
    out_w, up_w, down_w, a_m, b_m, c_m, d_m, a_t, b_t, c_t, d_t = rest[KMAX : KMAX + 11]
    o_ref, heads_ref, resid_ref, up_ref = rest[KMAX + 11 :]
    blk = pl.program_id(0)
    head = NODE_BLK
    scale = math.log2(math.e) / math.sqrt(head)
    count = count_ref[blk]
    rows_at = pl.ds(pl.multiple_of(blk * NODE_BLK, NODE_BLK), NODE_BLK)
    for h in range(HEADS):
        keys = [r[0, :, 2 * h * head : (2 * h + 1) * head] for r in kv_refs]
        vals = [r[0, :, (2 * h + 1) * head : (2 * h + 2) * head] for r in kv_refs]
        query = q_ref[:, h * head : (h + 1) * head]
        scores = lax.dot_general(
            query,
            jnp.concatenate(keys, axis=0),
            (((1,), (1,)), ((), ())),
            preferred_element_type=jnp.float32,
        )
        parts = [
            jnp.where(j < count, scores[:, j * NODE_BLK : (j + 1) * NODE_BLK], -1e30)
            for j in range(KMAX)
        ]
        top = functools.reduce(jnp.maximum, parts)
        top = jnp.max(top, axis=-1, keepdims=True)
        parts = [jnp.exp2((p - top) * scale) for p in parts]
        total = jnp.sum(functools.reduce(jnp.add, parts), axis=-1, keepdims=True)
        mixed = matmul(
            jnp.concatenate([bf(p) for p in parts], axis=1), jnp.concatenate(vals, axis=0)
        )
        heads_ref[rows_at, h * head : (h + 1) * head] = bf(mixed / total)

    @pl.when(blk == pl.num_programs(0) - 1)
    def _():
        width = x_ref.shape[2]
        half = width // 2
        mine = pl.ds(pl.multiple_of(place_ref[2] * half, half), half)
        theirs = pl.ds(pl.multiple_of((1 - place_ref[2]) * half, half), half)
        resid_ref[...] = x_ref[0].astype(jnp.float32) + matmul(heads_ref[:, :head], out_w[...])
        rest_heads = heads_ref[:, head:]
        at = width
        for where, trio in ((mine, (a_m, b_m, c_m)), (theirs, (a_t, b_t, c_t))):
            w = jnp.concatenate([r[at : at + head] for r in trio], axis=0)
            resid_ref[:, where] += matmul(rest_heads, w)
        normed = bf(normalise(resid_ref[...], norm_ref[2:3], norm_ref[3:4]))

        def act(v):
            return bf(0.5 * v * (1.0 + jnp.tanh(0.5 * v)))

        up_ref[:, : width] = act(matmul(normed, up_w[...]))
        for k, r in enumerate((a_m, a_t, b_m, b_t, c_m, c_t)):
            lo = width + k * half
            up_ref[:, lo : lo + half] = act(matmul(normed, r[:width]))
        at = width + head
        lows, highs = [down_w[:, :half]], [down_w[:, half:]]
        for r, base in ((a_m, at), (a_t, at), (b_m, at), (b_t, at), (d_m, 0), (d_t, 0)):
            lows.append(r[base : base + half])
            highs.append(r[base + half : base + 2 * half])
        hidden = up_ref[...]
        resid_ref[:, :half] += matmul(hidden, jnp.concatenate(lows, axis=0))
        resid_ref[:, half:] += matmul(hidden, jnp.concatenate(highs, axis=0))
        for r in range(HEADS):
            col = lax.rem(place_ref[3] + r, HEADS)
            cols = pl.ds(pl.multiple_of(col * head, head), head)
            o_ref[r] = bf(resid_ref[:, cols])


def attend(place, near, count, state, norms, query, kv, weights):
    rows, width = query.shape
    blocks = rows // NODE_BLK
    held = pl.BlockSpec(memory_space=pltpu.VMEM)

    def neighbour(j):
        return pl.BlockSpec(
            (1, NODE_BLK, kv.shape[2]), lambda i, p, n, c: (n[i * KMAX + j], 0, 0)
        )

    return pl.pallas_call(
        main_kernel,
        grid_spec=pltpu.PrefetchScalarGridSpec(
            num_scalar_prefetch=3,
            grid=(blocks,),
            in_specs=[
                pl.BlockSpec((1, rows, width), lambda i, p, n, c: (p[0], p[1], 0)),
                held,
                pl.BlockSpec((NODE_BLK, width), lambda i, p, n, c: (i, 0)),
            ]
            + [neighbour(j) for j in range(KMAX)]
            + [held] * len(weights),
            out_specs=pl.BlockSpec((HEADS, rows, width // HEADS), lambda i, p, n, c: (0, 0, 0)),
            scratch_shapes=[
                pltpu.VMEM((rows, width), jnp.bfloat16),
                pltpu.VMEM((rows, width), jnp.float32),
                pltpu.VMEM((rows, 4 * width), jnp.bfloat16),
            ],
        ),
        out_shape=jax.ShapeDtypeStruct((HEADS, rows, width // HEADS), jnp.bfloat16),
        name="attend_and_mlp",
        compiler_params=pltpu.CompilerParams(vmem_limit_bytes=VMEM_LIMIT),
        cost_estimate=pl.CostEstimate(
            flops=rows * width * (4 * KMAX * NODE_BLK + 2 * width + 16 * width),
            bytes_accessed=16 * 1024 * 1024,
            transcendentals=rows * HEADS * KMAX * NODE_BLK,
        ),
    )(place, near, count, state, norms, query, *([kv] * KMAX), *weights)


def place_kernel(place_ref, own, a, b, c, o_ref):
    rank = place_ref[3]
    for off, r in ((0, own), (3, a), (1, b), (2, c)):
        o_ref[lax.rem(rank + off, HEADS)] = r[...]


def local(
    state, norm_gain, norm_shift, qkv_weight, out_weight, up_weight, down_weight, neighbours, counts
):
    samples, row_count, width = state.shape
    per_dev = row_count // NODE_BLK
    doms = lax.axis_size("dom")
    tps = lax.axis_size("tp")
    dom = lax.axis_index("dom")
    rank = lax.axis_index("tp")
    par = lax.rem(dom, 2)
    per_sample = tps // samples
    sample = rank // per_sample
    share = lax.rem(rank, per_sample)
    rows = row_count // per_sample
    own_blocks = rows // NODE_BLK
    place = jnp.stack([sample, share, par, rank]).astype(jnp.int32)

    def hop(v, pairs):
        return lax.ppermute(v, "dom", pairs)

    def sign(i):
        return 1 if i % 2 == 0 else -1

    def swap(v):
        return hop(v, [(i ^ 1, i) for i in range(doms)])

    def near(v):
        return hop(v, [((i + 2 * sign(i)) % doms, i) for i in range(doms)])

    def far(v):
        return hop(v, [((i - 2 * sign(i)) % doms, i) for i in range(doms)])

    def up(v):
        return lax.ppermute(v, "tp", [(i, (i + 1) % tps) for i in range(tps)])

    def down(v):
        return lax.ppermute(v, "tp", [((i + 1) % tps, i) for i in range(tps)])

    def across(v):
        return lax.ppermute(v, "tp", [(i, (i + 2) % tps) for i in range(tps)])

    qkv = jnp.transpose(qkv_weight, (1, 0, 2))
    w1, w2 = up(qkv), down(qkv)
    mid = width // 2
    w3a, w3b = up(w1[:, :mid]), down(w2[:, mid:])
    qkv_all = (qkv, w1, w2, w3a, w3b)

    own = lax.dynamic_index_in_dim(state, sample, 0, keepdims=False)
    partner = swap(own)
    near_rows = near(own)
    own_late, near_rows = lax.optimization_barrier((own, near_rows))
    far_rows = far(own_late)
    relay = swap(near_rows)

    up_half = lax.dynamic_slice_in_dim(up_weight, par * mid, mid, 1)
    out_half = lax.dynamic_slice_in_dim(out_weight, par * mid, mid, 1)
    down_half = lax.dynamic_slice_in_dim(down_weight, par * mid, mid, 0)
    pack = jnp.concatenate([up_half, out_half, down_half[:, :mid], down_half[:, mid:]], axis=0)
    pack, w1_done, w2_done = lax.optimization_barrier((pack, w1, w2))
    cut = width + NODE_BLK
    a_m, b_m = up(pack), down(pack)
    c_m, d_m = up(a_m[:cut]), down(b_m[cut:])
    a_t, b_t, c_t, d_t = swap(a_m), swap(b_m), swap(c_m), swap(d_m)

    norms = jnp.concatenate(
        [
            lax.dynamic_index_in_dim(v, sample, 1)[i]
            for i in range(2)
            for v in (norm_gain, norm_shift)
        ],
        axis=0,
    )
    slots = 5
    kv = project_kv(own, norms, qkv_all, None, 0, per_dev, slots)
    kv = project_kv(partner, norms, qkv_all, kv, 1, per_dev, slots)
    query = project_q(place, state, norms, qkv_all, rows)
    kv = project_kv(near_rows, norms, qkv_all, kv, 2, per_dev, slots)
    kv = project_kv(relay, norms, qkv_all, kv, 4, per_dev, slots)
    kv = project_kv(far_rows, norms, qkv_all, kv, 3, per_dev, slots)

    listed = lax.dynamic_slice_in_dim(neighbours, share * own_blocks, own_blocks, 0)
    count = lax.dynamic_slice_in_dim(counts, share * own_blocks, own_blocks, 0)
    step = jnp.mod(listed // per_dev - dom + 2, doms) - 2
    slot = jnp.mod(jnp.where(par == 0, step, -step), slots)
    where = (slot * per_dev + jnp.mod(listed, per_dev)).astype(jnp.int32).reshape(-1)

    weights = (out_weight, up_weight, down_weight, a_m, b_m, c_m, d_m, a_t, b_t, c_t, d_t)
    mine = attend(place, where, count, state, norms, query, kv, weights)

    got = (mine[0], up(mine[1]), down(mine[3]), across(mine[2]))
    held = pl.BlockSpec(memory_space=pltpu.VMEM)
    out = pl.pallas_call(
        place_kernel,
        in_specs=[pl.BlockSpec(memory_space=pltpu.SMEM)] + [held] * 4,
        out_specs=held,
        out_shape=jax.ShapeDtypeStruct((tps, rows, width // tps), jnp.bfloat16),
        name="place_rows",
        cost_estimate=pl.CostEstimate(flops=0, bytes_accessed=4 * rows * width, transcendentals=0),
    )(place, *got)
    return out.reshape(samples, row_count, width // tps)


def solution(mesh):
    placed = (
        P(None, "dom", None),
        P(),
        P(),
        P(None, None, "tp"),
        P("tp", None),
        P(None, "tp"),
        P("tp", None),
        P("dom", None),
        P("dom"),
    )
    return jax.shard_map(
        local, mesh=mesh, in_specs=placed, out_specs=P(None, "dom", "tp"), check_vma=False
    )
```

time: 213 us -> 121 us (0.57)
  waiting for transfers between devices: 125 us -> 23.3 us
  Pallas kernels: 0 us -> 39.4 us
  starting transfers between devices: 9.43 us -> 34 us
  local copies, waits for them, and re-layouts: 35.7 us -> 21 us
  matrix products: 13.7 us -> 0 us
  between operations: 13.6 us -> 0.24 us
  other arithmetic: 14.9 us -> 2.51 us
    psum x1 -> x0, waiting for transfers between devices: 68.5 us -> none  [local(): lax.psum(partial_value.astype(jnp.bfloat16), 'tp').astype(jnp.float32)]
    pallas_call x0 -> x8, Pallas kernels: none -> 39.4 us  [the longest x5 19.9 us: project_kv(): pl.pallas_call(kv_kernel, grid=(steps,), in_specs=specs, out_specs=pl.Blo...]
    unnamed x3 -> x0, waiting for transfers between devices: 32.3 us -> none
    ppermute x4 -> x19, starting transfers between devices: 9.35 us -> 34 us  [the longest x8 26 us: hop(): return lax.ppermute(v, 'dom', pairs)]
    dot_general x5 -> x0, matrix products: 13.7 us -> none  [the longest x1 5.49 us: local(): jnp.einsum('srf,fd->srd', hidden, down_weight, preferred_element_type=jnp...]
    unnamed x32, local copies, waits for them, and re-layouts: 18.1 us -> 7.33 us
    gather x1 -> x0, local copies, waits for them, and re-layouts: 8.01 us -> none  [local(): chosen = window[window_idx]]
    reduce_sum x4 -> x0, other arithmetic: 7.51 us -> none  [the longest x2 3.44 us: layer_norm(): spread = jnp.mean(centred * centred, axis=-1, keepdims=True)]
  transfers between devices with their start and end apart: 6 -> 19, of which waited for: 4 -> 7; matrix products, arithmetic and copies ran while one was open for 4% -> 10% of each run, Pallas kernels for 0% -> 18%
where the time goes in v1:
time: 121 us
  Pallas kernels  39.4 us (33%)
  starting transfers between devices  34 us (28%)
  waiting for transfers between devices  23.3 us (19%)
  local copies, waits for them, and re-layouts  21 us (17%)
  other arithmetic  2.51 us (2%)
    ppermute x8, starting transfers between devices, hop(): return lax.ppermute(v, 'dom', pairs)  26 us
    pallas_call x5, Pallas kernels, project_kv(): pl.pallas_call(kv_kernel, grid=(steps,), in_specs=specs, out_specs=pl.Blo...  19.9 us
    ppermute x5, waiting for transfers between devices, up(): return lax.ppermute(v, 'tp', [(i, (i + 1) % tps) for i in range(tps)])  15.5 us
    pallas_call x1, Pallas kernels, attend(): pl.pallas_call(main_kernel, grid_spec=pltpu.PrefetchScalarGridSpec(num_sc...  15.4 us
    unnamed x32, local copies, waits for them, and re-layouts  7.33 us
    ppermute x5, waiting for transfers between devices, down(): return lax.ppermute(v, 'tp', [((i + 1) % tps, i) for i in range(tps)])  7.04 us
    ppermute x5, starting transfers between devices, down(): return lax.ppermute(v, 'tp', [((i + 1) % tps, i) for i in range(tps)])  6.37 us
    slice x2, local copies, waits for them, and re-layouts, local(): c_m, d_m = (up(a_m[:cut]), down(b_m[cut:]))  2.66 us
  transfers between devices with their start and end apart: 19, of which 7 were waited for; matrix products, arithmetic and copies ran while one was open for 10% of the time, Pallas kernels for 18%

profile of v1, /device:TPU:1, one launch (start us, length us, event | category | flops | bytes accessed | tf_op | source)
XLA Modules:
  0.0 120.5 jit_solution(2601023921263262932)
XLA Ops:
  0.0 2.3 %dynamic-slice_bitcast_fusion.x_ref = bf16[1024,512]{1,0:T(8,128)(2,1)} fusion(bf16[2,1024,512]{2,1,0:T(8,128)(2,1)} %x_ref.3, s32[]{:T(128)S(6)} %select_n.58), kind=kLoop, calls=%fused_computation | loop fusion | bytes 2097156 | tf_op jit(solution)/shard_map/jit(dynamic_index_in_dim)/squeeze | solution.py:264
  2.3 2.0 %collective-permute-start.4 = (bf16[1024,512]{1,0:T(8,128)(2,1)}, bf16[1024,512]{1,0:T(8,128)(2,1)}, u32[]{:S(2)}, u32[]{:S(2)}) collective-permute-start(bf16[1024,512]{1,0:T(8,128)(2,1)} %dynamic-slice_bitcast_fusion.x_ref), channel_id=1, source_target_pairs={{8,0},{252,4},{16,8},{4,12},{24,16},{12,20},{32,24},{20,28},{40,32... | collective-permute-start | bytes 3145736 | tf_op jit(solution)/shard_map/ppermute | solution.py:235
  10.7 1.7 %pad_maximum_fusion = bf16[1152,256]{1,0:T(8,128)(2,1)} fusion(bf16[256,256]{1,0:T(8,128)(2,1)S(1)} %get-tuple-element.16, bf16[256,256]{1,0:T(8,128)(2,1)S(1)} %get-tuple-element.15, bf16[128,256]{1,0:T(8,128)(2,1)} %constant_dynamic-slice_fusion.3, bf16[512,256]{1,0:T(8,128)(2,1)S(1)} %constant_dynamic-slice_fusion.4), kind=kLoop, calls=%fused_computation.1 | loop fusion | flops 2359296 | bytes 1179648 | tf_op jit(solution)/shard_map/concatenate | solution.py:274
  12.7 2.3 %collective-permute-start.9 = (bf16[1152,256]{1,0:T(8,128)(2,1)}, bf16[1152,256]{1,0:T(8,128)(2,1)}, u32[]{:S(2)}, u32[]{:S(2)}) collective-permute-start(bf16[1152,256]{1,0:T(8,128)(2,1)} %pad_maximum_fusion), channel_id=1, source_target_pairs={{1,0},{2,1},{3,2},{0,3},{5,4},{6,5},{7,6},{4,7},{9,8},{10,9},{11,1... | collective-permute-start | bytes 1769480 | tf_op jit(solution)/shard_map/ppermute | solution.py:253
  14.9 13.4 %collective-permute-start.7 = (bf16[1024,512]{1,0:T(8,128)(2,1)}, bf16[1024,512]{1,0:T(8,128)(2,1)}, u32[]{:S(2)}, u32[]{:S(2)}) collective-permute-start(bf16[1024,512]{1,0:T(8,128)(2,1)} %dynamic-slice_bitcast_fusion.x_ref), channel_id=1, source_target_pairs={{4,0},{0,4},{12,8},{8,12},{20,16},{16,20},{28,24},{24,28},{36,32},... | collective-permute-start | bytes 3145736 | tf_op jit(solution)/shard_map/ppermute | solution.py:235
  29.5 5.3 %collective-permute-start.5 = (bf16[1024,512]{1,0:T(8,128)(2,1)}, bf16[1024,512]{1,0:T(8,128)(2,1)}, u32[]{:S(2)}, u32[]{:S(2)}) collective-permute-start(bf16[1024,512]{1,0:T(8,128)(2,1)} %dynamic-slice_bitcast_fusion.x_ref), channel_id=1, source_target_pairs={{248,0},{12,4},{0,8},{20,12},{8,16},{28,20},{16,24},{36,28},{24,32... | collective-permute-start | bytes 3145736 | tf_op jit(solution)/shard_map/ppermute | solution.py:235
  35.4 1.7 %slice.59 = bf16[512,256]{1,0:T(8,128)(2,1)} slice(bf16[1152,256]{1,0:T(8,128)(2,1)} %collective-permute-done.9.rest_12_), slice={[640:1152], [0:256]} | slice | bytes 524288 | tf_op jit(solution)/shard_map/slice | solution.py:278
  37.1 11.9 %collective-permute-done.2.w3a = bf16[3,256,128]{2,1,0:T(8,128)(2,1)S(1)} collective-permute-done((bf16[3,256,128]{2,1,0:T(8,128)(2,1)}, bf16[3,256,128]{2,1,0:T(8,128)(2,1)S(1)}, u32[]{:S(2)}, u32[]{:S(2)}) %collective-permute-start.2) | collective-permute-done | bytes 196640 | tf_op jit(solution)/shard_map/ppermute | solution.py:250
  52.8 2.3 %collective-permute-done.3.w3b = bf16[3,256,128]{2,1,0:T(8,128)(2,1)} collective-permute-done((bf16[3,256,128]{2,1,0:T(8,128)(2,1)}, bf16[3,256,128]{2,1,0:T(8,128)(2,1)}, u32[]{:S(2)}, u32[]{:S(2)}) %collective-permute-start.3) | collective-permute-done | bytes 196640 | tf_op jit(solution)/shard_map/ppermute | solution.py:253
  55.1 2.8 %collective-permute-start.12 = (bf16[1152,256]{1,0:T(8,128)(2,1)}, bf16[1152,256]{1,0:T(8,128)(2,1)S(1)}, u32[]{:S(2)}, u32[]{:S(2)}) collective-permute-start(bf16[1152,256]{1,0:T(8,128)(2,1)} %collective-permute-done.8.rest_11_), channel_id=1, source_target_pairs={{4,0},{0,4},{12,8},{8,12},{20,16},{16,20},{28,24},{24,28},{36,32},... | collective-permute-start | bytes 1769480 | tf_op jit(solution)/shard_map/ppermute | solution.py:235
  57.9 2.8 %collective-permute-done.11.rest_14_ = bf16[512,256]{1,0:T(8,128)(2,1)} collective-permute-done((bf16[512,256]{1,0:T(8,128)(2,1)}, bf16[512,256]{1,0:T(8,128)(2,1)}, u32[]{:S(2)}, u32[]{:S(2)}) %collective-permute-start.11) | collective-permute-done | bytes 262176 | tf_op jit(solution)/shard_map/ppermute | solution.py:253
  62.3 2.2 %q_rows.1.q_ref = bf16[512,512]{1,0:T(8,128)(2,1)S(1)} custom-call(s32[4]{0:T(128)S(1)} %pad_add_fusion.place_ref, bf16[2,1024,512]{2,1,0:T(8,128)(2,1)S(1)} %copy-done.2, f32[4,512]{1,0:T(4,128)S(1)} %pad_maximum_fusion.1.norm_ref, bf16[3,512,128]{2,1,0:T(8,128)(2,1)S(1)} %bitcast.26, bf16[3,512,128]{2,1,0:T(8,128)(2,1)S(1)} %collective-permute-done.w1, ...), custom_call_target="tpu_custom_call" | custom-call | flops 268435456 | bytes 1048576 | tf_op jit(solution)/shard_map/q_rows/pallas_call | solution.py:84
  65.3 4.0 %kv_rows.5.rest_0_ = bf16[40,128,1024]{2,1,0:T(8,128)(2,1)S(1)} custom-call(bf16[1024,512]{1,0:T(8,128)(2,1)} %dynamic-slice_bitcast_fusion.x_ref, f32[4,512]{1,0:T(4,128)S(1)} %pad_maximum_fusion.1.norm_ref, bf16[3,512,128]{2,1,0:T(8,128)(2,1)S(1)} %bitcast.27, bf16[3,512,128]{2,1,0:T(8,128)(2,1)S(1)} %collective-permute-done.w1, ...), custom_call_target="tpu_custom_call" | custom-call | flops 1073741824 | bytes 3145728 | tf_op jit(solution)/shard_map/kv_rows/pallas_call | solution.py:58
  69.6 4.0 %kv_rows.6.rest_0_ = bf16[40,128,1024]{2,1,0:T(8,128)(2,1)S(1)} custom-call(bf16[1024,512]{1,0:T(8,128)(2,1)} %collective-permute-done.7.x_ref, f32[4,512]{1,0:T(4,128)S(1)} %pad_maximum_fusion.1.norm_ref, bf16[3,512,128]{2,1,0:T(8,128)(2,1)S(1)} %bitcast.28, bf16[3,512,128]{2,1,0:T(8,128)(2,1)S(1)} %collective-permute-done.w1, ...), custom_call_target="tpu_custom_call", output_to_operand_aliasing={{}: (7, {})} | custom-call | flops 1073741824 | bytes 3145728 | tf_op jit(solution)/shard_map/kv_rows/pallas_call | solution.py:58
  74.2 4.0 %kv_rows.7.rest_0_ = bf16[40,128,1024]{2,1,0:T(8,128)(2,1)S(1)} custom-call(bf16[1024,512]{1,0:T(8,128)(2,1)} %collective-permute-done.4.x_ref, f32[4,512]{1,0:T(4,128)S(1)} %pad_maximum_fusion.1.norm_ref, bf16[3,512,128]{2,1,0:T(8,128)(2,1)S(1)} %bitcast.29, bf16[3,512,128]{2,1,0:T(8,128)(2,1)S(1)} %collective-permute-done.w1, ...), custom_call_target="tpu_custom_call", output_to_operand_aliasing={{}: (7, {})} | custom-call | flops 1073741824 | bytes 3145728 | tf_op jit(solution)/shard_map/kv_rows/pallas_call | solution.py:58
  78.1 4.0 %kv_rows.8.rest_0_ = bf16[40,128,1024]{2,1,0:T(8,128)(2,1)S(1)} custom-call(bf16[1024,512]{1,0:T(8,128)(2,1)} %collective-permute-done.6.x_ref, f32[4,512]{1,0:T(4,128)S(1)} %pad_maximum_fusion.1.norm_ref, bf16[3,512,128]{2,1,0:T(8,128)(2,1)S(1)} %bitcast.30, bf16[3,512,128]{2,1,0:T(8,128)(2,1)S(1)} %collective-permute-done.w1, ...), custom_call_target="tpu_custom_call", output_to_operand_aliasing={{}: (7, {})} | custom-call | flops 1073741824 | bytes 3145728 | tf_op jit(solution)/shard_map/kv_rows/pallas_call | solution.py:58
  82.2 4.0 %kv_rows.9.rest_0_.rest_1_.rest_2_.rest_3_.rest_4_.rest_5_.rest_6_.rest_7_ = bf16[40,128,1024]{2,1,0:T(8,128)(2,1)S(1)} custom-call(bf16[1024,512]{1,0:T(8,128)(2,1)} %collective-permute-done.5.x_ref, f32[4,512]{1,0:T(4,128)S(1)} %pad_maximum_fusion.1.norm_ref, bf16[3,512,128]{2,1,0:T(8,128)(2,1)S(1)} %bitcast.31, ...), custom_call_target="tpu_custom_call", output_to_operand_aliasing={{}: (7, {})} | custom-call | flops 1073741824 | bytes 3145728 | tf_op jit(solution)/shard_map/kv_rows/pallas_call | solution.py:58
  86.2 4.0 %copy-done = bf16[40,128,1024]{2,1,0:T(8,128)(2,1)} copy-done((bf16[40,128,1024]{2,1,0:T(8,128)(2,1)}, bf16[40,128,1024]{2,1,0:T(8,128)(2,1)S(1)}, u32[]{:S(2)}) %copy-start) | copy-done | bytes 10485784
  92.1 15.4 %attend_and_mlp.1 = bf16[4,512,128]{2,1,0:T(8,128)(2,1)} custom-call(s32[4]{0:T(128)} %copy-done.5, s32[32]{0:T(128)} %reshape.6.near_ref, s32[4]{0:T(128)} %dynamic_slice.29.count_ref, bf16[2,1024,512]{2,1,0:T(8,128)(2,1)} %x_ref.3, f32[4,512]{1,0:T(4,128)} %copy-done.4, bf16[512,512]{1,0:T(8,128)(2,1)} %copy-done.3, bf16[40,128,1024]{2,1,0:T(8,128)(2,1)} %copy-done, ...), custom_call_target="tpu_custom_call" | custom-call | flops 3489660928 | bytes 16777216 | tf_op jit(solution)/shard_map/attend_and_mlp/pallas_call | solution.py:181
  107.5 1.8 %slice_bitcast_fusion = (bf16[512,128]{1,0:T(8,128)(2,1)S(1)}, bf16[512,128]{1,0:T(8,128)(2,1)S(1)}, bf16[512,128]{1,0:T(8,128)(2,1)S(1)}, bf16[512,128]{1,0:T(8,128)(2,1)}) fusion(bf16[4,512,128]{2,1,0:T(8,128)(2,1)} %attend_and_mlp.1), kind=kLoop, calls=%fused_computation.2 | loop fusion | bytes 1048576 | tf_op jit(solution)/shard_map/squeeze | solution.py:306
  109.3 2.7 %collective-permute-start.17 = (bf16[512,128]{1,0:T(8,128)(2,1)S(1)}, bf16[512,128]{1,0:T(8,128)(2,1)S(1)}, u32[]{:S(2)}, u32[]{:S(2)}) collective-permute-start(bf16[512,128]{1,0:T(8,128)(2,1)S(1)} %get-tuple-element.12), channel_id=1, source_target_pairs={{1,0},{2,1},{3,2},{0,3},{5,4},{6,5},{7,6},{4,7},{9,8},{10,9},{11,1... | collective-permute-start | bytes 393224 | tf_op jit(solution)/shard_map/ppermute | solution.py:253
  112.0 3.6 %collective-permute-done.16.a = bf16[512,128]{1,0:T(8,128)(2,1)S(1)} collective-permute-done((bf16[512,128]{1,0:T(8,128)(2,1)S(1)}, bf16[512,128]{1,0:T(8,128)(2,1)S(1)}, u32[]{:S(2)}, u32[]{:S(2)}) %collective-permute-start.16) | collective-permute-done | bytes 131104 | tf_op jit(solution)/shard_map/ppermute | solution.py:250
  115.6 1.6 %collective-permute-done.17.b = bf16[512,128]{1,0:T(8,128)(2,1)S(1)} collective-permute-done((bf16[512,128]{1,0:T(8,128)(2,1)S(1)}, bf16[512,128]{1,0:T(8,128)(2,1)S(1)}, u32[]{:S(2)}, u32[]{:S(2)}) %collective-permute-start.17) | collective-permute-done | bytes 131104 | tf_op jit(solution)/shard_map/ppermute | solution.py:253
  118.6 1.9 %place_rows.1 = bf16[4,512,128]{2,1,0:T(8,128)(2,1)} custom-call(s32[4]{0:T(128)} %copy-done.5, bf16[512,128]{1,0:T(8,128)(2,1)} %get-tuple-element.14.own, bf16[512,128]{1,0:T(8,128)(2,1)} %copy-done.11, bf16[512,128]{1,0:T(8,128)(2,1)} %copy-done.12, bf16[512,128]{1,0:T(8,128)(2,1)} %copy-done.13), custom_call_target="tpu_custom_call" | custom-call | bytes 1048576 | tf_op jit(solution)/shard_map/place_rows/pallas_call | solution.py:308
  (70 shorter events, 18.7 us)
Async XLA Ops:
  0.0 4.4 %copy-start.1 = (bf16[512,3,128]{2,0,1:T(8,128)(2,1)S(1)}, bf16[512,3,128]{2,0,1:T(8,128)(2,1)}, u32[]{:S(2)}) copy-start(bf16[512,3,128]{2,0,1:T(8,128)(2,1)} %param.12) | copy-start | bytes 1179652
  2.3 49.4 %copy-start.14 = (f32[2,2,512]{2,1,0:T(2,128)S(1)}, f32[2,2,512]{2,1,0:T(2,128)}, u32[]{:S(2)}) copy-start(f32[2,2,512]{2,1,0:T(2,128)} %param.10) | copy-start | bytes 24580
  2.3 49.4 %copy-start.15 = (f32[2,2,512]{2,1,0:T(2,128)S(1)}, f32[2,2,512]{2,1,0:T(2,128)}, u32[]{:S(2)}) copy-start(f32[2,2,512]{2,1,0:T(2,128)} %param.11) | copy-start | bytes 24580
  2.3 26.0 %collective-permute-start.4 = (bf16[1024,512]{1,0:T(8,128)(2,1)}, bf16[1024,512]{1,0:T(8,128)(2,1)}, u32[]{:S(2)}, u32[]{:S(2)}) collective-permute-start(bf16[1024,512]{1,0:T(8,128)(2,1)} %dynamic-slice_bitcast_fusion.x_ref), channel_id=1, source_target_pairs={{8,0},{252,4},{16,8},{4,12},{24,16},{12,20},{32,24},{20,28},{40,32... | collective-permute-start | bytes 3145736 | tf_op jit(solution)/shard_map/ppermute | solution.py:235
  4.4 8.0 %collective-permute-start = (bf16[3,512,128]{2,1,0:T(8,128)(2,1)S(1)}, bf16[3,512,128]{2,1,0:T(8,128)(2,1)S(1)}, u32[]{:S(2)}, u32[]{:S(2)}) collective-permute-start(bf16[3,512,128]{2,1,0:T(8,128)(2,1)S(1)} %bitcast.24), channel_id=1, source_target_pairs={{0,1},{1,2},{2,3},{3,0},{4,5},{5,6},{6,7},{7,4},{8,9},{9,10},{10,1... | collective-permute-start | bytes 1179656 | tf_op jit(solution)/shard_map/ppermute | solution.py:250
  5.7 7.0 %collective-permute-start.1 = (bf16[3,512,128]{2,1,0:T(8,128)(2,1)S(1)}, bf16[3,512,128]{2,1,0:T(8,128)(2,1)S(1)}, u32[]{:S(2)}, u32[]{:S(2)}) collective-permute-start(bf16[3,512,128]{2,1,0:T(8,128)(2,1)S(1)} %bitcast.25), channel_id=1, source_target_pairs={{1,0},{2,1},{3,2},{0,3},{5,4},{6,5},{7,6},{4,7},{9,8},{10,9},{11,1... | collective-permute-start | bytes 1179656 | tf_op jit(solution)/shard_map/ppermute | solution.py:253
  7.1 55.2 %copy-start.2 = (bf16[2,1024,512]{2,1,0:T(8,128)(2,1)S(1)}, bf16[2,1024,512]{2,1,0:T(8,128)(2,1)}, u32[]{:S(2)}) copy-start(bf16[2,1024,512]{2,1,0:T(8,128)(2,1)} %x_ref.3) | copy-start | bytes 6291460
  12.7 16.8 %collective-permute-start.9 = (bf16[1152,256]{1,0:T(8,128)(2,1)}, bf16[1152,256]{1,0:T(8,128)(2,1)}, u32[]{:S(2)}, u32[]{:S(2)}) collective-permute-start(bf16[1152,256]{1,0:T(8,128)(2,1)} %pad_maximum_fusion), channel_id=1, source_target_pairs={{1,0},{2,1},{3,2},{0,3},{5,4},{6,5},{7,6},{4,7},{9,8},{10,9},{11,1... | collective-permute-start | bytes 1769480 | tf_op jit(solution)/shard_map/ppermute | solution.py:253
  14.9 40.2 %collective-permute-start.7 = (bf16[1024,512]{1,0:T(8,128)(2,1)}, bf16[1024,512]{1,0:T(8,128)(2,1)}, u32[]{:S(2)}, u32[]{:S(2)}) collective-permute-start(bf16[1024,512]{1,0:T(8,128)(2,1)} %dynamic-slice_bitcast_fusion.x_ref), channel_id=1, source_target_pairs={{4,0},{0,4},{12,8},{8,12},{20,16},{16,20},{28,24},{24,28},{36,32},... | collective-permute-start | bytes 3145736 | tf_op jit(solution)/shard_map/ppermute | solution.py:235
  28.3 20.7 %collective-permute-start.8 = (bf16[1152,256]{1,0:T(8,128)(2,1)}, bf16[1152,256]{1,0:T(8,128)(2,1)}, u32[]{:S(2)}, u32[]{:S(2)}) collective-permute-start(bf16[1152,256]{1,0:T(8,128)(2,1)} %pad_maximum_fusion), channel_id=1, source_target_pairs={{0,1},{1,2},{2,3},{3,0},{4,5},{5,6},{6,7},{7,4},{8,9},{9,10},{10,1... | collective-permute-start | bytes 1769480 | tf_op jit(solution)/shard_map/ppermute | solution.py:250
  28.3 45.3 %collective-permute-start.6 = (bf16[1024,512]{1,0:T(8,128)(2,1)}, bf16[1024,512]{1,0:T(8,128)(2,1)}, u32[]{:S(2)}, u32[]{:S(2)}) collective-permute-start(bf16[1024,512]{1,0:T(8,128)(2,1)} %collective-permute-done.4.x_ref), channel_id=1, source_target_pairs={{4,0},{0,4},{12,8},{8,12},{20,16},{16,20},{28,24},{24,28},{36,32},... | collective-permute-start | bytes 3145736 | tf_op jit(solution)/shard_map/ppermute | solution.py:235
  29.1 19.9 %collective-permute-start.2 = (bf16[3,256,128]{2,1,0:T(8,128)(2,1)}, bf16[3,256,128]{2,1,0:T(8,128)(2,1)S(1)}, u32[]{:S(2)}, u32[]{:S(2)}) collective-permute-start(bf16[3,256,128]{2,1,0:T(8,128)(2,1)} %slice.56), channel_id=1, source_target_pairs={{0,1},{1,2},{2,3},{3,0},{4,5},{5,6},{6,7},{7,4},{8,9},{9,10},{10,1... | collective-permute-start | bytes 589832 | tf_op jit(solution)/shard_map/ppermute | solution.py:250
  29.5 52.7 %collective-permute-start.5 = (bf16[1024,512]{1,0:T(8,128)(2,1)}, bf16[1024,512]{1,0:T(8,128)(2,1)}, u32[]{:S(2)}, u32[]{:S(2)}) collective-permute-start(bf16[1024,512]{1,0:T(8,128)(2,1)} %dynamic-slice_bitcast_fusion.x_ref), channel_id=1, source_target_pairs={{248,0},{12,4},{0,8},{20,12},{8,16},{28,20},{16,24},{36,28},{24,32... | collective-permute-start | bytes 3145736 | tf_op jit(solution)/shard_map/ppermute | solution.py:235
  49.0 6.1 %collective-permute-start.3 = (bf16[3,256,128]{2,1,0:T(8,128)(2,1)}, bf16[3,256,128]{2,1,0:T(8,128)(2,1)}, u32[]{:S(2)}, u32[]{:S(2)}) collective-permute-start(bf16[3,256,128]{2,1,0:T(8,128)(2,1)} %slice.57), channel_id=1, source_target_pairs={{1,0},{2,1},{3,2},{0,3},{5,4},{6,5},{7,6},{4,7},{9,8},{10,9},{11,1... | collective-permute-start | bytes 589832 | tf_op jit(solution)/shard_map/ppermute | solution.py:253
  49.0 11.7 %collective-permute-start.11 = (bf16[512,256]{1,0:T(8,128)(2,1)}, bf16[512,256]{1,0:T(8,128)(2,1)}, u32[]{:S(2)}, u32[]{:S(2)}) collective-permute-start(bf16[512,256]{1,0:T(8,128)(2,1)} %slice.59), channel_id=1, source_target_pairs={{1,0},{2,1},{3,2},{0,3},{5,4},{6,5},{7,6},{4,7},{9,8},{10,9},{11,1... | collective-permute-start | bytes 786440 | tf_op jit(solution)/shard_map/ppermute | solution.py:253
  55.1 14.2 %collective-permute-start.10 = (bf16[640,256]{1,0:T(8,128)(2,1)S(1)}, bf16[640,256]{1,0:T(8,128)(2,1)S(1)}, u32[]{:S(2)}, u32[]{:S(2)}) collective-permute-start(bf16[640,256]{1,0:T(8,128)(2,1)S(1)} %slice.58), channel_id=1, source_target_pairs={{0,1},{1,2},{2,3},{3,0},{4,5},{5,6},{6,7},{7,4},{8,9},{9,10},{10,1... | collective-permute-start | bytes 983048 | tf_op jit(solution)/shard_map/ppermute | solution.py:250
  55.1 27.0 %copy-start.4 = (f32[4,512]{1,0:T(4,128)}, f32[4,512]{1,0:T(4,128)S(1)}, u32[]{:S(2)}) copy-start(f32[4,512]{1,0:T(4,128)S(1)} %pad_maximum_fusion.1.norm_ref) | copy-start | bytes 24580
  55.1 35.0 %collective-permute-start.12 = (bf16[1152,256]{1,0:T(8,128)(2,1)}, bf16[1152,256]{1,0:T(8,128)(2,1)S(1)}, u32[]{:S(2)}, u32[]{:S(2)}) collective-permute-start(bf16[1152,256]{1,0:T(8,128)(2,1)} %collective-permute-done.8.rest_11_), channel_id=1, source_target_pairs={{4,0},{0,4},{12,8},{8,12},{20,16},{16,20},{28,24},{24,28},{36,32},... | collective-permute-start | bytes 1769480 | tf_op jit(solution)/shard_map/ppermute | solution.py:235
  60.7 29.5 %collective-permute-start.13 = (bf16[1152,256]{1,0:T(8,128)(2,1)}, bf16[1152,256]{1,0:T(8,128)(2,1)S(1)}, u32[]{:S(2)}, u32[]{:S(2)}) collective-permute-start(bf16[1152,256]{1,0:T(8,128)(2,1)} %collective-permute-done.9.rest_12_), channel_id=1, source_target_pairs={{4,0},{0,4},{12,8},{8,12},{20,16},{16,20},{28,24},{24,28},{36,32},... | collective-permute-start | bytes 1769480 | tf_op jit(solution)/shard_map/ppermute | solution.py:235
  69.3 20.9 %collective-permute-start.14 = (bf16[640,256]{1,0:T(8,128)(2,1)S(1)}, bf16[640,256]{1,0:T(8,128)(2,1)S(1)}, u32[]{:S(2)}, u32[]{:S(2)}) collective-permute-start(bf16[640,256]{1,0:T(8,128)(2,1)S(1)} %collective-permute-done.10.rest_13_), channel_id=1, source_target_pairs={{4,0},{0,4},{12,8},{8,12},{20,16},{16,20},{28,24},{24,28},{36,32},... | collective-permute-start | bytes 983048 | tf_op jit(solution)/shard_map/ppermute | solution.py:235
  73.6 16.6 %collective-permute-start.15 = (bf16[512,256]{1,0:T(8,128)(2,1)}, bf16[512,256]{1,0:T(8,128)(2,1)S(1)}, u32[]{:S(2)}, u32[]{:S(2)}) collective-permute-start(bf16[512,256]{1,0:T(8,128)(2,1)} %collective-permute-done.11.rest_14_), channel_id=1, source_target_pairs={{4,0},{0,4},{12,8},{8,12},{20,16},{16,20},{28,24},{24,28},{36,32},... | collective-permute-start | bytes 786440 | tf_op jit(solution)/shard_map/ppermute | solution.py:235
  109.3 6.3 %collective-permute-start.16 = (bf16[512,128]{1,0:T(8,128)(2,1)S(1)}, bf16[512,128]{1,0:T(8,128)(2,1)S(1)}, u32[]{:S(2)}, u32[]{:S(2)}) collective-permute-start(bf16[512,128]{1,0:T(8,128)(2,1)S(1)} %get-tuple-element.13), channel_id=1, source_target_pairs={{0,1},{1,2},{2,3},{3,0},{4,5},{5,6},{6,7},{7,4},{8,9},{9,10},{10,1... | collective-permute-start | bytes 393224 | tf_op jit(solution)/shard_map/ppermute | solution.py:250
  109.3 7.9 %collective-permute-start.17 = (bf16[512,128]{1,0:T(8,128)(2,1)S(1)}, bf16[512,128]{1,0:T(8,128)(2,1)S(1)}, u32[]{:S(2)}, u32[]{:S(2)}) collective-permute-start(bf16[512,128]{1,0:T(8,128)(2,1)S(1)} %get-tuple-element.12), channel_id=1, source_target_pairs={{1,0},{2,1},{3,2},{0,3},{5,4},{6,5},{7,6},{4,7},{9,8},{10,9},{11,1... | collective-permute-start | bytes 393224 | tf_op jit(solution)/shard_map/ppermute | solution.py:253
  112.0 5.9 %collective-permute-start.18 = (bf16[512,128]{1,0:T(8,128)(2,1)S(1)}, bf16[512,128]{1,0:T(8,128)(2,1)S(1)}, u32[]{:S(2)}, u32[]{:S(2)}) collective-permute-start(bf16[512,128]{1,0:T(8,128)(2,1)S(1)} %get-tuple-element.11), channel_id=1, source_target_pairs={{0,2},{1,3},{2,0},{3,1},{4,6},{5,7},{6,4},{7,5},{8,10},{9,11},{10,... | collective-permute-start | bytes 393224 | tf_op jit(solution)/shard_map/ppermute | solution.py:256
  (11 other events, 18.5 us)

commit v2 on v0

v2 whole, which is shorter than its diff:
```python
import functools
import math

import jax
import jax.numpy as jnp
from jax import lax
from jax.experimental import pallas as pl
from jax.experimental.pallas import tpu as pltpu
from jax.sharding import PartitionSpec as P

HEADS = 4
NODE_BLK = 128
KMAX = 8
ROWS = 512
MIB = 1024 * 1024

VMEM = pl.BlockSpec(memory_space=pltpu.VMEM)
SMEM = pl.BlockSpec(memory_space=pltpu.SMEM)
ANY = pl.BlockSpec(memory_space=pl.ANY)


def bf(v):
    return v.astype(jnp.bfloat16)


def matmul(a, b):
    return jnp.dot(a, b, preferred_element_type=jnp.float32)


def aligned(i, step):
    return pl.ds(pl.multiple_of(i * step, step), step)


def shape(dims, dtype=jnp.bfloat16):
    return jax.ShapeDtypeStruct(dims, dtype)


def in_hbm(dims, dtype=jnp.bfloat16):
    return pltpu.HBM(dims, dtype)


def cost(flops, nbytes, exps=0):
    return pl.CostEstimate(flops=flops, bytes_accessed=nbytes, transcendentals=exps)


def normalise(values, gain, shift):
    mean = jnp.mean(values, axis=-1, keepdims=True)
    centred = values - mean
    spread = jnp.mean(centred * centred, axis=-1, keepdims=True)
    return centred * lax.rsqrt(spread + 1e-05) * gain + shift


def prepare_kernel(
    place_ref, x_ref, gain_ref, shift_ref, up_ref, out_ref, down_ref, o_ref, pack_ref
):
    s = pl.ds(place_ref[0], 1)
    o_ref[...] = bf(normalise(x_ref[0].astype(jnp.float32), gain_ref[0, s], shift_ref[0, s]))

    @pl.when(pl.program_id(0) == 0)
    def _():
        at = 0
        for r in (up_ref, out_ref, down_ref):
            pack_ref[at : at + r.shape[0]] = r[...]
            at += r.shape[0]


def prepare(place, state, gain, shift, up_w, out_w, down_w):
    _, rows, width = state.shape
    pack_rows = up_w.shape[0] + out_w.shape[0] + down_w.shape[0]
    return pl.pallas_call(
        prepare_kernel,
        grid_spec=pltpu.PrefetchScalarGridSpec(
            num_scalar_prefetch=1,
            grid=(rows // ROWS,),
            in_specs=[pl.BlockSpec((1, ROWS, width), lambda i, p: (p[0], i, 0))] + [VMEM] * 5,
            out_specs=[
                pl.BlockSpec((ROWS, width), lambda i, p: (i, 0)),
                pl.BlockSpec((pack_rows, width), lambda i, p: (0, 0)),
            ],
        ),
        out_shape=[in_hbm((rows, width)), in_hbm((pack_rows, width))],
        name="prepare",
        cost_estimate=cost(10 * rows * width, 4 * (rows + pack_rows) * width),
    )(place, state, gain, shift, up_w, out_w, down_w)


def kv_first_kernel(place_ref, xa, xb, w0, w1, w2, w3m, w3t, kv_ref, q_ref, wkv_ref, wq_ref):
    i = pl.program_id(0)
    head = NODE_BLK
    par = place_ref[2]

    @pl.when(i == 0)
    def _():
        half = w3m.shape[1]
        for h in range(HEADS):
            at = (h // 2) * 4 * head + (h % 2) * head
            spots = ((0, wq_ref, h * head), (1, wkv_ref, at), (2, wkv_ref, at + 2 * head))
            for c, dst, col in spots:
                if h < 3:
                    dst[:, col : col + head] = (w0, w1, w2)[h][c]
                else:
                    dst[aligned(par, half), col : col + head] = w3m[c]
                    dst[aligned(1 - par, half), col : col + head] = w3t[c]

    x = jnp.where(i < 2, xa[...], xb[...])
    kv_ref[...] = bf(matmul(x, wkv_ref[...])).reshape(kv_ref.shape)

    @pl.when(i == place_ref[1])
    def _():
        q_ref[...] = bf(matmul(xa[...], wq_ref[...]))


def kv_first(place, xa, xb, weights):
    rows, width = xa.shape
    steps = rows // ROWS
    per_step = ROWS // NODE_BLK
    blocks = 2 * rows // NODE_BLK
    return pl.pallas_call(
        kv_first_kernel,
        grid_spec=pltpu.PrefetchScalarGridSpec(
            num_scalar_prefetch=1,
            grid=(2 * steps,),
            in_specs=[
                pl.BlockSpec((ROWS, width), lambda i, p: (jnp.minimum(i, steps - 1), 0)),
                pl.BlockSpec((ROWS, width), lambda i, p: (jnp.maximum(i - steps, 0), 0)),
            ]
            + [VMEM] * len(weights),
            out_specs=[
                pl.BlockSpec((per_step, NODE_BLK, 2 * width), lambda i, p: (i, 0, 0)),
                pl.BlockSpec((ROWS, width), lambda i, p: (0, 0)),
                pl.BlockSpec((width, 2 * width), lambda i, p: (0, 0)),
            ],
            scratch_shapes=[pltpu.VMEM((width, width), jnp.bfloat16)],
        ),
        out_shape=[
            in_hbm((blocks, NODE_BLK, 2 * width)),
            shape((ROWS, width)),
            shape((width, 2 * width)),
        ],
        name="kv_first",
        compiler_params=pltpu.CompilerParams(vmem_limit_bytes=24 * MIB),
        cost_estimate=cost(8 * rows * width * width, 8 * MIB),
    )(place, xa, xb, *weights)


def kv_second_kernel(xa, xb, wkv_ref, kv_ref):
    x = jnp.where(pl.program_id(0) < 2, xa[...], xb[...])
    kv_ref[...] = bf(matmul(x, wkv_ref[...])).reshape(kv_ref.shape)


def kv_second(xa, xb, wkv):
    rows, width = xa.shape
    steps = rows // ROWS
    per_step = ROWS // NODE_BLK
    blocks = 2 * rows // NODE_BLK
    return pl.pallas_call(
        kv_second_kernel,
        grid=(2 * steps,),
        in_specs=[
            pl.BlockSpec((ROWS, width), lambda i: (jnp.minimum(i, steps - 1), 0)),
            pl.BlockSpec((ROWS, width), lambda i: (jnp.maximum(i - steps, 0), 0)),
            VMEM,
        ],
        out_specs=pl.BlockSpec((per_step, NODE_BLK, 2 * width), lambda i: (i, 0, 0)),
        out_shape=in_hbm((blocks, NODE_BLK, 2 * width)),
        name="kv_second",
        compiler_params=pltpu.CompilerParams(vmem_limit_bytes=24 * MIB),
        cost_estimate=cost(8 * rows * width * width, 7 * MIB),
    )(xa, xb, wkv)


def main_kernel(
    place_ref, list_ref, count_ref, far_ref, gain_ref, shift_ref, q_ref, wkv_ref,
    kv_a, kv_b, state_ref, out_w, up_w, down_w, p1, p1s, p2, p2s,
    o0, o1, o2, o3,
    kv, rows_in, wall, heads_ref, resid_ref, hidden_ref, sems, *, doms, per_dev,
):
    sample, share, par, rank, dom = [place_ref[k] for k in range(5)]
    head = NODE_BLK
    rows, width = q_ref.shape
    half_pack = p2.shape[0]
    early = kv_a.shape[0]
    jobs = [
        (kv_a, kv.at[pl.ds(0, early)]),
        (kv_b, kv.at[pl.ds(early, early)]),
        (state_ref.at[sample, aligned(share, rows)], rows_in),
        (out_w, wall.at[0, pl.ds(width, head)]),
        (up_w, wall.at[0, pl.ds(0, width)]),
        (down_w, wall.at[0, pl.ds(width + head, width)]),
        (p1, wall.at[1]),
        (p1s, wall.at[2]),
        (p2, wall.at[3, aligned(par, half_pack)]),
        (p2s, wall.at[3, aligned(1 - par, half_pack)]),
    ]
    copies = [pltpu.make_async_copy(a, b, sems.at[k]) for k, (a, b) in enumerate(jobs)]
    for c in copies:
        c.start()

    kv[2 * early :] = bf(matmul(far_ref[...], wkv_ref[...])).reshape(
        (per_dev, NODE_BLK, 2 * width)
    )
    for c in copies[:2]:
        c.wait()

    scale = math.log2(math.e) / math.sqrt(head)
    blocks = rows // NODE_BLK
    for b in range(blocks):
        row = share * blocks + b
        count = count_ref[row]
        where = []
        for j in range(KMAX):
            entry = list_ref[row, j]
            part = lax.div(entry, per_dev)
            step = lax.rem(part - dom + (doms + 2), doms) - 2
            turned = jnp.where(par == 0, step, -step)
            slot = jnp.where(
                turned >= 0, jnp.where(turned == 0, 0, turned), jnp.where(turned == -1, 3, 4)
            )
            where.append(slot * per_dev + lax.rem(entry, per_dev))
        at = slice(b * NODE_BLK, (b + 1) * NODE_BLK)
        for pair in range(HEADS // 2):
            col = pair * 4 * head
            keys = jnp.concatenate([kv[i, :, col : col + 2 * head] for i in where], axis=0)
            vals = jnp.concatenate(
                [kv[i, :, col + 2 * head : col + 4 * head] for i in where], axis=0
            )
            q0 = q_ref[at, 2 * pair * head : (2 * pair + 1) * head]
            q1 = q_ref[at, (2 * pair + 1) * head : (2 * pair + 2) * head]
            zero = jnp.zeros_like(q0)
            query = jnp.concatenate(
                [jnp.concatenate([q0, zero], axis=1), jnp.concatenate([zero, q1], axis=1)], axis=0
            )
            scores = lax.dot_general(
                query, keys, (((1,), (1,)), ((), ())), preferred_element_type=jnp.float32
            )
            parts = [
                jnp.where(j < count, scores[:, j * NODE_BLK : (j + 1) * NODE_BLK], -1e30)
                for j in range(KMAX)
            ]
            top = jnp.max(functools.reduce(jnp.maximum, parts), axis=-1, keepdims=True)
            parts = [jnp.exp2((p - top) * scale) for p in parts]
            total = jnp.sum(functools.reduce(jnp.add, parts), axis=-1, keepdims=True)
            mixed = matmul(jnp.concatenate([bf(p) for p in parts], axis=1), vals) / total
            heads_ref[at, 2 * pair * head : (2 * pair + 1) * head] = bf(mixed[:head, :head])
            heads_ref[at, (2 * pair + 1) * head : (2 * pair + 2) * head] = bf(mixed[head:, head:])

    for c in copies[2:]:
        c.wait()
    out_all = jnp.concatenate([wall[h, width : width + head] for h in range(HEADS)], axis=0)
    resid_ref[...] = rows_in[...].astype(jnp.float32) + matmul(heads_ref[...], out_all)
    s = pl.ds(sample, 1)
    normed = bf(normalise(resid_ref[...], gain_ref[1, s], shift_ref[1, s]))
    for h in range(HEADS):
        v = matmul(normed, wall[h, :width])
        hidden_ref[:, h * width : (h + 1) * width] = bf(0.5 * v * (1.0 + jnp.tanh(0.5 * v)))
    down_all = jnp.concatenate([wall[h, width + head :] for h in range(HEADS)], axis=0)
    resid_ref[...] += matmul(hidden_ref[...], down_all)
    for r, o_ref in enumerate((o0, o1, o2, o3)):
        o_ref[...] = bf(resid_ref[:, aligned(lax.rem(rank + r, HEADS), head)])


def attend(place, listed, counts, far, gain, shift, query, wkv, arrays, per_dev, doms):
    rows, width = query.shape
    head = NODE_BLK
    pack_rows = 2 * width + head
    return pl.pallas_call(
        functools.partial(main_kernel, doms=doms, per_dev=per_dev),
        in_specs=[SMEM] * 3 + [VMEM] * 5 + [ANY] * len(arrays),
        out_specs=[VMEM] * HEADS,
        out_shape=[shape((rows, head))] * HEADS,
        scratch_shapes=[
            pltpu.VMEM((5 * per_dev, NODE_BLK, 2 * width), jnp.bfloat16),
            pltpu.VMEM((rows, width), jnp.bfloat16),
            pltpu.VMEM((HEADS, pack_rows, width), jnp.bfloat16),
            pltpu.VMEM((rows, width), jnp.bfloat16),
            pltpu.VMEM((rows, width), jnp.float32),
            pltpu.VMEM((rows, HEADS * width), jnp.bfloat16),
            pltpu.SemaphoreType.DMA((10,)),
        ],
        name="attend_and_mlp",
        compiler_params=pltpu.CompilerParams(vmem_limit_bytes=48 * MIB),
        cost_estimate=cost(
            rows * width * (4 * KMAX * NODE_BLK + 2 * width + 16 * width) + 4 * rows * width**2,
            16 * MIB,
            rows * HEADS * KMAX * NODE_BLK,
        ),
    )(place, listed, counts, far, gain, shift, query, wkv, *arrays)


def place_kernel(place_ref, own, a, b, c, o_ref):
    rank = place_ref[3]
    for off, r in ((0, own), (3, a), (1, b), (2, c)):
        o_ref[lax.rem(rank + off, HEADS)] = r[...]


def placed_rows(place, pieces):
    rows, head = pieces[0].shape
    return pl.pallas_call(
        place_kernel,
        in_specs=[SMEM] + [VMEM] * HEADS,
        out_specs=VMEM,
        out_shape=shape((HEADS, rows, head)),
        name="place_rows",
        compiler_params=pltpu.CompilerParams(vmem_limit_bytes=4 * MIB),
        cost_estimate=cost(0, 16 * rows * head),
    )(place, *pieces)


def after(value, *deps):
    return lax.optimization_barrier((value, *deps))[0]


def local(
    state, norm_gain, norm_shift, qkv_weight, out_weight, up_weight, down_weight, neighbours, counts
):
    samples, row_count, width = state.shape
    per_dev = row_count // NODE_BLK
    doms = lax.axis_size("dom")
    tps = lax.axis_size("tp")
    dom = lax.axis_index("dom")
    rank = lax.axis_index("tp")
    par = lax.rem(dom, 2)
    per_sample = tps // samples
    place = jnp.stack([rank // per_sample, lax.rem(rank, per_sample), par, rank, dom])
    place = place.astype(jnp.int32)

    def hop(v, pairs):
        return lax.ppermute(v, "dom", pairs)

    def sign(i):
        return 1 if i % 2 == 0 else -1

    def swap(v):
        return hop(v, [(i ^ 1, i) for i in range(doms)])

    def near(v):
        return hop(v, [((i + 2 * sign(i)) % doms, i) for i in range(doms)])

    def far(v):
        return hop(v, [((i - 2 * sign(i)) % doms, i) for i in range(doms)])

    def ring(v):
        pairs = [
            (i * tps + (t - sign(i)) % tps, i * tps + t) for i in range(doms) for t in range(tps)
        ]
        return lax.ppermute(v, ("dom", "tp"), pairs)

    def up(v):
        return lax.ppermute(v, "tp", [(i, (i + 1) % tps) for i in range(tps)])

    def down(v):
        return lax.ppermute(v, "tp", [((i + 1) % tps, i) for i in range(tps)])

    def across(v):
        return lax.ppermute(v, "tp", [(i, (i + 2) % tps) for i in range(tps)])

    qkv = jnp.transpose(qkv_weight, (1, 0, 2))
    w1 = ring(qkv)
    own, pack = prepare(
        place, state, norm_gain, norm_shift, up_weight, out_weight, down_weight
    )
    near_rows = near(own)
    partner = swap(own)

    w1 = after(w1, own)
    w2 = swap(w1)
    mid = width // 2
    w1_half = lax.dynamic_slice_in_dim(w1, par * mid, mid, 1)
    w3m = ring(w1_half)
    w3t = swap(w3m)
    p1 = ring(after(pack, w1_half))

    kv_a, query, wkv = kv_first(place, own, partner, (qkv, w1, w2, w3m, w3t))
    far_rows = far(after(own, near_rows))
    relay = swap(near_rows)
    mid = pack.shape[0] // 2
    p1s = swap(p1)
    p2 = ring(lax.dynamic_slice_in_dim(p1, par * mid, mid, 0))
    p2s = swap(p2)
    kv_b = kv_second(near_rows, relay, wkv)

    mine = attend(
        place, neighbours, counts, far_rows, norm_gain, norm_shift, query, wkv,
        (kv_a, kv_b, state, out_weight, up_weight, down_weight, p1, p1s, p2, p2s),
        per_dev, doms,
    )
    out = placed_rows(place, (mine[0], up(mine[1]), down(mine[3]), across(mine[2])))
    return out.reshape(samples, row_count, width // tps)


def solution(mesh):
    placed = (
        P(None, "dom", None),
        P(),
        P(),
        P(None, None, "tp"),
        P("tp", None),
        P(None, "tp"),
        P("tp", None),
        P("dom", None),
        P("dom"),
    )
    return jax.shard_map(
        local, mesh=mesh, in_specs=placed, out_specs=P(None, "dom", "tp"), check_vma=False
    )
```

time: 213 us -> 78.9 us (0.37)
  waiting for transfers between devices: 125 us -> 13.1 us
  local copies, waits for them, and re-layouts: 35.7 us -> 3.53 us
  Pallas kernels: 0 us -> 27.3 us
  starting transfers between devices: 9.43 us -> 34.7 us
  other arithmetic: 14.9 us -> 0 us
  matrix products: 13.7 us -> 0 us
  between operations: 13.6 us -> 0.14 us
    psum x1 -> x0, waiting for transfers between devices: 68.5 us -> none  [local(): lax.psum(partial_value.astype(jnp.bfloat16), 'tp').astype(jnp.float32)]
    unnamed x3 -> x0, waiting for transfers between devices: 32.3 us -> none
    pallas_call x0 -> x5, Pallas kernels: none -> 27.3 us  [the longest x1 10.8 us: attend(): pl.pallas_call(functools.partial(main_kernel, doms=doms, per_dev=per_dev)...]
    ppermute x4 -> x15, starting transfers between devices: 9.35 us -> 34.7 us  [the longest x8 20.7 us: hop(): return lax.ppermute(v, 'dom', pairs)]
    unnamed x32 -> x22, local copies, waits for them, and re-layouts: 18.1 us -> 1.06 us
    dot_general x5 -> x0, matrix products: 13.7 us -> none  [the longest x1 5.49 us: local(): jnp.einsum('srf,fd->srd', hidden, down_weight, preferred_element_type=jnp...]
    ppermute x4 -> x15, waiting for transfers between devices: 24.7 us -> 13.1 us  [the longest x4 7.06 us: ring(): return lax.ppermute(v, ('dom', 'tp'), pairs)]
    gather x1 -> x0, local copies, waits for them, and re-layouts: 8.01 us -> none  [local(): chosen = window[window_idx]]
  transfers between devices with their start and end apart: 6 -> 15, of which waited for: 4 -> 6; matrix products, arithmetic and copies ran while one was open for 4% -> 2% of each run, Pallas kernels for 0% -> 19%
where the time goes in v2:
time: 78.9 us; the launch traced here: 78.8 us
  starting transfers between devices  34.7 us (44%)
  Pallas kernels  27.3 us (35%)
  waiting for transfers between devices  13.1 us (17%)
  local copies, waits for them, and re-layouts  3.53 us (4%)
    ppermute x8, starting transfers between devices, hop(): return lax.ppermute(v, 'dom', pairs)  20.7 us
    ppermute x4, starting transfers between devices, ring(): return lax.ppermute(v, ('dom', 'tp'), pairs)  11.3 us
    pallas_call x1, Pallas kernels, attend(): pl.pallas_call(functools.partial(main_kernel, doms=doms, per_dev=per_dev)...  10.8 us
    ppermute x4, waiting for transfers between devices, ring(): return lax.ppermute(v, ('dom', 'tp'), pairs)  7.06 us
    pallas_call x1, Pallas kernels, kv_first(): pl.pallas_call(kv_first_kernel, grid_spec=pltpu.PrefetchScalarGridSpec(nu...  6.61 us
    pallas_call x1, Pallas kernels, kv_second(): pl.pallas_call(kv_second_kernel, grid=(2 * steps,), in_specs=[pl.BlockSpe...  4.32 us
    pallas_call x1, Pallas kernels, prepare(): pl.pallas_call(prepare_kernel, grid_spec=pltpu.PrefetchScalarGridSpec(num...  4.21 us
    ppermute x1, waiting for transfers between devices, up(): return lax.ppermute(v, 'tp', [(i, (i + 1) % tps) for i in range(tps)])  3.65 us
  transfers between devices with their start and end apart: 15, of which 6 were waited for; matrix products, arithmetic and copies ran while one was open for 2% of the time, Pallas kernels for 19%

profile of v2, /device:TPU:1, one launch (start us, length us, event | category | flops | bytes accessed | tf_op | source)
XLA Modules:
  0.0 78.8 jit_solution(13027020255216683192)
XLA Ops:
  0.0 3.6 %collective-permute-start.3 = (bf16[3,512,128]{2,1,0:T(8,128)(2,1)}, bf16[3,512,128]{2,1,0:T(8,128)(2,1)S(1)}, u32[]{:S(2)}, u32[]{:S(2)}) collective-permute-start(bf16[3,512,128]{2,1,0:T(8,128)(2,1)} %bitcast.7), channel_id=1, source_target_pairs={{3,0},{0,1},{1,2},{2,3},{5,4},{6,5},{7,6},{4,7},{11,8},{8,9},{9,10... | collective-permute-start | bytes 1179656 | tf_op jit(solution)/shard_map/ppermute | solution.py:346
  3.6 0.7 stack.23.place_ref
  4.2 4.2 %prepare.1 = (bf16[1024,512]{1,0:T(8,128)(2,1)}, bf16[1152,512]{1,0:T(8,128)(2,1)}) custom-call(s32[5]{0:T(128)} %stack.23.place_ref, bf16[2,1024,512]{2,1,0:T(8,128)(2,1)} %state_ref.1, f32[2,2,512]{2,1,0:T(2,128)} %gain_ref.3, f32[2,2,512]{2,1,0:T(2,128)} %shift_ref.3, bf16[512,512]{1,0:T(8,128)(2,1)} %up_w.1, bf16[128,512]{1,0:T(8,128)(2,1)} %out_w.1, ...), custom_call_target="tpu_custom_call" | custom-call | flops 5242880 | bytes 4456448 | tf_op jit(solution)/shard_map/prepare/pallas_call | solution.py:70
  8.6 0.7 constant_dynamic-slice_fusion.1
  9.3 3.0 %collective-permute-start.8 = (bf16[1152,512]{1,0:T(8,128)(2,1)}, bf16[1152,512]{1,0:T(8,128)(2,1)}, u32[]{:S(2)}, u32[]{:S(2)}) collective-permute-start(bf16[1152,512]{1,0:T(8,128)(2,1)} %get-tuple-element.24), channel_id=1, source_target_pairs={{3,0},{0,1},{1,2},{2,3},{5,4},{6,5},{7,6},{4,7},{11,8},{8,9},{9,10... | collective-permute-start | bytes 3538952 | tf_op jit(solution)/shard_map/ppermute | solution.py:346
  12.3 1.2 %collective-permute-start = (bf16[1024,512]{1,0:T(8,128)(2,1)}, bf16[1024,512]{1,0:T(8,128)(2,1)S(1)}, u32[]{:S(2)}, u32[]{:S(2)}) collective-permute-start(bf16[1024,512]{1,0:T(8,128)(2,1)} %get-tuple-element.18.xa), channel_id=1, source_target_pairs={{8,0},{252,4},{16,8},{4,12},{24,16},{12,20},{32,24},{20,28},{40,32... | collective-permute-start | bytes 3145736 | tf_op jit(solution)/shard_map/ppermute | solution.py:328
  13.5 6.3 %collective-permute-start.4 = (bf16[3,512,128]{2,1,0:T(8,128)(2,1)S(1)}, bf16[3,512,128]{2,1,0:T(8,128)(2,1)}, u32[]{:S(2)}, u32[]{:S(2)}) collective-permute-start(bf16[3,512,128]{2,1,0:T(8,128)(2,1)S(1)} %collective-permute-done.3.w1), channel_id=1, source_target_pairs={{4,0},{0,4},{12,8},{8,12},{20,16},{16,20},{28,24},{24,28},{36,32},... | collective-permute-start | bytes 1179656 | tf_op jit(solution)/shard_map/ppermute | solution.py:328
  19.8 2.6 %collective-permute-start.5 = (bf16[3,256,128]{2,1,0:T(8,128)(2,1)}, bf16[3,256,128]{2,1,0:T(8,128)(2,1)}, u32[]{:S(2)}, u32[]{:S(2)}) collective-permute-start(bf16[3,256,128]{2,1,0:T(8,128)(2,1)} %constant_dynamic-slice_fusion.1), channel_id=1, source_target_pairs={{3,0},{0,1},{1,2},{2,3},{5,4},{6,5},{7,6},{4,7},{11,8},{8,9},{9,10... | collective-permute-start | bytes 589832 | tf_op jit(solution)/shard_map/ppermute | solution.py:346
  22.4 5.5 %collective-permute-done.5.w3m = bf16[3,256,128]{2,1,0:T(8,128)(2,1)} collective-permute-done((bf16[3,256,128]{2,1,0:T(8,128)(2,1)}, bf16[3,256,128]{2,1,0:T(8,128)(2,1)}, u32[]{:S(2)}, u32[]{:S(2)}) %collective-permute-start.5) | collective-permute-done | bytes 196640 | tf_op jit(solution)/shard_map/ppermute | solution.py:346
  27.9 5.1 %collective-permute-start.6 = (bf16[3,256,128]{2,1,0:T(8,128)(2,1)}, bf16[3,256,128]{2,1,0:T(8,128)(2,1)S(1)}, u32[]{:S(2)}, u32[]{:S(2)}) collective-permute-start(bf16[3,256,128]{2,1,0:T(8,128)(2,1)} %collective-permute-done.5.w3m), channel_id=1, source_target_pairs={{4,0},{0,4},{12,8},{8,12},{20,16},{16,20},{28,24},{24,28},{36,32},... | collective-permute-start | bytes 589832 | tf_op jit(solution)/shard_map/ppermute | solution.py:328
  33.0 1.1 %constant_dynamic-slice_fusion = bf16[576,512]{1,0:T(8,128)(2,1)S(1)} fusion(bf16[1152,512]{1,0:T(8,128)(2,1)} %collective-permute-done.8.p1, s32[]{:T(128)S(6)} %select_n.13), kind=kLoop, calls=%fused_computation | loop fusion | bytes 1179652 | tf_op jit(solution)/shard_map/dynamic_slice | solution.py:378
  34.1 2.1 %collective-permute-start.10 = (bf16[576,512]{1,0:T(8,128)(2,1)S(1)}, bf16[576,512]{1,0:T(8,128)(2,1)S(1)}, u32[]{:S(2)}, u32[]{:S(2)}) collective-permute-start(bf16[576,512]{1,0:T(8,128)(2,1)S(1)} %constant_dynamic-slice_fusion), channel_id=1, source_target_pairs={{3,0},{0,1},{1,2},{2,3},{5,4},{6,5},{7,6},{4,7},{11,8},{8,9},{9,10... | collective-permute-start | bytes 1769480 | tf_op jit(solution)/shard_map/ppermute | solution.py:346
  36.2 5.5 %collective-permute-start.1 = (bf16[1024,512]{1,0:T(8,128)(2,1)S(1)}, bf16[1024,512]{1,0:T(8,128)(2,1)S(1)}, u32[]{:S(2)}, u32[]{:S(2)}) collective-permute-start(bf16[1024,512]{1,0:T(8,128)(2,1)S(1)} %copy-done.8), channel_id=1, source_target_pairs={{248,0},{12,4},{0,8},{20,12},{8,16},{28,20},{16,24},{36,28},{24,32... | collective-permute-start | bytes 3145736 | tf_op jit(solution)/shard_map/ppermute | solution.py:328
  41.7 1.5 %collective-permute-done.10.p2 = bf16[576,512]{1,0:T(8,128)(2,1)S(1)} collective-permute-done((bf16[576,512]{1,0:T(8,128)(2,1)S(1)}, bf16[576,512]{1,0:T(8,128)(2,1)S(1)}, u32[]{:S(2)}, u32[]{:S(2)}) %collective-permute-start.10) | collective-permute-done | bytes 589856 | tf_op jit(solution)/shard_map/ppermute | solution.py:346
  43.2 2.6 %collective-permute-start.11 = (bf16[576,512]{1,0:T(8,128)(2,1)S(1)}, bf16[576,512]{1,0:T(8,128)(2,1)S(1)}, u32[]{:S(2)}, u32[]{:S(2)}) collective-permute-start(bf16[576,512]{1,0:T(8,128)(2,1)S(1)} %collective-permute-done.10.p2), channel_id=1, source_target_pairs={{4,0},{0,4},{12,8},{8,12},{20,16},{16,20},{28,24},{24,28},{36,32},... | collective-permute-start | bytes 1769480 | tf_op jit(solution)/shard_map/ppermute | solution.py:328
  45.8 6.6 %kv_first.1 = (bf16[16,128,1024]{2,1,0:T(8,128)(2,1)}, bf16[512,512]{1,0:T(8,128)(2,1)S(1)}, bf16[512,1024]{1,0:T(8,128)(2,1)S(1)}) custom-call(s32[5]{0:T(128)S(1)} %copy-done.5, bf16[1024,512]{1,0:T(8,128)(2,1)S(1)} %copy-done.8, bf16[1024,512]{1,0:T(8,128)(2,1)S(1)} %collective-permute-done.2.xb, bf16[3,512,128]{2,1,0:T(8,128)(2,1)S(1)} %bitcast.8, ...), custom_call_target="tpu_custom_call" | custom-call | flops 2147483648 | bytes 8388608 | tf_op jit(solution)/shard_map/kv_first/pallas_call | solution.py:118
  52.5 4.3 %kv_second.1.kv_b = bf16[16,128,1024]{2,1,0:T(8,128)(2,1)} custom-call(bf16[1024,512]{1,0:T(8,128)(2,1)S(1)} %collective-permute-done.xa, bf16[1024,512]{1,0:T(8,128)(2,1)S(1)} %collective-permute-done.7.xb, bf16[512,1024]{1,0:T(8,128)(2,1)S(1)} %get-tuple-element.21.wkv_ref), custom_call_target="tpu_custom_call" | custom-call | flops 2147483648 | bytes 7340032 | tf_op jit(solution)/shard_map/kv_second/pallas_call | solution.py:156
  56.8 1.0 %copy-done.10 = bf16[1152,512]{1,0:T(8,128)(2,1)} copy-done((bf16[1152,512]{1,0:T(8,128)(2,1)}, bf16[1152,512]{1,0:T(8,128)(2,1)S(1)}, u32[]{:S(2)}) %copy-start.10) | copy-done | bytes 1179672
  57.9 10.8 %attend_and_mlp.1 = (bf16[512,128]{1,0:T(8,128)(2,1)S(1)}, bf16[512,128]{1,0:T(8,128)(2,1)S(1)}, bf16[512,128]{1,0:T(8,128)(2,1)S(1)}, bf16[512,128]{1,0:T(8,128)(2,1)S(1)}) custom-call(s32[5]{0:T(128)S(1)} %copy-done.5, s32[8,8]{1,0:T(8,128)S(1)} %copy-done.6, s32[8]{0:T(128)S(1)} %copy-done.7, bf16[1024,512]{1,0:T(8,128)(2,1)S(1)} %collective-permute-done.1.far_ref, ...), custom_call_target="tpu_custom_call" | custom-call | flops 4026531840 | bytes 16777216 | tf_op jit(solution)/shard_map/attend_and_mlp/pallas_call | solution.py:266
  68.7 2.7 %collective-permute-start.13 = (bf16[512,128]{1,0:T(8,128)(2,1)S(1)}, bf16[512,128]{1,0:T(8,128)(2,1)S(1)}, u32[]{:S(2)}, u32[]{:S(2)}) collective-permute-start(bf16[512,128]{1,0:T(8,128)(2,1)S(1)} %get-tuple-element.27), channel_id=1, source_target_pairs={{1,0},{2,1},{3,2},{0,3},{5,4},{6,5},{7,6},{4,7},{9,8},{10,9},{11,1... | collective-permute-start | bytes 393224 | tf_op jit(solution)/shard_map/ppermute | solution.py:352
  71.4 3.7 %collective-permute-done.12.a = bf16[512,128]{1,0:T(8,128)(2,1)S(1)} collective-permute-done((bf16[512,128]{1,0:T(8,128)(2,1)S(1)}, bf16[512,128]{1,0:T(8,128)(2,1)S(1)}, u32[]{:S(2)}, u32[]{:S(2)}) %collective-permute-start.12) | collective-permute-done | bytes 131104 | tf_op jit(solution)/shard_map/ppermute | solution.py:349
  75.0 1.6 %collective-permute-done.13.b = bf16[512,128]{1,0:T(8,128)(2,1)S(1)} collective-permute-done((bf16[512,128]{1,0:T(8,128)(2,1)S(1)}, bf16[512,128]{1,0:T(8,128)(2,1)S(1)}, u32[]{:S(2)}, u32[]{:S(2)}) %collective-permute-start.13) | collective-permute-done | bytes 131104 | tf_op jit(solution)/shard_map/ppermute | solution.py:352
  76.7 0.7 collective-permute-done.14.c
  77.4 1.4 %place_rows.1 = bf16[4,512,128]{2,1,0:T(8,128)(2,1)} custom-call(s32[5]{0:T(128)S(1)} %copy-done.5, bf16[512,128]{1,0:T(8,128)(2,1)S(1)} %get-tuple-element.25.own, bf16[512,128]{1,0:T(8,128)(2,1)S(1)} %collective-permute-done.12.a, bf16[512,128]{1,0:T(8,128)(2,1)S(1)} %collective-permute-done.13.b, bf16[512,128]{1,0:T(8,128)(2,1)S(1)} %collective-permute-done.14.c), custom_call_target="tpu_custom_call" | custom-call | bytes 1048576 | tf_op jit(solution)/shard_map/place_rows/pallas_call | solution.py:298
  (36 shorter events, 0.3 us)
Async XLA Ops:
  0.0 8.6 %collective-permute-start.3 = (bf16[3,512,128]{2,1,0:T(8,128)(2,1)}, bf16[3,512,128]{2,1,0:T(8,128)(2,1)S(1)}, u32[]{:S(2)}, u32[]{:S(2)}) collective-permute-start(bf16[3,512,128]{2,1,0:T(8,128)(2,1)} %bitcast.7), channel_id=1, source_target_pairs={{3,0},{0,1},{1,2},{2,3},{5,4},{6,5},{7,6},{4,7},{11,8},{8,9},{9,10... | collective-permute-start | bytes 1179656 | tf_op jit(solution)/shard_map/ppermute | solution.py:346
  8.5 27.8 %copy-start.8 = (bf16[1024,512]{1,0:T(8,128)(2,1)S(1)}, bf16[1024,512]{1,0:T(8,128)(2,1)}, u32[]{:S(2)}) copy-start(bf16[1024,512]{1,0:T(8,128)(2,1)} %get-tuple-element.18.xa) | copy-start | bytes 3145732
  8.5 37.3 %copy-start.5 = (s32[5]{0:T(128)S(1)}, s32[5]{0:T(128)}, u32[]{:S(2)}) copy-start(s32[5]{0:T(128)} %stack.23.place_ref) | copy-start | bytes 64
  9.3 23.7 %collective-permute-start.8 = (bf16[1152,512]{1,0:T(8,128)(2,1)}, bf16[1152,512]{1,0:T(8,128)(2,1)}, u32[]{:S(2)}, u32[]{:S(2)}) collective-permute-start(bf16[1152,512]{1,0:T(8,128)(2,1)} %get-tuple-element.24), channel_id=1, source_target_pairs={{3,0},{0,1},{1,2},{2,3},{5,4},{6,5},{7,6},{4,7},{11,8},{8,9},{9,10... | collective-permute-start | bytes 3538952 | tf_op jit(solution)/shard_map/ppermute | solution.py:346
  12.3 20.7 %collective-permute-start = (bf16[1024,512]{1,0:T(8,128)(2,1)}, bf16[1024,512]{1,0:T(8,128)(2,1)S(1)}, u32[]{:S(2)}, u32[]{:S(2)}) collective-permute-start(bf16[1024,512]{1,0:T(8,128)(2,1)} %get-tuple-element.18.xa), channel_id=1, source_target_pairs={{8,0},{252,4},{16,8},{4,12},{24,16},{12,20},{32,24},{20,28},{40,32... | collective-permute-start | bytes 3145736 | tf_op jit(solution)/shard_map/ppermute | solution.py:328
  13.5 22.7 %collective-permute-start.4 = (bf16[3,512,128]{2,1,0:T(8,128)(2,1)S(1)}, bf16[3,512,128]{2,1,0:T(8,128)(2,1)}, u32[]{:S(2)}, u32[]{:S(2)}) collective-permute-start(bf16[3,512,128]{2,1,0:T(8,128)(2,1)S(1)} %collective-permute-done.3.w1), channel_id=1, source_target_pairs={{4,0},{0,4},{12,8},{8,12},{20,16},{16,20},{28,24},{24,28},{36,32},... | collective-permute-start | bytes 1179656 | tf_op jit(solution)/shard_map/ppermute | solution.py:328
  19.8 8.1 %collective-permute-start.5 = (bf16[3,256,128]{2,1,0:T(8,128)(2,1)}, bf16[3,256,128]{2,1,0:T(8,128)(2,1)}, u32[]{:S(2)}, u32[]{:S(2)}) collective-permute-start(bf16[3,256,128]{2,1,0:T(8,128)(2,1)} %constant_dynamic-slice_fusion.1), channel_id=1, source_target_pairs={{3,0},{0,1},{1,2},{2,3},{5,4},{6,5},{7,6},{4,7},{11,8},{8,9},{9,10... | collective-permute-start | bytes 589832 | tf_op jit(solution)/shard_map/ppermute | solution.py:346
  22.4 23.4 %collective-permute-start.2 = (bf16[1024,512]{1,0:T(8,128)(2,1)}, bf16[1024,512]{1,0:T(8,128)(2,1)S(1)}, u32[]{:S(2)}, u32[]{:S(2)}) collective-permute-start(bf16[1024,512]{1,0:T(8,128)(2,1)} %get-tuple-element.18.xa), channel_id=1, source_target_pairs={{4,0},{0,4},{12,8},{8,12},{20,16},{16,20},{28,24},{24,28},{36,32},... | collective-permute-start | bytes 3145736 | tf_op jit(solution)/shard_map/ppermute | solution.py:328
  22.4 23.4 %copy-start.9 = (bf16[512,3,128]{2,0,1:T(8,128)(2,1)S(1)}, bf16[512,3,128]{2,0,1:T(8,128)(2,1)}, u32[]{:S(2)}) copy-start(bf16[512,3,128]{2,0,1:T(8,128)(2,1)} %param.12) | copy-start | bytes 1179652
  27.9 8.4 %collective-permute-start.6 = (bf16[3,256,128]{2,1,0:T(8,128)(2,1)}, bf16[3,256,128]{2,1,0:T(8,128)(2,1)S(1)}, u32[]{:S(2)}, u32[]{:S(2)}) collective-permute-start(bf16[3,256,128]{2,1,0:T(8,128)(2,1)} %collective-permute-done.5.w3m), channel_id=1, source_target_pairs={{4,0},{0,4},{12,8},{8,12},{20,16},{16,20},{28,24},{24,28},{36,32},... | collective-permute-start | bytes 589832 | tf_op jit(solution)/shard_map/ppermute | solution.py:328
  33.0 19.4 %collective-permute-start.7 = (bf16[1024,512]{1,0:T(8,128)(2,1)S(1)}, bf16[1024,512]{1,0:T(8,128)(2,1)S(1)}, u32[]{:S(2)}, u32[]{:S(2)}) collective-permute-start(bf16[1024,512]{1,0:T(8,128)(2,1)S(1)} %collective-permute-done.xa), channel_id=1, source_target_pairs={{4,0},{0,4},{12,8},{8,12},{20,16},{16,20},{28,24},{24,28},{36,32},... | collective-permute-start | bytes 3145736 | tf_op jit(solution)/shard_map/ppermute | solution.py:328
  34.1 9.1 %collective-permute-start.10 = (bf16[576,512]{1,0:T(8,128)(2,1)S(1)}, bf16[576,512]{1,0:T(8,128)(2,1)S(1)}, u32[]{:S(2)}, u32[]{:S(2)}) collective-permute-start(bf16[576,512]{1,0:T(8,128)(2,1)S(1)} %constant_dynamic-slice_fusion), channel_id=1, source_target_pairs={{3,0},{0,1},{1,2},{2,3},{5,4},{6,5},{7,6},{4,7},{11,8},{8,9},{9,10... | collective-permute-start | bytes 1769480 | tf_op jit(solution)/shard_map/ppermute | solution.py:346
  36.2 20.6 %collective-permute-start.9 = (bf16[1152,512]{1,0:T(8,128)(2,1)}, bf16[1152,512]{1,0:T(8,128)(2,1)S(1)}, u32[]{:S(2)}, u32[]{:S(2)}) collective-permute-start(bf16[1152,512]{1,0:T(8,128)(2,1)} %collective-permute-done.8.p1), channel_id=1, source_target_pairs={{4,0},{0,4},{12,8},{8,12},{20,16},{16,20},{28,24},{24,28},{36,32},... | collective-permute-start | bytes 3538952 | tf_op jit(solution)/shard_map/ppermute | solution.py:328
  36.2 20.5 %collective-permute-start.1 = (bf16[1024,512]{1,0:T(8,128)(2,1)S(1)}, bf16[1024,512]{1,0:T(8,128)(2,1)S(1)}, u32[]{:S(2)}, u32[]{:S(2)}) collective-permute-start(bf16[1024,512]{1,0:T(8,128)(2,1)S(1)} %copy-done.8), channel_id=1, source_target_pairs={{248,0},{12,4},{0,8},{20,12},{8,16},{28,20},{16,24},{36,28},{24,32... | collective-permute-start | bytes 3145736 | tf_op jit(solution)/shard_map/ppermute | solution.py:328
  43.2 13.6 %collective-permute-start.11 = (bf16[576,512]{1,0:T(8,128)(2,1)S(1)}, bf16[576,512]{1,0:T(8,128)(2,1)S(1)}, u32[]{:S(2)}, u32[]{:S(2)}) collective-permute-start(bf16[576,512]{1,0:T(8,128)(2,1)S(1)} %collective-permute-done.10.p2), channel_id=1, source_target_pairs={{4,0},{0,4},{12,8},{8,12},{20,16},{16,20},{28,24},{24,28},{36,32},... | collective-permute-start | bytes 1769480 | tf_op jit(solution)/shard_map/ppermute | solution.py:328
  52.4 5.4 %copy-start = (bf16[512,512]{1,0:T(8,128)(2,1)S(1)}, bf16[512,512]{1,0:T(8,128)(2,1)}, u32[]{:S(2)}) copy-start(bf16[512,512]{1,0:T(8,128)(2,1)} %up_w.1) | copy-start | bytes 1572868
  52.4 5.4 %copy-start.1 = (bf16[512,512]{1,0:T(8,128)(2,1)S(1)}, bf16[512,512]{1,0:T(8,128)(2,1)}, u32[]{:S(2)}) copy-start(bf16[512,512]{1,0:T(8,128)(2,1)} %down_w.1) | copy-start | bytes 1572868
  52.4 5.4 %copy-start.2 = (bf16[128,512]{1,0:T(8,128)(2,1)S(1)}, bf16[128,512]{1,0:T(8,128)(2,1)}, u32[]{:S(2)}) copy-start(bf16[128,512]{1,0:T(8,128)(2,1)} %out_w.1) | copy-start | bytes 393220
  52.4 5.4 %copy-start.3 = (f32[2,2,512]{2,1,0:T(2,128)S(1)}, f32[2,2,512]{2,1,0:T(2,128)}, u32[]{:S(2)}) copy-start(f32[2,2,512]{2,1,0:T(2,128)} %gain_ref.3) | copy-start | bytes 24580
  52.4 5.4 %copy-start.4 = (f32[2,2,512]{2,1,0:T(2,128)S(1)}, f32[2,2,512]{2,1,0:T(2,128)}, u32[]{:S(2)}) copy-start(f32[2,2,512]{2,1,0:T(2,128)} %shift_ref.3) | copy-start | bytes 24580
  52.4 5.4 %copy-start.6 = (s32[8,8]{1,0:T(8,128)S(1)}, s32[8,8]{1,0:T(8,128)}, u32[]{:S(2)}) copy-start(s32[8,8]{1,0:T(8,128)} %list_ref.1) | copy-start | bytes 772
  68.6 6.4 %collective-permute-start.12 = (bf16[512,128]{1,0:T(8,128)(2,1)S(1)}, bf16[512,128]{1,0:T(8,128)(2,1)S(1)}, u32[]{:S(2)}, u32[]{:S(2)}) collective-permute-start(bf16[512,128]{1,0:T(8,128)(2,1)S(1)} %get-tuple-element.26), channel_id=1, source_target_pairs={{0,1},{1,2},{2,3},{3,0},{4,5},{5,6},{6,7},{7,4},{8,9},{9,10},{10,1... | collective-permute-start | bytes 393224 | tf_op jit(solution)/shard_map/ppermute | solution.py:349
  68.7 7.9 %collective-permute-start.13 = (bf16[512,128]{1,0:T(8,128)(2,1)S(1)}, bf16[512,128]{1,0:T(8,128)(2,1)S(1)}, u32[]{:S(2)}, u32[]{:S(2)}) collective-permute-start(bf16[512,128]{1,0:T(8,128)(2,1)S(1)} %get-tuple-element.27), channel_id=1, source_target_pairs={{1,0},{2,1},{3,2},{0,3},{5,4},{6,5},{7,6},{4,7},{9,8},{10,9},{11,1... | collective-permute-start | bytes 393224 | tf_op jit(solution)/shard_map/ppermute | solution.py:352
  71.4 6.0 %collective-permute-start.14 = (bf16[512,128]{1,0:T(8,128)(2,1)S(1)}, bf16[512,128]{1,0:T(8,128)(2,1)S(1)}, u32[]{:S(2)}, u32[]{:S(2)}) collective-permute-start(bf16[512,128]{1,0:T(8,128)(2,1)S(1)} %get-tuple-element.28), channel_id=1, source_target_pairs={{0,2},{1,3},{2,0},{3,1},{4,6},{5,7},{6,4},{7,5},{8,10},{9,11},{10,... | collective-permute-start | bytes 393224 | tf_op jit(solution)/shard_map/ppermute | solution.py:355
  (2 other events, 6.4 us)

commit v3 on v2

v3 whole, which is shorter than its diff:
```python
import functools
import math

import jax
import jax.numpy as jnp
from jax import lax
from jax.experimental import pallas as pl
from jax.experimental.pallas import tpu as pltpu
from jax.sharding import PartitionSpec as P

HEADS = 4
NODE_BLK = 128
KMAX = 8
ROWS = 512
MIB = 1024 * 1024

VMEM = pl.BlockSpec(memory_space=pltpu.VMEM)
SMEM = pl.BlockSpec(memory_space=pltpu.SMEM)
HBM = pl.BlockSpec(memory_space=pltpu.HBM)


def bf(v):
    return v.astype(jnp.bfloat16)


def matmul(a, b):
    return jnp.dot(a, b, preferred_element_type=jnp.float32)


def aligned(i, step):
    return pl.ds(pl.multiple_of(i * step, step), step)


def shape(dims, dtype=jnp.bfloat16):
    return jax.ShapeDtypeStruct(dims, dtype)


def in_hbm(dims, dtype=jnp.bfloat16):
    return pltpu.HBM(dims, dtype)


def cost(flops, nbytes, exps=0):
    return pl.CostEstimate(flops=flops, bytes_accessed=nbytes, transcendentals=exps)


def normalise(values, gain, shift):
    mean = jnp.mean(values, axis=-1, keepdims=True)
    centred = values - mean
    spread = jnp.mean(centred * centred, axis=-1, keepdims=True)
    return centred * lax.rsqrt(spread + 1e-05) * gain + shift


def my_place():
    dom = lax.axis_index("dom")
    rank = lax.axis_index("tp")
    return lax.div(rank, 2), lax.rem(rank, 2), lax.rem(dom, 2), rank, dom


def norm_kernel(state_ref, gain_ref, shift_ref, o_ref, x_in, x_out, sems):
    sample = my_place()[0]
    s = pl.ds(sample, 1)
    chunks = sems.shape[1]
    step = x_in.shape[0] // chunks
    spans = [pl.ds(k * step, step) for k in range(chunks)]
    loads = [
        pltpu.make_async_copy(state_ref.at[sample, at], x_in.at[at], sems.at[0, k])
        for k, at in enumerate(spans)
    ]
    stores = [
        pltpu.make_async_copy(x_out.at[at], o_ref.at[at], sems.at[1, k])
        for k, at in enumerate(spans)
    ]
    for c in loads:
        c.start()
    gain, shift = gain_ref[0, s], shift_ref[0, s]
    for k, at in enumerate(spans):
        loads[k].wait()
        x_out[at] = bf(normalise(x_in[at].astype(jnp.float32), gain, shift))
        stores[k].start()
    for c in stores:
        c.wait()


def normed_rows(state, gain, shift):
    _, rows, width = state.shape
    return pl.pallas_call(
        norm_kernel,
        in_specs=[HBM, VMEM, VMEM],
        out_specs=HBM,
        out_shape=in_hbm((rows, width)),
        scratch_shapes=[
            pltpu.VMEM((rows, width), jnp.bfloat16),
            pltpu.VMEM((rows, width), jnp.bfloat16),
            pltpu.SemaphoreType.DMA((2, 8)),
        ],
        name="norm_rows",
        compiler_params=pltpu.CompilerParams(vmem_limit_bytes=24 * MIB),
        cost_estimate=cost(10 * rows * width, 4 * rows * width),
    )(state, gain, shift)


def pack_kernel(up_ref, out_ref, down_ref, o_ref):
    at = 0
    for r in (up_ref, out_ref, down_ref):
        o_ref[at : at + r.shape[0]] = r[...]
        at += r.shape[0]


def packed(up_w, out_w, down_w):
    rows = up_w.shape[0] + out_w.shape[0] + down_w.shape[0]
    return pl.pallas_call(
        pack_kernel,
        in_specs=[VMEM] * 3,
        out_specs=VMEM,
        out_shape=in_hbm((rows, up_w.shape[1])),
        name="pack_weights",
        compiler_params=pltpu.CompilerParams(vmem_limit_bytes=8 * MIB),
        cost_estimate=cost(0, 4 * rows * up_w.shape[1]),
    )(up_w, out_w, down_w)


def kv_first_kernel(xa, xb, w0, w1, w2, w3m, w3t, kv_ref, q_ref, wkv_ref, wq_ref):
    i = pl.program_id(0)
    head = NODE_BLK
    _, share, par, _, _ = my_place()

    @pl.when(i == 0)
    def _():
        half = w3m.shape[1]
        for h in range(HEADS):
            at = (h // 2) * 4 * head + (h % 2) * head
            spots = ((0, wq_ref, h * head), (1, wkv_ref, at), (2, wkv_ref, at + 2 * head))
            for c, dst, col in spots:
                if h < 3:
                    dst[:, col : col + head] = (w0, w1, w2)[h][c]
                else:
                    dst[aligned(par, half), col : col + head] = w3m[c]
                    dst[aligned(1 - par, half), col : col + head] = w3t[c]

    x = jnp.where(i < 2, xa[...], xb[...])
    kv_ref[...] = bf(matmul(x, wkv_ref[...])).reshape(kv_ref.shape)

    @pl.when(i == share)
    def _():
        q_ref[...] = bf(matmul(xa[...], wq_ref[...]))


def kv_first(xa, xb, weights):
    rows, width = xa.shape
    steps = rows // ROWS
    per_step = ROWS // NODE_BLK
    blocks = 2 * rows // NODE_BLK
    return pl.pallas_call(
        kv_first_kernel,
        grid=(2 * steps,),
        in_specs=[
            pl.BlockSpec((ROWS, width), lambda i: (jnp.minimum(i, steps - 1), 0)),
            pl.BlockSpec((ROWS, width), lambda i: (jnp.maximum(i - steps, 0), 0)),
        ]
        + [VMEM] * len(weights),
        out_specs=[
            pl.BlockSpec((per_step, NODE_BLK, 2 * width), lambda i: (i, 0, 0)),
            pl.BlockSpec((ROWS, width), lambda i: (0, 0)),
            pl.BlockSpec((width, 2 * width), lambda i: (0, 0)),
        ],
        scratch_shapes=[pltpu.VMEM((width, width), jnp.bfloat16)],
        out_shape=[
            in_hbm((blocks, NODE_BLK, 2 * width)),
            shape((ROWS, width)),
            shape((width, 2 * width)),
        ],
        name="kv_first",
        compiler_params=pltpu.CompilerParams(vmem_limit_bytes=24 * MIB),
        cost_estimate=cost(8 * rows * width * width, 8 * MIB),
    )(xa, xb, *weights)


def kv_second_kernel(xa, xb, wkv_ref, kv_ref):
    x = jnp.where(pl.program_id(0) < 2, xa[...], xb[...])
    kv_ref[...] = bf(matmul(x, wkv_ref[...])).reshape(kv_ref.shape)


def kv_second(xa, xb, wkv):
    rows, width = xa.shape
    steps = rows // ROWS
    per_step = ROWS // NODE_BLK
    blocks = 2 * rows // NODE_BLK
    return pl.pallas_call(
        kv_second_kernel,
        grid=(2 * steps,),
        in_specs=[
            pl.BlockSpec((ROWS, width), lambda i: (jnp.minimum(i, steps - 1), 0)),
            pl.BlockSpec((ROWS, width), lambda i: (jnp.maximum(i - steps, 0), 0)),
            VMEM,
        ],
        out_specs=pl.BlockSpec((per_step, NODE_BLK, 2 * width), lambda i: (i, 0, 0)),
        out_shape=in_hbm((blocks, NODE_BLK, 2 * width)),
        name="kv_second",
        compiler_params=pltpu.CompilerParams(vmem_limit_bytes=24 * MIB),
        cost_estimate=cost(8 * rows * width * width, 7 * MIB),
    )(xa, xb, wkv)


def attend_kernel(
    list_ref, count_ref, far_ref, q_ref, wkv_ref, kv_a, kv_b, heads_ref, kv, sems, *, doms, per_dev
):
    _, share, par, _, dom = my_place()
    head = NODE_BLK
    rows, width = q_ref.shape
    early = kv_a.shape[0]
    copies = [
        pltpu.make_async_copy(kv_a, kv.at[pl.ds(0, early)], sems.at[0]),
        pltpu.make_async_copy(kv_b, kv.at[pl.ds(early, early)], sems.at[1]),
    ]
    for c in copies:
        c.start()

    kv[2 * early :] = bf(matmul(far_ref[...], wkv_ref[...])).reshape(
        (per_dev, NODE_BLK, 2 * width)
    )
    for c in copies:
        c.wait()

    scale = math.log2(math.e) / math.sqrt(head)
    blocks = rows // NODE_BLK
    for b in range(blocks):
        row = share * blocks + b
        count = count_ref[row]
        where = []
        for j in range(KMAX):
            entry = list_ref[row, j]
            part = lax.div(entry, per_dev)
            step = lax.rem(part - dom + (doms + 2), doms) - 2
            turned = jnp.where(par == 0, step, -step)
            slot = jnp.where(
                turned >= 0, jnp.where(turned == 0, 0, turned), jnp.where(turned == -1, 3, 4)
            )
            where.append(slot * per_dev + lax.rem(entry, per_dev))
        at = slice(b * NODE_BLK, (b + 1) * NODE_BLK)
        for pair in range(HEADS // 2):
            col = pair * 4 * head
            keys = jnp.concatenate([kv[i, :, col : col + 2 * head] for i in where], axis=0)
            vals = jnp.concatenate(
                [kv[i, :, col + 2 * head : col + 4 * head] for i in where], axis=0
            )
            q0 = q_ref[at, 2 * pair * head : (2 * pair + 1) * head]
            q1 = q_ref[at, (2 * pair + 1) * head : (2 * pair + 2) * head]
            zero = jnp.zeros_like(q0)
            query = jnp.concatenate(
                [jnp.concatenate([q0, zero], axis=1), jnp.concatenate([zero, q1], axis=1)], axis=0
            )
            scores = lax.dot_general(
                query, keys, (((1,), (1,)), ((), ())), preferred_element_type=jnp.float32
            )
            parts = [
                jnp.where(j < count, scores[:, j * NODE_BLK : (j + 1) * NODE_BLK], -1e30)
                for j in range(KMAX)
            ]
            top = jnp.max(functools.reduce(jnp.maximum, parts), axis=-1, keepdims=True)
            parts = [jnp.exp2((p - top) * scale) for p in parts]
            total = jnp.sum(functools.reduce(jnp.add, parts), axis=-1, keepdims=True)
            mixed = matmul(jnp.concatenate([bf(p) for p in parts], axis=1), vals) / total
            heads_ref[at, 2 * pair * head : (2 * pair + 1) * head] = bf(mixed[:head, :head])
            heads_ref[at, (2 * pair + 1) * head : (2 * pair + 2) * head] = bf(mixed[head:, head:])


def attend(listed, counts, far, query, wkv, kv_a, kv_b, per_dev, doms):
    rows, width = query.shape
    return pl.pallas_call(
        functools.partial(attend_kernel, doms=doms, per_dev=per_dev),
        in_specs=[SMEM] * 2 + [VMEM] * 3 + [HBM] * 2,
        out_specs=VMEM,
        out_shape=shape((rows, width)),
        scratch_shapes=[
            pltpu.VMEM((5 * per_dev, NODE_BLK, 2 * width), jnp.bfloat16),
            pltpu.SemaphoreType.DMA((2,)),
        ],
        name="attend",
        compiler_params=pltpu.CompilerParams(vmem_limit_bytes=32 * MIB),
        cost_estimate=cost(
            4 * rows * width * KMAX * NODE_BLK + 4 * rows * width**2,
            10 * MIB,
            rows * HEADS * KMAX * NODE_BLK,
        ),
    )(listed, counts, far, query, wkv, kv_a, kv_b)


def mlp_kernel(
    heads_ref, gain_ref, shift_ref, out_w, up_w, down_w, p1, p1s, p2, p2s, state_ref,
    o0, o1, o2, o3,
    rows_in, last, resid_ref, hidden_ref, sem,
):
    sample, share, par, rank, _ = my_place()
    head = NODE_BLK
    rows, width = heads_ref.shape
    copy = pltpu.make_async_copy(state_ref.at[sample, aligned(share, rows)], rows_in, sem)
    copy.start()
    half = p2.shape[0]
    last[aligned(par, half)] = p2[...]
    last[aligned(1 - par, half)] = p2s[...]
    packs = (p1, p1s, last)
    out_all = jnp.concatenate([out_w[...]] + [p[width : width + head] for p in packs], axis=0)
    mixed = matmul(heads_ref[...], out_all)
    copy.wait()
    resid_ref[...] = rows_in[...].astype(jnp.float32) + mixed
    s = pl.ds(sample, 1)
    normed = bf(normalise(resid_ref[...], gain_ref[1, s], shift_ref[1, s]))
    for h in range(HEADS):
        v = matmul(normed, up_w[...] if h == 0 else packs[h - 1][:width])
        hidden_ref[:, h * width : (h + 1) * width] = bf(0.5 * v * (1.0 + jnp.tanh(0.5 * v)))
    down_all = jnp.concatenate([down_w[...]] + [p[width + head :] for p in packs], axis=0)
    resid_ref[...] += matmul(hidden_ref[...], down_all)
    for r, o_ref in enumerate((o0, o1, o2, o3)):
        o_ref[...] = bf(resid_ref[:, aligned(lax.rem(rank + r, HEADS), head)])


def mlp(heads, gain, shift, weights, state):
    rows, width = heads.shape
    head = NODE_BLK
    return pl.pallas_call(
        mlp_kernel,
        in_specs=[VMEM] * (3 + len(weights)) + [HBM],
        out_specs=[VMEM] * HEADS,
        out_shape=[shape((rows, head))] * HEADS,
        scratch_shapes=[
            pltpu.VMEM((rows, width), jnp.bfloat16),
            pltpu.VMEM((2 * width + head, width), jnp.bfloat16),
            pltpu.VMEM((rows, width), jnp.float32),
            pltpu.VMEM((rows, HEADS * width), jnp.bfloat16),
            pltpu.SemaphoreType.DMA,
        ],
        name="mlp",
        compiler_params=pltpu.CompilerParams(vmem_limit_bytes=24 * MIB),
        cost_estimate=cost(18 * rows * width * width, 8 * MIB, rows * HEADS * width),
    )(heads, gain, shift, *weights, state)


def place_kernel(own, a, b, c, o_ref):
    rank = my_place()[3]
    for off, r in ((0, own), (3, a), (1, b), (2, c)):
        o_ref[lax.rem(rank + off, HEADS)] = r[...]


def placed_rows(pieces):
    rows, head = pieces[0].shape
    return pl.pallas_call(
        place_kernel,
        in_specs=[VMEM] * HEADS,
        out_specs=VMEM,
        out_shape=shape((HEADS, rows, head)),
        name="place_rows",
        compiler_params=pltpu.CompilerParams(vmem_limit_bytes=4 * MIB),
        cost_estimate=cost(0, 16 * rows * head),
    )(*pieces)


def after(value, *deps):
    return lax.optimization_barrier((value, *deps))[0]


def local(
    state, norm_gain, norm_shift, qkv_weight, out_weight, up_weight, down_weight, neighbours, counts
):
    samples, row_count, width = state.shape
    per_dev = row_count // NODE_BLK
    doms = lax.axis_size("dom")
    tps = lax.axis_size("tp")
    dom = lax.axis_index("dom")
    par = lax.rem(dom, 2)

    def hop(v, pairs):
        return lax.ppermute(v, "dom", pairs)

    def sign(i):
        return 1 if i % 2 == 0 else -1

    def swap(v):
        return hop(v, [(i ^ 1, i) for i in range(doms)])

    def near(v):
        return hop(v, [((i + 2 * sign(i)) % doms, i) for i in range(doms)])

    def far(v):
        return hop(v, [((i - 2 * sign(i)) % doms, i) for i in range(doms)])

    def ring(v):
        pairs = [
            (i * tps + (t - sign(i)) % tps, i * tps + t) for i in range(doms) for t in range(tps)
        ]
        return lax.ppermute(v, ("dom", "tp"), pairs)

    def up(v):
        return lax.ppermute(v, "tp", [(i, (i + 1) % tps) for i in range(tps)])

    def down(v):
        return lax.ppermute(v, "tp", [((i + 1) % tps, i) for i in range(tps)])

    def across(v):
        return lax.ppermute(v, "tp", [(i, (i + 2) % tps) for i in range(tps)])

    qkv = jnp.transpose(qkv_weight, (1, 0, 2))
    w1 = ring(qkv)
    own = normed_rows(state, norm_gain, norm_shift)
    near_rows = near(own)
    partner = swap(own)
    pack = packed(after(up_weight, own), out_weight, down_weight)

    w1 = after(w1, own)
    w2 = swap(w1)
    mid = width // 2
    w1_half = lax.dynamic_slice_in_dim(w1, par * mid, mid, 1)
    w3m = ring(w1_half)
    w3t = swap(w3m)
    p1 = ring(after(pack, w1_half))

    own_late, near_rows = lax.optimization_barrier((own, near_rows))
    far_rows = far(own_late)
    relay = swap(near_rows)
    kv_a, query, wkv = kv_first(own_late, partner, (qkv, w1, w2, w3m, w3t))
    mid = pack.shape[0] // 2
    p1 = after(p1, query)
    p1s = swap(p1)
    p2 = ring(lax.dynamic_slice_in_dim(p1, par * mid, mid, 0))
    kv_b = kv_second(near_rows, relay, wkv)
    p2 = after(p2, kv_b)
    p2s = swap(p2)

    heads = attend(neighbours, counts, far_rows, query, wkv, kv_a, kv_b, per_dev, doms)
    weights = (out_weight, up_weight, down_weight, p1, p1s, p2, p2s)
    mine = mlp(heads, norm_gain, norm_shift, weights, state)
    out = placed_rows((mine[0], up(mine[1]), down(mine[3]), across(mine[2])))
    return out.reshape(samples, row_count, width // tps)


def solution(mesh):
    placed = (
        P(None, "dom", None),
        P(),
        P(),
        P(None, None, "tp"),
        P("tp", None),
        P(None, "tp"),
        P("tp", None),
        P("dom", None),
        P("dom"),
    )
    return jax.shard_map(
        local, mesh=mesh, in_specs=placed, out_specs=P(None, "dom", "tp"), check_vma=False
    )
```

time: 78.9 us -> 83.1 us (1.053)
  starting transfers between devices: 34.7 us -> 23.2 us
  waiting for transfers between devices: 13.1 us -> 23.6 us
  local copies, waits for them, and re-layouts: 3.53 us -> 7.99 us
    ppermute x8, waiting for transfers between devices: 0.02 us -> 8.36 us  [hop(): return lax.ppermute(v, 'dom', pairs)]
    ppermute x8, starting transfers between devices: 20.7 us -> 13.3 us  [hop(): return lax.ppermute(v, 'dom', pairs)]
    unnamed x22 -> x34, local copies, waits for them, and re-layouts: 1.06 us -> 7.94 us
    ppermute x4, starting transfers between devices: 11.3 us -> 7.08 us  [ring(): return lax.ppermute(v, ('dom', 'tp'), pairs)]
    ppermute x4, waiting for transfers between devices: 7.06 us -> 9.29 us  [ring(): return lax.ppermute(v, ('dom', 'tp'), pairs)]
    pallas_call x1, Pallas kernels: 4.32 us -> 6.04 us  [kv_second(): pl.pallas_call(kv_second_kernel, grid=(2 * steps,), in_specs=[pl.BlockSpe...]
    pallas_call x4 -> x6, Pallas kernels: 23 us -> 21.8 us  [the longest x1 6.67 us: kv_first(): pl.pallas_call(kv_first_kernel, grid=(2 * steps,), in_specs=[pl.BlockSpec...]
    dynamic_slice x1, local copies, waits for them, and re-layouts: 1.11 us -> 0.04 us  [local(): p2 = ring(lax.dynamic_slice_in_dim(p1, par * mid, mid, 0))]
  transfers between devices with their start and end apart: 15 -> 15, of which waited for: 6 -> 7; matrix products, arithmetic and copies ran while one was open for 2% -> 0% of each run, Pallas kernels for 19% -> 28%
where the time goes in v3:
time: 83.1 us; the launch traced here: 82.7 us
  Pallas kernels  27.8 us (33%)
  waiting for transfers between devices  23.6 us (28%)
  starting transfers between devices  23.2 us (28%)
  local copies, waits for them, and re-layouts  7.99 us (10%)
    ppermute x8, starting transfers between devices, hop(): return lax.ppermute(v, 'dom', pairs)  13.3 us
    ppermute x4, waiting for transfers between devices, ring(): return lax.ppermute(v, ('dom', 'tp'), pairs)  9.29 us
    ppermute x8, waiting for transfers between devices, hop(): return lax.ppermute(v, 'dom', pairs)  8.36 us
    unnamed x34, local copies, waits for them, and re-layouts  7.94 us
    ppermute x4, starting transfers between devices, ring(): return lax.ppermute(v, ('dom', 'tp'), pairs)  7.08 us
    pallas_call x1, Pallas kernels, kv_first(): pl.pallas_call(kv_first_kernel, grid=(2 * steps,), in_specs=[pl.BlockSpec...  6.67 us
    pallas_call x1, Pallas kernels, kv_second(): pl.pallas_call(kv_second_kernel, grid=(2 * steps,), in_specs=[pl.BlockSpe...  6.04 us
    pallas_call x1, Pallas kernels, attend(): pl.pallas_call(functools.partial(attend_kernel, doms=doms, per_dev=per_de...  5.85 us
  transfers between devices with their start and end apart: 15, of which 7 were waited for; matrix products, arithmetic and copies ran while one was open for 0% of the time, Pallas kernels for 28%

profile of v3, /device:TPU:1, one launch (start us, length us, event | category | flops | bytes accessed | tf_op | source)
XLA Modules:
  0.0 82.7 jit_solution(364058162957444457)
XLA Ops:
  0.0 3.6 %collective-permute-start.3 = (bf16[3,512,128]{2,1,0:T(8,128)(2,1)}, bf16[3,512,128]{2,1,0:T(8,128)(2,1)S(1)}, u32[]{:S(2)}, u32[]{:S(2)}) collective-permute-start(bf16[3,512,128]{2,1,0:T(8,128)(2,1)} %bitcast.2), channel_id=1, source_target_pairs={{3,0},{0,1},{1,2},{2,3},{5,4},{6,5},{7,6},{4,7},{11,8},{8,9},{9,10... | collective-permute-start | bytes 1179656 | tf_op jit(solution)/shard_map/ppermute | solution.py:390
  3.6 1.6 %copy-done.2 = bf16[2,1024,512]{2,1,0:T(8,128)(2,1)S(1)} copy-done((bf16[2,1024,512]{2,1,0:T(8,128)(2,1)S(1)}, bf16[2,1024,512]{2,1,0:T(8,128)(2,1)}, u32[]{:S(2)}) %copy-start.2) | copy-done | bytes 2097176
  6.6 3.8 %norm_rows.1.xa = bf16[1024,512]{1,0:T(8,128)(2,1)} custom-call(bf16[2,1024,512]{2,1,0:T(8,128)(2,1)S(1)} %copy-done.2, f32[2,2,512]{2,1,0:T(2,128)S(1)} %copy-done.10, f32[2,2,512]{2,1,0:T(2,128)S(1)} %copy-done.12), custom_call_target="tpu_custom_call" | custom-call | flops 5242880 | bytes 2097152 | tf_op jit(solution)/shard_map/norm_rows/pallas_call | solution.py:86
  10.4 1.3 %collective-permute-start = (bf16[1024,512]{1,0:T(8,128)(2,1)}, bf16[1024,512]{1,0:T(8,128)(2,1)}, u32[]{:S(2)}, u32[]{:S(2)}) collective-permute-start(bf16[1024,512]{1,0:T(8,128)(2,1)} %norm_rows.1.xa), channel_id=1, source_target_pairs={{8,0},{252,4},{16,8},{4,12},{24,16},{12,20},{32,24},{20,28},{40,32... | collective-permute-start | bytes 3145736 | tf_op jit(solution)/shard_map/ppermute | solution.py:372
  11.7 6.4 %collective-permute-start.2 = (bf16[1024,512]{1,0:T(8,128)(2,1)}, bf16[1024,512]{1,0:T(8,128)(2,1)}, u32[]{:S(2)}, u32[]{:S(2)}) collective-permute-start(bf16[1024,512]{1,0:T(8,128)(2,1)} %norm_rows.1.xa), channel_id=1, source_target_pairs={{4,0},{0,4},{12,8},{8,12},{20,16},{16,20},{28,24},{24,28},{36,32},... | collective-permute-start | bytes 3145736 | tf_op jit(solution)/shard_map/ppermute | solution.py:372
  18.0 1.1 %pack_weights.1 = bf16[1152,512]{1,0:T(8,128)(2,1)} custom-call(bf16[512,512]{1,0:T(8,128)(2,1)S(1)} %copy-done.5, bf16[128,512]{1,0:T(8,128)(2,1)S(1)} %copy-done.7, bf16[512,512]{1,0:T(8,128)(2,1)S(1)} %copy-done.6), custom_call_target="tpu_custom_call" | custom-call | bytes 2359296 | tf_op jit(solution)/shard_map/pack_weights/pallas_call | solution.py:111
  19.9 1.5 %collective-permute-start.8 = (bf16[1152,512]{1,0:T(8,128)(2,1)}, bf16[1152,512]{1,0:T(8,128)(2,1)S(1)}, u32[]{:S(2)}, u32[]{:S(2)}) collective-permute-start(bf16[1152,512]{1,0:T(8,128)(2,1)} %pack_weights.1), channel_id=1, source_target_pairs={{3,0},{0,1},{1,2},{2,3},{5,4},{6,5},{7,6},{4,7},{11,8},{8,9},{9,10... | collective-permute-start | bytes 3538952 | tf_op jit(solution)/shard_map/ppermute | solution.py:390
  21.6 1.4 %collective-permute-start.5 = (bf16[3,256,128]{2,1,0:T(8,128)(2,1)S(1)}, bf16[3,256,128]{2,1,0:T(8,128)(2,1)}, u32[]{:S(2)}, u32[]{:S(2)}) collective-permute-start(bf16[3,256,128]{2,1,0:T(8,128)(2,1)S(1)} %constant_dynamic-slice_fusion.1), channel_id=1, source_target_pairs={{3,0},{0,1},{1,2},{2,3},{5,4},{6,5},{7,6},{4,7},{11,8},{8,9},{9,10... | collective-permute-start | bytes 589832 | tf_op jit(solution)/shard_map/ppermute | solution.py:390
  23.0 7.7 %collective-permute-done.xa = bf16[1024,512]{1,0:T(8,128)(2,1)} collective-permute-done((bf16[1024,512]{1,0:T(8,128)(2,1)}, bf16[1024,512]{1,0:T(8,128)(2,1)}, u32[]{:S(2)}, u32[]{:S(2)}) %collective-permute-start) | collective-permute-done | bytes 1048608 | tf_op jit(solution)/shard_map/ppermute | solution.py:372
  30.7 7.1 %collective-permute-done.5.w3m = bf16[3,256,128]{2,1,0:T(8,128)(2,1)} collective-permute-done((bf16[3,256,128]{2,1,0:T(8,128)(2,1)S(1)}, bf16[3,256,128]{2,1,0:T(8,128)(2,1)}, u32[]{:S(2)}, u32[]{:S(2)}) %collective-permute-start.5) | collective-permute-done | bytes 196640 | tf_op jit(solution)/shard_map/ppermute | solution.py:390
  37.8 2.1 %collective-permute-start.6 = (bf16[3,256,128]{2,1,0:T(8,128)(2,1)}, bf16[3,256,128]{2,1,0:T(8,128)(2,1)}, u32[]{:S(2)}, u32[]{:S(2)}) collective-permute-start(bf16[3,256,128]{2,1,0:T(8,128)(2,1)} %collective-permute-done.5.w3m), channel_id=1, source_target_pairs={{4,0},{0,4},{12,8},{8,12},{20,16},{16,20},{28,24},{24,28},{36,32},... | collective-permute-start | bytes 589832 | tf_op jit(solution)/shard_map/ppermute | solution.py:372
  41.3 1.0 %copy-done.9 = bf16[3,512,128]{2,1,0:T(8,128)(2,1)S(1)} copy-done((bf16[3,512,128]{2,1,0:T(8,128)(2,1)S(1)}, bf16[3,512,128]{2,1,0:T(8,128)(2,1)}, u32[]{:S(2)}) %copy-start.9) | copy-done | bytes 393240
  42.3 1.0 %copy-done.16 = bf16[512,3,128]{2,0,1:T(8,128)(2,1)S(1)} copy-done((bf16[512,3,128]{2,0,1:T(8,128)(2,1)S(1)}, bf16[512,3,128]{2,0,1:T(8,128)(2,1)}, u32[]{:S(2)}) %copy-start.16) | copy-done | bytes 393240
  43.3 6.7 %kv_first.1 = (bf16[16,128,1024]{2,1,0:T(8,128)(2,1)}, bf16[512,512]{1,0:T(8,128)(2,1)S(1)}, bf16[512,1024]{1,0:T(8,128)(2,1)S(1)}) custom-call(bf16[1024,512]{1,0:T(8,128)(2,1)S(1)} %copy-done.4, bf16[1024,512]{1,0:T(8,128)(2,1)} %collective-permute-done.2.xb, bf16[3,512,128]{2,1,0:T(8,128)(2,1)S(1)} %bitcast.3, bf16[3,512,128]{2,1,0:T(8,128)(2,1)S(1)} %copy-done.9, ...), custom_call_target="tpu_custom_call" | custom-call | flops 2147483648 | bytes 8388608 | tf_op jit(solution)/shard_map/kv_first/pallas_call | solution.py:153
  50.8 6.0 %kv_second.1.kv_b = bf16[16,128,1024]{2,1,0:T(8,128)(2,1)} custom-call(bf16[1024,512]{1,0:T(8,128)(2,1)} %collective-permute-done.xa, bf16[1024,512]{1,0:T(8,128)(2,1)} %collective-permute-done.7.xb, bf16[512,1024]{1,0:T(8,128)(2,1)S(1)} %get-tuple-element.22.wkv_ref), custom_call_target="tpu_custom_call" | custom-call | flops 2147483648 | bytes 7340032 | tf_op jit(solution)/shard_map/kv_second/pallas_call | solution.py:188
  56.9 2.2 %collective-permute-done.10.p2 = bf16[576,512]{1,0:T(8,128)(2,1)S(1)} collective-permute-done((bf16[576,512]{1,0:T(8,128)(2,1)S(1)}, bf16[576,512]{1,0:T(8,128)(2,1)S(1)}, u32[]{:S(2)}, u32[]{:S(2)}) %collective-permute-start.10) | collective-permute-done | bytes 589856 | tf_op jit(solution)/shard_map/ppermute | solution.py:390
  59.1 2.4 %collective-permute-start.11 = (bf16[576,512]{1,0:T(8,128)(2,1)S(1)}, bf16[576,512]{1,0:T(8,128)(2,1)S(1)}, u32[]{:S(2)}, u32[]{:S(2)}) collective-permute-start(bf16[576,512]{1,0:T(8,128)(2,1)S(1)} %collective-permute-done.10.p2), channel_id=1, source_target_pairs={{4,0},{0,4},{12,8},{8,12},{20,16},{16,20},{28,24},{24,28},{36,32},... | collective-permute-start | bytes 1769480 | tf_op jit(solution)/shard_map/ppermute | solution.py:372
  61.6 2.2 %copy-done.1 = bf16[16,128,1024]{2,1,0:T(8,128)(2,1)S(1)} copy-done((bf16[16,128,1024]{2,1,0:T(8,128)(2,1)S(1)}, bf16[16,128,1024]{2,1,0:T(8,128)(2,1)}, u32[]{:S(2)}) %copy-start.1) | copy-done | bytes 4194328
  63.8 5.9 %attend.1.heads_ref = bf16[512,512]{1,0:T(8,128)(2,1)S(1)} custom-call(s32[8,8]{1,0:T(8,128)S(1)} %copy-done.14, s32[8]{0:T(128)S(1)} %copy-done.15, bf16[1024,512]{1,0:T(8,128)(2,1)S(1)} %collective-permute-done.1.far_ref, bf16[512,512]{1,0:T(8,128)(2,1)S(1)} %get-tuple-element.21.q_ref, bf16[512,1024]{1,0:T(8,128)(2,1)S(1)} %get-tuple-element.22.wkv_ref, ...), custom_call_target="tpu_custom_call" | custom-call | flops 1610612736 | bytes 10485760 | tf_op jit(solution)/shard_map/attend/pallas_call | solution.py:269
  69.7 3.5 %mlp.1 = (bf16[512,128]{1,0:T(8,128)(2,1)S(1)}, bf16[512,128]{1,0:T(8,128)(2,1)S(1)}, bf16[512,128]{1,0:T(8,128)(2,1)S(1)}, bf16[512,128]{1,0:T(8,128)(2,1)S(1)}) custom-call(bf16[512,512]{1,0:T(8,128)(2,1)S(1)} %attend.1.heads_ref, f32[2,2,512]{2,1,0:T(2,128)S(1)} %copy-done.11, f32[2,2,512]{2,1,0:T(2,128)S(1)} %copy-done.13, ...), custom_call_target="tpu_custom_call" | custom-call | flops 2415919104 | bytes 8388608 | tf_op jit(solution)/shard_map/mlp/pallas_call | solution.py:320
  73.2 2.7 %collective-permute-start.13 = (bf16[512,128]{1,0:T(8,128)(2,1)S(1)}, bf16[512,128]{1,0:T(8,128)(2,1)S(1)}, u32[]{:S(2)}, u32[]{:S(2)}) collective-permute-start(bf16[512,128]{1,0:T(8,128)(2,1)S(1)} %get-tuple-element.31), channel_id=1, source_target_pairs={{1,0},{2,1},{3,2},{0,3},{5,4},{6,5},{7,6},{4,7},{9,8},{10,9},{11,1... | collective-permute-start | bytes 393224 | tf_op jit(solution)/shard_map/ppermute | solution.py:396
  75.9 3.6 %collective-permute-done.12.a = bf16[512,128]{1,0:T(8,128)(2,1)S(1)} collective-permute-done((bf16[512,128]{1,0:T(8,128)(2,1)S(1)}, bf16[512,128]{1,0:T(8,128)(2,1)S(1)}, u32[]{:S(2)}, u32[]{:S(2)}) %collective-permute-start.12) | collective-permute-done | bytes 131104 | tf_op jit(solution)/shard_map/ppermute | solution.py:393
  79.5 1.6 %collective-permute-done.13.b = bf16[512,128]{1,0:T(8,128)(2,1)S(1)} collective-permute-done((bf16[512,128]{1,0:T(8,128)(2,1)S(1)}, bf16[512,128]{1,0:T(8,128)(2,1)S(1)}, u32[]{:S(2)}, u32[]{:S(2)}) %collective-permute-start.13) | collective-permute-done | bytes 131104 | tf_op jit(solution)/shard_map/ppermute | solution.py:396
  81.9 0.8 %place_rows.1 = bf16[4,512,128]{2,1,0:T(8,128)(2,1)} custom-call(bf16[512,128]{1,0:T(8,128)(2,1)S(1)} %get-tuple-element.29.own, bf16[512,128]{1,0:T(8,128)(2,1)S(1)} %collective-permute-done.12.a, bf16[512,128]{1,0:T(8,128)(2,1)S(1)} %collective-permute-done.13.b, bf16[512,128]{1,0:T(8,128)(2,1)S(1)} %collective-permute-done.14.c), custom_call_target="tpu_custom_call" | custom-call | bytes 1048576 | tf_op jit(solution)/shard_map/place_rows/pallas_call | solution.py:346
  (49 shorter events, 5.5 us)
Async XLA Ops:
  0.0 19.2 %collective-permute-start.3 = (bf16[3,512,128]{2,1,0:T(8,128)(2,1)}, bf16[3,512,128]{2,1,0:T(8,128)(2,1)S(1)}, u32[]{:S(2)}, u32[]{:S(2)}) collective-permute-start(bf16[3,512,128]{2,1,0:T(8,128)(2,1)} %bitcast.2), channel_id=1, source_target_pairs={{3,0},{0,1},{1,2},{2,3},{5,4},{6,5},{7,6},{4,7},{11,8},{8,9},{9,10... | collective-permute-start | bytes 1179656 | tf_op jit(solution)/shard_map/ppermute | solution.py:390
  6.6 11.5 %copy-start.5 = (bf16[512,512]{1,0:T(8,128)(2,1)S(1)}, bf16[512,512]{1,0:T(8,128)(2,1)}, u32[]{:S(2)}) copy-start(bf16[512,512]{1,0:T(8,128)(2,1)} %up_w.1) | copy-start | bytes 1572868
  6.6 11.5 %copy-start.6 = (bf16[512,512]{1,0:T(8,128)(2,1)S(1)}, bf16[512,512]{1,0:T(8,128)(2,1)}, u32[]{:S(2)}) copy-start(bf16[512,512]{1,0:T(8,128)(2,1)} %down_w.1) | copy-start | bytes 1572868
  6.6 11.5 %copy-start.7 = (bf16[128,512]{1,0:T(8,128)(2,1)S(1)}, bf16[128,512]{1,0:T(8,128)(2,1)}, u32[]{:S(2)}) copy-start(bf16[128,512]{1,0:T(8,128)(2,1)} %out_w.1) | copy-start | bytes 393220
  10.4 20.4 %collective-permute-start = (bf16[1024,512]{1,0:T(8,128)(2,1)}, bf16[1024,512]{1,0:T(8,128)(2,1)}, u32[]{:S(2)}, u32[]{:S(2)}) collective-permute-start(bf16[1024,512]{1,0:T(8,128)(2,1)} %norm_rows.1.xa), channel_id=1, source_target_pairs={{8,0},{252,4},{16,8},{4,12},{24,16},{12,20},{32,24},{20,28},{40,32... | collective-permute-start | bytes 3145736 | tf_op jit(solution)/shard_map/ppermute | solution.py:372
  11.7 29.6 %collective-permute-start.2 = (bf16[1024,512]{1,0:T(8,128)(2,1)}, bf16[1024,512]{1,0:T(8,128)(2,1)}, u32[]{:S(2)}, u32[]{:S(2)}) collective-permute-start(bf16[1024,512]{1,0:T(8,128)(2,1)} %norm_rows.1.xa), channel_id=1, source_target_pairs={{4,0},{0,4},{12,8},{8,12},{20,16},{16,20},{28,24},{24,28},{36,32},... | collective-permute-start | bytes 3145736 | tf_op jit(solution)/shard_map/ppermute | solution.py:372
  18.0 21.9 %copy-start.4 = (bf16[1024,512]{1,0:T(8,128)(2,1)S(1)}, bf16[1024,512]{1,0:T(8,128)(2,1)}, u32[]{:S(2)}) copy-start(bf16[1024,512]{1,0:T(8,128)(2,1)} %norm_rows.1.xa) | copy-start | bytes 3145732
  19.9 30.0 %collective-permute-start.8 = (bf16[1152,512]{1,0:T(8,128)(2,1)}, bf16[1152,512]{1,0:T(8,128)(2,1)S(1)}, u32[]{:S(2)}, u32[]{:S(2)}) collective-permute-start(bf16[1152,512]{1,0:T(8,128)(2,1)} %pack_weights.1), channel_id=1, source_target_pairs={{3,0},{0,1},{1,2},{2,3},{5,4},{6,5},{7,6},{4,7},{11,8},{8,9},{9,10... | collective-permute-start | bytes 3538952 | tf_op jit(solution)/shard_map/ppermute | solution.py:390
  21.4 18.5 %collective-permute-start.4 = (bf16[3,512,128]{2,1,0:T(8,128)(2,1)}, bf16[3,512,128]{2,1,0:T(8,128)(2,1)}, u32[]{:S(2)}, u32[]{:S(2)}) collective-permute-start(bf16[3,512,128]{2,1,0:T(8,128)(2,1)} %copy-done.8), channel_id=1, source_target_pairs={{4,0},{0,4},{12,8},{8,12},{20,16},{16,20},{28,24},{24,28},{36,32},... | collective-permute-start | bytes 1179656 | tf_op jit(solution)/shard_map/ppermute | solution.py:372
  21.6 16.2 %collective-permute-start.5 = (bf16[3,256,128]{2,1,0:T(8,128)(2,1)S(1)}, bf16[3,256,128]{2,1,0:T(8,128)(2,1)}, u32[]{:S(2)}, u32[]{:S(2)}) collective-permute-start(bf16[3,256,128]{2,1,0:T(8,128)(2,1)S(1)} %constant_dynamic-slice_fusion.1), channel_id=1, source_target_pairs={{3,0},{0,1},{1,2},{2,3},{5,4},{6,5},{7,6},{4,7},{11,8},{8,9},{9,10... | collective-permute-start | bytes 589832 | tf_op jit(solution)/shard_map/ppermute | solution.py:390
  30.7 20.1 %collective-permute-start.7 = (bf16[1024,512]{1,0:T(8,128)(2,1)}, bf16[1024,512]{1,0:T(8,128)(2,1)}, u32[]{:S(2)}, u32[]{:S(2)}) collective-permute-start(bf16[1024,512]{1,0:T(8,128)(2,1)} %collective-permute-done.xa), channel_id=1, source_target_pairs={{4,0},{0,4},{12,8},{8,12},{20,16},{16,20},{28,24},{24,28},{36,32},... | collective-permute-start | bytes 3145736 | tf_op jit(solution)/shard_map/ppermute | solution.py:372
  37.8 3.5 %collective-permute-start.6 = (bf16[3,256,128]{2,1,0:T(8,128)(2,1)}, bf16[3,256,128]{2,1,0:T(8,128)(2,1)}, u32[]{:S(2)}, u32[]{:S(2)}) collective-permute-start(bf16[3,256,128]{2,1,0:T(8,128)(2,1)} %collective-permute-done.5.w3m), channel_id=1, source_target_pairs={{4,0},{0,4},{12,8},{8,12},{20,16},{16,20},{28,24},{24,28},{36,32},... | collective-permute-start | bytes 589832 | tf_op jit(solution)/shard_map/ppermute | solution.py:372
  39.9 21.7 %collective-permute-start.1 = (bf16[1024,512]{1,0:T(8,128)(2,1)S(1)}, bf16[1024,512]{1,0:T(8,128)(2,1)S(1)}, u32[]{:S(2)}, u32[]{:S(2)}) collective-permute-start(bf16[1024,512]{1,0:T(8,128)(2,1)S(1)} %copy-done.4), channel_id=1, source_target_pairs={{248,0},{12,4},{0,8},{20,12},{8,16},{28,20},{16,24},{36,28},{24,32... | collective-permute-start | bytes 3145736 | tf_op jit(solution)/shard_map/ppermute | solution.py:372
  50.0 9.1 %collective-permute-start.10 = (bf16[576,512]{1,0:T(8,128)(2,1)S(1)}, bf16[576,512]{1,0:T(8,128)(2,1)S(1)}, u32[]{:S(2)}, u32[]{:S(2)}) collective-permute-start(bf16[576,512]{1,0:T(8,128)(2,1)S(1)} %constant_dynamic-slice_fusion), channel_id=1, source_target_pairs={{3,0},{0,1},{1,2},{2,3},{5,4},{6,5},{7,6},{4,7},{11,8},{8,9},{9,10... | collective-permute-start | bytes 1769480 | tf_op jit(solution)/shard_map/ppermute | solution.py:390
  50.7 19.0 %collective-permute-start.9 = (bf16[1152,512]{1,0:T(8,128)(2,1)S(1)}, bf16[1152,512]{1,0:T(8,128)(2,1)S(1)}, u32[]{:S(2)}, u32[]{:S(2)}) collective-permute-start(bf16[1152,512]{1,0:T(8,128)(2,1)S(1)} %collective-permute-done.8.p1), channel_id=1, source_target_pairs={{4,0},{0,4},{12,8},{8,12},{20,16},{16,20},{28,24},{24,28},{36,32},... | collective-permute-start | bytes 3538952 | tf_op jit(solution)/shard_map/ppermute | solution.py:372
  50.8 10.7 %copy-start = (bf16[16,128,1024]{2,1,0:T(8,128)(2,1)S(1)}, bf16[16,128,1024]{2,1,0:T(8,128)(2,1)}, u32[]{:S(2)}) copy-start(bf16[16,128,1024]{2,1,0:T(8,128)(2,1)} %get-tuple-element.23.kv_a) | copy-start | bytes 12582916
  50.8 10.7 %copy-start.14 = (s32[8,8]{1,0:T(8,128)S(1)}, s32[8,8]{1,0:T(8,128)}, u32[]{:S(2)}) copy-start(s32[8,8]{1,0:T(8,128)} %list_ref.1) | copy-start | bytes 772
  50.8 10.7 %copy-start.15 = (s32[8]{0:T(128)S(1)}, s32[8]{0:T(128)}, u32[]{:S(2)}) copy-start(s32[8]{0:T(128)} %count_ref.1) | copy-start | bytes 100
  59.1 10.5 %collective-permute-start.11 = (bf16[576,512]{1,0:T(8,128)(2,1)S(1)}, bf16[576,512]{1,0:T(8,128)(2,1)S(1)}, u32[]{:S(2)}, u32[]{:S(2)}) collective-permute-start(bf16[576,512]{1,0:T(8,128)(2,1)S(1)} %collective-permute-done.10.p2), channel_id=1, source_target_pairs={{4,0},{0,4},{12,8},{8,12},{20,16},{16,20},{28,24},{24,28},{36,32},... | collective-permute-start | bytes 1769480 | tf_op jit(solution)/shard_map/ppermute | solution.py:372
  63.8 5.9 %copy-start.11 = (f32[2,2,512]{2,1,0:T(2,128)S(1)}, f32[2,2,512]{2,1,0:T(2,128)}, u32[]{:S(2)}) copy-start(f32[2,2,512]{2,1,0:T(2,128)} %gain_ref.3) | copy-start | bytes 24580
  63.8 5.9 %copy-start.13 = (f32[2,2,512]{2,1,0:T(2,128)S(1)}, f32[2,2,512]{2,1,0:T(2,128)}, u32[]{:S(2)}) copy-start(f32[2,2,512]{2,1,0:T(2,128)} %shift_ref.3) | copy-start | bytes 24580
  73.1 6.4 %collective-permute-start.12 = (bf16[512,128]{1,0:T(8,128)(2,1)S(1)}, bf16[512,128]{1,0:T(8,128)(2,1)S(1)}, u32[]{:S(2)}, u32[]{:S(2)}) collective-permute-start(bf16[512,128]{1,0:T(8,128)(2,1)S(1)} %get-tuple-element.30), channel_id=1, source_target_pairs={{0,1},{1,2},{2,3},{3,0},{4,5},{5,6},{6,7},{7,4},{8,9},{9,10},{10,1... | collective-permute-start | bytes 393224 | tf_op jit(solution)/shard_map/ppermute | solution.py:393
  73.2 7.9 %collective-permute-start.13 = (bf16[512,128]{1,0:T(8,128)(2,1)S(1)}, bf16[512,128]{1,0:T(8,128)(2,1)S(1)}, u32[]{:S(2)}, u32[]{:S(2)}) collective-permute-start(bf16[512,128]{1,0:T(8,128)(2,1)S(1)} %get-tuple-element.31), channel_id=1, source_target_pairs={{1,0},{2,1},{3,2},{0,3},{5,4},{6,5},{7,6},{4,7},{9,8},{10,9},{11,1... | collective-permute-start | bytes 393224 | tf_op jit(solution)/shard_map/ppermute | solution.py:396
  75.9 6.0 %collective-permute-start.14 = (bf16[512,128]{1,0:T(8,128)(2,1)S(1)}, bf16[512,128]{1,0:T(8,128)(2,1)S(1)}, u32[]{:S(2)}, u32[]{:S(2)}) collective-permute-start(bf16[512,128]{1,0:T(8,128)(2,1)S(1)} %get-tuple-element.32), channel_id=1, source_target_pairs={{0,2},{1,3},{2,0},{3,1},{4,6},{5,7},{6,4},{7,5},{8,10},{9,11},{10,... | collective-permute-start | bytes 393224 | tf_op jit(solution)/shard_map/ppermute | solution.py:399
  (8 other events, 13.8 us)

commit v4 on v3

--- a/solution.py
+++ b/solution.py
@@ -39,6 +39,14 @@
     return pltpu.HBM(dims, dtype)
 
 
+def in_vmem(dims, dtype=jnp.bfloat16):
+    return pltpu.VMEM(dims, dtype)
+
+
+def kept_in_hbm(v):
+    return pltpu.with_memory_space_constraint(v, pltpu.HBM)
+
+
 def cost(flops, nbytes, exps=0):
     return pl.CostEstimate(flops=flops, bytes_accessed=nbytes, transcendentals=exps)
 
@@ -56,47 +64,46 @@
     return lax.div(rank, 2), lax.rem(rank, 2), lax.rem(dom, 2), rank, dom
 
 
-def norm_kernel(state_ref, gain_ref, shift_ref, o_ref, x_in, x_out, sems):
+def norm_kernel(state_ref, gain_ref, shift_ref, o_ref, x_in, affine, sems):
     sample = my_place()[0]
     s = pl.ds(sample, 1)
-    chunks = sems.shape[1]
+    chunks = sems.shape[0] - 2
     step = x_in.shape[0] // chunks
     spans = [pl.ds(k * step, step) for k in range(chunks)]
     loads = [
-        pltpu.make_async_copy(state_ref.at[sample, at], x_in.at[at], sems.at[0, k])
+        pltpu.make_async_copy(state_ref.at[sample, at], x_in.at[at], sems.at[k])
         for k, at in enumerate(spans)
     ]
-    stores = [
-        pltpu.make_async_copy(x_out.at[at], o_ref.at[at], sems.at[1, k])
-        for k, at in enumerate(spans)
+    small = [
+        pltpu.make_async_copy(r, affine.at[k], sems.at[chunks + k])
+        for k, r in enumerate((gain_ref, shift_ref))
     ]
-    for c in loads:
+    for c in loads[:1] + small + loads[1:]:
         c.start()
-    gain, shift = gain_ref[0, s], shift_ref[0, s]
-    for k, at in enumerate(spans):
-        loads[k].wait()
-        x_out[at] = bf(normalise(x_in[at].astype(jnp.float32), gain, shift))
-        stores[k].start()
-    for c in stores:
+    for c in small:
         c.wait()
+    gain, shift = affine[0, 0, s], affine[1, 0, s]
+    for c, at in zip(loads, spans):
+        c.wait()
+        o_ref[at] = bf(normalise(x_in[at].astype(jnp.float32), gain, shift))
 
 
 def normed_rows(state, gain, shift):
     _, rows, width = state.shape
     return pl.pallas_call(
         norm_kernel,
-        in_specs=[HBM, VMEM, VMEM],
-        out_specs=HBM,
-        out_shape=in_hbm((rows, width)),
+        in_specs=[HBM] * 3,
+        out_specs=VMEM,
+        out_shape=in_vmem((rows, width)),
         scratch_shapes=[
             pltpu.VMEM((rows, width), jnp.bfloat16),
-            pltpu.VMEM((rows, width), jnp.bfloat16),
-            pltpu.SemaphoreType.DMA((2, 8)),
+            pltpu.VMEM((2, *gain.shape), jnp.float32),
+            pltpu.SemaphoreType.DMA((6,)),
         ],
         name="norm_rows",
-        compiler_params=pltpu.CompilerParams(vmem_limit_bytes=24 * MIB),
+        compiler_params=pltpu.CompilerParams(vmem_limit_bytes=8 * MIB),
         cost_estimate=cost(10 * rows * width, 4 * rows * width),
-    )(state, gain, shift)
+    )(kept_in_hbm(state), kept_in_hbm(gain), kept_in_hbm(shift))
 
 
 def pack_kernel(up_ref, out_ref, down_ref, o_ref):
@@ -119,107 +126,77 @@
     )(up_w, out_w, down_w)
 
 
+def write_kv(x_ref, wkv_ref, kv_ref, first):
+    rows, width = x_ref.shape
+    for r in range(0, rows, ROWS):
+        out = bf(matmul(x_ref[r : r + ROWS], wkv_ref[...]))
+        at = first + r // NODE_BLK
+        kv_ref[at : at + ROWS // NODE_BLK] = out.reshape((ROWS // NODE_BLK, NODE_BLK, 2 * width))
+
+
 def kv_first_kernel(xa, xb, w0, w1, w2, w3m, w3t, kv_ref, q_ref, wkv_ref, wq_ref):
-    i = pl.program_id(0)
     head = NODE_BLK
     _, share, par, _, _ = my_place()
-
-    @pl.when(i == 0)
-    def _():
-        half = w3m.shape[1]
-        for h in range(HEADS):
-            at = (h // 2) * 4 * head + (h % 2) * head
-            spots = ((0, wq_ref, h * head), (1, wkv_ref, at), (2, wkv_ref, at + 2 * head))
-            for c, dst, col in spots:
-                if h < 3:
-                    dst[:, col : col + head] = (w0, w1, w2)[h][c]
-                else:
-                    dst[aligned(par, half), col : col + head] = w3m[c]
-                    dst[aligned(1 - par, half), col : col + head] = w3t[c]
-
-    x = jnp.where(i < 2, xa[...], xb[...])
-    kv_ref[...] = bf(matmul(x, wkv_ref[...])).reshape(kv_ref.shape)
-
-    @pl.when(i == share)
-    def _():
-        q_ref[...] = bf(matmul(xa[...], wq_ref[...]))
-
-
-def kv_first(xa, xb, weights):
+    half = w3m.shape[1]
+    for h in range(HEADS):
+        at = (h // 2) * 4 * head + (h % 2) * head
+        spots = ((0, wq_ref, h * head), (1, wkv_ref, at), (2, wkv_ref, at + 2 * head))
+        for c, dst, col in spots:
+            if h < 3:
+                dst[:, col : col + head] = (w0, w1, w2)[h][c]
+            else:
+                dst[aligned(par, half), col : col + head] = w3m[c]
+                dst[aligned(1 - par, half), col : col + head] = w3t[c]
+    write_kv(xa, wkv_ref, kv_ref, 0)
+    write_kv(xb, wkv_ref, kv_ref, xa.shape[0] // NODE_BLK)
+    q_ref[...] = bf(matmul(xa[aligned(share, q_ref.shape[0])], wq_ref[...]))
+
+
+def kv_first(xa, xb, weights, slots):
     rows, width = xa.shape
-    steps = rows // ROWS
-    per_step = ROWS // NODE_BLK
-    blocks = 2 * rows // NODE_BLK
     return pl.pallas_call(
         kv_first_kernel,
-        grid=(2 * steps,),
-        in_specs=[
-            pl.BlockSpec((ROWS, width), lambda i: (jnp.minimum(i, steps - 1), 0)),
-            pl.BlockSpec((ROWS, width), lambda i: (jnp.maximum(i - steps, 0), 0)),
-        ]
-        + [VMEM] * len(weights),
-        out_specs=[
-            pl.BlockSpec((per_step, NODE_BLK, 2 * width), lambda i: (i, 0, 0)),
-            pl.BlockSpec((ROWS, width), lambda i: (0, 0)),
-            pl.BlockSpec((width, 2 * width), lambda i: (0, 0)),
-        ],
+        in_specs=[VMEM] * (2 + len(weights)),
+        out_specs=[VMEM] * 3,
         scratch_shapes=[pltpu.VMEM((width, width), jnp.bfloat16)],
         out_shape=[
-            in_hbm((blocks, NODE_BLK, 2 * width)),
-            shape((ROWS, width)),
-            shape((width, 2 * width)),
+            in_vmem((slots * rows // NODE_BLK, NODE_BLK, 2 * width)),
+            in_vmem((rows // 2, width)),
+            in_vmem((width, 2 * width)),
         ],
         name="kv_first",
-        compiler_params=pltpu.CompilerParams(vmem_limit_bytes=24 * MIB),
+        compiler_params=pltpu.CompilerParams(vmem_limit_bytes=16 * MIB),
         cost_estimate=cost(8 * rows * width * width, 8 * MIB),
     )(xa, xb, *weights)
 
 
-def kv_second_kernel(xa, xb, wkv_ref, kv_ref):
-    x = jnp.where(pl.program_id(0) < 2, xa[...], xb[...])
-    kv_ref[...] = bf(matmul(x, wkv_ref[...])).reshape(kv_ref.shape)
-
-
-def kv_second(xa, xb, wkv):
+def kv_second_kernel(xa, xb, wkv_ref, kv_in, kv_ref):
+    first = 2 * xa.shape[0] // NODE_BLK
+    write_kv(xa, wkv_ref, kv_ref, first)
+    write_kv(xb, wkv_ref, kv_ref, first + xa.shape[0] // NODE_BLK)
+
+
+def kv_second(xa, xb, wkv, kv):
     rows, width = xa.shape
-    steps = rows // ROWS
-    per_step = ROWS // NODE_BLK
-    blocks = 2 * rows // NODE_BLK
     return pl.pallas_call(
         kv_second_kernel,
-        grid=(2 * steps,),
-        in_specs=[
-            pl.BlockSpec((ROWS, width), lambda i: (jnp.minimum(i, steps - 1), 0)),
-            pl.BlockSpec((ROWS, width), lambda i: (jnp.maximum(i - steps, 0), 0)),
-            VMEM,
-        ],
-        out_specs=pl.BlockSpec((per_step, NODE_BLK, 2 * width), lambda i: (i, 0, 0)),
-        out_shape=in_hbm((blocks, NODE_BLK, 2 * width)),
+        in_specs=[VMEM] * 4,
+        out_specs=VMEM,
+        out_shape=in_vmem(kv.shape),
+        input_output_aliases={3: 0},
         name="kv_second",
-        compiler_params=pltpu.CompilerParams(vmem_limit_bytes=24 * MIB),
+        compiler_params=pltpu.CompilerParams(vmem_limit_bytes=16 * MIB),
         cost_estimate=cost(8 * rows * width * width, 7 * MIB),
-    )(xa, xb, wkv)
+    )(xa, xb, wkv, kv)
 
 
 def attend_kernel(
-    list_ref, count_ref, far_ref, q_ref, wkv_ref, kv_a, kv_b, heads_ref, kv, sems, *, doms, per_dev
+    list_ref, count_ref, far_ref, q_ref, wkv_ref, kv_in, heads_ref, kv, *, doms, per_dev
 ):
     _, share, par, _, dom = my_place()
     head = NODE_BLK
     rows, width = q_ref.shape
-    early = kv_a.shape[0]
-    copies = [
-        pltpu.make_async_copy(kv_a, kv.at[pl.ds(0, early)], sems.at[0]),
-        pltpu.make_async_copy(kv_b, kv.at[pl.ds(early, early)], sems.at[1]),
-    ]
-    for c in copies:
-        c.start()
-
-    kv[2 * early :] = bf(matmul(far_ref[...], wkv_ref[...])).reshape(
-        (per_dev, NODE_BLK, 2 * width)
-    )
-    for c in copies:
-        c.wait()
+    write_kv(far_ref, wkv_ref, kv, 4 * per_dev)
 
     scale = math.log2(math.e) / math.sqrt(head)
     blocks = rows // NODE_BLK
@@ -264,25 +241,22 @@
             heads_ref[at, (2 * pair + 1) * head : (2 * pair + 2) * head] = bf(mixed[head:, head:])
 
 
-def attend(listed, counts, far, query, wkv, kv_a, kv_b, per_dev, doms):
+def attend(listed, counts, far, query, wkv, kv, per_dev, doms):
     rows, width = query.shape
     return pl.pallas_call(
         functools.partial(attend_kernel, doms=doms, per_dev=per_dev),
-        in_specs=[SMEM] * 2 + [VMEM] * 3 + [HBM] * 2,
-        out_specs=VMEM,
-        out_shape=shape((rows, width)),
-        scratch_shapes=[
-            pltpu.VMEM((5 * per_dev, NODE_BLK, 2 * width), jnp.bfloat16),
-            pltpu.SemaphoreType.DMA((2,)),
-        ],
+        in_specs=[SMEM] * 2 + [VMEM] * 4,
+        out_specs=[VMEM] * 2,
+        out_shape=[in_vmem((rows, width)), in_vmem(kv.shape)],
+        input_output_aliases={5: 1},
         name="attend",
-        compiler_params=pltpu.CompilerParams(vmem_limit_bytes=32 * MIB),
+        compiler_params=pltpu.CompilerParams(vmem_limit_bytes=16 * MIB),
         cost_estimate=cost(
             4 * rows * width * KMAX * NODE_BLK + 4 * rows * width**2,
             10 * MIB,
             rows * HEADS * KMAX * NODE_BLK,
         ),
-    )(listed, counts, far, query, wkv, kv_a, kv_b)
+    )(listed, counts, far, query, wkv, kv)[0]
 
 
 def mlp_kernel(
@@ -332,7 +306,7 @@
         name="mlp",
         compiler_params=pltpu.CompilerParams(vmem_limit_bytes=24 * MIB),
         cost_estimate=cost(18 * rows * width * width, 8 * MIB, rows * HEADS * width),
-    )(heads, gain, shift, *weights, state)
+    )(heads, gain, shift, *weights, kept_in_hbm(state))
 
 
 def place_kernel(own, a, b, c, o_ref):
@@ -398,34 +372,32 @@
     def across(v):
         return lax.ppermute(v, "tp", [(i, (i + 2) % tps) for i in range(tps)])
 
+    own = normed_rows(state, norm_gain, norm_shift)
     qkv = jnp.transpose(qkv_weight, (1, 0, 2))
-    w1 = ring(qkv)
-    own = normed_rows(state, norm_gain, norm_shift)
+    w1 = ring(after(qkv, own))
     near_rows = near(own)
     partner = swap(own)
     pack = packed(after(up_weight, own), out_weight, down_weight)
 
-    w1 = after(w1, own)
     w2 = swap(w1)
     mid = width // 2
-    w1_half = lax.dynamic_slice_in_dim(w1, par * mid, mid, 1)
-    w3m = ring(w1_half)
+    w3m = ring(lax.dynamic_slice_in_dim(w1, par * mid, mid, 1))
     w3t = swap(w3m)
-    p1 = ring(after(pack, w1_half))
+    p1 = ring(after(pack, w3m))
 
     own_late, near_rows = lax.optimization_barrier((own, near_rows))
     far_rows = far(own_late)
     relay = swap(near_rows)
-    kv_a, query, wkv = kv_first(own_late, partner, (qkv, w1, w2, w3m, w3t))
+    kv, query, wkv = kv_first(own_late, partner, (qkv, w1, w2, w3m, w3t), 5)
     mid = pack.shape[0] // 2
     p1 = after(p1, query)
     p1s = swap(p1)
     p2 = ring(lax.dynamic_slice_in_dim(p1, par * mid, mid, 0))
-    kv_b = kv_second(near_rows, relay, wkv)
-    p2 = after(p2, kv_b)
+    kv = kv_second(near_rows, relay, wkv, kv)
+    p2, kv = lax.optimization_barrier((p2, kv))
     p2s = swap(p2)
 
-    heads = attend(neighbours, counts, far_rows, query, wkv, kv_a, kv_b, per_dev, doms)
+    heads = attend(neighbours, counts, far_rows, query, wkv, kv, per_dev, doms)
     weights = (out_weight, up_weight, down_weight, p1, p1s, p2, p2s)
     mine = mlp(heads, norm_gain, norm_shift, weights, state)
     out = placed_rows((mine[0], up(mine[1]), down(mine[3]), across(mine[2])))

time: 83.1 us -> 73.6 us (0.89)
  starting transfers between devices: 23.2 us -> 29.7 us
  Pallas kernels: 27.8 us -> 21.7 us
  local copies, waits for them, and re-layouts: 7.99 us -> 2.09 us
  waiting for transfers between devices: 23.6 us -> 19.6 us
    unnamed x34 -> x18, local copies, waits for them, and re-layouts: 7.94 us -> 0.04 us
    pallas_call x3, Pallas kernels: 16.5 us -> 8.75 us  [the longest x1 4.31 us: kv_first(): pl.pallas_call(kv_first_kernel, in_specs=[VMEM] * (2 + len(weights)), out...]
    ppermute x4, starting transfers between devices: 7.08 us -> 11.4 us  [ring(): return lax.ppermute(v, ('dom', 'tp'), pairs)]
    ppermute x8, waiting for transfers between devices: 8.36 us -> 5.29 us  [hop(): return lax.ppermute(v, 'dom', pairs)]
    ppermute x8, starting transfers between devices: 13.3 us -> 15.5 us  [hop(): return lax.ppermute(v, 'dom', pairs)]
    pallas_call x1, Pallas kernels: 3.47 us -> 5.54 us  [mlp(): pl.pallas_call(mlp_kernel, in_specs=[VMEM] * (3 + len(weights)) + [HBM],...]
    dynamic_slice x1, local copies, waits for them, and re-layouts: 0.04 us -> 1.11 us  [local(): p2 = ring(lax.dynamic_slice_in_dim(p1, par * mid, mid, 0))]
    dynamic_slice x1, local copies, waits for them, and re-layouts: 0.01 us -> 0.94 us  [local(): w3m = ring(lax.dynamic_slice_in_dim(w1, par * mid, mid, 1))]
  transfers between devices with their start and end apart: 15 -> 15, of which waited for: 7 -> 8; matrix products, arithmetic and copies ran while one was open for 0% -> 3% of each run, Pallas kernels for 28% -> 18%
where the time goes in v4:
time: 73.6 us; the launch traced here: 73.3 us
  starting transfers between devices  29.7 us (40%)
  Pallas kernels  21.7 us (29%)
  waiting for transfers between devices  19.6 us (27%)
  local copies, waits for them, and re-layouts  2.09 us (3%)
    ppermute x8, starting transfers between devices, hop(): return lax.ppermute(v, 'dom', pairs)  15.5 us
    ppermute x4, starting transfers between devices, ring(): return lax.ppermute(v, ('dom', 'tp'), pairs)  11.4 us
    ppermute x4, waiting for transfers between devices, ring(): return lax.ppermute(v, ('dom', 'tp'), pairs)  8.36 us
    pallas_call x1, Pallas kernels, mlp(): pl.pallas_call(mlp_kernel, in_specs=[VMEM] * (3 + len(weights)) + [HBM],...  5.54 us
    pallas_call x1, Pallas kernels, attend(): pl.pallas_call(functools.partial(attend_kernel, doms=doms, per_dev=per_de...  5.43 us
    ppermute x8, waiting for transfers between devices, hop(): return lax.ppermute(v, 'dom', pairs)  5.29 us
    pallas_call x1, Pallas kernels, kv_first(): pl.pallas_call(kv_first_kernel, in_specs=[VMEM] * (2 + len(weights)), out...  4.31 us
    ppermute x1, waiting for transfers between devices, up(): return lax.ppermute(v, 'tp', [(i, (i + 1) % tps) for i in range(tps)])  3.65 us
  transfers between devices with their start and end apart: 15, of which 8 were waited for; matrix products, arithmetic and copies ran while one was open for 3% of the time, Pallas kernels for 18%

profile of v4, /device:TPU:1, one launch (start us, length us, event | category | flops | bytes accessed | tf_op | source)
XLA Modules:
  0.0 73.3 jit_solution(8283536040183027309)
XLA Ops:
  0.0 2.1 %norm_rows.1.xa = bf16[1024,512]{1,0:T(8,128)(2,1)S(1)} custom-call(bf16[2,1024,512]{2,1,0:T(8,128)(2,1)} %state_ref.3, f32[2,2,512]{2,1,0:T(2,128)} %gain_ref.3, f32[2,2,512]{2,1,0:T(2,128)} %shift_ref.3), custom_call_target="tpu_custom_call" | custom-call | flops 5242880 | bytes 2097152 | tf_op jit(solution)/shard_map/norm_rows/pallas_call | solution.py:93
  2.1 3.6 %collective-permute-start.3 = (bf16[3,512,128]{2,1,0:T(8,128)(2,1)}, bf16[3,512,128]{2,1,0:T(8,128)(2,1)}, u32[]{:S(2)}, u32[]{:S(2)}) collective-permute-start(bf16[3,512,128]{2,1,0:T(8,128)(2,1)} %bitcast.w0), channel_id=1, source_target_pairs={{3,0},{0,1},{1,2},{2,3},{5,4},{6,5},{7,6},{4,7},{11,8},{8,9},{9,10... | collective-permute-start | bytes 1179656 | tf_op jit(solution)/shard_map/ppermute | solution.py:364
  5.8 1.2 %collective-permute-start = (bf16[1024,512]{1,0:T(8,128)(2,1)S(1)}, bf16[1024,512]{1,0:T(8,128)(2,1)S(1)}, u32[]{:S(2)}, u32[]{:S(2)}) collective-permute-start(bf16[1024,512]{1,0:T(8,128)(2,1)S(1)} %norm_rows.1.xa), channel_id=1, source_target_pairs={{8,0},{252,4},{16,8},{4,12},{24,16},{12,20},{32,24},{20,28},{40,32... | collective-permute-start | bytes 3145736 | tf_op jit(solution)/shard_map/ppermute | solution.py:346
  7.0 3.8 %collective-permute-done.3.w1 = bf16[3,512,128]{2,1,0:T(8,128)(2,1)} collective-permute-done((bf16[3,512,128]{2,1,0:T(8,128)(2,1)}, bf16[3,512,128]{2,1,0:T(8,128)(2,1)}, u32[]{:S(2)}, u32[]{:S(2)}) %collective-permute-start.3) | collective-permute-done | bytes 393248 | tf_op jit(solution)/shard_map/ppermute | solution.py:364
  11.7 3.2 %collective-permute-start.5 = (bf16[3,256,128]{2,1,0:T(8,128)(2,1)S(1)}, bf16[3,256,128]{2,1,0:T(8,128)(2,1)S(1)}, u32[]{:S(2)}, u32[]{:S(2)}) collective-permute-start(bf16[3,256,128]{2,1,0:T(8,128)(2,1)S(1)} %constant_dynamic-slice_fusion.1), channel_id=1, source_target_pairs={{3,0},{0,1},{1,2},{2,3},{5,4},{6,5},{7,6},{4,7},{11,8},{8,9},{9,10... | collective-permute-start | bytes 589832 | tf_op jit(solution)/shard_map/ppermute | solution.py:364
  14.9 1.0 %collective-permute-start.2 = (bf16[1024,512]{1,0:T(8,128)(2,1)S(1)}, bf16[1024,512]{1,0:T(8,128)(2,1)}, u32[]{:S(2)}, u32[]{:S(2)}) collective-permute-start(bf16[1024,512]{1,0:T(8,128)(2,1)S(1)} %norm_rows.1.xa), channel_id=1, source_target_pairs={{4,0},{0,4},{12,8},{8,12},{20,16},{16,20},{28,24},{24,28},{36,32},... | collective-permute-start | bytes 3145736 | tf_op jit(solution)/shard_map/ppermute | solution.py:346
  15.9 1.1 %pack_weights.1 = bf16[1152,512]{1,0:T(8,128)(2,1)} custom-call(bf16[512,512]{1,0:T(8,128)(2,1)S(1)} %copy-done, bf16[128,512]{1,0:T(8,128)(2,1)S(1)} %copy-done.4, bf16[512,512]{1,0:T(8,128)(2,1)S(1)} %copy-done.2), custom_call_target="tpu_custom_call" | custom-call | bytes 2359296 | tf_op jit(solution)/shard_map/pack_weights/pallas_call | solution.py:118
  17.5 3.1 %collective-permute-start.7 = (bf16[1152,512]{1,0:T(8,128)(2,1)}, bf16[1152,512]{1,0:T(8,128)(2,1)}, u32[]{:S(2)}, u32[]{:S(2)}) collective-permute-start(bf16[1152,512]{1,0:T(8,128)(2,1)} %pack_weights.1), channel_id=1, source_target_pairs={{3,0},{0,1},{1,2},{2,3},{5,4},{6,5},{7,6},{4,7},{11,8},{8,9},{9,10... | collective-permute-start | bytes 3538952 | tf_op jit(solution)/shard_map/ppermute | solution.py:364
  20.7 2.0 %collective-permute-start.4 = (bf16[3,512,128]{2,1,0:T(8,128)(2,1)}, bf16[3,512,128]{2,1,0:T(8,128)(2,1)}, u32[]{:S(2)}, u32[]{:S(2)}) collective-permute-start(bf16[3,512,128]{2,1,0:T(8,128)(2,1)} %collective-permute-done.3.w1), channel_id=1, source_target_pairs={{4,0},{0,4},{12,8},{8,12},{20,16},{16,20},{28,24},{24,28},{36,32},... | collective-permute-start | bytes 1179656 | tf_op jit(solution)/shard_map/ppermute | solution.py:346
  22.6 3.1 %collective-permute-done.xa = bf16[1024,512]{1,0:T(8,128)(2,1)S(1)} collective-permute-done((bf16[1024,512]{1,0:T(8,128)(2,1)S(1)}, bf16[1024,512]{1,0:T(8,128)(2,1)S(1)}, u32[]{:S(2)}, u32[]{:S(2)}) %collective-permute-start) | collective-permute-done | bytes 1048608 | tf_op jit(solution)/shard_map/ppermute | solution.py:346
  26.2 2.2 %collective-permute-done.6.w3t = bf16[3,256,128]{2,1,0:T(8,128)(2,1)} collective-permute-done((bf16[3,256,128]{2,1,0:T(8,128)(2,1)S(1)}, bf16[3,256,128]{2,1,0:T(8,128)(2,1)}, u32[]{:S(2)}, u32[]{:S(2)}) %collective-permute-start.6) | collective-permute-done | bytes 196640 | tf_op jit(solution)/shard_map/ppermute | solution.py:346
  28.4 5.3 %collective-permute-start.1 = (bf16[1024,512]{1,0:T(8,128)(2,1)S(1)}, bf16[1024,512]{1,0:T(8,128)(2,1)S(1)}, u32[]{:S(2)}, u32[]{:S(2)}) collective-permute-start(bf16[1024,512]{1,0:T(8,128)(2,1)S(1)} %norm_rows.1.xa), channel_id=1, source_target_pairs={{248,0},{12,4},{0,8},{20,12},{8,16},{28,20},{16,24},{36,28},{24,32... | collective-permute-start | bytes 3145736 | tf_op jit(solution)/shard_map/ppermute | solution.py:346
  33.7 4.3 %kv_first.1 = (bf16[40,128,1024]{2,1,0:T(8,128)(2,1)S(1)}, bf16[512,512]{1,0:T(8,128)(2,1)S(1)}, bf16[512,1024]{1,0:T(8,128)(2,1)S(1)}) custom-call(bf16[1024,512]{1,0:T(8,128)(2,1)S(1)} %norm_rows.1.xa, bf16[1024,512]{1,0:T(8,128)(2,1)} %collective-permute-done.2.xb, bf16[3,512,128]{2,1,0:T(8,128)(2,1)} %bitcast.w0, ...), custom_call_target="tpu_custom_call" | custom-call | flops 2147483648 | bytes 8388608 | tf_op jit(solution)/shard_map/kv_first/pallas_call | solution.py:157
  38.1 1.1 %constant_dynamic-slice_fusion = bf16[576,512]{1,0:T(8,128)(2,1)S(1)} fusion(bf16[1152,512]{1,0:T(8,128)(2,1)} %collective-permute-done.7.p1, s32[]{:T(128)S(6)} %select_n.7), kind=kLoop, calls=%fused_computation | loop fusion | bytes 1179652 | tf_op jit(solution)/shard_map/dynamic_slice | solution.py:395
  39.2 1.5 %collective-permute-start.8 = (bf16[576,512]{1,0:T(8,128)(2,1)S(1)}, bf16[576,512]{1,0:T(8,128)(2,1)S(1)}, u32[]{:S(2)}, u32[]{:S(2)}) collective-permute-start(bf16[576,512]{1,0:T(8,128)(2,1)S(1)} %constant_dynamic-slice_fusion), channel_id=1, source_target_pairs={{3,0},{0,1},{1,2},{2,3},{5,4},{6,5},{7,6},{4,7},{11,8},{8,9},{9,10... | collective-permute-start | bytes 1769480 | tf_op jit(solution)/shard_map/ppermute | solution.py:364
  40.6 1.2 %collective-permute-start.10 = (bf16[1152,512]{1,0:T(8,128)(2,1)}, bf16[1152,512]{1,0:T(8,128)(2,1)S(1)}, u32[]{:S(2)}, u32[]{:S(2)}) collective-permute-start(bf16[1152,512]{1,0:T(8,128)(2,1)} %collective-permute-done.7.p1), channel_id=1, source_target_pairs={{4,0},{0,4},{12,8},{8,12},{20,16},{16,20},{28,24},{24,28},{36,32},... | collective-permute-start | bytes 3538952 | tf_op jit(solution)/shard_map/ppermute | solution.py:346
  41.8 2.3 %kv_second.1.kv_in = bf16[40,128,1024]{2,1,0:T(8,128)(2,1)S(1)} custom-call(bf16[1024,512]{1,0:T(8,128)(2,1)S(1)} %collective-permute-done.xa, bf16[1024,512]{1,0:T(8,128)(2,1)S(1)} %collective-permute-done.9.xb, bf16[512,1024]{1,0:T(8,128)(2,1)S(1)} %get-tuple-element.24.wkv_ref, ...), custom_call_target="tpu_custom_call", output_to_operand_aliasing={{}: (3, {})} | custom-call | flops 2147483648 | bytes 7340032 | tf_op jit(solution)/shard_map/kv_second/pallas_call | solution.py:181
  44.2 4.1 %collective-permute-done.8.p2 = bf16[576,512]{1,0:T(8,128)(2,1)S(1)} collective-permute-done((bf16[576,512]{1,0:T(8,128)(2,1)S(1)}, bf16[576,512]{1,0:T(8,128)(2,1)S(1)}, u32[]{:S(2)}, u32[]{:S(2)}) %collective-permute-start.8) | collective-permute-done | bytes 589856 | tf_op jit(solution)/shard_map/ppermute | solution.py:364
  48.3 4.4 %collective-permute-start.11 = (bf16[576,512]{1,0:T(8,128)(2,1)S(1)}, bf16[576,512]{1,0:T(8,128)(2,1)S(1)}, u32[]{:S(2)}, u32[]{:S(2)}) collective-permute-start(bf16[576,512]{1,0:T(8,128)(2,1)S(1)} %collective-permute-done.8.p2), channel_id=1, source_target_pairs={{4,0},{0,4},{12,8},{8,12},{20,16},{16,20},{28,24},{24,28},{36,32},... | collective-permute-start | bytes 1769480 | tf_op jit(solution)/shard_map/ppermute | solution.py:346
  52.6 5.4 %attend.1 = (bf16[512,512]{1,0:T(8,128)(2,1)S(1)}, bf16[40,128,1024]{2,1,0:T(8,128)(2,1)S(1)}) custom-call(s32[8,8]{1,0:T(8,128)S(1)} %copy-done.7, s32[8]{0:T(128)S(1)} %copy-done.8, bf16[1024,512]{1,0:T(8,128)(2,1)S(1)} %collective-permute-done.1.far_ref, bf16[512,512]{1,0:T(8,128)(2,1)S(1)} %get-tuple-element.23.q_ref, ...), custom_call_target="tpu_custom_call", output_to_operand_aliasing={{1}: (5, {})} | custom-call | flops 1610612736 | bytes 10485760 | tf_op jit(solution)/shard_map/attend/pallas_call | solution.py:246
  58.1 5.5 %mlp.1 = (bf16[512,128]{1,0:T(8,128)(2,1)S(1)}, bf16[512,128]{1,0:T(8,128)(2,1)S(1)}, bf16[512,128]{1,0:T(8,128)(2,1)S(1)}, bf16[512,128]{1,0:T(8,128)(2,1)S(1)}) custom-call(bf16[512,512]{1,0:T(8,128)(2,1)S(1)} %get-tuple-element.31.heads_ref, f32[2,2,512]{2,1,0:T(2,128)S(1)} %copy-done.5, f32[2,2,512]{2,1,0:T(2,128)S(1)} %copy-done.6, ...), custom_call_target="tpu_custom_call" | custom-call | flops 2415919104 | bytes 8388608 | tf_op jit(solution)/shard_map/mlp/pallas_call | solution.py:294
  63.8 2.7 %collective-permute-start.13 = (bf16[512,128]{1,0:T(8,128)(2,1)S(1)}, bf16[512,128]{1,0:T(8,128)(2,1)S(1)}, u32[]{:S(2)}, u32[]{:S(2)}) collective-permute-start(bf16[512,128]{1,0:T(8,128)(2,1)S(1)} %get-tuple-element.35), channel_id=1, source_target_pairs={{1,0},{2,1},{3,2},{0,3},{5,4},{6,5},{7,6},{4,7},{9,8},{10,9},{11,1... | collective-permute-start | bytes 393224 | tf_op jit(solution)/shard_map/ppermute | solution.py:370
  66.4 3.7 %collective-permute-done.12.a = bf16[512,128]{1,0:T(8,128)(2,1)S(1)} collective-permute-done((bf16[512,128]{1,0:T(8,128)(2,1)S(1)}, bf16[512,128]{1,0:T(8,128)(2,1)S(1)}, u32[]{:S(2)}, u32[]{:S(2)}) %collective-permute-start.12) | collective-permute-done | bytes 131104 | tf_op jit(solution)/shard_map/ppermute | solution.py:367
  70.1 1.6 %collective-permute-done.13.b = bf16[512,128]{1,0:T(8,128)(2,1)S(1)} collective-permute-done((bf16[512,128]{1,0:T(8,128)(2,1)S(1)}, bf16[512,128]{1,0:T(8,128)(2,1)S(1)}, u32[]{:S(2)}, u32[]{:S(2)}) %collective-permute-start.13) | collective-permute-done | bytes 131104 | tf_op jit(solution)/shard_map/ppermute | solution.py:370
  (33 shorter events, 3.6 us)
Async XLA Ops:
  0.0 15.9 %copy-start = (bf16[512,512]{1,0:T(8,128)(2,1)S(1)}, bf16[512,512]{1,0:T(8,128)(2,1)}, u32[]{:S(2)}) copy-start(bf16[512,512]{1,0:T(8,128)(2,1)} %up_w.1) | copy-start | bytes 1572868
  0.0 15.9 %copy-start.4 = (bf16[128,512]{1,0:T(8,128)(2,1)S(1)}, bf16[128,512]{1,0:T(8,128)(2,1)}, u32[]{:S(2)}) copy-start(bf16[128,512]{1,0:T(8,128)(2,1)} %out_w.1) | copy-start | bytes 393220
  0.0 15.9 %copy-start.2 = (bf16[512,512]{1,0:T(8,128)(2,1)S(1)}, bf16[512,512]{1,0:T(8,128)(2,1)}, u32[]{:S(2)}) copy-start(bf16[512,512]{1,0:T(8,128)(2,1)} %down_w.1) | copy-start | bytes 1572868
  2.1 8.7 %collective-permute-start.3 = (bf16[3,512,128]{2,1,0:T(8,128)(2,1)}, bf16[3,512,128]{2,1,0:T(8,128)(2,1)}, u32[]{:S(2)}, u32[]{:S(2)}) collective-permute-start(bf16[3,512,128]{2,1,0:T(8,128)(2,1)} %bitcast.w0), channel_id=1, source_target_pairs={{3,0},{0,1},{1,2},{2,3},{5,4},{6,5},{7,6},{4,7},{11,8},{8,9},{9,10... | collective-permute-start | bytes 1179656 | tf_op jit(solution)/shard_map/ppermute | solution.py:364
  5.8 20.0 %collective-permute-start = (bf16[1024,512]{1,0:T(8,128)(2,1)S(1)}, bf16[1024,512]{1,0:T(8,128)(2,1)S(1)}, u32[]{:S(2)}, u32[]{:S(2)}) collective-permute-start(bf16[1024,512]{1,0:T(8,128)(2,1)S(1)} %norm_rows.1.xa), channel_id=1, source_target_pairs={{8,0},{252,4},{16,8},{4,12},{24,16},{12,20},{32,24},{20,28},{40,32... | collective-permute-start | bytes 3145736 | tf_op jit(solution)/shard_map/ppermute | solution.py:346
  11.7 5.8 %collective-permute-start.5 = (bf16[3,256,128]{2,1,0:T(8,128)(2,1)S(1)}, bf16[3,256,128]{2,1,0:T(8,128)(2,1)S(1)}, u32[]{:S(2)}, u32[]{:S(2)}) collective-permute-start(bf16[3,256,128]{2,1,0:T(8,128)(2,1)S(1)} %constant_dynamic-slice_fusion.1), channel_id=1, source_target_pairs={{3,0},{0,1},{1,2},{2,3},{5,4},{6,5},{7,6},{4,7},{11,8},{8,9},{9,10... | collective-permute-start | bytes 589832 | tf_op jit(solution)/shard_map/ppermute | solution.py:364
  14.9 18.8 %collective-permute-start.2 = (bf16[1024,512]{1,0:T(8,128)(2,1)S(1)}, bf16[1024,512]{1,0:T(8,128)(2,1)}, u32[]{:S(2)}, u32[]{:S(2)}) collective-permute-start(bf16[1024,512]{1,0:T(8,128)(2,1)S(1)} %norm_rows.1.xa), channel_id=1, source_target_pairs={{4,0},{0,4},{12,8},{8,12},{20,16},{16,20},{28,24},{24,28},{36,32},... | collective-permute-start | bytes 3145736 | tf_op jit(solution)/shard_map/ppermute | solution.py:346
  17.5 20.5 %collective-permute-start.7 = (bf16[1152,512]{1,0:T(8,128)(2,1)}, bf16[1152,512]{1,0:T(8,128)(2,1)}, u32[]{:S(2)}, u32[]{:S(2)}) collective-permute-start(bf16[1152,512]{1,0:T(8,128)(2,1)} %pack_weights.1), channel_id=1, source_target_pairs={{3,0},{0,1},{1,2},{2,3},{5,4},{6,5},{7,6},{4,7},{11,8},{8,9},{9,10... | collective-permute-start | bytes 3538952 | tf_op jit(solution)/shard_map/ppermute | solution.py:364
  20.7 13.1 %collective-permute-start.4 = (bf16[3,512,128]{2,1,0:T(8,128)(2,1)}, bf16[3,512,128]{2,1,0:T(8,128)(2,1)}, u32[]{:S(2)}, u32[]{:S(2)}) collective-permute-start(bf16[3,512,128]{2,1,0:T(8,128)(2,1)} %collective-permute-done.3.w1), channel_id=1, source_target_pairs={{4,0},{0,4},{12,8},{8,12},{20,16},{16,20},{28,24},{24,28},{36,32},... | collective-permute-start | bytes 1179656 | tf_op jit(solution)/shard_map/ppermute | solution.py:346
  25.7 16.1 %collective-permute-start.9 = (bf16[1024,512]{1,0:T(8,128)(2,1)S(1)}, bf16[1024,512]{1,0:T(8,128)(2,1)S(1)}, u32[]{:S(2)}, u32[]{:S(2)}) collective-permute-start(bf16[1024,512]{1,0:T(8,128)(2,1)S(1)} %collective-permute-done.xa), channel_id=1, source_target_pairs={{4,0},{0,4},{12,8},{8,12},{20,16},{16,20},{28,24},{24,28},{36,32},... | collective-permute-start | bytes 3145736 | tf_op jit(solution)/shard_map/ppermute | solution.py:346
  25.7 2.7 %collective-permute-start.6 = (bf16[3,256,128]{2,1,0:T(8,128)(2,1)S(1)}, bf16[3,256,128]{2,1,0:T(8,128)(2,1)}, u32[]{:S(2)}, u32[]{:S(2)}) collective-permute-start(bf16[3,256,128]{2,1,0:T(8,128)(2,1)S(1)} %collective-permute-done.5.w3m), channel_id=1, source_target_pairs={{4,0},{0,4},{12,8},{8,12},{20,16},{16,20},{28,24},{24,28},{36,32},... | collective-permute-start | bytes 589832 | tf_op jit(solution)/shard_map/ppermute | solution.py:346
  28.4 24.2 %collective-permute-start.1 = (bf16[1024,512]{1,0:T(8,128)(2,1)S(1)}, bf16[1024,512]{1,0:T(8,128)(2,1)S(1)}, u32[]{:S(2)}, u32[]{:S(2)}) collective-permute-start(bf16[1024,512]{1,0:T(8,128)(2,1)S(1)} %norm_rows.1.xa), channel_id=1, source_target_pairs={{248,0},{12,4},{0,8},{20,12},{8,16},{28,20},{16,24},{36,28},{24,32... | collective-permute-start | bytes 3145736 | tf_op jit(solution)/shard_map/ppermute | solution.py:346
  39.2 9.1 %collective-permute-start.8 = (bf16[576,512]{1,0:T(8,128)(2,1)S(1)}, bf16[576,512]{1,0:T(8,128)(2,1)S(1)}, u32[]{:S(2)}, u32[]{:S(2)}) collective-permute-start(bf16[576,512]{1,0:T(8,128)(2,1)S(1)} %constant_dynamic-slice_fusion), channel_id=1, source_target_pairs={{3,0},{0,1},{1,2},{2,3},{5,4},{6,5},{7,6},{4,7},{11,8},{8,9},{9,10... | collective-permute-start | bytes 1769480 | tf_op jit(solution)/shard_map/ppermute | solution.py:364
  40.6 17.5 %collective-permute-start.10 = (bf16[1152,512]{1,0:T(8,128)(2,1)}, bf16[1152,512]{1,0:T(8,128)(2,1)S(1)}, u32[]{:S(2)}, u32[]{:S(2)}) collective-permute-start(bf16[1152,512]{1,0:T(8,128)(2,1)} %collective-permute-done.7.p1), channel_id=1, source_target_pairs={{4,0},{0,4},{12,8},{8,12},{20,16},{16,20},{28,24},{24,28},{36,32},... | collective-permute-start | bytes 3538952 | tf_op jit(solution)/shard_map/ppermute | solution.py:346
  41.8 10.8 %copy-start.7 = (s32[8,8]{1,0:T(8,128)S(1)}, s32[8,8]{1,0:T(8,128)}, u32[]{:S(2)}) copy-start(s32[8,8]{1,0:T(8,128)} %list_ref.1) | copy-start | bytes 772
  41.8 10.8 %copy-start.8 = (s32[8]{0:T(128)S(1)}, s32[8]{0:T(128)}, u32[]{:S(2)}) copy-start(s32[8]{0:T(128)} %count_ref.1) | copy-start | bytes 100
  44.2 13.9 %copy-start.1 = (bf16[512,512]{1,0:T(8,128)(2,1)S(1)}, bf16[512,512]{1,0:T(8,128)(2,1)}, u32[]{:S(2)}) copy-start(bf16[512,512]{1,0:T(8,128)(2,1)} %up_w.1) | copy-start | bytes 1572868
  44.2 13.9 %copy-start.3 = (bf16[512,512]{1,0:T(8,128)(2,1)S(1)}, bf16[512,512]{1,0:T(8,128)(2,1)}, u32[]{:S(2)}) copy-start(bf16[512,512]{1,0:T(8,128)(2,1)} %down_w.1) | copy-start | bytes 1572868
  44.2 13.9 %copy-start.5 = (f32[2,2,512]{2,1,0:T(2,128)S(1)}, f32[2,2,512]{2,1,0:T(2,128)}, u32[]{:S(2)}) copy-start(f32[2,2,512]{2,1,0:T(2,128)} %gain_ref.3) | copy-start | bytes 24580
  44.2 13.9 %copy-start.6 = (f32[2,2,512]{2,1,0:T(2,128)S(1)}, f32[2,2,512]{2,1,0:T(2,128)}, u32[]{:S(2)}) copy-start(f32[2,2,512]{2,1,0:T(2,128)} %shift_ref.3) | copy-start | bytes 24580
  48.3 9.8 %collective-permute-start.11 = (bf16[576,512]{1,0:T(8,128)(2,1)S(1)}, bf16[576,512]{1,0:T(8,128)(2,1)S(1)}, u32[]{:S(2)}, u32[]{:S(2)}) collective-permute-start(bf16[576,512]{1,0:T(8,128)(2,1)S(1)} %collective-permute-done.8.p2), channel_id=1, source_target_pairs={{4,0},{0,4},{12,8},{8,12},{20,16},{16,20},{28,24},{24,28},{36,32},... | collective-permute-start | bytes 1769480 | tf_op jit(solution)/shard_map/ppermute | solution.py:346
  63.7 6.4 %collective-permute-start.12 = (bf16[512,128]{1,0:T(8,128)(2,1)S(1)}, bf16[512,128]{1,0:T(8,128)(2,1)S(1)}, u32[]{:S(2)}, u32[]{:S(2)}) collective-permute-start(bf16[512,128]{1,0:T(8,128)(2,1)S(1)} %get-tuple-element.34), channel_id=1, source_target_pairs={{0,1},{1,2},{2,3},{3,0},{4,5},{5,6},{6,7},{7,4},{8,9},{9,10},{10,1... | collective-permute-start | bytes 393224 | tf_op jit(solution)/shard_map/ppermute | solution.py:367
  63.8 7.9 %collective-permute-start.13 = (bf16[512,128]{1,0:T(8,128)(2,1)S(1)}, bf16[512,128]{1,0:T(8,128)(2,1)S(1)}, u32[]{:S(2)}, u32[]{:S(2)}) collective-permute-start(bf16[512,128]{1,0:T(8,128)(2,1)S(1)} %get-tuple-element.35), channel_id=1, source_target_pairs={{1,0},{2,1},{3,2},{0,3},{5,4},{6,5},{7,6},{4,7},{9,8},{10,9},{11,1... | collective-permute-start | bytes 393224 | tf_op jit(solution)/shard_map/ppermute | solution.py:370
  66.4 6.0 %collective-permute-start.14 = (bf16[512,128]{1,0:T(8,128)(2,1)S(1)}, bf16[512,128]{1,0:T(8,128)(2,1)S(1)}, u32[]{:S(2)}, u32[]{:S(2)}) collective-permute-start(bf16[512,128]{1,0:T(8,128)(2,1)S(1)} %get-tuple-element.36), channel_id=1, source_target_pairs={{0,2},{1,3},{2,0},{3,1},{4,6},{5,7},{6,4},{7,5},{8,10},{9,11},{10,... | collective-permute-start | bytes 393224 | tf_op jit(solution)/shard_map/ppermute | solution.py:373

commit v5 on v4

--- a/solution.py
+++ b/solution.py
@@ -45,10 +45,6 @@
 
 def kept_in_hbm(v):
     return pltpu.with_memory_space_constraint(v, pltpu.HBM)
-
-
-def cost(flops, nbytes, exps=0):
-    return pl.CostEstimate(flops=flops, bytes_accessed=nbytes, transcendentals=exps)
 
 
 def normalise(values, gain, shift):
@@ -102,28 +98,50 @@
         ],
         name="norm_rows",
         compiler_params=pltpu.CompilerParams(vmem_limit_bytes=8 * MIB),
-        cost_estimate=cost(10 * rows * width, 4 * rows * width),
     )(kept_in_hbm(state), kept_in_hbm(gain), kept_in_hbm(shift))
 
 
-def pack_kernel(up_ref, out_ref, down_ref, o_ref):
-    at = 0
-    for r in (up_ref, out_ref, down_ref):
-        o_ref[at : at + r.shape[0]] = r[...]
-        at += r.shape[0]
-
-
-def packed(up_w, out_w, down_w):
-    rows = up_w.shape[0] + out_w.shape[0] + down_w.shape[0]
+def pack_kernel(qkv_ref, out_ref, o_ref):
+    parts = qkv_ref.shape[0]
+    head = NODE_BLK
+    o_ref[:parts] = qkv_ref[...]
+    for k in range(HEADS):
+        o_ref[parts, k * head : (k + 1) * head] = out_ref[:, k * head : (k + 1) * head]
+
+
+def packed(qkv, out_w):
+    parts, width, head = qkv.shape
     return pl.pallas_call(
         pack_kernel,
-        in_specs=[VMEM] * 3,
+        in_specs=[VMEM] * 2,
         out_specs=VMEM,
-        out_shape=in_hbm((rows, up_w.shape[1])),
+        out_shape=in_vmem((parts + 1, width, head)),
         name="pack_weights",
-        compiler_params=pltpu.CompilerParams(vmem_limit_bytes=8 * MIB),
-        cost_estimate=cost(0, 4 * rows * up_w.shape[1]),
-    )(up_w, out_w, down_w)
+        compiler_params=pltpu.CompilerParams(vmem_limit_bytes=4 * MIB),
+    )(qkv, out_w)
+
+
+def relay_kernel(a_ref, b_ref, o_ref):
+    par = my_place()[2]
+
+    @pl.when(par == 0)
+    def _():
+        o_ref[...] = a_ref[...]
+
+    @pl.when(par == 1)
+    def _():
+        o_ref[...] = b_ref[...]
+
+
+def one_to_relay(a, b):
+    return pl.pallas_call(
+        relay_kernel,
+        in_specs=[VMEM] * 2,
+        out_specs=VMEM,
+        out_shape=in_vmem(a.shape),
+        name="one_to_relay",
+        compiler_params=pltpu.CompilerParams(vmem_limit_bytes=4 * MIB),
+    )(a, b)
 
 
 def write_kv(x_ref, wkv_ref, kv_ref, first):
@@ -134,10 +152,11 @@
         kv_ref[at : at + ROWS // NODE_BLK] = out.reshape((ROWS // NODE_BLK, NODE_BLK, 2 * width))
 
 
-def kv_first_kernel(xa, xb, w0, w1, w2, w3m, w3t, kv_ref, q_ref, wkv_ref, wq_ref):
+def kv_first_kernel(xa, xb, w0, w1, w2, w3m, w3t, kv_ref, q_ref, wkv_ref, wo_ref, wq_ref):
     head = NODE_BLK
     _, share, par, _, _ = my_place()
     half = w3m.shape[1]
+    halves = ((par, w3m), (1 - par, w3t))
     for h in range(HEADS):
         at = (h // 2) * 4 * head + (h % 2) * head
         spots = ((0, wq_ref, h * head), (1, wkv_ref, at), (2, wkv_ref, at + 2 * head))
@@ -145,8 +164,18 @@
             if h < 3:
                 dst[:, col : col + head] = (w0, w1, w2)[h][c]
             else:
-                dst[aligned(par, half), col : col + head] = w3m[c]
-                dst[aligned(1 - par, half), col : col + head] = w3t[c]
+                for which, w in halves:
+                    dst[aligned(which, half), col : col + head] = w[c]
+        rows = slice(h * head, (h + 1) * head)
+        if h < 3:
+            for k in range(HEADS):
+                wo_ref[rows, k * head : (k + 1) * head] = (w0, w1, w2)[h][3, k * head : (k + 1) * head]
+        else:
+            for which, w in halves:
+                for k in range(HEADS // 2):
+                    wo_ref[rows, aligned(which * (HEADS // 2) + k, head)] = w[
+                        3, k * head : (k + 1) * head
+                    ]
     write_kv(xa, wkv_ref, kv_ref, 0)
     write_kv(xb, wkv_ref, kv_ref, xa.shape[0] // NODE_BLK)
     q_ref[...] = bf(matmul(xa[aligned(share, q_ref.shape[0])], wq_ref[...]))
@@ -157,16 +186,16 @@
     return pl.pallas_call(
         kv_first_kernel,
         in_specs=[VMEM] * (2 + len(weights)),
-        out_specs=[VMEM] * 3,
+        out_specs=[VMEM] * 4,
         scratch_shapes=[pltpu.VMEM((width, width), jnp.bfloat16)],
         out_shape=[
             in_vmem((slots * rows // NODE_BLK, NODE_BLK, 2 * width)),
             in_vmem((rows // 2, width)),
             in_vmem((width, 2 * width)),
+            in_vmem((width, width)),
         ],
         name="kv_first",
         compiler_params=pltpu.CompilerParams(vmem_limit_bytes=16 * MIB),
-        cost_estimate=cost(8 * rows * width * width, 8 * MIB),
     )(xa, xb, *weights)
 
 
@@ -186,17 +215,16 @@
         input_output_aliases={3: 0},
         name="kv_second",
         compiler_params=pltpu.CompilerParams(vmem_limit_bytes=16 * MIB),
-        cost_estimate=cost(8 * rows * width * width, 7 * MIB),
     )(xa, xb, wkv, kv)
 
 
 def attend_kernel(
-    list_ref, count_ref, far_ref, q_ref, wkv_ref, kv_in, heads_ref, kv, *, doms, per_dev
+    list_ref, count_ref, relay_ref, q_ref, wkv_ref, kv_in, heads_ref, kv, *, doms, per_dev
 ):
     _, share, par, _, dom = my_place()
     head = NODE_BLK
     rows, width = q_ref.shape
-    write_kv(far_ref, wkv_ref, kv, 4 * per_dev)
+    write_kv(relay_ref, wkv_ref, kv, 4 * per_dev)
 
     scale = math.log2(math.e) / math.sqrt(head)
     blocks = rows // NODE_BLK
@@ -209,9 +237,7 @@
             part = lax.div(entry, per_dev)
             step = lax.rem(part - dom + (doms + 2), doms) - 2
             turned = jnp.where(par == 0, step, -step)
-            slot = jnp.where(
-                turned >= 0, jnp.where(turned == 0, 0, turned), jnp.where(turned == -1, 3, 4)
-            )
+            slot = jnp.where(turned >= 0, turned, turned + 5)
             where.append(slot * per_dev + lax.rem(entry, per_dev))
         at = slice(b * NODE_BLK, (b + 1) * NODE_BLK)
         for pair in range(HEADS // 2):
@@ -241,7 +267,7 @@
             heads_ref[at, (2 * pair + 1) * head : (2 * pair + 2) * head] = bf(mixed[head:, head:])
 
 
-def attend(listed, counts, far, query, wkv, kv, per_dev, doms):
+def attend(listed, counts, relay, query, wkv, kv, per_dev, doms):
     rows, width = query.shape
     return pl.pallas_call(
         functools.partial(attend_kernel, doms=doms, per_dev=per_dev),
@@ -251,62 +277,85 @@
         input_output_aliases={5: 1},
         name="attend",
         compiler_params=pltpu.CompilerParams(vmem_limit_bytes=16 * MIB),
-        cost_estimate=cost(
-            4 * rows * width * KMAX * NODE_BLK + 4 * rows * width**2,
-            10 * MIB,
-            rows * HEADS * KMAX * NODE_BLK,
-        ),
-    )(listed, counts, far, query, wkv, kv)[0]
-
-
-def mlp_kernel(
-    heads_ref, gain_ref, shift_ref, out_w, up_w, down_w, p1, p1s, p2, p2s, state_ref,
-    o0, o1, o2, o3,
-    rows_in, last, resid_ref, hidden_ref, sem,
+    )(listed, counts, relay, query, wkv, kv)[0]
+
+
+def silu(v):
+    return 0.5 * v * (1.0 + jnp.tanh(0.5 * v))
+
+
+def mlp_first_kernel(
+    heads_ref, gain_ref, shift_ref, wo_ref, u0, d0, u1, d1, u2, d2, state_ref,
+    resid_ref, normed_ref,
+    rows_in, hidden_ref, sem,
 ):
-    sample, share, par, rank, _ = my_place()
-    head = NODE_BLK
+    sample, share, _, _, _ = my_place()
     rows, width = heads_ref.shape
     copy = pltpu.make_async_copy(state_ref.at[sample, aligned(share, rows)], rows_in, sem)
     copy.start()
-    half = p2.shape[0]
-    last[aligned(par, half)] = p2[...]
-    last[aligned(1 - par, half)] = p2s[...]
-    packs = (p1, p1s, last)
-    out_all = jnp.concatenate([out_w[...]] + [p[width : width + head] for p in packs], axis=0)
-    mixed = matmul(heads_ref[...], out_all)
+    mixed = matmul(heads_ref[...], wo_ref[...])
     copy.wait()
     resid_ref[...] = rows_in[...].astype(jnp.float32) + mixed
     s = pl.ds(sample, 1)
-    normed = bf(normalise(resid_ref[...], gain_ref[1, s], shift_ref[1, s]))
-    for h in range(HEADS):
-        v = matmul(normed, up_w[...] if h == 0 else packs[h - 1][:width])
-        hidden_ref[:, h * width : (h + 1) * width] = bf(0.5 * v * (1.0 + jnp.tanh(0.5 * v)))
-    down_all = jnp.concatenate([down_w[...]] + [p[width + head :] for p in packs], axis=0)
-    resid_ref[...] += matmul(hidden_ref[...], down_all)
-    for r, o_ref in enumerate((o0, o1, o2, o3)):
-        o_ref[...] = bf(resid_ref[:, aligned(lax.rem(rank + r, HEADS), head)])
-
-
-def mlp(heads, gain, shift, weights, state):
+    normed_ref[...] = bf(normalise(resid_ref[...], gain_ref[1, s], shift_ref[1, s]))
+    for k, u in enumerate((u0, u1, u2)):
+        hidden_ref[:, k * width : (k + 1) * width] = bf(silu(matmul(normed_ref[...], u[...])))
+    downs = jnp.concatenate([d0[...], d1[...], d2[...]], axis=0)
+    resid_ref[...] += matmul(hidden_ref[...], downs)
+
+
+def mlp_first(heads, gain, shift, wo, weights, state):
     rows, width = heads.shape
-    head = NODE_BLK
-    return pl.pallas_call(
-        mlp_kernel,
-        in_specs=[VMEM] * (3 + len(weights)) + [HBM],
-        out_specs=[VMEM] * HEADS,
-        out_shape=[shape((rows, head))] * HEADS,
+    return pl.pallas_call(
+        mlp_first_kernel,
+        in_specs=[VMEM] * (4 + len(weights)) + [HBM],
+        out_specs=[VMEM] * 2,
+        out_shape=[in_vmem((rows, width), jnp.float32), in_vmem((rows, width))],
         scratch_shapes=[
             pltpu.VMEM((rows, width), jnp.bfloat16),
-            pltpu.VMEM((2 * width + head, width), jnp.bfloat16),
-            pltpu.VMEM((rows, width), jnp.float32),
-            pltpu.VMEM((rows, HEADS * width), jnp.bfloat16),
+            pltpu.VMEM((rows, 3 * width), jnp.bfloat16),
             pltpu.SemaphoreType.DMA,
         ],
-        name="mlp",
-        compiler_params=pltpu.CompilerParams(vmem_limit_bytes=24 * MIB),
-        cost_estimate=cost(18 * rows * width * width, 8 * MIB, rows * HEADS * width),
-    )(heads, gain, shift, *weights, kept_in_hbm(state))
+        name="mlp_first",
+        compiler_params=pltpu.CompilerParams(vmem_limit_bytes=16 * MIB),
+    )(heads, gain, shift, wo, *weights, kept_in_hbm(state))
+
+
+def mlp_second_kernel(resid_ref, normed_ref, mine, theirs, o0, o1, o2, o3, total_ref, up_ref, down_ref):
+    _, _, par, rank, _ = my_place()
+    head = NODE_BLK
+
+    @pl.when(par == 0)
+    def _():
+        up_ref[...] = mine[...]
+        down_ref[...] = theirs[...]
+
+    @pl.when(par == 1)
+    def _():
+        up_ref[...] = theirs[...]
+        down_ref[...] = mine[...]
+
+    hidden = bf(silu(matmul(normed_ref[...], up_ref[...])))
+    total_ref[...] = resid_ref[...] + matmul(hidden, down_ref[...])
+    for r, o_ref in enumerate((o0, o1, o2, o3)):
+        o_ref[...] = bf(total_ref[:, aligned(lax.rem(rank + r, HEADS), head)])
+
+
+def mlp_second(resid, normed, mine, theirs):
+    rows, width = normed.shape
+    return pl.pallas_call(
+        mlp_second_kernel,
+        in_specs=[VMEM] * 4,
+        out_specs=[VMEM] * HEADS,
+        out_shape=[in_vmem((rows, width // HEADS))] * HEADS,
+        scratch_shapes=[
+            pltpu.VMEM((rows, width), jnp.float32),
+            pltpu.VMEM(mine.shape, jnp.bfloat16),
+            pltpu.VMEM(mine.shape, jnp.bfloat16),
+        ],
+        name="mlp_second",
+        compiler_params=pltpu.CompilerParams(vmem_limit_bytes=16 * MIB),
+    )(resid, normed, mine, theirs)
 
 
 def place_kernel(own, a, b, c, o_ref):
@@ -324,7 +373,6 @@
         out_shape=shape((HEADS, rows, head)),
         name="place_rows",
         compiler_params=pltpu.CompilerParams(vmem_limit_bytes=4 * MIB),
-        cost_estimate=cost(0, 16 * rows * head),
     )(*pieces)
 
 
@@ -372,34 +420,35 @@
     def across(v):
         return lax.ppermute(v, "tp", [(i, (i + 2) % tps) for i in range(tps)])
 
-    own = normed_rows(state, norm_gain, norm_shift)
-    qkv = jnp.transpose(qkv_weight, (1, 0, 2))
-    w1 = ring(after(qkv, own))
-    near_rows = near(own)
+    w0 = packed(jnp.transpose(qkv_weight, (1, 0, 2)), out_weight)
+    w1 = ring(w0)
+    own = normed_rows(after(state, w0), norm_gain, norm_shift)
     partner = swap(own)
-    pack = packed(after(up_weight, own), out_weight, down_weight)
-
+    near_rows, far_rows = near(own), far(own)
+
+    w1 = after(w1, partner)
     w2 = swap(w1)
     mid = width // 2
-    w3m = ring(lax.dynamic_slice_in_dim(w1, par * mid, mid, 1))
+    w1_half = lax.dynamic_slice_in_dim(w1, par * mid, mid, 1)
+    w3m = ring(w1_half)
     w3t = swap(w3m)
-    p1 = ring(after(pack, w3m))
-
-    own_late, near_rows = lax.optimization_barrier((own, near_rows))
-    far_rows = far(own_late)
+    up_late, down_late, w1_half = lax.optimization_barrier((up_weight, down_weight, w1_half))
+    u1, d1 = ring(up_late), ring(down_late)
+
+    kv, query, wkv, wo = kv_first(own, partner, (w0, w1, w2, w3m, w3t), 5)
+    near_rows, far_rows, query = lax.optimization_barrier((near_rows, far_rows, query))
     relay = swap(near_rows)
-    kv, query, wkv = kv_first(own_late, partner, (qkv, w1, w2, w3m, w3t), 5)
-    mid = pack.shape[0] // 2
-    p1 = after(p1, query)
-    p1s = swap(p1)
-    p2 = ring(lax.dynamic_slice_in_dim(p1, par * mid, mid, 0))
-    kv = kv_second(near_rows, relay, wkv, kv)
-    p2, kv = lax.optimization_barrier((p2, kv))
-    p2s = swap(p2)
-
-    heads = attend(neighbours, counts, far_rows, query, wkv, kv, per_dev, doms)
-    weights = (out_weight, up_weight, down_weight, p1, p1s, p2, p2s)
-    mine = mlp(heads, norm_gain, norm_shift, weights, state)
+    u1, d1 = lax.optimization_barrier((u1, d1, query))[:2]
+    u2, d2 = swap(u1), swap(d1)
+    last = ring(one_to_relay(u1, d1))
+    kv = kv_second(near_rows, far_rows, wkv, kv)
+
+    heads = attend(neighbours, counts, relay, query, wkv, kv, per_dev, doms)
+    last, heads = lax.optimization_barrier((last, heads))
+    last_too = swap(last)
+    weights = (up_weight, down_weight, u1, d1, u2, d2)
+    resid, normed = mlp_first(heads, norm_gain, norm_shift, wo, weights, state)
+    mine = mlp_second(resid, normed, last, last_too)
     out = placed_rows((mine[0], up(mine[1]), down(mine[3]), across(mine[2])))
     return out.reshape(samples, row_count, width // tps)
 

time: 73.6 us -> 67.9 us (0.923)
  starting transfers between devices: 29.7 us -> 24 us
  waiting for transfers between devices: 19.6 us -> 21 us
  Pallas kernels: 21.7 us -> 20.4 us
    ppermute x4 -> x5, starting transfers between devices: 11.4 us -> 1.63 us  [ring(): return lax.ppermute(v, ('dom', 'tp'), pairs)]
    ppermute x8 -> x9, waiting for transfers between devices: 5.29 us -> 8.95 us  [hop(): return lax.ppermute(v, 'dom', pairs)]
    ppermute x8 -> x9, starting transfers between devices: 15.5 us -> 18.8 us  [hop(): return lax.ppermute(v, 'dom', pairs)]
    ppermute x4 -> x5, waiting for transfers between devices: 8.36 us -> 5.62 us  [ring(): return lax.ppermute(v, ('dom', 'tp'), pairs)]
    pallas_call x2 -> x4, Pallas kernels: 6.67 us -> 4.57 us  [the longest x1 3.49 us: mlp_first(): pl.pallas_call(mlp_first_kernel, in_specs=[VMEM] * (4 + len(weights)) + [...]
    dynamic_slice x2 -> x1, local copies, waits for them, and re-layouts: 2.05 us -> 0.02 us  [local(): w1_half = lax.dynamic_slice_in_dim(w1, par * mid, mid, 1)]
    unnamed x18 -> x16, local copies, waits for them, and re-layouts: 0.04 us -> 1.93 us
    ppermute x1, waiting for transfers between devices: 0.72 us -> 2 us  [across(): return lax.ppermute(v, 'tp', [(i, (i + 2) % tps) for i in range(tps)])]
  transfers between devices with their start and end apart: 15 -> 17, of which waited for: 8 -> 7; matrix products, arithmetic and copies ran while one was open for 3% -> 0% of each run, Pallas kernels for 18% -> 24%
where the time goes in v5:
time: 67.9 us; the launch traced here: 67.6 us
  starting transfers between devices  24 us (35%)
  waiting for transfers between devices  21 us (31%)
  Pallas kernels  20.4 us (30%)
  local copies, waits for them, and re-layouts  1.95 us (3%)
    ppermute x9, starting transfers between devices, hop(): return lax.ppermute(v, 'dom', pairs)  18.8 us
    ppermute x9, waiting for transfers between devices, hop(): return lax.ppermute(v, 'dom', pairs)  8.95 us
    ppermute x5, waiting for transfers between devices, ring(): return lax.ppermute(v, ('dom', 'tp'), pairs)  5.62 us
    pallas_call x1, Pallas kernels, attend(): pl.pallas_call(functools.partial(attend_kernel, doms=doms, per_dev=per_de...  5.42 us
    pallas_call x1, Pallas kernels, kv_first(): pl.pallas_call(kv_first_kernel, in_specs=[VMEM] * (2 + len(weights)), out...  4 us
    pallas_call x1, Pallas kernels, kv_second(): pl.pallas_call(kv_second_kernel, in_specs=[VMEM] * 4, out_specs=VMEM, out...  3.59 us
    pallas_call x1, Pallas kernels, mlp_first(): pl.pallas_call(mlp_first_kernel, in_specs=[VMEM] * (4 + len(weights)) + [...  3.49 us
    ppermute x1, waiting for transfers between devices, up(): return lax.ppermute(v, 'tp', [(i, (i + 1) % tps) for i in range(tps)])  2.82 us
  transfers between devices with their start and end apart: 17, of which 7 were waited for; matrix products, arithmetic and copies ran while one was open for 0% of the time, Pallas kernels for 24%

profile of v5, /device:TPU:1, one launch (start us, length us, event | category | flops | bytes accessed | tf_op | source)
XLA Modules:
  0.0 67.6 jit_solution(720668058085879525)
XLA Ops:
  0.0 1.0 %copy-done.2 = bf16[512,3,128]{2,0,1:T(8,128)(2,1)S(1)} copy-done((bf16[512,3,128]{2,0,1:T(8,128)(2,1)S(1)}, bf16[512,3,128]{2,0,1:T(8,128)(2,1)}, u32[]{:S(2)}) %copy-start.2) | copy-done | bytes 393240
  1.0 0.9 %copy-done.3 = bf16[128,512]{1,0:T(8,128)(2,1)S(1)} copy-done((bf16[128,512]{1,0:T(8,128)(2,1)S(1)}, bf16[128,512]{1,0:T(8,128)(2,1)}, u32[]{:S(2)}) %copy-start.3) | copy-done | bytes 131096
  2.0 2.0 %norm_rows.1.xa = bf16[1024,512]{1,0:T(8,128)(2,1)S(1)} custom-call(bf16[2,1024,512]{2,1,0:T(8,128)(2,1)} %state_ref.2, f32[2,2,512]{2,1,0:T(2,128)} %gain_ref.3, f32[2,2,512]{2,1,0:T(2,128)} %shift_ref.3), custom_call_target="tpu_custom_call" | custom-call | tf_op jit(solution)/shard_map/norm_rows/pallas_call | solution.py:89
  4.0 3.3 %collective-permute-start.1 = (bf16[1024,512]{1,0:T(8,128)(2,1)S(1)}, bf16[1024,512]{1,0:T(8,128)(2,1)}, u32[]{:S(2)}, u32[]{:S(2)}) collective-permute-start(bf16[1024,512]{1,0:T(8,128)(2,1)S(1)} %norm_rows.1.xa), channel_id=1, source_target_pairs={{4,0},{0,4},{12,8},{8,12},{20,16},{16,20},{28,24},{24,28},{36,32},... | collective-permute-start | bytes 3145736 | tf_op jit(solution)/shard_map/ppermute | solution.py:394
  7.3 1.0 %collective-permute-start = (bf16[4,512,128]{2,1,0:T(8,128)(2,1)S(1)}, bf16[4,512,128]{2,1,0:T(8,128)(2,1)S(1)}, u32[]{:S(2)}, u32[]{:S(2)}) collective-permute-start(bf16[4,512,128]{2,1,0:T(8,128)(2,1)S(1)} %pack_weights.1.w0), channel_id=1, source_target_pairs={{3,0},{0,1},{1,2},{2,3},{5,4},{6,5},{7,6},{4,7},{11,8},{8,9},{9,10... | collective-permute-start | bytes 1572872 | tf_op jit(solution)/shard_map/ppermute | solution.py:412
  8.3 1.2 %collective-permute-start.4 = (bf16[1024,512]{1,0:T(8,128)(2,1)S(1)}, bf16[1024,512]{1,0:T(8,128)(2,1)S(1)}, u32[]{:S(2)}, u32[]{:S(2)}) collective-permute-start(bf16[1024,512]{1,0:T(8,128)(2,1)S(1)} %norm_rows.1.xa), channel_id=1, source_target_pairs={{8,0},{252,4},{16,8},{4,12},{24,16},{12,20},{32,24},{20,28},{40,32... | collective-permute-start | bytes 3145736 | tf_op jit(solution)/shard_map/ppermute | solution.py:394
  9.5 6.6 %collective-permute-start.5 = (bf16[1024,512]{1,0:T(8,128)(2,1)S(1)}, bf16[1024,512]{1,0:T(8,128)(2,1)}, u32[]{:S(2)}, u32[]{:S(2)}) collective-permute-start(bf16[1024,512]{1,0:T(8,128)(2,1)S(1)} %norm_rows.1.xa), channel_id=1, source_target_pairs={{248,0},{12,4},{0,8},{20,12},{8,16},{28,20},{16,24},{36,28},{24,32... | collective-permute-start | bytes 3145736 | tf_op jit(solution)/shard_map/ppermute | solution.py:394
  16.1 1.7 %collective-permute-start.6 = (bf16[4,512,128]{2,1,0:T(8,128)(2,1)S(1)}, bf16[4,512,128]{2,1,0:T(8,128)(2,1)S(1)}, u32[]{:S(2)}, u32[]{:S(2)}) collective-permute-start(bf16[4,512,128]{2,1,0:T(8,128)(2,1)S(1)} %collective-permute-done.w1), channel_id=1, source_target_pairs={{4,0},{0,4},{12,8},{8,12},{20,16},{16,20},{28,24},{24,28},{36,32},... | collective-permute-start | bytes 1572872 | tf_op jit(solution)/shard_map/ppermute | solution.py:394
  17.9 5.6 %collective-permute-done.7.w3m = bf16[4,256,128]{2,1,0:T(8,128)(2,1)S(1)} collective-permute-done((bf16[4,256,128]{2,1,0:T(8,128)(2,1)S(1)}, bf16[4,256,128]{2,1,0:T(8,128)(2,1)S(1)}, u32[]{:S(2)}, u32[]{:S(2)}) %collective-permute-start.7) | collective-permute-done | bytes 262176 | tf_op jit(solution)/shard_map/ppermute | solution.py:412
  23.5 2.0 %collective-permute-start.8 = (bf16[4,256,128]{2,1,0:T(8,128)(2,1)S(1)}, bf16[4,256,128]{2,1,0:T(8,128)(2,1)S(1)}, u32[]{:S(2)}, u32[]{:S(2)}) collective-permute-start(bf16[4,256,128]{2,1,0:T(8,128)(2,1)S(1)} %collective-permute-done.7.w3m), channel_id=1, source_target_pairs={{4,0},{0,4},{12,8},{8,12},{20,16},{16,20},{28,24},{24,28},{36,32},... | collective-permute-start | bytes 786440 | tf_op jit(solution)/shard_map/ppermute | solution.py:394
  25.5 1.1 %collective-permute-done.8.w3t = bf16[4,256,128]{2,1,0:T(8,128)(2,1)S(1)} collective-permute-done((bf16[4,256,128]{2,1,0:T(8,128)(2,1)S(1)}, bf16[4,256,128]{2,1,0:T(8,128)(2,1)S(1)}, u32[]{:S(2)}, u32[]{:S(2)}) %collective-permute-start.8) | collective-permute-done | bytes 262176 | tf_op jit(solution)/shard_map/ppermute | solution.py:394
  26.6 4.0 %kv_first.1 = (bf16[40,128,1024]{2,1,0:T(8,128)(2,1)S(1)}, bf16[512,512]{1,0:T(8,128)(2,1)S(1)}, bf16[512,1024]{1,0:T(8,128)(2,1)S(1)}, bf16[512,512]{1,0:T(8,128)(2,1)S(1)}) custom-call(bf16[1024,512]{1,0:T(8,128)(2,1)S(1)} %norm_rows.1.xa, bf16[1024,512]{1,0:T(8,128)(2,1)} %collective-permute-done.1.xb, bf16[4,512,128]{2,1,0:T(8,128)(2,1)S(1)} %pack_weights.1.w0, ...), custom_call_target="tpu_custom_call" | custom-call | tf_op jit(solution)/shard_map/kv_first/pallas_call | solution.py:186
  30.6 4.7 %collective-permute-done.4.xa = bf16[1024,512]{1,0:T(8,128)(2,1)S(1)} collective-permute-done((bf16[1024,512]{1,0:T(8,128)(2,1)S(1)}, bf16[1024,512]{1,0:T(8,128)(2,1)S(1)}, u32[]{:S(2)}, u32[]{:S(2)}) %collective-permute-start.4) | collective-permute-done | bytes 1048608 | tf_op jit(solution)/shard_map/ppermute | solution.py:394
  35.4 3.1 %collective-permute-done.5.xb = bf16[1024,512]{1,0:T(8,128)(2,1)} collective-permute-done((bf16[1024,512]{1,0:T(8,128)(2,1)S(1)}, bf16[1024,512]{1,0:T(8,128)(2,1)}, u32[]{:S(2)}, u32[]{:S(2)}) %collective-permute-start.5) | collective-permute-done | bytes 1048608 | tf_op jit(solution)/shard_map/ppermute | solution.py:394
  38.4 1.8 %collective-permute-start.10 = (bf16[1024,512]{1,0:T(8,128)(2,1)S(1)}, bf16[1024,512]{1,0:T(8,128)(2,1)S(1)}, u32[]{:S(2)}, u32[]{:S(2)}) collective-permute-start(bf16[1024,512]{1,0:T(8,128)(2,1)S(1)} %collective-permute-done.4.xa), channel_id=1, source_target_pairs={{4,0},{0,4},{12,8},{8,12},{20,16},{16,20},{28,24},{24,28},{36,32},... | collective-permute-start | bytes 3145736 | tf_op jit(solution)/shard_map/ppermute | solution.py:394
  40.9 1.0 %collective-permute-start.11 = (bf16[512,512]{1,0:T(8,128)(2,1)S(1)}, bf16[512,512]{1,0:T(8,128)(2,1)S(1)}, u32[]{:S(2)}, u32[]{:S(2)}) collective-permute-start(bf16[512,512]{1,0:T(8,128)(2,1)S(1)} %collective-permute-done.2.a_ref.u1), channel_id=1, source_target_pairs={{4,0},{0,4},{12,8},{8,12},{20,16},{16,20},{28,24},{24,28},{36,32},... | collective-permute-start | bytes 1572872 | tf_op jit(solution)/shard_map/ppermute | solution.py:394
  42.2 3.6 %kv_second.1.kv_in = bf16[40,128,1024]{2,1,0:T(8,128)(2,1)S(1)} custom-call(bf16[1024,512]{1,0:T(8,128)(2,1)S(1)} %collective-permute-done.4.xa, bf16[1024,512]{1,0:T(8,128)(2,1)} %collective-permute-done.5.xb, bf16[512,1024]{1,0:T(8,128)(2,1)S(1)} %get-tuple-element.36.wkv_ref, ...), custom_call_target="tpu_custom_call", output_to_operand_aliasing={{}: (3, {})} | custom-call | tf_op jit(solution)/shard_map/kv_second/pallas_call | solution.py:210
  45.9 5.4 %attend.1 = (bf16[512,512]{1,0:T(8,128)(2,1)S(1)}, bf16[40,128,1024]{2,1,0:T(8,128)(2,1)S(1)}) custom-call(s32[8,8]{1,0:T(8,128)S(1)} %copy-done.6, s32[8]{0:T(128)S(1)} %copy-done.7, bf16[1024,512]{1,0:T(8,128)(2,1)S(1)} %collective-permute-done.10.relay_ref, bf16[512,512]{1,0:T(8,128)(2,1)S(1)} %get-tuple-element.32.q_ref, ...), custom_call_target="tpu_custom_call", output_to_operand_aliasing={{1}: (5, {})} | custom-call | tf_op jit(solution)/shard_map/attend/pallas_call | solution.py:272
  52.2 3.5 %mlp_first.1 = (f32[512,512]{1,0:T(8,128)S(1)}, bf16[512,512]{1,0:T(8,128)(2,1)S(1)}) custom-call(bf16[512,512]{1,0:T(8,128)(2,1)S(1)} %get-tuple-element.40.heads_ref, f32[2,2,512]{2,1,0:T(2,128)S(1)} %copy-done.4, f32[2,2,512]{2,1,0:T(2,128)S(1)} %copy-done.5, bf16[512,512]{1,0:T(8,128)(2,1)S(1)} %get-tuple-element.41.wo_ref, ...), custom_call_target="tpu_custom_call" | custom-call | tf_op jit(solution)/shard_map/mlp_first/pallas_call | solution.py:309
  55.8 1.0 %mlp_second.1 = (bf16[512,128]{1,0:T(8,128)(2,1)S(1)}, bf16[512,128]{1,0:T(8,128)(2,1)S(1)}, bf16[512,128]{1,0:T(8,128)(2,1)S(1)}, bf16[512,128]{1,0:T(8,128)(2,1)S(1)}) custom-call(f32[512,512]{1,0:T(8,128)S(1)} %get-tuple-element.42.resid_ref, bf16[512,512]{1,0:T(8,128)(2,1)S(1)} %get-tuple-element.43.normed_ref, ...), custom_call_target="tpu_custom_call" | custom-call | tf_op jit(solution)/shard_map/mlp_second/pallas_call | solution.py:346
  56.9 2.7 %collective-permute-start.15 = (bf16[512,128]{1,0:T(8,128)(2,1)S(1)}, bf16[512,128]{1,0:T(8,128)(2,1)S(1)}, u32[]{:S(2)}, u32[]{:S(2)}) collective-permute-start(bf16[512,128]{1,0:T(8,128)(2,1)S(1)} %get-tuple-element.47), channel_id=1, source_target_pairs={{1,0},{2,1},{3,2},{0,3},{5,4},{6,5},{7,6},{4,7},{9,8},{10,9},{11,1... | collective-permute-start | bytes 393224 | tf_op jit(solution)/shard_map/ppermute | solution.py:418
  60.3 2.8 %collective-permute-done.14.a = bf16[512,128]{1,0:T(8,128)(2,1)S(1)} collective-permute-done((bf16[512,128]{1,0:T(8,128)(2,1)S(1)}, bf16[512,128]{1,0:T(8,128)(2,1)S(1)}, u32[]{:S(2)}, u32[]{:S(2)}) %collective-permute-start.14) | collective-permute-done | bytes 131104 | tf_op jit(solution)/shard_map/ppermute | solution.py:415
  63.2 1.6 %collective-permute-done.15.b = bf16[512,128]{1,0:T(8,128)(2,1)S(1)} collective-permute-done((bf16[512,128]{1,0:T(8,128)(2,1)S(1)}, bf16[512,128]{1,0:T(8,128)(2,1)S(1)}, u32[]{:S(2)}, u32[]{:S(2)}) %collective-permute-start.15) | collective-permute-done | bytes 131104 | tf_op jit(solution)/shard_map/ppermute | solution.py:418
  64.8 2.0 %collective-permute-done.16.c = bf16[512,128]{1,0:T(8,128)(2,1)S(1)} collective-permute-done((bf16[512,128]{1,0:T(8,128)(2,1)S(1)}, bf16[512,128]{1,0:T(8,128)(2,1)S(1)}, u32[]{:S(2)}, u32[]{:S(2)}) %collective-permute-start.16) | collective-permute-done | bytes 131104 | tf_op jit(solution)/shard_map/ppermute | solution.py:421
  (36 shorter events, 3.7 us)
Async XLA Ops:
  0.0 1.0 %copy-start.2 = (bf16[512,3,128]{2,0,1:T(8,128)(2,1)S(1)}, bf16[512,3,128]{2,0,1:T(8,128)(2,1)}, u32[]{:S(2)}) copy-start(bf16[512,3,128]{2,0,1:T(8,128)(2,1)} %param.12) | copy-start | bytes 1179652
  4.0 12.1 %collective-permute-start.1 = (bf16[1024,512]{1,0:T(8,128)(2,1)S(1)}, bf16[1024,512]{1,0:T(8,128)(2,1)}, u32[]{:S(2)}, u32[]{:S(2)}) collective-permute-start(bf16[1024,512]{1,0:T(8,128)(2,1)S(1)} %norm_rows.1.xa), channel_id=1, source_target_pairs={{4,0},{0,4},{12,8},{8,12},{20,16},{16,20},{28,24},{24,28},{36,32},... | collective-permute-start | bytes 3145736 | tf_op jit(solution)/shard_map/ppermute | solution.py:394
  7.3 8.8 %collective-permute-start = (bf16[4,512,128]{2,1,0:T(8,128)(2,1)S(1)}, bf16[4,512,128]{2,1,0:T(8,128)(2,1)S(1)}, u32[]{:S(2)}, u32[]{:S(2)}) collective-permute-start(bf16[4,512,128]{2,1,0:T(8,128)(2,1)S(1)} %pack_weights.1.w0), channel_id=1, source_target_pairs={{3,0},{0,1},{1,2},{2,3},{5,4},{6,5},{7,6},{4,7},{11,8},{8,9},{9,10... | collective-permute-start | bytes 1572872 | tf_op jit(solution)/shard_map/ppermute | solution.py:412
  8.3 27.1 %collective-permute-start.4 = (bf16[1024,512]{1,0:T(8,128)(2,1)S(1)}, bf16[1024,512]{1,0:T(8,128)(2,1)S(1)}, u32[]{:S(2)}, u32[]{:S(2)}) collective-permute-start(bf16[1024,512]{1,0:T(8,128)(2,1)S(1)} %norm_rows.1.xa), channel_id=1, source_target_pairs={{8,0},{252,4},{16,8},{4,12},{24,16},{12,20},{32,24},{20,28},{40,32... | collective-permute-start | bytes 3145736 | tf_op jit(solution)/shard_map/ppermute | solution.py:394
  9.5 28.9 %collective-permute-start.5 = (bf16[1024,512]{1,0:T(8,128)(2,1)S(1)}, bf16[1024,512]{1,0:T(8,128)(2,1)}, u32[]{:S(2)}, u32[]{:S(2)}) collective-permute-start(bf16[1024,512]{1,0:T(8,128)(2,1)S(1)} %norm_rows.1.xa), channel_id=1, source_target_pairs={{248,0},{12,4},{0,8},{20,12},{8,16},{28,20},{16,24},{36,28},{24,32... | collective-permute-start | bytes 3145736 | tf_op jit(solution)/shard_map/ppermute | solution.py:394
  16.1 9.4 %collective-permute-start.6 = (bf16[4,512,128]{2,1,0:T(8,128)(2,1)S(1)}, bf16[4,512,128]{2,1,0:T(8,128)(2,1)S(1)}, u32[]{:S(2)}, u32[]{:S(2)}) collective-permute-start(bf16[4,512,128]{2,1,0:T(8,128)(2,1)S(1)} %collective-permute-done.w1), channel_id=1, source_target_pairs={{4,0},{0,4},{12,8},{8,12},{20,16},{16,20},{28,24},{24,28},{36,32},... | collective-permute-start | bytes 1572872 | tf_op jit(solution)/shard_map/ppermute | solution.py:394
  17.8 5.7 %collective-permute-start.7 = (bf16[4,256,128]{2,1,0:T(8,128)(2,1)S(1)}, bf16[4,256,128]{2,1,0:T(8,128)(2,1)S(1)}, u32[]{:S(2)}, u32[]{:S(2)}) collective-permute-start(bf16[4,256,128]{2,1,0:T(8,128)(2,1)S(1)} %constant_dynamic-slice_fusion), channel_id=1, source_target_pairs={{3,0},{0,1},{1,2},{2,3},{5,4},{6,5},{7,6},{4,7},{11,8},{8,9},{9,10... | collective-permute-start | bytes 786440 | tf_op jit(solution)/shard_map/ppermute | solution.py:412
  23.5 3.1 %collective-permute-start.8 = (bf16[4,256,128]{2,1,0:T(8,128)(2,1)S(1)}, bf16[4,256,128]{2,1,0:T(8,128)(2,1)S(1)}, u32[]{:S(2)}, u32[]{:S(2)}) collective-permute-start(bf16[4,256,128]{2,1,0:T(8,128)(2,1)S(1)} %collective-permute-done.7.w3m), channel_id=1, source_target_pairs={{4,0},{0,4},{12,8},{8,12},{20,16},{16,20},{28,24},{24,28},{36,32},... | collective-permute-start | bytes 786440 | tf_op jit(solution)/shard_map/ppermute | solution.py:394
  25.5 14.8 %collective-permute-start.2 = (bf16[512,512]{1,0:T(8,128)(2,1)}, bf16[512,512]{1,0:T(8,128)(2,1)S(1)}, u32[]{:S(2)}, u32[]{:S(2)}) collective-permute-start(bf16[512,512]{1,0:T(8,128)(2,1)} %u0.1), channel_id=1, source_target_pairs={{3,0},{0,1},{1,2},{2,3},{5,4},{6,5},{7,6},{4,7},{11,8},{8,9},{9,10... | collective-permute-start | bytes 1572872 | tf_op jit(solution)/shard_map/ppermute | solution.py:412
  25.5 14.8 %collective-permute-start.3 = (bf16[512,512]{1,0:T(8,128)(2,1)}, bf16[512,512]{1,0:T(8,128)(2,1)S(1)}, u32[]{:S(2)}, u32[]{:S(2)}) collective-permute-start(bf16[512,512]{1,0:T(8,128)(2,1)} %d0.1), channel_id=1, source_target_pairs={{3,0},{0,1},{1,2},{2,3},{5,4},{6,5},{7,6},{4,7},{11,8},{8,9},{9,10... | collective-permute-start | bytes 1572872 | tf_op jit(solution)/shard_map/ppermute | solution.py:412
  38.4 7.4 %collective-permute-start.10 = (bf16[1024,512]{1,0:T(8,128)(2,1)S(1)}, bf16[1024,512]{1,0:T(8,128)(2,1)S(1)}, u32[]{:S(2)}, u32[]{:S(2)}) collective-permute-start(bf16[1024,512]{1,0:T(8,128)(2,1)S(1)} %collective-permute-done.4.xa), channel_id=1, source_target_pairs={{4,0},{0,4},{12,8},{8,12},{20,16},{16,20},{28,24},{24,28},{36,32},... | collective-permute-start | bytes 3145736 | tf_op jit(solution)/shard_map/ppermute | solution.py:394
  40.3 11.0 %collective-permute-start.9 = (bf16[512,512]{1,0:T(8,128)(2,1)S(1)}, bf16[512,512]{1,0:T(8,128)(2,1)S(1)}, u32[]{:S(2)}, u32[]{:S(2)}) collective-permute-start(bf16[512,512]{1,0:T(8,128)(2,1)S(1)} %one_to_relay.1), channel_id=1, source_target_pairs={{3,0},{0,1},{1,2},{2,3},{5,4},{6,5},{7,6},{4,7},{11,8},{8,9},{9,10... | collective-permute-start | bytes 1572872 | tf_op jit(solution)/shard_map/ppermute | solution.py:412
  40.9 11.3 %collective-permute-start.11 = (bf16[512,512]{1,0:T(8,128)(2,1)S(1)}, bf16[512,512]{1,0:T(8,128)(2,1)S(1)}, u32[]{:S(2)}, u32[]{:S(2)}) collective-permute-start(bf16[512,512]{1,0:T(8,128)(2,1)S(1)} %collective-permute-done.2.a_ref.u1), channel_id=1, source_target_pairs={{4,0},{0,4},{12,8},{8,12},{20,16},{16,20},{28,24},{24,28},{36,32},... | collective-permute-start | bytes 1572872 | tf_op jit(solution)/shard_map/ppermute | solution.py:394
  41.9 10.3 %collective-permute-start.12 = (bf16[512,512]{1,0:T(8,128)(2,1)S(1)}, bf16[512,512]{1,0:T(8,128)(2,1)S(1)}, u32[]{:S(2)}, u32[]{:S(2)}) collective-permute-start(bf16[512,512]{1,0:T(8,128)(2,1)S(1)} %collective-permute-done.3.b_ref.d1), channel_id=1, source_target_pairs={{4,0},{0,4},{12,8},{8,12},{20,16},{16,20},{28,24},{24,28},{36,32},... | collective-permute-start | bytes 1572872 | tf_op jit(solution)/shard_map/ppermute | solution.py:394
  42.2 3.7 %copy-start.6 = (s32[8,8]{1,0:T(8,128)S(1)}, s32[8,8]{1,0:T(8,128)}, u32[]{:S(2)}) copy-start(s32[8,8]{1,0:T(8,128)} %list_ref.1) | copy-start | bytes 772
  42.2 3.7 %copy-start.7 = (s32[8]{0:T(128)S(1)}, s32[8]{0:T(128)}, u32[]{:S(2)}) copy-start(s32[8]{0:T(128)} %count_ref.1) | copy-start | bytes 100
  45.8 6.4 %copy-start = (bf16[512,512]{1,0:T(8,128)(2,1)S(1)}, bf16[512,512]{1,0:T(8,128)(2,1)}, u32[]{:S(2)}) copy-start(bf16[512,512]{1,0:T(8,128)(2,1)} %u0.1) | copy-start | bytes 1572868
  45.8 6.4 %copy-start.1 = (bf16[512,512]{1,0:T(8,128)(2,1)S(1)}, bf16[512,512]{1,0:T(8,128)(2,1)}, u32[]{:S(2)}) copy-start(bf16[512,512]{1,0:T(8,128)(2,1)} %d0.1) | copy-start | bytes 1572868
  45.8 6.4 %copy-start.4 = (f32[2,2,512]{2,1,0:T(2,128)S(1)}, f32[2,2,512]{2,1,0:T(2,128)}, u32[]{:S(2)}) copy-start(f32[2,2,512]{2,1,0:T(2,128)} %gain_ref.3) | copy-start | bytes 24580
  45.8 6.4 %copy-start.5 = (f32[2,2,512]{2,1,0:T(2,128)S(1)}, f32[2,2,512]{2,1,0:T(2,128)}, u32[]{:S(2)}) copy-start(f32[2,2,512]{2,1,0:T(2,128)} %shift_ref.3) | copy-start | bytes 24580
  51.3 4.4 %collective-permute-start.13 = (bf16[512,512]{1,0:T(8,128)(2,1)S(1)}, bf16[512,512]{1,0:T(8,128)(2,1)S(1)}, u32[]{:S(2)}, u32[]{:S(2)}) collective-permute-start(bf16[512,512]{1,0:T(8,128)(2,1)S(1)} %collective-permute-done.9.mine), channel_id=1, source_target_pairs={{4,0},{0,4},{12,8},{8,12},{20,16},{16,20},{28,24},{24,28},{36,32},... | collective-permute-start | bytes 1572872 | tf_op jit(solution)/shard_map/ppermute | solution.py:394
  56.8 6.4 %collective-permute-start.14 = (bf16[512,128]{1,0:T(8,128)(2,1)S(1)}, bf16[512,128]{1,0:T(8,128)(2,1)S(1)}, u32[]{:S(2)}, u32[]{:S(2)}) collective-permute-start(bf16[512,128]{1,0:T(8,128)(2,1)S(1)} %get-tuple-element.46), channel_id=1, source_target_pairs={{0,1},{1,2},{2,3},{3,0},{4,5},{5,6},{6,7},{7,4},{8,9},{9,10},{10,1... | collective-permute-start | bytes 393224 | tf_op jit(solution)/shard_map/ppermute | solution.py:415
  56.9 7.9 %collective-permute-start.15 = (bf16[512,128]{1,0:T(8,128)(2,1)S(1)}, bf16[512,128]{1,0:T(8,128)(2,1)S(1)}, u32[]{:S(2)}, u32[]{:S(2)}) collective-permute-start(bf16[512,128]{1,0:T(8,128)(2,1)S(1)} %get-tuple-element.47), channel_id=1, source_target_pairs={{1,0},{2,1},{3,2},{0,3},{5,4},{6,5},{7,6},{4,7},{9,8},{10,9},{11,1... | collective-permute-start | bytes 393224 | tf_op jit(solution)/shard_map/ppermute | solution.py:418
  59.5 7.3 %collective-permute-start.16 = (bf16[512,128]{1,0:T(8,128)(2,1)S(1)}, bf16[512,128]{1,0:T(8,128)(2,1)S(1)}, u32[]{:S(2)}, u32[]{:S(2)}) collective-permute-start(bf16[512,128]{1,0:T(8,128)(2,1)S(1)} %get-tuple-element.48), channel_id=1, source_target_pairs={{0,2},{1,3},{2,0},{3,1},{4,6},{5,7},{6,4},{7,5},{8,10},{9,11},{10,... | collective-permute-start | bytes 393224 | tf_op jit(solution)/shard_map/ppermute | solution.py:421
  (1 other events, 0.9 us)

commit v6 on v5

--- a/solution.py
+++ b/solution.py
@@ -60,65 +60,51 @@
     return lax.div(rank, 2), lax.rem(rank, 2), lax.rem(dom, 2), rank, dom
 
 
-def norm_kernel(state_ref, gain_ref, shift_ref, o_ref, x_in, affine, sems):
+def prepare_kernel(
+    state_ref, gain_ref, shift_ref, qkv_ref, out_ref, o_ref, w_ref, x_in, affine, sems
+):
     sample = my_place()[0]
     s = pl.ds(sample, 1)
-    chunks = sems.shape[0] - 2
+    head = NODE_BLK
+    chunks = 4
     step = x_in.shape[0] // chunks
+    parts = qkv_ref.shape[0]
     spans = [pl.ds(k * step, step) for k in range(chunks)]
-    loads = [
-        pltpu.make_async_copy(state_ref.at[sample, at], x_in.at[at], sems.at[k])
-        for k, at in enumerate(spans)
+    jobs = [(state_ref.at[sample, at], x_in.at[at]) for at in spans]
+    jobs += [(gain_ref, affine.at[0]), (shift_ref, affine.at[1]), (qkv_ref, w_ref.at[pl.ds(0, parts)])]
+    jobs += [
+        (out_ref.at[:, pl.ds(k * head, head)], w_ref.at[parts, pl.ds(k * head, head)])
+        for k in range(HEADS)
     ]
-    small = [
-        pltpu.make_async_copy(r, affine.at[k], sems.at[chunks + k])
-        for k, r in enumerate((gain_ref, shift_ref))
-    ]
-    for c in loads[:1] + small + loads[1:]:
-        c.start()
-    for c in small:
+    copies = [pltpu.make_async_copy(a, b, sems.at[k]) for k, (a, b) in enumerate(jobs)]
+    for k in (0, chunks, chunks + 1, *range(1, chunks), *range(chunks + 2, len(jobs))):
+        copies[k].start()
+    for c in copies[chunks : chunks + 2]:
         c.wait()
     gain, shift = affine[0, 0, s], affine[1, 0, s]
-    for c, at in zip(loads, spans):
+    for c, at in zip(copies, spans):
         c.wait()
         o_ref[at] = bf(normalise(x_in[at].astype(jnp.float32), gain, shift))
-
-
-def normed_rows(state, gain, shift):
+    for c in copies[chunks + 2 :]:
+        c.wait()
+
+
+def prepare(state, gain, shift, qkv, out_w):
     _, rows, width = state.shape
-    return pl.pallas_call(
-        norm_kernel,
-        in_specs=[HBM] * 3,
-        out_specs=VMEM,
-        out_shape=in_vmem((rows, width)),
+    parts, _, head = qkv.shape
+    return pl.pallas_call(
+        prepare_kernel,
+        in_specs=[HBM] * 5,
+        out_specs=[VMEM] * 2,
+        out_shape=[in_vmem((rows, width)), in_vmem((parts + 1, width, head))],
         scratch_shapes=[
             pltpu.VMEM((rows, width), jnp.bfloat16),
             pltpu.VMEM((2, *gain.shape), jnp.float32),
-            pltpu.SemaphoreType.DMA((6,)),
+            pltpu.SemaphoreType.DMA((7 + HEADS,)),
         ],
-        name="norm_rows",
-        compiler_params=pltpu.CompilerParams(vmem_limit_bytes=8 * MIB),
-    )(kept_in_hbm(state), kept_in_hbm(gain), kept_in_hbm(shift))
-
-
-def pack_kernel(qkv_ref, out_ref, o_ref):
-    parts = qkv_ref.shape[0]
-    head = NODE_BLK
-    o_ref[:parts] = qkv_ref[...]
-    for k in range(HEADS):
-        o_ref[parts, k * head : (k + 1) * head] = out_ref[:, k * head : (k + 1) * head]
-
-
-def packed(qkv, out_w):
-    parts, width, head = qkv.shape
-    return pl.pallas_call(
-        pack_kernel,
-        in_specs=[VMEM] * 2,
-        out_specs=VMEM,
-        out_shape=in_vmem((parts + 1, width, head)),
-        name="pack_weights",
-        compiler_params=pltpu.CompilerParams(vmem_limit_bytes=4 * MIB),
-    )(qkv, out_w)
+        name="prepare",
+        compiler_params=pltpu.CompilerParams(vmem_limit_bytes=6 * MIB),
+    )(*[kept_in_hbm(v) for v in (state, gain, shift, qkv, out_w)])
 
 
 def relay_kernel(a_ref, b_ref, o_ref):
@@ -195,7 +181,7 @@
             in_vmem((width, width)),
         ],
         name="kv_first",
-        compiler_params=pltpu.CompilerParams(vmem_limit_bytes=16 * MIB),
+        compiler_params=pltpu.CompilerParams(vmem_limit_bytes=12 * MIB),
     )(xa, xb, *weights)
 
 
@@ -214,7 +200,7 @@
         out_shape=in_vmem(kv.shape),
         input_output_aliases={3: 0},
         name="kv_second",
-        compiler_params=pltpu.CompilerParams(vmem_limit_bytes=16 * MIB),
+        compiler_params=pltpu.CompilerParams(vmem_limit_bytes=12 * MIB),
     )(xa, xb, wkv, kv)
 
 
@@ -276,7 +262,7 @@
         out_shape=[in_vmem((rows, width)), in_vmem(kv.shape)],
         input_output_aliases={5: 1},
         name="attend",
-        compiler_params=pltpu.CompilerParams(vmem_limit_bytes=16 * MIB),
+        compiler_params=pltpu.CompilerParams(vmem_limit_bytes=12 * MIB),
     )(listed, counts, relay, query, wkv, kv)[0]
 
 
@@ -317,7 +303,7 @@
             pltpu.SemaphoreType.DMA,
         ],
         name="mlp_first",
-        compiler_params=pltpu.CompilerParams(vmem_limit_bytes=16 * MIB),
+        compiler_params=pltpu.CompilerParams(vmem_limit_bytes=12 * MIB),
     )(heads, gain, shift, wo, *weights, kept_in_hbm(state))
 
 
@@ -354,13 +340,13 @@
             pltpu.VMEM(mine.shape, jnp.bfloat16),
         ],
         name="mlp_second",
-        compiler_params=pltpu.CompilerParams(vmem_limit_bytes=16 * MIB),
+        compiler_params=pltpu.CompilerParams(vmem_limit_bytes=12 * MIB),
     )(resid, normed, mine, theirs)
 
 
-def place_kernel(own, a, b, c, o_ref):
+def place_kernel(own, across, after, before, o_ref):
     rank = my_place()[3]
-    for off, r in ((0, own), (3, a), (1, b), (2, c)):
+    for off, r in ((0, own), (2, across), (1, after), (3, before)):
         o_ref[lax.rem(rank + off, HEADS)] = r[...]
 
 
@@ -420,11 +406,12 @@
     def across(v):
         return lax.ppermute(v, "tp", [(i, (i + 2) % tps) for i in range(tps)])
 
-    w0 = packed(jnp.transpose(qkv_weight, (1, 0, 2)), out_weight)
+    qkv = jnp.transpose(qkv_weight, (1, 0, 2))
+    own, w0 = prepare(state, norm_gain, norm_shift, qkv, out_weight)
     w1 = ring(w0)
-    own = normed_rows(after(state, w0), norm_gain, norm_shift)
     partner = swap(own)
     near_rows, far_rows = near(own), far(own)
+    u1 = ring(after(up_weight, own))
 
     w1 = after(w1, partner)
     w2 = swap(w1)
@@ -432,16 +419,18 @@
     w1_half = lax.dynamic_slice_in_dim(w1, par * mid, mid, 1)
     w3m = ring(w1_half)
     w3t = swap(w3m)
-    up_late, down_late, w1_half = lax.optimization_barrier((up_weight, down_weight, w1_half))
-    u1, d1 = ring(up_late), ring(down_late)
-
-    kv, query, wkv, wo = kv_first(own, partner, (w0, w1, w2, w3m, w3t), 5)
-    near_rows, far_rows, query = lax.optimization_barrier((near_rows, far_rows, query))
+    d1 = ring(after(down_weight, w3m))
+
+    own_late, u1 = lax.optimization_barrier((own, u1))
+    kv, query, wkv, wo = kv_first(own_late, partner, (w0, w1, w2, w3m, w3t), 5)
+    relayed = one_to_relay(u1, d1)
+    near_rows, far_rows, query, relayed = lax.optimization_barrier(
+        (near_rows, far_rows, query, relayed)
+    )
+    last = ring(relayed)
     relay = swap(near_rows)
-    u1, d1 = lax.optimization_barrier((u1, d1, query))[:2]
+    kv = kv_second(near_rows, far_rows, wkv, kv)
     u2, d2 = swap(u1), swap(d1)
-    last = ring(one_to_relay(u1, d1))
-    kv = kv_second(near_rows, far_rows, wkv, kv)
 
     heads = attend(neighbours, counts, relay, query, wkv, kv, per_dev, doms)
     last, heads = lax.optimization_barrier((last, heads))
@@ -449,7 +438,7 @@
     weights = (up_weight, down_weight, u1, d1, u2, d2)
     resid, normed = mlp_first(heads, norm_gain, norm_shift, wo, weights, state)
     mine = mlp_second(resid, normed, last, last_too)
-    out = placed_rows((mine[0], up(mine[1]), down(mine[3]), across(mine[2])))
+    out = placed_rows((mine[0], across(mine[2]), down(mine[3]), up(mine[1])))
     return out.reshape(samples, row_count, width // tps)
 
 

time: 67.9 us -> 64.8 us (0.954)
  waiting for transfers between devices: 21 us -> 16.9 us
  starting transfers between devices: 24 us -> 27 us
  local copies, waits for them, and re-layouts: 1.95 us -> 0.05 us
    ppermute x9, waiting for transfers between devices: 8.95 us -> 3.27 us  [hop(): return lax.ppermute(v, 'dom', pairs)]
    ppermute x5, starting transfers between devices: 1.63 us -> 5.77 us  [ring(): return lax.ppermute(v, ('dom', 'tp'), pairs)]
    ppermute x1, waiting for transfers between devices: 2 us -> 4.59 us  [across(): return lax.ppermute(v, 'tp', [(i, (i + 2) % tps) for i in range(tps)])]
    unnamed x16 -> x12, local copies, waits for them, and re-layouts: 1.93 us -> 0.03 us
    ppermute x1, waiting for transfers between devices: 2.82 us -> 1.14 us  [up(): return lax.ppermute(v, 'tp', [(i, (i + 1) % tps) for i in range(tps)])]
    pallas_call x1, Pallas kernels: 3.59 us -> 2.34 us  [kv_second(): pl.pallas_call(kv_second_kernel, in_specs=[VMEM] * 4, out_specs=VMEM, out...]
    pallas_call x2 -> x1, Pallas kernels: 2.05 us -> 3.05 us  [prepare(): pl.pallas_call(prepare_kernel, in_specs=[HBM] * 5, out_specs=[VMEM] * 2,...]
    ppermute x5, waiting for transfers between devices: 5.62 us -> 6.38 us  [ring(): return lax.ppermute(v, ('dom', 'tp'), pairs)]
where the time goes in v6:
time: 64.8 us; the launch traced here: 64.7 us
  starting transfers between devices  27 us (42%)
  Pallas kernels  20.5 us (32%)
  waiting for transfers between devices  16.9 us (26%)
    ppermute x9, starting transfers between devices, hop(): return lax.ppermute(v, 'dom', pairs)  19.1 us
    ppermute x5, waiting for transfers between devices, ring(): return lax.ppermute(v, ('dom', 'tp'), pairs)  6.38 us
    ppermute x5, starting transfers between devices, ring(): return lax.ppermute(v, ('dom', 'tp'), pairs)  5.77 us
    pallas_call x1, Pallas kernels, attend(): pl.pallas_call(functools.partial(attend_kernel, doms=doms, per_dev=per_de...  5.43 us
    ppermute x1, waiting for transfers between devices, across(): return lax.ppermute(v, 'tp', [(i, (i + 2) % tps) for i in range(tps)])  4.59 us
    pallas_call x1, Pallas kernels, kv_first(): pl.pallas_call(kv_first_kernel, in_specs=[VMEM] * (2 + len(weights)), out...  4.32 us
    pallas_call x1, Pallas kernels, mlp_first(): pl.pallas_call(mlp_first_kernel, in_specs=[VMEM] * (4 + len(weights)) + [...  3.5 us
    ppermute x9, waiting for transfers between devices, hop(): return lax.ppermute(v, 'dom', pairs)  3.27 us
  transfers between devices with their start and end apart: 17, of which 7 were waited for; matrix products, arithmetic and copies ran while one was open for 0% of the time, Pallas kernels for 24%

profile of v6, /device:TPU:1, one launch (start us, length us, event | category | flops | bytes accessed | tf_op | source)
XLA Modules:
  0.0 64.7 jit_solution(9865042467424319850)
XLA Ops:
  0.0 3.1 %prepare.1 = (bf16[1024,512]{1,0:T(8,128)(2,1)}, bf16[4,512,128]{2,1,0:T(8,128)(2,1)S(1)}) custom-call(bf16[2,1024,512]{2,1,0:T(8,128)(2,1)} %state_ref.3, f32[2,2,512]{2,1,0:T(2,128)} %gain_ref.3, f32[2,2,512]{2,1,0:T(2,128)} %shift_ref.3, bf16[3,512,128]{2,1,0:T(8,128)(2,1)} %bitcast.2, bf16[128,512]{1,0:T(8,128)(2,1)} %out_ref.1), custom_call_target="tpu_custom_call" | custom-call | tf_op jit(solution)/shard_map/prepare/pallas_call | solution.py:95
  3.1 3.3 %collective-permute-start.3 = (bf16[1024,512]{1,0:T(8,128)(2,1)}, bf16[1024,512]{1,0:T(8,128)(2,1)}, u32[]{:S(2)}, u32[]{:S(2)}) collective-permute-start(bf16[1024,512]{1,0:T(8,128)(2,1)} %get-tuple-element.31.xa), channel_id=1, source_target_pairs={{4,0},{0,4},{12,8},{8,12},{20,16},{16,20},{28,24},{24,28},{36,32},... | collective-permute-start | bytes 3145736 | tf_op jit(solution)/shard_map/ppermute | solution.py:380
  6.4 1.0 %collective-permute-start.4 = (bf16[4,512,128]{2,1,0:T(8,128)(2,1)S(1)}, bf16[4,512,128]{2,1,0:T(8,128)(2,1)S(1)}, u32[]{:S(2)}, u32[]{:S(2)}) collective-permute-start(bf16[4,512,128]{2,1,0:T(8,128)(2,1)S(1)} %get-tuple-element.32.w0), channel_id=1, source_target_pairs={{3,0},{0,1},{1,2},{2,3},{5,4},{6,5},{7,6},{4,7},{11,8},{8,9},{9,10... | collective-permute-start | bytes 1572872 | tf_op jit(solution)/shard_map/ppermute | solution.py:398
  7.4 1.2 %collective-permute-start = (bf16[1024,512]{1,0:T(8,128)(2,1)}, bf16[1024,512]{1,0:T(8,128)(2,1)S(1)}, u32[]{:S(2)}, u32[]{:S(2)}) collective-permute-start(bf16[1024,512]{1,0:T(8,128)(2,1)} %get-tuple-element.31.xa), channel_id=1, source_target_pairs={{8,0},{252,4},{16,8},{4,12},{24,16},{12,20},{32,24},{20,28},{40,32... | collective-permute-start | bytes 3145736 | tf_op jit(solution)/shard_map/ppermute | solution.py:380
  8.6 6.6 %collective-permute-start.1 = (bf16[1024,512]{1,0:T(8,128)(2,1)}, bf16[1024,512]{1,0:T(8,128)(2,1)S(1)}, u32[]{:S(2)}, u32[]{:S(2)}) collective-permute-start(bf16[1024,512]{1,0:T(8,128)(2,1)} %get-tuple-element.31.xa), channel_id=1, source_target_pairs={{248,0},{12,4},{0,8},{20,12},{8,16},{28,20},{16,24},{36,28},{24,32... | collective-permute-start | bytes 3145736 | tf_op jit(solution)/shard_map/ppermute | solution.py:380
  15.2 1.5 %collective-permute-start.6 = (bf16[4,256,128]{2,1,0:T(8,128)(2,1)S(1)}, bf16[4,256,128]{2,1,0:T(8,128)(2,1)S(1)}, u32[]{:S(2)}, u32[]{:S(2)}) collective-permute-start(bf16[4,256,128]{2,1,0:T(8,128)(2,1)S(1)} %constant_dynamic-slice_fusion), channel_id=1, source_target_pairs={{3,0},{0,1},{1,2},{2,3},{5,4},{6,5},{7,6},{4,7},{11,8},{8,9},{9,10... | collective-permute-start | bytes 786440 | tf_op jit(solution)/shard_map/ppermute | solution.py:398
  17.4 3.4 %collective-permute-done.6.w3m = bf16[4,256,128]{2,1,0:T(8,128)(2,1)S(1)} collective-permute-done((bf16[4,256,128]{2,1,0:T(8,128)(2,1)S(1)}, bf16[4,256,128]{2,1,0:T(8,128)(2,1)S(1)}, u32[]{:S(2)}, u32[]{:S(2)}) %collective-permute-start.6) | collective-permute-done | bytes 262176 | tf_op jit(solution)/shard_map/ppermute | solution.py:398
  20.8 2.7 %collective-permute-start.8 = (bf16[512,512]{1,0:T(8,128)(2,1)}, bf16[512,512]{1,0:T(8,128)(2,1)S(1)}, u32[]{:S(2)}, u32[]{:S(2)}) collective-permute-start(bf16[512,512]{1,0:T(8,128)(2,1)} %d0.1), channel_id=1, source_target_pairs={{3,0},{0,1},{1,2},{2,3},{5,4},{6,5},{7,6},{4,7},{11,8},{8,9},{9,10... | collective-permute-start | bytes 1572872 | tf_op jit(solution)/shard_map/ppermute | solution.py:398
  23.5 2.9 %collective-permute-done.2.a_ref.u1 = bf16[512,512]{1,0:T(8,128)(2,1)S(1)} collective-permute-done((bf16[512,512]{1,0:T(8,128)(2,1)}, bf16[512,512]{1,0:T(8,128)(2,1)S(1)}, u32[]{:S(2)}, u32[]{:S(2)}) %collective-permute-start.2) | collective-permute-done | bytes 524320 | tf_op jit(solution)/shard_map/ppermute | solution.py:398
  26.4 3.8 %collective-permute-start.7 = (bf16[4,256,128]{2,1,0:T(8,128)(2,1)S(1)}, bf16[4,256,128]{2,1,0:T(8,128)(2,1)S(1)}, u32[]{:S(2)}, u32[]{:S(2)}) collective-permute-start(bf16[4,256,128]{2,1,0:T(8,128)(2,1)S(1)} %collective-permute-done.6.w3m), channel_id=1, source_target_pairs={{4,0},{0,4},{12,8},{8,12},{20,16},{16,20},{28,24},{24,28},{36,32},... | collective-permute-start | bytes 786440 | tf_op jit(solution)/shard_map/ppermute | solution.py:380
  30.2 1.2 %collective-permute-done.7.w3t = bf16[4,256,128]{2,1,0:T(8,128)(2,1)S(1)} collective-permute-done((bf16[4,256,128]{2,1,0:T(8,128)(2,1)S(1)}, bf16[4,256,128]{2,1,0:T(8,128)(2,1)S(1)}, u32[]{:S(2)}, u32[]{:S(2)}) %collective-permute-start.7) | collective-permute-done | bytes 262176 | tf_op jit(solution)/shard_map/ppermute | solution.py:380
  31.3 4.3 %kv_first.1 = (bf16[40,128,1024]{2,1,0:T(8,128)(2,1)S(1)}, bf16[512,512]{1,0:T(8,128)(2,1)S(1)}, bf16[512,1024]{1,0:T(8,128)(2,1)S(1)}, bf16[512,512]{1,0:T(8,128)(2,1)S(1)}) custom-call(bf16[1024,512]{1,0:T(8,128)(2,1)} %get-tuple-element.31.xa, bf16[1024,512]{1,0:T(8,128)(2,1)} %collective-permute-done.3.xb, ...), custom_call_target="tpu_custom_call" | custom-call | tf_op jit(solution)/shard_map/kv_first/pallas_call | solution.py:172
  35.8 2.1 %collective-permute-done.1.xb = bf16[1024,512]{1,0:T(8,128)(2,1)S(1)} collective-permute-done((bf16[1024,512]{1,0:T(8,128)(2,1)}, bf16[1024,512]{1,0:T(8,128)(2,1)S(1)}, u32[]{:S(2)}, u32[]{:S(2)}) %collective-permute-start.1) | collective-permute-done | bytes 1048608 | tf_op jit(solution)/shard_map/ppermute | solution.py:380
  37.8 1.6 %collective-permute-start.10 = (bf16[1024,512]{1,0:T(8,128)(2,1)S(1)}, bf16[1024,512]{1,0:T(8,128)(2,1)S(1)}, u32[]{:S(2)}, u32[]{:S(2)}) collective-permute-start(bf16[1024,512]{1,0:T(8,128)(2,1)S(1)} %collective-permute-done.xa), channel_id=1, source_target_pairs={{4,0},{0,4},{12,8},{8,12},{20,16},{16,20},{28,24},{24,28},{36,32},... | collective-permute-start | bytes 3145736 | tf_op jit(solution)/shard_map/ppermute | solution.py:380
  40.0 2.3 %kv_second.1.kv_in = bf16[40,128,1024]{2,1,0:T(8,128)(2,1)S(1)} custom-call(bf16[1024,512]{1,0:T(8,128)(2,1)S(1)} %collective-permute-done.xa, bf16[1024,512]{1,0:T(8,128)(2,1)S(1)} %collective-permute-done.1.xb, bf16[512,1024]{1,0:T(8,128)(2,1)S(1)} %get-tuple-element.40.wkv_ref, ...), custom_call_target="tpu_custom_call", output_to_operand_aliasing={{}: (3, {})} | custom-call | tf_op jit(solution)/shard_map/kv_second/pallas_call | solution.py:196
  43.0 5.4 %attend.1 = (bf16[512,512]{1,0:T(8,128)(2,1)S(1)}, bf16[40,128,1024]{2,1,0:T(8,128)(2,1)S(1)}) custom-call(s32[8,8]{1,0:T(8,128)S(1)} %copy-done.4, s32[8]{0:T(128)S(1)} %copy-done.5, bf16[1024,512]{1,0:T(8,128)(2,1)S(1)} %collective-permute-done.10.relay_ref, bf16[512,512]{1,0:T(8,128)(2,1)S(1)} %get-tuple-element.39.q_ref, ...), custom_call_target="tpu_custom_call", output_to_operand_aliasing={{1}: (5, {})} | custom-call | tf_op jit(solution)/shard_map/attend/pallas_call | solution.py:258
  48.4 1.5 %collective-permute-start.13 = (bf16[512,512]{1,0:T(8,128)(2,1)S(1)}, bf16[512,512]{1,0:T(8,128)(2,1)S(1)}, u32[]{:S(2)}, u32[]{:S(2)}) collective-permute-start(bf16[512,512]{1,0:T(8,128)(2,1)S(1)} %collective-permute-done.9.mine), channel_id=1, source_target_pairs={{4,0},{0,4},{12,8},{8,12},{20,16},{16,20},{28,24},{24,28},{36,32},... | collective-permute-start | bytes 1572872 | tf_op jit(solution)/shard_map/ppermute | solution.py:380
  49.9 3.5 %mlp_first.1 = (f32[512,512]{1,0:T(8,128)S(1)}, bf16[512,512]{1,0:T(8,128)(2,1)S(1)}) custom-call(bf16[512,512]{1,0:T(8,128)(2,1)S(1)} %get-tuple-element.44.heads_ref, f32[2,2,512]{2,1,0:T(2,128)S(1)} %copy-done.2, f32[2,2,512]{2,1,0:T(2,128)S(1)} %copy-done.3, bf16[512,512]{1,0:T(8,128)(2,1)S(1)} %get-tuple-element.45.wo_ref, ...), custom_call_target="tpu_custom_call" | custom-call | tf_op jit(solution)/shard_map/mlp_first/pallas_call | solution.py:295
  53.4 1.0 %mlp_second.1 = (bf16[512,128]{1,0:T(8,128)(2,1)S(1)}, bf16[512,128]{1,0:T(8,128)(2,1)S(1)}, bf16[512,128]{1,0:T(8,128)(2,1)S(1)}, bf16[512,128]{1,0:T(8,128)(2,1)S(1)}) custom-call(f32[512,512]{1,0:T(8,128)S(1)} %get-tuple-element.46.resid_ref, bf16[512,512]{1,0:T(8,128)(2,1)S(1)} %get-tuple-element.47.normed_ref, ...), custom_call_target="tpu_custom_call" | custom-call | tf_op jit(solution)/shard_map/mlp_second/pallas_call | solution.py:332
  54.6 2.0 %collective-permute-start.15 = (bf16[512,128]{1,0:T(8,128)(2,1)S(1)}, bf16[512,128]{1,0:T(8,128)(2,1)S(1)}, u32[]{:S(2)}, u32[]{:S(2)}) collective-permute-start(bf16[512,128]{1,0:T(8,128)(2,1)S(1)} %get-tuple-element.51), channel_id=1, source_target_pairs={{1,0},{2,1},{3,2},{0,3},{5,4},{6,5},{7,6},{4,7},{9,8},{10,9},{11,1... | collective-permute-start | bytes 393224 | tf_op jit(solution)/shard_map/ppermute | solution.py:404
  56.6 4.6 %collective-permute-done.14.across = bf16[512,128]{1,0:T(8,128)(2,1)S(1)} collective-permute-done((bf16[512,128]{1,0:T(8,128)(2,1)S(1)}, bf16[512,128]{1,0:T(8,128)(2,1)S(1)}, u32[]{:S(2)}, u32[]{:S(2)}) %collective-permute-start.14) | collective-permute-done | bytes 131104 | tf_op jit(solution)/shard_map/ppermute | solution.py:407
  61.2 1.5 %collective-permute-done.15.after = bf16[512,128]{1,0:T(8,128)(2,1)S(1)} collective-permute-done((bf16[512,128]{1,0:T(8,128)(2,1)S(1)}, bf16[512,128]{1,0:T(8,128)(2,1)S(1)}, u32[]{:S(2)}, u32[]{:S(2)}) %collective-permute-start.15) | collective-permute-done | bytes 131104 | tf_op jit(solution)/shard_map/ppermute | solution.py:404
  62.7 1.1 %collective-permute-done.16.before = bf16[512,128]{1,0:T(8,128)(2,1)S(1)} collective-permute-done((bf16[512,128]{1,0:T(8,128)(2,1)S(1)}, bf16[512,128]{1,0:T(8,128)(2,1)S(1)}, u32[]{:S(2)}, u32[]{:S(2)}) %collective-permute-start.16) | collective-permute-done | bytes 131104 | tf_op jit(solution)/shard_map/ppermute | solution.py:401
  63.8 0.8 %place_rows.1 = bf16[4,512,128]{2,1,0:T(8,128)(2,1)} custom-call(bf16[512,128]{1,0:T(8,128)(2,1)S(1)} %get-tuple-element.49.own, bf16[512,128]{1,0:T(8,128)(2,1)S(1)} %collective-permute-done.14.across, bf16[512,128]{1,0:T(8,128)(2,1)S(1)} %collective-permute-done.15.after, bf16[512,128]{1,0:T(8,128)(2,1)S(1)} %collective-permute-done.16.before), custom_call_target="tpu_custom_call" | custom-call | tf_op jit(solution)/shard_map/place_rows/pallas_call | solution.py:355
  (31 shorter events, 2.0 us)
Async XLA Ops:
  3.1 12.1 %collective-permute-start.3 = (bf16[1024,512]{1,0:T(8,128)(2,1)}, bf16[1024,512]{1,0:T(8,128)(2,1)}, u32[]{:S(2)}, u32[]{:S(2)}) collective-permute-start(bf16[1024,512]{1,0:T(8,128)(2,1)} %get-tuple-element.31.xa), channel_id=1, source_target_pairs={{4,0},{0,4},{12,8},{8,12},{20,16},{16,20},{28,24},{24,28},{36,32},... | collective-permute-start | bytes 3145736 | tf_op jit(solution)/shard_map/ppermute | solution.py:380
  6.4 8.8 %collective-permute-start.4 = (bf16[4,512,128]{2,1,0:T(8,128)(2,1)S(1)}, bf16[4,512,128]{2,1,0:T(8,128)(2,1)S(1)}, u32[]{:S(2)}, u32[]{:S(2)}) collective-permute-start(bf16[4,512,128]{2,1,0:T(8,128)(2,1)S(1)} %get-tuple-element.32.w0), channel_id=1, source_target_pairs={{3,0},{0,1},{1,2},{2,3},{5,4},{6,5},{7,6},{4,7},{11,8},{8,9},{9,10... | collective-permute-start | bytes 1572872 | tf_op jit(solution)/shard_map/ppermute | solution.py:398
  7.4 28.4 %collective-permute-start = (bf16[1024,512]{1,0:T(8,128)(2,1)}, bf16[1024,512]{1,0:T(8,128)(2,1)S(1)}, u32[]{:S(2)}, u32[]{:S(2)}) collective-permute-start(bf16[1024,512]{1,0:T(8,128)(2,1)} %get-tuple-element.31.xa), channel_id=1, source_target_pairs={{8,0},{252,4},{16,8},{4,12},{24,16},{12,20},{32,24},{20,28},{40,32... | collective-permute-start | bytes 3145736 | tf_op jit(solution)/shard_map/ppermute | solution.py:380
  8.6 29.2 %collective-permute-start.1 = (bf16[1024,512]{1,0:T(8,128)(2,1)}, bf16[1024,512]{1,0:T(8,128)(2,1)S(1)}, u32[]{:S(2)}, u32[]{:S(2)}) collective-permute-start(bf16[1024,512]{1,0:T(8,128)(2,1)} %get-tuple-element.31.xa), channel_id=1, source_target_pairs={{248,0},{12,4},{0,8},{20,12},{8,16},{28,20},{16,24},{36,28},{24,32... | collective-permute-start | bytes 3145736 | tf_op jit(solution)/shard_map/ppermute | solution.py:380
  15.2 5.6 %collective-permute-start.6 = (bf16[4,256,128]{2,1,0:T(8,128)(2,1)S(1)}, bf16[4,256,128]{2,1,0:T(8,128)(2,1)S(1)}, u32[]{:S(2)}, u32[]{:S(2)}) collective-permute-start(bf16[4,256,128]{2,1,0:T(8,128)(2,1)S(1)} %constant_dynamic-slice_fusion), channel_id=1, source_target_pairs={{3,0},{0,1},{1,2},{2,3},{5,4},{6,5},{7,6},{4,7},{11,8},{8,9},{9,10... | collective-permute-start | bytes 786440 | tf_op jit(solution)/shard_map/ppermute | solution.py:398
  16.7 9.7 %collective-permute-start.2 = (bf16[512,512]{1,0:T(8,128)(2,1)}, bf16[512,512]{1,0:T(8,128)(2,1)S(1)}, u32[]{:S(2)}, u32[]{:S(2)}) collective-permute-start(bf16[512,512]{1,0:T(8,128)(2,1)} %u0.1), channel_id=1, source_target_pairs={{3,0},{0,1},{1,2},{2,3},{5,4},{6,5},{7,6},{4,7},{11,8},{8,9},{9,10... | collective-permute-start | bytes 1572872 | tf_op jit(solution)/shard_map/ppermute | solution.py:398
  16.8 13.4 %collective-permute-start.5 = (bf16[4,512,128]{2,1,0:T(8,128)(2,1)S(1)}, bf16[4,512,128]{2,1,0:T(8,128)(2,1)S(1)}, u32[]{:S(2)}, u32[]{:S(2)}) collective-permute-start(bf16[4,512,128]{2,1,0:T(8,128)(2,1)S(1)} %collective-permute-done.4.w1), channel_id=1, source_target_pairs={{4,0},{0,4},{12,8},{8,12},{20,16},{16,20},{28,24},{24,28},{36,32},... | collective-permute-start | bytes 1572872 | tf_op jit(solution)/shard_map/ppermute | solution.py:380
  20.8 14.9 %collective-permute-start.8 = (bf16[512,512]{1,0:T(8,128)(2,1)}, bf16[512,512]{1,0:T(8,128)(2,1)S(1)}, u32[]{:S(2)}, u32[]{:S(2)}) collective-permute-start(bf16[512,512]{1,0:T(8,128)(2,1)} %d0.1), channel_id=1, source_target_pairs={{3,0},{0,1},{1,2},{2,3},{5,4},{6,5},{7,6},{4,7},{11,8},{8,9},{9,10... | collective-permute-start | bytes 1572872 | tf_op jit(solution)/shard_map/ppermute | solution.py:398
  26.4 4.9 %collective-permute-start.7 = (bf16[4,256,128]{2,1,0:T(8,128)(2,1)S(1)}, bf16[4,256,128]{2,1,0:T(8,128)(2,1)S(1)}, u32[]{:S(2)}, u32[]{:S(2)}) collective-permute-start(bf16[4,256,128]{2,1,0:T(8,128)(2,1)S(1)} %collective-permute-done.6.w3m), channel_id=1, source_target_pairs={{4,0},{0,4},{12,8},{8,12},{20,16},{16,20},{28,24},{24,28},{36,32},... | collective-permute-start | bytes 786440 | tf_op jit(solution)/shard_map/ppermute | solution.py:380
  37.8 5.1 %collective-permute-start.10 = (bf16[1024,512]{1,0:T(8,128)(2,1)S(1)}, bf16[1024,512]{1,0:T(8,128)(2,1)S(1)}, u32[]{:S(2)}, u32[]{:S(2)}) collective-permute-start(bf16[1024,512]{1,0:T(8,128)(2,1)S(1)} %collective-permute-done.xa), channel_id=1, source_target_pairs={{4,0},{0,4},{12,8},{8,12},{20,16},{16,20},{28,24},{24,28},{36,32},... | collective-permute-start | bytes 3145736 | tf_op jit(solution)/shard_map/ppermute | solution.py:380
  39.5 8.9 %collective-permute-start.9 = (bf16[512,512]{1,0:T(8,128)(2,1)S(1)}, bf16[512,512]{1,0:T(8,128)(2,1)S(1)}, u32[]{:S(2)}, u32[]{:S(2)}) collective-permute-start(bf16[512,512]{1,0:T(8,128)(2,1)S(1)} %one_to_relay.1), channel_id=1, source_target_pairs={{3,0},{0,1},{1,2},{2,3},{5,4},{6,5},{7,6},{4,7},{11,8},{8,9},{9,10... | collective-permute-start | bytes 1572872 | tf_op jit(solution)/shard_map/ppermute | solution.py:398
  39.9 9.9 %collective-permute-start.11 = (bf16[512,512]{1,0:T(8,128)(2,1)S(1)}, bf16[512,512]{1,0:T(8,128)(2,1)S(1)}, u32[]{:S(2)}, u32[]{:S(2)}) collective-permute-start(bf16[512,512]{1,0:T(8,128)(2,1)S(1)} %collective-permute-done.2.a_ref.u1), channel_id=1, source_target_pairs={{4,0},{0,4},{12,8},{8,12},{20,16},{16,20},{28,24},{24,28},{36,32},... | collective-permute-start | bytes 1572872 | tf_op jit(solution)/shard_map/ppermute | solution.py:380
  39.9 3.0 %copy-start.4 = (s32[8,8]{1,0:T(8,128)S(1)}, s32[8,8]{1,0:T(8,128)}, u32[]{:S(2)}) copy-start(s32[8,8]{1,0:T(8,128)} %list_ref.1) | copy-start | bytes 772
  40.0 3.0 %copy-start.5 = (s32[8]{0:T(128)S(1)}, s32[8]{0:T(128)}, u32[]{:S(2)}) copy-start(s32[8]{0:T(128)} %count_ref.1) | copy-start | bytes 100
  42.3 7.6 %copy-start = (bf16[512,512]{1,0:T(8,128)(2,1)S(1)}, bf16[512,512]{1,0:T(8,128)(2,1)}, u32[]{:S(2)}) copy-start(bf16[512,512]{1,0:T(8,128)(2,1)} %u0.1) | copy-start | bytes 1572868
  42.3 7.6 %copy-start.1 = (bf16[512,512]{1,0:T(8,128)(2,1)S(1)}, bf16[512,512]{1,0:T(8,128)(2,1)}, u32[]{:S(2)}) copy-start(bf16[512,512]{1,0:T(8,128)(2,1)} %d0.1) | copy-start | bytes 1572868
  42.3 7.6 %copy-start.2 = (f32[2,2,512]{2,1,0:T(2,128)S(1)}, f32[2,2,512]{2,1,0:T(2,128)}, u32[]{:S(2)}) copy-start(f32[2,2,512]{2,1,0:T(2,128)} %gain_ref.3) | copy-start | bytes 24580
  42.3 7.6 %copy-start.3 = (f32[2,2,512]{2,1,0:T(2,128)S(1)}, f32[2,2,512]{2,1,0:T(2,128)}, u32[]{:S(2)}) copy-start(f32[2,2,512]{2,1,0:T(2,128)} %shift_ref.3) | copy-start | bytes 24580
  42.4 7.5 %collective-permute-start.12 = (bf16[512,512]{1,0:T(8,128)(2,1)S(1)}, bf16[512,512]{1,0:T(8,128)(2,1)S(1)}, u32[]{:S(2)}, u32[]{:S(2)}) collective-permute-start(bf16[512,512]{1,0:T(8,128)(2,1)S(1)} %collective-permute-done.8.b_ref.d1), channel_id=1, source_target_pairs={{4,0},{0,4},{12,8},{8,12},{20,16},{16,20},{28,24},{24,28},{36,32},... | collective-permute-start | bytes 1572872 | tf_op jit(solution)/shard_map/ppermute | solution.py:380
  48.4 5.0 %collective-permute-start.13 = (bf16[512,512]{1,0:T(8,128)(2,1)S(1)}, bf16[512,512]{1,0:T(8,128)(2,1)S(1)}, u32[]{:S(2)}, u32[]{:S(2)}) collective-permute-start(bf16[512,512]{1,0:T(8,128)(2,1)S(1)} %collective-permute-done.9.mine), channel_id=1, source_target_pairs={{4,0},{0,4},{12,8},{8,12},{20,16},{16,20},{28,24},{24,28},{36,32},... | collective-permute-start | bytes 1572872 | tf_op jit(solution)/shard_map/ppermute | solution.py:380
  54.4 6.7 %collective-permute-start.14 = (bf16[512,128]{1,0:T(8,128)(2,1)S(1)}, bf16[512,128]{1,0:T(8,128)(2,1)S(1)}, u32[]{:S(2)}, u32[]{:S(2)}) collective-permute-start(bf16[512,128]{1,0:T(8,128)(2,1)S(1)} %get-tuple-element.50), channel_id=1, source_target_pairs={{0,2},{1,3},{2,0},{3,1},{4,6},{5,7},{6,4},{7,5},{8,10},{9,11},{10,... | collective-permute-start | bytes 393224 | tf_op jit(solution)/shard_map/ppermute | solution.py:407
  54.6 8.1 %collective-permute-start.15 = (bf16[512,128]{1,0:T(8,128)(2,1)S(1)}, bf16[512,128]{1,0:T(8,128)(2,1)S(1)}, u32[]{:S(2)}, u32[]{:S(2)}) collective-permute-start(bf16[512,128]{1,0:T(8,128)(2,1)S(1)} %get-tuple-element.51), channel_id=1, source_target_pairs={{1,0},{2,1},{3,2},{0,3},{5,4},{6,5},{7,6},{4,7},{9,8},{10,9},{11,1... | collective-permute-start | bytes 393224 | tf_op jit(solution)/shard_map/ppermute | solution.py:404
  56.6 7.3 %collective-permute-start.16 = (bf16[512,128]{1,0:T(8,128)(2,1)S(1)}, bf16[512,128]{1,0:T(8,128)(2,1)S(1)}, u32[]{:S(2)}, u32[]{:S(2)}) collective-permute-start(bf16[512,128]{1,0:T(8,128)(2,1)S(1)} %get-tuple-element.52), channel_id=1, source_target_pairs={{0,1},{1,2},{2,3},{3,0},{4,5},{5,6},{6,7},{7,4},{8,9},{9,10},{10,1... | collective-permute-start | bytes 393224 | tf_op jit(solution)/shard_map/ppermute | solution.py:401

commit v7 on v5

--- a/solution.py
+++ b/solution.py
@@ -63,23 +63,18 @@
 def norm_kernel(state_ref, gain_ref, shift_ref, o_ref, x_in, affine, sems):
     sample = my_place()[0]
     s = pl.ds(sample, 1)
-    chunks = sems.shape[0] - 2
+    chunks = 4
     step = x_in.shape[0] // chunks
     spans = [pl.ds(k * step, step) for k in range(chunks)]
-    loads = [
-        pltpu.make_async_copy(state_ref.at[sample, at], x_in.at[at], sems.at[k])
-        for k, at in enumerate(spans)
-    ]
-    small = [
-        pltpu.make_async_copy(r, affine.at[k], sems.at[chunks + k])
-        for k, r in enumerate((gain_ref, shift_ref))
-    ]
-    for c in loads[:1] + small + loads[1:]:
-        c.start()
-    for c in small:
+    jobs = [(state_ref.at[sample, at], x_in.at[at]) for at in spans]
+    jobs += [(gain_ref, affine.at[0]), (shift_ref, affine.at[1])]
+    copies = [pltpu.make_async_copy(a, b, sems.at[k]) for k, (a, b) in enumerate(jobs)]
+    for k in (0, chunks, chunks + 1, *range(1, chunks)):
+        copies[k].start()
+    for c in copies[chunks:]:
         c.wait()
     gain, shift = affine[0, 0, s], affine[1, 0, s]
-    for c, at in zip(loads, spans):
+    for c, at in zip(copies, spans):
         c.wait()
         o_ref[at] = bf(normalise(x_in[at].astype(jnp.float32), gain, shift))
 
@@ -97,51 +92,36 @@
             pltpu.SemaphoreType.DMA((6,)),
         ],
         name="norm_rows",
-        compiler_params=pltpu.CompilerParams(vmem_limit_bytes=8 * MIB),
-    )(kept_in_hbm(state), kept_in_hbm(gain), kept_in_hbm(shift))
-
-
-def pack_kernel(qkv_ref, out_ref, o_ref):
+        compiler_params=pltpu.CompilerParams(vmem_limit_bytes=6 * MIB),
+    )(*[kept_in_hbm(v) for v in (state, gain, shift)])
+
+
+def pack_kernel(qkv_ref, out_ref, w_ref, sems):
+    head = NODE_BLK
     parts = qkv_ref.shape[0]
-    head = NODE_BLK
-    o_ref[:parts] = qkv_ref[...]
-    for k in range(HEADS):
-        o_ref[parts, k * head : (k + 1) * head] = out_ref[:, k * head : (k + 1) * head]
+    jobs = [(qkv_ref, w_ref.at[pl.ds(0, parts)])]
+    jobs += [
+        (out_ref.at[:, pl.ds(k * head, head)], w_ref.at[parts, pl.ds(k * head, head)])
+        for k in range(HEADS)
+    ]
+    copies = [pltpu.make_async_copy(a, b, sems.at[k]) for k, (a, b) in enumerate(jobs)]
+    for c in copies:
+        c.start()
+    for c in copies:
+        c.wait()
 
 
 def packed(qkv, out_w):
     parts, width, head = qkv.shape
     return pl.pallas_call(
         pack_kernel,
-        in_specs=[VMEM] * 2,
+        in_specs=[HBM] * 2,
         out_specs=VMEM,
         out_shape=in_vmem((parts + 1, width, head)),
+        scratch_shapes=[pltpu.SemaphoreType.DMA((1 + HEADS,))],
         name="pack_weights",
         compiler_params=pltpu.CompilerParams(vmem_limit_bytes=4 * MIB),
-    )(qkv, out_w)
-
-
-def relay_kernel(a_ref, b_ref, o_ref):
-    par = my_place()[2]
-
-    @pl.when(par == 0)
-    def _():
-        o_ref[...] = a_ref[...]
-
-    @pl.when(par == 1)
-    def _():
-        o_ref[...] = b_ref[...]
-
-
-def one_to_relay(a, b):
-    return pl.pallas_call(
-        relay_kernel,
-        in_specs=[VMEM] * 2,
-        out_specs=VMEM,
-        out_shape=in_vmem(a.shape),
-        name="one_to_relay",
-        compiler_params=pltpu.CompilerParams(vmem_limit_bytes=4 * MIB),
-    )(a, b)
+    )(kept_in_hbm(qkv), kept_in_hbm(out_w))
 
 
 def write_kv(x_ref, wkv_ref, kv_ref, first):
@@ -152,30 +132,17 @@
         kv_ref[at : at + ROWS // NODE_BLK] = out.reshape((ROWS // NODE_BLK, NODE_BLK, 2 * width))
 
 
-def kv_first_kernel(xa, xb, w0, w1, w2, w3m, w3t, kv_ref, q_ref, wkv_ref, wo_ref, wq_ref):
+def kv_first_kernel(xa, xb, w0, w1, w2, w3, kv_ref, q_ref, wkv_ref, wo_ref, wq_ref):
     head = NODE_BLK
-    _, share, par, _, _ = my_place()
-    half = w3m.shape[1]
-    halves = ((par, w3m), (1 - par, w3t))
-    for h in range(HEADS):
+    share = my_place()[1]
+    for h, w in enumerate((w0, w1, w2, w3)):
         at = (h // 2) * 4 * head + (h % 2) * head
-        spots = ((0, wq_ref, h * head), (1, wkv_ref, at), (2, wkv_ref, at + 2 * head))
-        for c, dst, col in spots:
-            if h < 3:
-                dst[:, col : col + head] = (w0, w1, w2)[h][c]
-            else:
-                for which, w in halves:
-                    dst[aligned(which, half), col : col + head] = w[c]
-        rows = slice(h * head, (h + 1) * head)
-        if h < 3:
-            for k in range(HEADS):
-                wo_ref[rows, k * head : (k + 1) * head] = (w0, w1, w2)[h][3, k * head : (k + 1) * head]
-        else:
-            for which, w in halves:
-                for k in range(HEADS // 2):
-                    wo_ref[rows, aligned(which * (HEADS // 2) + k, head)] = w[
-                        3, k * head : (k + 1) * head
-                    ]
+        wq_ref[:, h * head : (h + 1) * head] = w[0]
+        wkv_ref[:, at : at + head] = w[1]
+        wkv_ref[:, at + 2 * head : at + 3 * head] = w[2]
+        for k in range(HEADS):
+            block = slice(k * head, (k + 1) * head)
+            wo_ref[h * head : (h + 1) * head, block] = w[3, block]
     write_kv(xa, wkv_ref, kv_ref, 0)
     write_kv(xb, wkv_ref, kv_ref, xa.shape[0] // NODE_BLK)
     q_ref[...] = bf(matmul(xa[aligned(share, q_ref.shape[0])], wq_ref[...]))
@@ -195,7 +162,7 @@
             in_vmem((width, width)),
         ],
         name="kv_first",
-        compiler_params=pltpu.CompilerParams(vmem_limit_bytes=16 * MIB),
+        compiler_params=pltpu.CompilerParams(vmem_limit_bytes=12 * MIB),
     )(xa, xb, *weights)
 
 
@@ -214,7 +181,7 @@
         out_shape=in_vmem(kv.shape),
         input_output_aliases={3: 0},
         name="kv_second",
-        compiler_params=pltpu.CompilerParams(vmem_limit_bytes=16 * MIB),
+        compiler_params=pltpu.CompilerParams(vmem_limit_bytes=12 * MIB),
     )(xa, xb, wkv, kv)
 
 
@@ -276,7 +243,7 @@
         out_shape=[in_vmem((rows, width)), in_vmem(kv.shape)],
         input_output_aliases={5: 1},
         name="attend",
-        compiler_params=pltpu.CompilerParams(vmem_limit_bytes=16 * MIB),
+        compiler_params=pltpu.CompilerParams(vmem_limit_bytes=12 * MIB),
     )(listed, counts, relay, query, wkv, kv)[0]
 
 
@@ -317,50 +284,35 @@
             pltpu.SemaphoreType.DMA,
         ],
         name="mlp_first",
-        compiler_params=pltpu.CompilerParams(vmem_limit_bytes=16 * MIB),
+        compiler_params=pltpu.CompilerParams(vmem_limit_bytes=12 * MIB),
     )(heads, gain, shift, wo, *weights, kept_in_hbm(state))
 
 
-def mlp_second_kernel(resid_ref, normed_ref, mine, theirs, o0, o1, o2, o3, total_ref, up_ref, down_ref):
-    _, _, par, rank, _ = my_place()
+def mlp_second_kernel(resid_ref, normed_ref, u_ref, d_ref, o0, o1, o2, o3, total_ref):
+    rank = my_place()[3]
     head = NODE_BLK
-
-    @pl.when(par == 0)
-    def _():
-        up_ref[...] = mine[...]
-        down_ref[...] = theirs[...]
-
-    @pl.when(par == 1)
-    def _():
-        up_ref[...] = theirs[...]
-        down_ref[...] = mine[...]
-
-    hidden = bf(silu(matmul(normed_ref[...], up_ref[...])))
-    total_ref[...] = resid_ref[...] + matmul(hidden, down_ref[...])
+    hidden = bf(silu(matmul(normed_ref[...], u_ref[...])))
+    total_ref[...] = resid_ref[...] + matmul(hidden, d_ref[...])
     for r, o_ref in enumerate((o0, o1, o2, o3)):
         o_ref[...] = bf(total_ref[:, aligned(lax.rem(rank + r, HEADS), head)])
 
 
-def mlp_second(resid, normed, mine, theirs):
+def mlp_second(resid, normed, u, d):
     rows, width = normed.shape
     return pl.pallas_call(
         mlp_second_kernel,
         in_specs=[VMEM] * 4,
         out_specs=[VMEM] * HEADS,
         out_shape=[in_vmem((rows, width // HEADS))] * HEADS,
-        scratch_shapes=[
-            pltpu.VMEM((rows, width), jnp.float32),
-            pltpu.VMEM(mine.shape, jnp.bfloat16),
-            pltpu.VMEM(mine.shape, jnp.bfloat16),
-        ],
+        scratch_shapes=[pltpu.VMEM((rows, width), jnp.float32)],
         name="mlp_second",
-        compiler_params=pltpu.CompilerParams(vmem_limit_bytes=16 * MIB),
-    )(resid, normed, mine, theirs)
-
-
-def place_kernel(own, a, b, c, o_ref):
+        compiler_params=pltpu.CompilerParams(vmem_limit_bytes=12 * MIB),
+    )(resid, normed, u, d)
+
+
+def place_kernel(own, across, after, before, o_ref):
     rank = my_place()[3]
-    for off, r in ((0, own), (3, a), (1, b), (2, c)):
+    for off, r in ((0, own), (2, across), (1, after), (3, before)):
         o_ref[lax.rem(rank + off, HEADS)] = r[...]
 
 
@@ -387,9 +339,6 @@
     per_dev = row_count // NODE_BLK
     doms = lax.axis_size("dom")
     tps = lax.axis_size("tp")
-    dom = lax.axis_index("dom")
-    par = lax.rem(dom, 2)
-
     def hop(v, pairs):
         return lax.ppermute(v, "dom", pairs)
 
@@ -420,36 +369,37 @@
     def across(v):
         return lax.ppermute(v, "tp", [(i, (i + 2) % tps) for i in range(tps)])
 
-    w0 = packed(jnp.transpose(qkv_weight, (1, 0, 2)), out_weight)
-    w1 = ring(w0)
-    own = normed_rows(after(state, w0), norm_gain, norm_shift)
+    own = normed_rows(state, norm_gain, norm_shift)
     partner = swap(own)
     near_rows, far_rows = near(own), far(own)
 
-    w1 = after(w1, partner)
-    w2 = swap(w1)
-    mid = width // 2
-    w1_half = lax.dynamic_slice_in_dim(w1, par * mid, mid, 1)
-    w3m = ring(w1_half)
-    w3t = swap(w3m)
-    up_late, down_late, w1_half = lax.optimization_barrier((up_weight, down_weight, w1_half))
-    u1, d1 = ring(up_late), ring(down_late)
-
-    kv, query, wkv, wo = kv_first(own, partner, (w0, w1, w2, w3m, w3t), 5)
+    qkv, own = lax.optimization_barrier((qkv_weight, own))
+    w0 = packed(jnp.transpose(qkv, (1, 0, 2)), out_weight)
+
+    def gather(own_w, own_up):
+        first = ring(own_w)
+        return first, swap(first), ring(first), ring(own_up)
+
+    def never(own_w, own_up):
+        return own_w, own_w, own_w, own_up
+
+    w1, w2, w3, u1 = lax.cond(lax.axis_index("tp") >= 0, gather, never, w0, up_weight)
+    d1 = ring(after(down_weight, w1))
+
+    kv, query, wkv, wo = kv_first(own, partner, (w0, w1, w2, w3), 5)
+    u1, query = lax.optimization_barrier((u1, query))
+    u3 = ring(u1)
     near_rows, far_rows, query = lax.optimization_barrier((near_rows, far_rows, query))
     relay = swap(near_rows)
-    u1, d1 = lax.optimization_barrier((u1, d1, query))[:2]
-    u2, d2 = swap(u1), swap(d1)
-    last = ring(one_to_relay(u1, d1))
     kv = kv_second(near_rows, far_rows, wkv, kv)
+    u1, d1, kv = lax.optimization_barrier((u1, d1, kv))
+    u2, d2, d3 = swap(u1), swap(d1), ring(d1)
 
     heads = attend(neighbours, counts, relay, query, wkv, kv, per_dev, doms)
-    last, heads = lax.optimization_barrier((last, heads))
-    last_too = swap(last)
     weights = (up_weight, down_weight, u1, d1, u2, d2)
     resid, normed = mlp_first(heads, norm_gain, norm_shift, wo, weights, state)
-    mine = mlp_second(resid, normed, last, last_too)
-    out = placed_rows((mine[0], up(mine[1]), down(mine[3]), across(mine[2])))
+    mine = mlp_second(resid, normed, u3, d3)
+    out = placed_rows((mine[0], across(mine[2]), down(mine[3]), up(mine[1])))
     return out.reshape(samples, row_count, width // tps)
 
 

time: 67.9 us -> 81.4 us (1.20)
  starting transfers between devices: 24 us -> 32.6 us
  waiting for transfers between devices: 21 us -> 26.7 us
  local copies, waits for them, and re-layouts: 1.95 us -> 0.03 us
  Pallas kernels: 20.4 us -> 21.6 us
    ppermute x5 -> x6, waiting for transfers between devices: 5.62 us -> 14.3 us  [ring(): return lax.ppermute(v, ('dom', 'tp'), pairs)]
    ppermute x5 -> x6, starting transfers between devices: 1.63 us -> 9.37 us  [ring(): return lax.ppermute(v, ('dom', 'tp'), pairs)]
    ppermute x9 -> x7, waiting for transfers between devices: 8.95 us -> 5.99 us  [hop(): return lax.ppermute(v, 'dom', pairs)]
    ppermute x1, waiting for transfers between devices: 2.82 us -> 0.07 us  [up(): return lax.ppermute(v, 'tp', [(i, (i + 1) % tps) for i in range(tps)])]
    ppermute x1, waiting for transfers between devices: 1.61 us -> 4.19 us  [down(): return lax.ppermute(v, 'tp', [((i + 1) % tps, i) for i in range(tps)])]
    unnamed x16 -> x12, local copies, waits for them, and re-layouts: 1.93 us -> 0.03 us
    ppermute x1, starting transfers between devices: 2.66 us -> 0.84 us  [down(): return lax.ppermute(v, 'tp', [((i + 1) % tps, i) for i in range(tps)])]
    pallas_call x1, Pallas kernels: 3.59 us -> 2.34 us  [kv_second(): pl.pallas_call(kv_second_kernel, in_specs=[VMEM] * 4, out_specs=VMEM, out...]
  transfers between devices with their start and end apart: 17 -> 16, of which waited for: 7 -> 8; matrix products, arithmetic and copies ran while one was open for 0% -> 0% of each run, Pallas kernels for 24% -> 22%
where the time goes in v7:
time: 81.4 us; the launch traced here: 81.1 us
  starting transfers between devices  32.6 us (40%)
  waiting for transfers between devices  26.7 us (33%)
  Pallas kernels  21.6 us (27%)
    ppermute x7, starting transfers between devices, hop(): return lax.ppermute(v, 'dom', pairs)  19.9 us
    ppermute x6, waiting for transfers between devices, ring(): return lax.ppermute(v, ('dom', 'tp'), pairs)  14.3 us
    ppermute x6, starting transfers between devices, ring(): return lax.ppermute(v, ('dom', 'tp'), pairs)  9.37 us
    ppermute x7, waiting for transfers between devices, hop(): return lax.ppermute(v, 'dom', pairs)  5.99 us
    pallas_call x1, Pallas kernels, attend(): pl.pallas_call(functools.partial(attend_kernel, doms=doms, per_dev=per_de...  5.43 us
    pallas_call x1, Pallas kernels, mlp_first(): pl.pallas_call(mlp_first_kernel, in_specs=[VMEM] * (4 + len(weights)) + [...  4.54 us
    pallas_call x1, Pallas kernels, kv_first(): pl.pallas_call(kv_first_kernel, in_specs=[VMEM] * (2 + len(weights)), out...  4.48 us
    ppermute x1, waiting for transfers between devices, down(): return lax.ppermute(v, 'tp', [((i + 1) % tps, i) for i in range(tps)])  4.19 us
  transfers between devices with their start and end apart: 16, of which 8 were waited for; matrix products, arithmetic and copies ran while one was open for 0% of the time, Pallas kernels for 22%

profile of v7, /device:TPU:1, one launch (start us, length us, event | category | flops | bytes accessed | tf_op | source)
XLA Modules:
  0.0 81.1 jit_solution(1151412837687347814)
XLA Ops:
  0.0 2.0 %norm_rows.1.xa = bf16[1024,512]{1,0:T(8,128)(2,1)S(1)} custom-call(bf16[2,1024,512]{2,1,0:T(8,128)(2,1)} %state_ref.3, f32[2,2,512]{2,1,0:T(2,128)} %gain_ref.3, f32[2,2,512]{2,1,0:T(2,128)} %shift_ref.3), custom_call_target="tpu_custom_call" | custom-call | tf_op jit(solution)/shard_map/norm_rows/pallas_call | solution.py:84
  2.0 3.3 %collective-permute-start.6 = (bf16[1024,512]{1,0:T(8,128)(2,1)S(1)}, bf16[1024,512]{1,0:T(8,128)(2,1)}, u32[]{:S(2)}, u32[]{:S(2)}) collective-permute-start(bf16[1024,512]{1,0:T(8,128)(2,1)S(1)} %norm_rows.1.xa), channel_id=1, source_target_pairs={{4,0},{0,4},{12,8},{8,12},{20,16},{16,20},{28,24},{24,28},{36,32},... | collective-permute-start | bytes 3145736 | tf_op jit(solution)/shard_map/ppermute | solution.py:343
  5.3 1.0 %pack_weights.1.w0 = bf16[4,512,128]{2,1,0:T(8,128)(2,1)S(1)} custom-call(bf16[3,512,128]{2,1,0:T(8,128)(2,1)} %bitcast.2, bf16[128,512]{1,0:T(8,128)(2,1)} %out_ref.1), custom_call_target="tpu_custom_call" | custom-call | tf_op jit(solution)/shard_map/pack_weights/pallas_call | solution.py:116
  6.4 25.6 %conditional.1 = (bf16[4,512,128]{2,1,0:T(8,128)(2,1)}, bf16[4,512,128]{2,1,0:T(8,128)(2,1)}, bf16[4,512,128]{2,1,0:T(8,128)(2,1)}, bf16[512,512]{1,0:T(8,128)(2,1)}) conditional(s32[]{:T(128)} %convert_element_type.3, (bf16[4,512,128]{2,1,0:T(8,128)(2,1)S(1)}, bf16[512,512]{1,0:T(8,128)(2,1)}) %tuple.19, (bf16[4,512,128]{2,1,0:T(8,128)(2,1)S(1)}, ...), branch_computations={%region_0.0_spmd, %region_1.0_spmd} | conditional | bytes 8388800 | solution.py:386
  6.4 2.3 %collective-permute-start = (bf16[4,512,128]{2,1,0:T(8,128)(2,1)S(1)}, bf16[4,512,128]{2,1,0:T(8,128)(2,1)}, u32[]{:S(2)}, u32[]{:S(2)}) collective-permute-start(bf16[4,512,128]{2,1,0:T(8,128)(2,1)S(1)} %get-tuple-element.15), channel_id=1, source_target_pairs={{3,0},{0,1},{1,2},{2,3},{5,4},{6,5},{7,6},{4,7},{11,8},{8,9},{9,10... | collective-permute-start | bytes 1572872 | tf_op jit(solution)/shard_map/cond/branch_1_fun/ppermute | solution.py:361
  9.1 5.7 %collective-permute-done = bf16[4,512,128]{2,1,0:T(8,128)(2,1)} collective-permute-done((bf16[4,512,128]{2,1,0:T(8,128)(2,1)S(1)}, bf16[4,512,128]{2,1,0:T(8,128)(2,1)}, u32[]{:S(2)}, u32[]{:S(2)}) %collective-permute-start) | collective-permute-done | bytes 524320 | tf_op jit(solution)/shard_map/cond/branch_1_fun/ppermute | solution.py:361
  14.8 8.6 %collective-permute-start.1 = (bf16[4,512,128]{2,1,0:T(8,128)(2,1)}, bf16[4,512,128]{2,1,0:T(8,128)(2,1)}, u32[]{:S(2)}, u32[]{:S(2)}) collective-permute-start(bf16[4,512,128]{2,1,0:T(8,128)(2,1)} %collective-permute-done), channel_id=1, source_target_pairs={{4,0},{0,4},{12,8},{8,12},{20,16},{16,20},{28,24},{24,28},{36,32},... | collective-permute-start | bytes 1572872 | tf_op jit(solution)/shard_map/cond/branch_1_fun/ppermute | solution.py:343
  23.4 1.5 %collective-permute-start.2 = (bf16[4,512,128]{2,1,0:T(8,128)(2,1)}, bf16[4,512,128]{2,1,0:T(8,128)(2,1)}, u32[]{:S(2)}, u32[]{:S(2)}) collective-permute-start(bf16[4,512,128]{2,1,0:T(8,128)(2,1)} %collective-permute-done), channel_id=1, source_target_pairs={{3,0},{0,1},{1,2},{2,3},{5,4},{6,5},{7,6},{4,7},{11,8},{8,9},{9,10... | collective-permute-start | bytes 1572872 | tf_op jit(solution)/shard_map/cond/branch_1_fun/ppermute | solution.py:361
  25.2 6.8 %collective-permute-done.2 = bf16[4,512,128]{2,1,0:T(8,128)(2,1)} collective-permute-done((bf16[4,512,128]{2,1,0:T(8,128)(2,1)}, bf16[4,512,128]{2,1,0:T(8,128)(2,1)}, u32[]{:S(2)}, u32[]{:S(2)}) %collective-permute-start.2) | collective-permute-done | bytes 524320 | tf_op jit(solution)/shard_map/cond/branch_1_fun/ppermute | solution.py:361
  32.7 3.1 %collective-permute-start.8 = (bf16[512,512]{1,0:T(8,128)(2,1)}, bf16[512,512]{1,0:T(8,128)(2,1)S(1)}, u32[]{:S(2)}, u32[]{:S(2)}) collective-permute-start(bf16[512,512]{1,0:T(8,128)(2,1)} %d0.1), channel_id=1, source_target_pairs={{3,0},{0,1},{1,2},{2,3},{5,4},{6,5},{7,6},{4,7},{11,8},{8,9},{9,10... | collective-permute-start | bytes 1572872 | tf_op jit(solution)/shard_map/ppermute | solution.py:361
  35.8 4.5 %kv_first.1 = (bf16[40,128,1024]{2,1,0:T(8,128)(2,1)S(1)}, bf16[512,512]{1,0:T(8,128)(2,1)S(1)}, bf16[512,1024]{1,0:T(8,128)(2,1)S(1)}, bf16[512,512]{1,0:T(8,128)(2,1)S(1)}) custom-call(bf16[1024,512]{1,0:T(8,128)(2,1)S(1)} %norm_rows.1.xa, bf16[1024,512]{1,0:T(8,128)(2,1)} %collective-permute-done.6.xb, bf16[4,512,128]{2,1,0:T(8,128)(2,1)S(1)} %pack_weights.1.w0, ...), custom_call_target="tpu_custom_call" | custom-call | tf_op jit(solution)/shard_map/kv_first/pallas_call | solution.py:153
  40.3 5.6 %collective-permute-done.5.xb = bf16[1024,512]{1,0:T(8,128)(2,1)S(1)} collective-permute-done((bf16[1024,512]{1,0:T(8,128)(2,1)S(1)}, bf16[1024,512]{1,0:T(8,128)(2,1)S(1)}, u32[]{:S(2)}, u32[]{:S(2)}) %collective-permute-start.5) | collective-permute-done | bytes 1048608 | tf_op jit(solution)/shard_map/ppermute | solution.py:343
  46.0 6.8 %collective-permute-start.7 = (bf16[1024,512]{1,0:T(8,128)(2,1)S(1)}, bf16[1024,512]{1,0:T(8,128)(2,1)S(1)}, u32[]{:S(2)}, u32[]{:S(2)}) collective-permute-start(bf16[1024,512]{1,0:T(8,128)(2,1)S(1)} %collective-permute-done.4.xa), channel_id=1, source_target_pairs={{4,0},{0,4},{12,8},{8,12},{20,16},{16,20},{28,24},{24,28},{36,32},... | collective-permute-start | bytes 3145736 | tf_op jit(solution)/shard_map/ppermute | solution.py:343
  52.7 2.3 %kv_second.1.kv_in = bf16[40,128,1024]{2,1,0:T(8,128)(2,1)S(1)} custom-call(bf16[1024,512]{1,0:T(8,128)(2,1)S(1)} %collective-permute-done.4.xa, bf16[1024,512]{1,0:T(8,128)(2,1)S(1)} %collective-permute-done.5.xb, bf16[512,1024]{1,0:T(8,128)(2,1)S(1)} %get-tuple-element.53.wkv_ref, ...), custom_call_target="tpu_custom_call", output_to_operand_aliasing={{}: (3, {})} | custom-call | tf_op jit(solution)/shard_map/kv_second/pallas_call | solution.py:177
  55.7 1.5 %collective-permute-start.12 = (bf16[512,512]{1,0:T(8,128)(2,1)S(1)}, bf16[512,512]{1,0:T(8,128)(2,1)S(1)}, u32[]{:S(2)}, u32[]{:S(2)}) collective-permute-start(bf16[512,512]{1,0:T(8,128)(2,1)S(1)} %collective-permute-done.8.d1), channel_id=1, source_target_pairs={{3,0},{0,1},{1,2},{2,3},{5,4},{6,5},{7,6},{4,7},{11,8},{8,9},{9,10... | collective-permute-start | bytes 1572872 | tf_op jit(solution)/shard_map/ppermute | solution.py:361
  57.7 5.4 %attend.1 = (bf16[512,512]{1,0:T(8,128)(2,1)S(1)}, bf16[40,128,1024]{2,1,0:T(8,128)(2,1)S(1)}) custom-call(s32[8,8]{1,0:T(8,128)S(1)} %copy-done.3, s32[8]{0:T(128)S(1)} %copy-done.4, bf16[1024,512]{1,0:T(8,128)(2,1)S(1)} %collective-permute-done.7.relay_ref, bf16[512,512]{1,0:T(8,128)(2,1)S(1)} %get-tuple-element.52.q_ref, ...), custom_call_target="tpu_custom_call", output_to_operand_aliasing={{1}: (5, {})} | custom-call | tf_op jit(solution)/shard_map/attend/pallas_call | solution.py:239
  63.2 4.5 %mlp_first.1 = (f32[512,512]{1,0:T(8,128)S(1)}, bf16[512,512]{1,0:T(8,128)(2,1)S(1)}) custom-call(bf16[512,512]{1,0:T(8,128)(2,1)S(1)} %get-tuple-element.59.heads_ref, f32[2,2,512]{2,1,0:T(2,128)S(1)} %copy-done.1, f32[2,2,512]{2,1,0:T(2,128)S(1)} %copy-done.2, bf16[512,512]{1,0:T(8,128)(2,1)S(1)} %get-tuple-element.60.wo_ref, ...), custom_call_target="tpu_custom_call" | custom-call | tf_op jit(solution)/shard_map/mlp_first/pallas_call | solution.py:276
  67.8 1.9 %collective-permute-done.11.u_ref = bf16[512,512]{1,0:T(8,128)(2,1)S(1)} collective-permute-done((bf16[512,512]{1,0:T(8,128)(2,1)}, bf16[512,512]{1,0:T(8,128)(2,1)S(1)}, u32[]{:S(2)}, u32[]{:S(2)}) %collective-permute-start.11) | collective-permute-done | bytes 524320 | tf_op jit(solution)/shard_map/ppermute | solution.py:361
  69.7 0.9 %mlp_second.1 = (bf16[512,128]{1,0:T(8,128)(2,1)S(1)}, bf16[512,128]{1,0:T(8,128)(2,1)S(1)}, bf16[512,128]{1,0:T(8,128)(2,1)S(1)}, bf16[512,128]{1,0:T(8,128)(2,1)S(1)}) custom-call(f32[512,512]{1,0:T(8,128)S(1)} %get-tuple-element.63.resid_ref, bf16[512,512]{1,0:T(8,128)(2,1)S(1)} %get-tuple-element.64.normed_ref, ...), custom_call_target="tpu_custom_call" | custom-call | tf_op jit(solution)/shard_map/mlp_second/pallas_call | solution.py:302
  70.6 1.8 %collective-permute-start.13 = (bf16[512,128]{1,0:T(8,128)(2,1)S(1)}, bf16[512,128]{1,0:T(8,128)(2,1)S(1)}, u32[]{:S(2)}, u32[]{:S(2)}) collective-permute-start(bf16[512,128]{1,0:T(8,128)(2,1)S(1)} %get-tuple-element.66), channel_id=1, source_target_pairs={{0,2},{1,3},{2,0},{3,1},{4,6},{5,7},{6,4},{7,5},{8,10},{9,11},{10,... | collective-permute-start | bytes 393224 | tf_op jit(solution)/shard_map/ppermute | solution.py:370
  72.4 0.8 %collective-permute-start.14 = (bf16[512,128]{1,0:T(8,128)(2,1)S(1)}, bf16[512,128]{1,0:T(8,128)(2,1)S(1)}, u32[]{:S(2)}, u32[]{:S(2)}) collective-permute-start(bf16[512,128]{1,0:T(8,128)(2,1)S(1)} %get-tuple-element.67), channel_id=1, source_target_pairs={{1,0},{2,1},{3,2},{0,3},{5,4},{6,5},{7,6},{4,7},{9,8},{10,9},{11,1... | collective-permute-start | bytes 393224 | tf_op jit(solution)/shard_map/ppermute | solution.py:367
  73.9 2.2 %collective-permute-done.13.across = bf16[512,128]{1,0:T(8,128)(2,1)S(1)} collective-permute-done((bf16[512,128]{1,0:T(8,128)(2,1)S(1)}, bf16[512,128]{1,0:T(8,128)(2,1)S(1)}, u32[]{:S(2)}, u32[]{:S(2)}) %collective-permute-start.13) | collective-permute-done | bytes 131104 | tf_op jit(solution)/shard_map/ppermute | solution.py:370
  76.0 4.2 %collective-permute-done.14.after = bf16[512,128]{1,0:T(8,128)(2,1)S(1)} collective-permute-done((bf16[512,128]{1,0:T(8,128)(2,1)S(1)}, bf16[512,128]{1,0:T(8,128)(2,1)S(1)}, u32[]{:S(2)}, u32[]{:S(2)}) %collective-permute-start.14) | collective-permute-done | bytes 131104 | tf_op jit(solution)/shard_map/ppermute | solution.py:367
  80.3 0.8 %place_rows.1 = bf16[4,512,128]{2,1,0:T(8,128)(2,1)} custom-call(bf16[512,128]{1,0:T(8,128)(2,1)S(1)} %get-tuple-element.65.own, bf16[512,128]{1,0:T(8,128)(2,1)S(1)} %collective-permute-done.13.across, bf16[512,128]{1,0:T(8,128)(2,1)S(1)} %collective-permute-done.14.after, bf16[512,128]{1,0:T(8,128)(2,1)S(1)} %collective-permute-done.15.before), custom_call_target="tpu_custom_call" | custom-call | tf_op jit(solution)/shard_map/place_rows/pallas_call | solution.py:321
  (29 shorter events, 3.3 us)
Async XLA Ops:
  2.0 33.8 %collective-permute-start.6 = (bf16[1024,512]{1,0:T(8,128)(2,1)S(1)}, bf16[1024,512]{1,0:T(8,128)(2,1)}, u32[]{:S(2)}, u32[]{:S(2)}) collective-permute-start(bf16[1024,512]{1,0:T(8,128)(2,1)S(1)} %norm_rows.1.xa), channel_id=1, source_target_pairs={{4,0},{0,4},{12,8},{8,12},{20,16},{16,20},{28,24},{24,28},{36,32},... | collective-permute-start | bytes 3145736 | tf_op jit(solution)/shard_map/ppermute | solution.py:343
  5.3 35.0 %collective-permute-start.4 = (bf16[1024,512]{1,0:T(8,128)(2,1)S(1)}, bf16[1024,512]{1,0:T(8,128)(2,1)S(1)}, u32[]{:S(2)}, u32[]{:S(2)}) collective-permute-start(bf16[1024,512]{1,0:T(8,128)(2,1)S(1)} %norm_rows.1.xa), channel_id=1, source_target_pairs={{8,0},{252,4},{16,8},{4,12},{24,16},{12,20},{32,24},{20,28},{40,32... | collective-permute-start | bytes 3145736 | tf_op jit(solution)/shard_map/ppermute | solution.py:343
  6.4 8.4 %collective-permute-start = (bf16[4,512,128]{2,1,0:T(8,128)(2,1)S(1)}, bf16[4,512,128]{2,1,0:T(8,128)(2,1)}, u32[]{:S(2)}, u32[]{:S(2)}) collective-permute-start(bf16[4,512,128]{2,1,0:T(8,128)(2,1)S(1)} %get-tuple-element.15), channel_id=1, source_target_pairs={{3,0},{0,1},{1,2},{2,3},{5,4},{6,5},{7,6},{4,7},{11,8},{8,9},{9,10... | collective-permute-start | bytes 1572872 | tf_op jit(solution)/shard_map/cond/branch_1_fun/ppermute | solution.py:361
  8.7 16.2 %collective-permute-start.3 = (bf16[512,512]{1,0:T(8,128)(2,1)}, bf16[512,512]{1,0:T(8,128)(2,1)}, u32[]{:S(2)}, u32[]{:S(2)}) collective-permute-start(bf16[512,512]{1,0:T(8,128)(2,1)} %get-tuple-element.16), channel_id=1, source_target_pairs={{3,0},{0,1},{1,2},{2,3},{5,4},{6,5},{7,6},{4,7},{11,8},{8,9},{9,10... | collective-permute-start | bytes 1572872 | tf_op jit(solution)/shard_map/cond/branch_1_fun/ppermute | solution.py:361
  14.8 10.4 %collective-permute-start.1 = (bf16[4,512,128]{2,1,0:T(8,128)(2,1)}, bf16[4,512,128]{2,1,0:T(8,128)(2,1)}, u32[]{:S(2)}, u32[]{:S(2)}) collective-permute-start(bf16[4,512,128]{2,1,0:T(8,128)(2,1)} %collective-permute-done), channel_id=1, source_target_pairs={{4,0},{0,4},{12,8},{8,12},{20,16},{16,20},{28,24},{24,28},{36,32},... | collective-permute-start | bytes 1572872 | tf_op jit(solution)/shard_map/cond/branch_1_fun/ppermute | solution.py:343
  23.4 8.6 %collective-permute-start.2 = (bf16[4,512,128]{2,1,0:T(8,128)(2,1)}, bf16[4,512,128]{2,1,0:T(8,128)(2,1)}, u32[]{:S(2)}, u32[]{:S(2)}) collective-permute-start(bf16[4,512,128]{2,1,0:T(8,128)(2,1)} %collective-permute-done), channel_id=1, source_target_pairs={{3,0},{0,1},{1,2},{2,3},{5,4},{6,5},{7,6},{4,7},{11,8},{8,9},{9,10... | collective-permute-start | bytes 1572872 | tf_op jit(solution)/shard_map/cond/branch_1_fun/ppermute | solution.py:361
  32.0 13.9 %collective-permute-start.5 = (bf16[1024,512]{1,0:T(8,128)(2,1)S(1)}, bf16[1024,512]{1,0:T(8,128)(2,1)S(1)}, u32[]{:S(2)}, u32[]{:S(2)}) collective-permute-start(bf16[1024,512]{1,0:T(8,128)(2,1)S(1)} %norm_rows.1.xa), channel_id=1, source_target_pairs={{248,0},{12,4},{0,8},{20,12},{8,16},{28,20},{16,24},{36,28},{24,32... | collective-permute-start | bytes 3145736 | tf_op jit(solution)/shard_map/ppermute | solution.py:343
  32.7 22.4 %collective-permute-start.8 = (bf16[512,512]{1,0:T(8,128)(2,1)}, bf16[512,512]{1,0:T(8,128)(2,1)S(1)}, u32[]{:S(2)}, u32[]{:S(2)}) collective-permute-start(bf16[512,512]{1,0:T(8,128)(2,1)} %d0.1), channel_id=1, source_target_pairs={{3,0},{0,1},{1,2},{2,3},{5,4},{6,5},{7,6},{4,7},{11,8},{8,9},{9,10... | collective-permute-start | bytes 1572872 | tf_op jit(solution)/shard_map/ppermute | solution.py:361
  46.0 11.8 %collective-permute-start.7 = (bf16[1024,512]{1,0:T(8,128)(2,1)S(1)}, bf16[1024,512]{1,0:T(8,128)(2,1)S(1)}, u32[]{:S(2)}, u32[]{:S(2)}) collective-permute-start(bf16[1024,512]{1,0:T(8,128)(2,1)S(1)} %collective-permute-done.4.xa), channel_id=1, source_target_pairs={{4,0},{0,4},{12,8},{8,12},{20,16},{16,20},{28,24},{24,28},{36,32},... | collective-permute-start | bytes 3145736 | tf_op jit(solution)/shard_map/ppermute | solution.py:343
  52.7 5.0 %copy-start.3 = (s32[8,8]{1,0:T(8,128)S(1)}, s32[8,8]{1,0:T(8,128)}, u32[]{:S(2)}) copy-start(s32[8,8]{1,0:T(8,128)} %list_ref.1) | copy-start | bytes 772
  52.7 5.0 %copy-start.4 = (s32[8]{0:T(128)S(1)}, s32[8]{0:T(128)}, u32[]{:S(2)}) copy-start(s32[8]{0:T(128)} %count_ref.1) | copy-start | bytes 100
  55.1 8.1 %copy-start = (bf16[512,512]{1,0:T(8,128)(2,1)S(1)}, bf16[512,512]{1,0:T(8,128)(2,1)}, u32[]{:S(2)}) copy-start(bf16[512,512]{1,0:T(8,128)(2,1)} %d0.1) | copy-start | bytes 1572868
  55.1 8.1 %copy-start.1 = (f32[2,2,512]{2,1,0:T(2,128)S(1)}, f32[2,2,512]{2,1,0:T(2,128)}, u32[]{:S(2)}) copy-start(f32[2,2,512]{2,1,0:T(2,128)} %gain_ref.3) | copy-start | bytes 24580
  55.1 8.1 %copy-start.2 = (f32[2,2,512]{2,1,0:T(2,128)S(1)}, f32[2,2,512]{2,1,0:T(2,128)}, u32[]{:S(2)}) copy-start(f32[2,2,512]{2,1,0:T(2,128)} %shift_ref.3) | copy-start | bytes 24580
  55.1 8.1 %copy-start.5 = (bf16[512,512]{1,0:T(8,128)(2,1)S(1)}, bf16[512,512]{1,0:T(8,128)(2,1)}, u32[]{:S(2)}) copy-start(bf16[512,512]{1,0:T(8,128)(2,1)} %u0.1) | copy-start | bytes 1572868
  55.1 8.0 %collective-permute-start.10 = (bf16[512,512]{1,0:T(8,128)(2,1)S(1)}, bf16[512,512]{1,0:T(8,128)(2,1)S(1)}, u32[]{:S(2)}, u32[]{:S(2)}) collective-permute-start(bf16[512,512]{1,0:T(8,128)(2,1)S(1)} %collective-permute-done.8.d1), channel_id=1, source_target_pairs={{4,0},{0,4},{12,8},{8,12},{20,16},{16,20},{28,24},{24,28},{36,32},... | collective-permute-start | bytes 1572872 | tf_op jit(solution)/shard_map/ppermute | solution.py:343
  55.2 7.9 %collective-permute-start.9 = (bf16[512,512]{1,0:T(8,128)(2,1)}, bf16[512,512]{1,0:T(8,128)(2,1)S(1)}, u32[]{:S(2)}, u32[]{:S(2)}) collective-permute-start(bf16[512,512]{1,0:T(8,128)(2,1)} %get-tuple-element.61.u1), channel_id=1, source_target_pairs={{4,0},{0,4},{12,8},{8,12},{20,16},{16,20},{28,24},{24,28},{36,32},... | collective-permute-start | bytes 1572872 | tf_op jit(solution)/shard_map/ppermute | solution.py:343
  55.7 12.0 %collective-permute-start.12 = (bf16[512,512]{1,0:T(8,128)(2,1)S(1)}, bf16[512,512]{1,0:T(8,128)(2,1)S(1)}, u32[]{:S(2)}, u32[]{:S(2)}) collective-permute-start(bf16[512,512]{1,0:T(8,128)(2,1)S(1)} %collective-permute-done.8.d1), channel_id=1, source_target_pairs={{3,0},{0,1},{1,2},{2,3},{5,4},{6,5},{7,6},{4,7},{11,8},{8,9},{9,10... | collective-permute-start | bytes 1572872 | tf_op jit(solution)/shard_map/ppermute | solution.py:361
  57.3 12.4 %collective-permute-start.11 = (bf16[512,512]{1,0:T(8,128)(2,1)}, bf16[512,512]{1,0:T(8,128)(2,1)S(1)}, u32[]{:S(2)}, u32[]{:S(2)}) collective-permute-start(bf16[512,512]{1,0:T(8,128)(2,1)} %get-tuple-element.61.u1), channel_id=1, source_target_pairs={{3,0},{0,1},{1,2},{2,3},{5,4},{6,5},{7,6},{4,7},{11,8},{8,9},{9,10... | collective-permute-start | bytes 1572872 | tf_op jit(solution)/shard_map/ppermute | solution.py:361
  70.6 5.4 %collective-permute-start.13 = (bf16[512,128]{1,0:T(8,128)(2,1)S(1)}, bf16[512,128]{1,0:T(8,128)(2,1)S(1)}, u32[]{:S(2)}, u32[]{:S(2)}) collective-permute-start(bf16[512,128]{1,0:T(8,128)(2,1)S(1)} %get-tuple-element.66), channel_id=1, source_target_pairs={{0,2},{1,3},{2,0},{3,1},{4,6},{5,7},{6,4},{7,5},{8,10},{9,11},{10,... | collective-permute-start | bytes 393224 | tf_op jit(solution)/shard_map/ppermute | solution.py:370
  72.4 7.8 %collective-permute-start.14 = (bf16[512,128]{1,0:T(8,128)(2,1)S(1)}, bf16[512,128]{1,0:T(8,128)(2,1)S(1)}, u32[]{:S(2)}, u32[]{:S(2)}) collective-permute-start(bf16[512,128]{1,0:T(8,128)(2,1)S(1)} %get-tuple-element.67), channel_id=1, source_target_pairs={{1,0},{2,1},{3,2},{0,3},{5,4},{6,5},{7,6},{4,7},{9,8},{10,9},{11,1... | collective-permute-start | bytes 393224 | tf_op jit(solution)/shard_map/ppermute | solution.py:367
  73.2 7.0 %collective-permute-start.15 = (bf16[512,128]{1,0:T(8,128)(2,1)S(1)}, bf16[512,128]{1,0:T(8,128)(2,1)S(1)}, u32[]{:S(2)}, u32[]{:S(2)}) collective-permute-start(bf16[512,128]{1,0:T(8,128)(2,1)S(1)} %get-tuple-element.68), channel_id=1, source_target_pairs={{0,1},{1,2},{2,3},{3,0},{4,5},{5,6},{6,7},{7,4},{8,9},{9,10},{10,1... | collective-permute-start | bytes 393224 | tf_op jit(solution)/shard_map/ppermute | solution.py:364

commit v8 on v6

--- a/solution.py
+++ b/solution.py
@@ -61,7 +61,7 @@
 
 
 def prepare_kernel(
-    state_ref, gain_ref, shift_ref, qkv_ref, out_ref, o_ref, w_ref, x_in, affine, sems
+    state_ref, gain_ref, shift_ref, qkv_ref, out_ref, o_ref, w_ref, x_in, out_in, affine, sems
 ):
     sample = my_place()[0]
     s = pl.ds(sample, 1)
@@ -71,11 +71,8 @@
     parts = qkv_ref.shape[0]
     spans = [pl.ds(k * step, step) for k in range(chunks)]
     jobs = [(state_ref.at[sample, at], x_in.at[at]) for at in spans]
-    jobs += [(gain_ref, affine.at[0]), (shift_ref, affine.at[1]), (qkv_ref, w_ref.at[pl.ds(0, parts)])]
-    jobs += [
-        (out_ref.at[:, pl.ds(k * head, head)], w_ref.at[parts, pl.ds(k * head, head)])
-        for k in range(HEADS)
-    ]
+    jobs += [(gain_ref, affine.at[0]), (shift_ref, affine.at[1])]
+    jobs += [(qkv_ref, w_ref.at[pl.ds(0, parts)]), (out_ref, out_in)]
     copies = [pltpu.make_async_copy(a, b, sems.at[k]) for k, (a, b) in enumerate(jobs)]
     for k in (0, chunks, chunks + 1, *range(1, chunks), *range(chunks + 2, len(jobs))):
         copies[k].start()
@@ -87,6 +84,9 @@
         o_ref[at] = bf(normalise(x_in[at].astype(jnp.float32), gain, shift))
     for c in copies[chunks + 2 :]:
         c.wait()
+    for k in range(HEADS):
+        block = slice(k * head, (k + 1) * head)
+        w_ref[parts, block] = out_in[:, block]
 
 
 def prepare(state, gain, shift, qkv, out_w):
@@ -99,8 +99,9 @@
         out_shape=[in_vmem((rows, width)), in_vmem((parts + 1, width, head))],
         scratch_shapes=[
             pltpu.VMEM((rows, width), jnp.bfloat16),
+            pltpu.VMEM(out_w.shape, jnp.bfloat16),
             pltpu.VMEM((2, *gain.shape), jnp.float32),
-            pltpu.SemaphoreType.DMA((7 + HEADS,)),
+            pltpu.SemaphoreType.DMA((8,)),
         ],
         name="prepare",
         compiler_params=pltpu.CompilerParams(vmem_limit_bytes=6 * MIB),
@@ -223,7 +224,8 @@
             part = lax.div(entry, per_dev)
             step = lax.rem(part - dom + (doms + 2), doms) - 2
             turned = jnp.where(par == 0, step, -step)
-            slot = jnp.where(turned >= 0, turned, turned + 5)
+            close = jnp.where(turned < 0, 4, turned)
+            slot = jnp.where(step == 2, 2, jnp.where(step == -2, 3, close))
             where.append(slot * per_dev + lax.rem(entry, per_dev))
         at = slice(b * NODE_BLK, (b + 1) * NODE_BLK)
         for pair in range(HEADS // 2):
@@ -385,11 +387,8 @@
     def swap(v):
         return hop(v, [(i ^ 1, i) for i in range(doms)])
 
-    def near(v):
-        return hop(v, [((i + 2 * sign(i)) % doms, i) for i in range(doms)])
-
-    def far(v):
-        return hop(v, [((i - 2 * sign(i)) % doms, i) for i in range(doms)])
+    def shifted(v, by):
+        return hop(v, [(i, (i + by) % doms) for i in range(doms)])
 
     def ring(v):
         pairs = [
@@ -410,7 +409,7 @@
     own, w0 = prepare(state, norm_gain, norm_shift, qkv, out_weight)
     w1 = ring(w0)
     partner = swap(own)
-    near_rows, far_rows = near(own), far(own)
+    before, beyond = shifted(own, 2), shifted(own, -2)
     u1 = ring(after(up_weight, own))
 
     w1 = after(w1, partner)
@@ -419,18 +418,16 @@
     w1_half = lax.dynamic_slice_in_dim(w1, par * mid, mid, 1)
     w3m = ring(w1_half)
     w3t = swap(w3m)
-    d1 = ring(after(down_weight, w3m))
+    d1 = ring(after(down_weight, w3t))
 
     own_late, u1 = lax.optimization_barrier((own, u1))
     kv, query, wkv, wo = kv_first(own_late, partner, (w0, w1, w2, w3m, w3t), 5)
-    relayed = one_to_relay(u1, d1)
-    near_rows, far_rows, query, relayed = lax.optimization_barrier(
-        (near_rows, far_rows, query, relayed)
-    )
+    before, beyond, query = lax.optimization_barrier((before, beyond, query))
+    relay = swap(one_to_relay(beyond, before))
+    kv = kv_second(beyond, before, wkv, kv)
+    u2, d2 = swap(u1), swap(d1)
+    relayed, kv = lax.optimization_barrier((one_to_relay(u1, d1), kv))
     last = ring(relayed)
-    relay = swap(near_rows)
-    kv = kv_second(near_rows, far_rows, wkv, kv)
-    u2, d2 = swap(u1), swap(d1)
 
     heads = attend(neighbours, counts, relay, query, wkv, kv, per_dev, doms)
     last, heads = lax.optimization_barrier((last, heads))

time: 64.8 us -> 67.2 us (1.037)
  waiting for transfers between devices: 16.9 us -> 22.5 us
  starting transfers between devices: 27 us -> 23.5 us
    ppermute x9, starting transfers between devices: 19.1 us -> 15.6 us  [hop(): return lax.ppermute(v, 'dom', pairs)]
    ppermute x5, waiting for transfers between devices: 6.38 us -> 9.53 us  [ring(): return lax.ppermute(v, ('dom', 'tp'), pairs)]
    ppermute x1, waiting for transfers between devices: 1.14 us -> 2.8 us  [up(): return lax.ppermute(v, 'tp', [(i, (i + 1) % tps) for i in range(tps)])]
    ppermute x9, waiting for transfers between devices: 3.27 us -> 4.9 us  [hop(): return lax.ppermute(v, 'dom', pairs)]
    ppermute x1, waiting for transfers between devices: 1.53 us -> 0.28 us  [down(): return lax.ppermute(v, 'tp', [((i + 1) % tps, i) for i in range(tps)])]
    ppermute x1, starting transfers between devices: 1.97 us -> 0.79 us  [down(): return lax.ppermute(v, 'tp', [((i + 1) % tps, i) for i in range(tps)])]
    ppermute x1, starting transfers between devices: 0.01 us -> 0.68 us  [up(): return lax.ppermute(v, 'tp', [(i, (i + 1) % tps) for i in range(tps)])]
where the time goes in v8:
time: 67.2 us; the launch traced here: 67 us
  starting transfers between devices  23.5 us (35%)
  waiting for transfers between devices  22.5 us (33%)
  Pallas kernels  20.8 us (31%)
    ppermute x9, starting transfers between devices, hop(): return lax.ppermute(v, 'dom', pairs)  15.6 us
    ppermute x5, waiting for transfers between devices, ring(): return lax.ppermute(v, ('dom', 'tp'), pairs)  9.53 us
    ppermute x5, starting transfers between devices, ring(): return lax.ppermute(v, ('dom', 'tp'), pairs)  6.08 us
    pallas_call x1, Pallas kernels, attend(): pl.pallas_call(functools.partial(attend_kernel, doms=doms, per_dev=per_de...  5.44 us
    ppermute x1, waiting for transfers between devices, across(): return lax.ppermute(v, 'tp', [(i, (i + 2) % tps) for i in range(tps)])  4.95 us
    ppermute x9, waiting for transfers between devices, hop(): return lax.ppermute(v, 'dom', pairs)  4.9 us
    pallas_call x1, Pallas kernels, kv_first(): pl.pallas_call(kv_first_kernel, in_specs=[VMEM] * (2 + len(weights)), out...  4.45 us
    pallas_call x1, Pallas kernels, mlp_first(): pl.pallas_call(mlp_first_kernel, in_specs=[VMEM] * (4 + len(weights)) + [...  3.49 us
  transfers between devices with their start and end apart: 17, of which 7 were waited for; matrix products, arithmetic and copies ran while one was open for 0% of the time, Pallas kernels for 24%

profile of v8, /device:TPU:1, one launch (start us, length us, event | category | flops | bytes accessed | tf_op | source)
XLA Modules:
  0.0 67.0 jit_solution(4243681319127647577)
XLA Ops:
  0.0 3.1 %prepare.1 = (bf16[1024,512]{1,0:T(8,128)(2,1)}, bf16[4,512,128]{2,1,0:T(8,128)(2,1)}) custom-call(bf16[2,1024,512]{2,1,0:T(8,128)(2,1)} %state_ref.3, f32[2,2,512]{2,1,0:T(2,128)} %gain_ref.3, f32[2,2,512]{2,1,0:T(2,128)} %shift_ref.3, bf16[3,512,128]{2,1,0:T(8,128)(2,1)} %bitcast.2, bf16[128,512]{1,0:T(8,128)(2,1)} %out_ref.1), custom_call_target="tpu_custom_call" | custom-call | tf_op jit(solution)/shard_map/prepare/pallas_call | solution.py:95
  3.2 3.3 %collective-permute-start.2 = (bf16[1024,512]{1,0:T(8,128)(2,1)}, bf16[1024,512]{1,0:T(8,128)(2,1)}, u32[]{:S(2)}, u32[]{:S(2)}) collective-permute-start(bf16[1024,512]{1,0:T(8,128)(2,1)} %get-tuple-element.36.xa), channel_id=1, source_target_pairs={{4,0},{0,4},{12,8},{8,12},{20,16},{16,20},{28,24},{24,28},{36,32},... | collective-permute-start | bytes 3145736 | tf_op jit(solution)/shard_map/ppermute | solution.py:382
  6.5 1.0 %collective-permute-start.1 = (bf16[4,512,128]{2,1,0:T(8,128)(2,1)}, bf16[4,512,128]{2,1,0:T(8,128)(2,1)S(1)}, u32[]{:S(2)}, u32[]{:S(2)}) collective-permute-start(bf16[4,512,128]{2,1,0:T(8,128)(2,1)} %get-tuple-element.33.w0), channel_id=1, source_target_pairs={{3,0},{0,1},{1,2},{2,3},{5,4},{6,5},{7,6},{4,7},{11,8},{8,9},{9,10... | collective-permute-start | bytes 1572872 | tf_op jit(solution)/shard_map/ppermute | solution.py:397
  7.5 1.2 %collective-permute-start.6 = (bf16[1024,512]{1,0:T(8,128)(2,1)}, bf16[1024,512]{1,0:T(8,128)(2,1)S(1)}, u32[]{:S(2)}, u32[]{:S(2)}) collective-permute-start(bf16[1024,512]{1,0:T(8,128)(2,1)} %get-tuple-element.36.xa), channel_id=1, source_target_pairs={{0,8},{4,12},{8,16},{12,20},{16,24},{20,28},{24,32},{28,36},{32,40... | collective-permute-start | bytes 3145736 | tf_op jit(solution)/shard_map/ppermute | solution.py:382
  8.7 6.6 %collective-permute-start.7 = (bf16[1024,512]{1,0:T(8,128)(2,1)}, bf16[1024,512]{1,0:T(8,128)(2,1)S(1)}, u32[]{:S(2)}, u32[]{:S(2)}) collective-permute-start(bf16[1024,512]{1,0:T(8,128)(2,1)} %get-tuple-element.36.xa), channel_id=1, source_target_pairs={{0,248},{4,252},{8,0},{12,4},{16,8},{20,12},{24,16},{28,20},{32,24... | collective-permute-start | bytes 3145736 | tf_op jit(solution)/shard_map/ppermute | solution.py:382
  15.8 1.6 %collective-permute-start.3 = (bf16[4,256,128]{2,1,0:T(8,128)(2,1)S(1)}, bf16[4,256,128]{2,1,0:T(8,128)(2,1)S(1)}, u32[]{:S(2)}, u32[]{:S(2)}) collective-permute-start(bf16[4,256,128]{2,1,0:T(8,128)(2,1)S(1)} %constant_dynamic-slice_fusion), channel_id=1, source_target_pairs={{3,0},{0,1},{1,2},{2,3},{5,4},{6,5},{7,6},{4,7},{11,8},{8,9},{9,10... | collective-permute-start | bytes 786440 | tf_op jit(solution)/shard_map/ppermute | solution.py:397
  17.4 9.2 %collective-permute-done.3.w3m = bf16[4,256,128]{2,1,0:T(8,128)(2,1)S(1)} collective-permute-done((bf16[4,256,128]{2,1,0:T(8,128)(2,1)S(1)}, bf16[4,256,128]{2,1,0:T(8,128)(2,1)S(1)}, u32[]{:S(2)}, u32[]{:S(2)}) %collective-permute-start.3) | collective-permute-done | bytes 262176 | tf_op jit(solution)/shard_map/ppermute | solution.py:397
  26.6 1.3 %collective-permute-start.4 = (bf16[4,256,128]{2,1,0:T(8,128)(2,1)S(1)}, bf16[4,256,128]{2,1,0:T(8,128)(2,1)S(1)}, u32[]{:S(2)}, u32[]{:S(2)}) collective-permute-start(bf16[4,256,128]{2,1,0:T(8,128)(2,1)S(1)} %collective-permute-done.3.w3m), channel_id=1, source_target_pairs={{4,0},{0,4},{12,8},{8,12},{20,16},{16,20},{28,24},{24,28},{36,32},... | collective-permute-start | bytes 786440 | tf_op jit(solution)/shard_map/ppermute | solution.py:382
  27.9 1.2 %collective-permute-done.4.w3t = bf16[4,256,128]{2,1,0:T(8,128)(2,1)S(1)} collective-permute-done((bf16[4,256,128]{2,1,0:T(8,128)(2,1)S(1)}, bf16[4,256,128]{2,1,0:T(8,128)(2,1)S(1)}, u32[]{:S(2)}, u32[]{:S(2)}) %collective-permute-start.4) | collective-permute-done | bytes 262176 | tf_op jit(solution)/shard_map/ppermute | solution.py:382
  29.0 0.8 %collective-permute-start.5 = (bf16[512,512]{1,0:T(8,128)(2,1)}, bf16[512,512]{1,0:T(8,128)(2,1)S(1)}, u32[]{:S(2)}, u32[]{:S(2)}) collective-permute-start(bf16[512,512]{1,0:T(8,128)(2,1)} %d0.1), channel_id=1, source_target_pairs={{3,0},{0,1},{1,2},{2,3},{5,4},{6,5},{7,6},{4,7},{11,8},{8,9},{9,10... | collective-permute-start | bytes 1572872 | tf_op jit(solution)/shard_map/ppermute | solution.py:397
  29.8 4.5 %kv_first.1 = (bf16[40,128,1024]{2,1,0:T(8,128)(2,1)S(1)}, bf16[512,512]{1,0:T(8,128)(2,1)S(1)}, bf16[512,1024]{1,0:T(8,128)(2,1)S(1)}, bf16[512,512]{1,0:T(8,128)(2,1)S(1)}) custom-call(bf16[1024,512]{1,0:T(8,128)(2,1)} %get-tuple-element.36.xa, bf16[1024,512]{1,0:T(8,128)(2,1)} %collective-permute-done.2.xb, bf16[4,512,128]{2,1,0:T(8,128)(2,1)} %get-tuple-element.33.w0, ...), custom_call_target="tpu_custom_call" | custom-call | tf_op jit(solution)/shard_map/kv_first/pallas_call | solution.py:173
  34.3 3.7 %collective-permute-done.6.xb.b_ref = bf16[1024,512]{1,0:T(8,128)(2,1)S(1)} collective-permute-done((bf16[1024,512]{1,0:T(8,128)(2,1)}, bf16[1024,512]{1,0:T(8,128)(2,1)S(1)}, u32[]{:S(2)}, u32[]{:S(2)}) %collective-permute-start.6) | collective-permute-done | bytes 1048608 | tf_op jit(solution)/shard_map/ppermute | solution.py:382
  38.2 2.3 %kv_second.1.kv_in = bf16[40,128,1024]{2,1,0:T(8,128)(2,1)S(1)} custom-call(bf16[1024,512]{1,0:T(8,128)(2,1)S(1)} %collective-permute-done.7.xa.a_ref, bf16[1024,512]{1,0:T(8,128)(2,1)S(1)} %collective-permute-done.6.xb.b_ref, bf16[512,1024]{1,0:T(8,128)(2,1)S(1)} %get-tuple-element.40.wkv_ref, ...), custom_call_target="tpu_custom_call", output_to_operand_aliasing={{}: (3, {})} | custom-call | tf_op jit(solution)/shard_map/kv_second/pallas_call | solution.py:197
  40.7 2.3 %collective-permute-start.9 = (bf16[512,512]{1,0:T(8,128)(2,1)S(1)}, bf16[512,512]{1,0:T(8,128)(2,1)S(1)}, u32[]{:S(2)}, u32[]{:S(2)}) collective-permute-start(bf16[512,512]{1,0:T(8,128)(2,1)S(1)} %one_to_relay.2), channel_id=1, source_target_pairs={{3,0},{0,1},{1,2},{2,3},{5,4},{6,5},{7,6},{4,7},{11,8},{8,9},{9,10... | collective-permute-start | bytes 1572872 | tf_op jit(solution)/shard_map/ppermute | solution.py:397
  42.9 0.5 collective-permute-start.12
  43.5 5.4 %attend.1 = (bf16[512,512]{1,0:T(8,128)(2,1)S(1)}, bf16[40,128,1024]{2,1,0:T(8,128)(2,1)S(1)}) custom-call(s32[8,8]{1,0:T(8,128)S(1)} %copy-done.4, s32[8]{0:T(128)S(1)} %copy-done.5, bf16[1024,512]{1,0:T(8,128)(2,1)S(1)} %collective-permute-done.10.relay_ref, bf16[512,512]{1,0:T(8,128)(2,1)S(1)} %get-tuple-element.43.q_ref, ...), custom_call_target="tpu_custom_call", output_to_operand_aliasing={{1}: (5, {})} | custom-call | tf_op jit(solution)/shard_map/attend/pallas_call | solution.py:260
  49.3 2.5 %collective-permute-start.13 = (bf16[512,512]{1,0:T(8,128)(2,1)S(1)}, bf16[512,512]{1,0:T(8,128)(2,1)S(1)}, u32[]{:S(2)}, u32[]{:S(2)}) collective-permute-start(bf16[512,512]{1,0:T(8,128)(2,1)S(1)} %collective-permute-done.9.mine), channel_id=1, source_target_pairs={{4,0},{0,4},{12,8},{8,12},{20,16},{16,20},{28,24},{24,28},{36,32},... | collective-permute-start | bytes 1572872 | tf_op jit(solution)/shard_map/ppermute | solution.py:382
  51.8 3.5 %mlp_first.1 = (f32[512,512]{1,0:T(8,128)S(1)}, bf16[512,512]{1,0:T(8,128)(2,1)S(1)}) custom-call(bf16[512,512]{1,0:T(8,128)(2,1)S(1)} %get-tuple-element.46.heads_ref, f32[2,2,512]{2,1,0:T(2,128)S(1)} %copy-done.2, f32[2,2,512]{2,1,0:T(2,128)S(1)} %copy-done.3, bf16[512,512]{1,0:T(8,128)(2,1)S(1)} %get-tuple-element.47.wo_ref, ...), custom_call_target="tpu_custom_call" | custom-call | tf_op jit(solution)/shard_map/mlp_first/pallas_call | solution.py:297
  55.4 1.0 %mlp_second.1 = (bf16[512,128]{1,0:T(8,128)(2,1)S(1)}, bf16[512,128]{1,0:T(8,128)(2,1)S(1)}, bf16[512,128]{1,0:T(8,128)(2,1)S(1)}, bf16[512,128]{1,0:T(8,128)(2,1)S(1)}) custom-call(f32[512,512]{1,0:T(8,128)S(1)} %get-tuple-element.48.resid_ref, bf16[512,512]{1,0:T(8,128)(2,1)S(1)} %get-tuple-element.49.normed_ref, ...), custom_call_target="tpu_custom_call" | custom-call | tf_op jit(solution)/shard_map/mlp_second/pallas_call | solution.py:334
  56.7 0.8 %collective-permute-start.15 = (bf16[512,128]{1,0:T(8,128)(2,1)S(1)}, bf16[512,128]{1,0:T(8,128)(2,1)S(1)}, u32[]{:S(2)}, u32[]{:S(2)}) collective-permute-start(bf16[512,128]{1,0:T(8,128)(2,1)S(1)} %get-tuple-element.53), channel_id=1, source_target_pairs={{1,0},{2,1},{3,2},{0,3},{5,4},{6,5},{7,6},{4,7},{9,8},{10,9},{11,1... | collective-permute-start | bytes 393224 | tf_op jit(solution)/shard_map/ppermute | solution.py:403
  57.5 0.7 %collective-permute-start.16 = (bf16[512,128]{1,0:T(8,128)(2,1)S(1)}, bf16[512,128]{1,0:T(8,128)(2,1)S(1)}, u32[]{:S(2)}, u32[]{:S(2)}) collective-permute-start(bf16[512,128]{1,0:T(8,128)(2,1)S(1)} %get-tuple-element.54), channel_id=1, source_target_pairs={{0,1},{1,2},{2,3},{3,0},{4,5},{5,6},{6,7},{7,4},{8,9},{9,10},{10,1... | collective-permute-start | bytes 393224 | tf_op jit(solution)/shard_map/ppermute | solution.py:400
  58.2 4.9 %collective-permute-done.14.across = bf16[512,128]{1,0:T(8,128)(2,1)S(1)} collective-permute-done((bf16[512,128]{1,0:T(8,128)(2,1)S(1)}, bf16[512,128]{1,0:T(8,128)(2,1)S(1)}, u32[]{:S(2)}, u32[]{:S(2)}) %collective-permute-start.14) | collective-permute-done | bytes 131104 | tf_op jit(solution)/shard_map/ppermute | solution.py:406
  63.4 2.8 %collective-permute-done.16.before = bf16[512,128]{1,0:T(8,128)(2,1)S(1)} collective-permute-done((bf16[512,128]{1,0:T(8,128)(2,1)S(1)}, bf16[512,128]{1,0:T(8,128)(2,1)S(1)}, u32[]{:S(2)}, u32[]{:S(2)}) %collective-permute-start.16) | collective-permute-done | bytes 131104 | tf_op jit(solution)/shard_map/ppermute | solution.py:400
  66.2 0.8 %place_rows.1 = bf16[4,512,128]{2,1,0:T(8,128)(2,1)} custom-call(bf16[512,128]{1,0:T(8,128)(2,1)S(1)} %get-tuple-element.51.own, bf16[512,128]{1,0:T(8,128)(2,1)S(1)} %collective-permute-done.14.across, bf16[512,128]{1,0:T(8,128)(2,1)S(1)} %collective-permute-done.15.after, bf16[512,128]{1,0:T(8,128)(2,1)S(1)} %collective-permute-done.16.before), custom_call_target="tpu_custom_call" | custom-call | tf_op jit(solution)/shard_map/place_rows/pallas_call | solution.py:357
  (32 shorter events, 1.8 us)
Async XLA Ops:
  3.2 12.6 %collective-permute-start.2 = (bf16[1024,512]{1,0:T(8,128)(2,1)}, bf16[1024,512]{1,0:T(8,128)(2,1)}, u32[]{:S(2)}, u32[]{:S(2)}) collective-permute-start(bf16[1024,512]{1,0:T(8,128)(2,1)} %get-tuple-element.36.xa), channel_id=1, source_target_pairs={{4,0},{0,4},{12,8},{8,12},{20,16},{16,20},{28,24},{24,28},{36,32},... | collective-permute-start | bytes 3145736 | tf_op jit(solution)/shard_map/ppermute | solution.py:382
  6.5 9.2 %collective-permute-start.1 = (bf16[4,512,128]{2,1,0:T(8,128)(2,1)}, bf16[4,512,128]{2,1,0:T(8,128)(2,1)S(1)}, u32[]{:S(2)}, u32[]{:S(2)}) collective-permute-start(bf16[4,512,128]{2,1,0:T(8,128)(2,1)} %get-tuple-element.33.w0), channel_id=1, source_target_pairs={{3,0},{0,1},{1,2},{2,3},{5,4},{6,5},{7,6},{4,7},{11,8},{8,9},{9,10... | collective-permute-start | bytes 1572872 | tf_op jit(solution)/shard_map/ppermute | solution.py:397
  7.5 30.5 %collective-permute-start.6 = (bf16[1024,512]{1,0:T(8,128)(2,1)}, bf16[1024,512]{1,0:T(8,128)(2,1)S(1)}, u32[]{:S(2)}, u32[]{:S(2)}) collective-permute-start(bf16[1024,512]{1,0:T(8,128)(2,1)} %get-tuple-element.36.xa), channel_id=1, source_target_pairs={{0,8},{4,12},{8,16},{12,20},{16,24},{20,28},{24,32},{28,36},{32,40... | collective-permute-start | bytes 3145736 | tf_op jit(solution)/shard_map/ppermute | solution.py:382
  8.7 29.3 %collective-permute-start.7 = (bf16[1024,512]{1,0:T(8,128)(2,1)}, bf16[1024,512]{1,0:T(8,128)(2,1)S(1)}, u32[]{:S(2)}, u32[]{:S(2)}) collective-permute-start(bf16[1024,512]{1,0:T(8,128)(2,1)} %get-tuple-element.36.xa), channel_id=1, source_target_pairs={{0,248},{4,252},{8,0},{12,4},{16,8},{20,12},{24,16},{28,20},{32,24... | collective-permute-start | bytes 3145736 | tf_op jit(solution)/shard_map/ppermute | solution.py:382
  15.3 12.6 %collective-permute-start = (bf16[512,512]{1,0:T(8,128)(2,1)}, bf16[512,512]{1,0:T(8,128)(2,1)S(1)}, u32[]{:S(2)}, u32[]{:S(2)}) collective-permute-start(bf16[512,512]{1,0:T(8,128)(2,1)} %u0.1), channel_id=1, source_target_pairs={{3,0},{0,1},{1,2},{2,3},{5,4},{6,5},{7,6},{4,7},{11,8},{8,9},{9,10... | collective-permute-start | bytes 1572872 | tf_op jit(solution)/shard_map/ppermute | solution.py:397
  15.8 10.9 %collective-permute-start.3 = (bf16[4,256,128]{2,1,0:T(8,128)(2,1)S(1)}, bf16[4,256,128]{2,1,0:T(8,128)(2,1)S(1)}, u32[]{:S(2)}, u32[]{:S(2)}) collective-permute-start(bf16[4,256,128]{2,1,0:T(8,128)(2,1)S(1)} %constant_dynamic-slice_fusion), channel_id=1, source_target_pairs={{3,0},{0,1},{1,2},{2,3},{5,4},{6,5},{7,6},{4,7},{11,8},{8,9},{9,10... | collective-permute-start | bytes 786440 | tf_op jit(solution)/shard_map/ppermute | solution.py:397
  17.3 12.5 %collective-permute-start.8 = (bf16[4,512,128]{2,1,0:T(8,128)(2,1)S(1)}, bf16[4,512,128]{2,1,0:T(8,128)(2,1)S(1)}, u32[]{:S(2)}, u32[]{:S(2)}) collective-permute-start(bf16[4,512,128]{2,1,0:T(8,128)(2,1)S(1)} %collective-permute-done.1.w1), channel_id=1, source_target_pairs={{4,0},{0,4},{12,8},{8,12},{20,16},{16,20},{28,24},{24,28},{36,32},... | collective-permute-start | bytes 1572872 | tf_op jit(solution)/shard_map/ppermute | solution.py:382
  26.6 2.4 %collective-permute-start.4 = (bf16[4,256,128]{2,1,0:T(8,128)(2,1)S(1)}, bf16[4,256,128]{2,1,0:T(8,128)(2,1)S(1)}, u32[]{:S(2)}, u32[]{:S(2)}) collective-permute-start(bf16[4,256,128]{2,1,0:T(8,128)(2,1)S(1)} %collective-permute-done.3.w3m), channel_id=1, source_target_pairs={{4,0},{0,4},{12,8},{8,12},{20,16},{16,20},{28,24},{24,28},{36,32},... | collective-permute-start | bytes 786440 | tf_op jit(solution)/shard_map/ppermute | solution.py:382
  29.0 11.6 %collective-permute-start.5 = (bf16[512,512]{1,0:T(8,128)(2,1)}, bf16[512,512]{1,0:T(8,128)(2,1)S(1)}, u32[]{:S(2)}, u32[]{:S(2)}) collective-permute-start(bf16[512,512]{1,0:T(8,128)(2,1)} %d0.1), channel_id=1, source_target_pairs={{3,0},{0,1},{1,2},{2,3},{5,4},{6,5},{7,6},{4,7},{11,8},{8,9},{9,10... | collective-permute-start | bytes 1572872 | tf_op jit(solution)/shard_map/ppermute | solution.py:397
  38.1 5.4 %collective-permute-start.10 = (bf16[1024,512]{1,0:T(8,128)(2,1)S(1)}, bf16[1024,512]{1,0:T(8,128)(2,1)S(1)}, u32[]{:S(2)}, u32[]{:S(2)}) collective-permute-start(bf16[1024,512]{1,0:T(8,128)(2,1)S(1)} %one_to_relay.3), channel_id=1, source_target_pairs={{4,0},{0,4},{12,8},{8,12},{20,16},{16,20},{28,24},{24,28},{36,32},... | collective-permute-start | bytes 3145736 | tf_op jit(solution)/shard_map/ppermute | solution.py:382
  38.2 5.3 %copy-start.4 = (s32[8,8]{1,0:T(8,128)S(1)}, s32[8,8]{1,0:T(8,128)}, u32[]{:S(2)}) copy-start(s32[8,8]{1,0:T(8,128)} %list_ref.1) | copy-start | bytes 772
  38.2 5.3 %copy-start.5 = (s32[8]{0:T(128)S(1)}, s32[8]{0:T(128)}, u32[]{:S(2)}) copy-start(s32[8]{0:T(128)} %count_ref.1) | copy-start | bytes 100
  40.6 11.3 %copy-start = (bf16[512,512]{1,0:T(8,128)(2,1)S(1)}, bf16[512,512]{1,0:T(8,128)(2,1)}, u32[]{:S(2)}) copy-start(bf16[512,512]{1,0:T(8,128)(2,1)} %u0.1) | copy-start | bytes 1572868
  40.6 11.2 %copy-start.1 = (bf16[512,512]{1,0:T(8,128)(2,1)S(1)}, bf16[512,512]{1,0:T(8,128)(2,1)}, u32[]{:S(2)}) copy-start(bf16[512,512]{1,0:T(8,128)(2,1)} %d0.1) | copy-start | bytes 1572868
  40.6 11.2 %copy-start.2 = (f32[2,2,512]{2,1,0:T(2,128)S(1)}, f32[2,2,512]{2,1,0:T(2,128)}, u32[]{:S(2)}) copy-start(f32[2,2,512]{2,1,0:T(2,128)} %gain_ref.3) | copy-start | bytes 24580
  40.6 11.2 %copy-start.3 = (f32[2,2,512]{2,1,0:T(2,128)S(1)}, f32[2,2,512]{2,1,0:T(2,128)}, u32[]{:S(2)}) copy-start(f32[2,2,512]{2,1,0:T(2,128)} %shift_ref.3) | copy-start | bytes 24580
  40.7 8.6 %collective-permute-start.9 = (bf16[512,512]{1,0:T(8,128)(2,1)S(1)}, bf16[512,512]{1,0:T(8,128)(2,1)S(1)}, u32[]{:S(2)}, u32[]{:S(2)}) collective-permute-start(bf16[512,512]{1,0:T(8,128)(2,1)S(1)} %one_to_relay.2), channel_id=1, source_target_pairs={{3,0},{0,1},{1,2},{2,3},{5,4},{6,5},{7,6},{4,7},{11,8},{8,9},{9,10... | collective-permute-start | bytes 1572872 | tf_op jit(solution)/shard_map/ppermute | solution.py:397
  42.9 8.9 %collective-permute-start.11 = (bf16[512,512]{1,0:T(8,128)(2,1)S(1)}, bf16[512,512]{1,0:T(8,128)(2,1)S(1)}, u32[]{:S(2)}, u32[]{:S(2)}) collective-permute-start(bf16[512,512]{1,0:T(8,128)(2,1)S(1)} %collective-permute-done.a_ref.u1), channel_id=1, source_target_pairs={{4,0},{0,4},{12,8},{8,12},{20,16},{16,20},{28,24},{24,28},{36,32},... | collective-permute-start | bytes 1572872 | tf_op jit(solution)/shard_map/ppermute | solution.py:382
  42.9 8.9 %collective-permute-start.12 = (bf16[512,512]{1,0:T(8,128)(2,1)S(1)}, bf16[512,512]{1,0:T(8,128)(2,1)S(1)}, u32[]{:S(2)}, u32[]{:S(2)}) collective-permute-start(bf16[512,512]{1,0:T(8,128)(2,1)S(1)} %collective-permute-done.5.b_ref.d1), channel_id=1, source_target_pairs={{4,0},{0,4},{12,8},{8,12},{20,16},{16,20},{28,24},{24,28},{36,32},... | collective-permute-start | bytes 1572872 | tf_op jit(solution)/shard_map/ppermute | solution.py:382
  49.3 6.1 %collective-permute-start.13 = (bf16[512,512]{1,0:T(8,128)(2,1)S(1)}, bf16[512,512]{1,0:T(8,128)(2,1)S(1)}, u32[]{:S(2)}, u32[]{:S(2)}) collective-permute-start(bf16[512,512]{1,0:T(8,128)(2,1)S(1)} %collective-permute-done.9.mine), channel_id=1, source_target_pairs={{4,0},{0,4},{12,8},{8,12},{20,16},{16,20},{28,24},{24,28},{36,32},... | collective-permute-start | bytes 1572872 | tf_op jit(solution)/shard_map/ppermute | solution.py:382
  56.4 6.7 %collective-permute-start.14 = (bf16[512,128]{1,0:T(8,128)(2,1)S(1)}, bf16[512,128]{1,0:T(8,128)(2,1)S(1)}, u32[]{:S(2)}, u32[]{:S(2)}) collective-permute-start(bf16[512,128]{1,0:T(8,128)(2,1)S(1)} %get-tuple-element.52), channel_id=1, source_target_pairs={{0,2},{1,3},{2,0},{3,1},{4,6},{5,7},{6,4},{7,5},{8,10},{9,11},{10,... | collective-permute-start | bytes 393224 | tf_op jit(solution)/shard_map/ppermute | solution.py:406
  56.7 6.7 %collective-permute-start.15 = (bf16[512,128]{1,0:T(8,128)(2,1)S(1)}, bf16[512,128]{1,0:T(8,128)(2,1)S(1)}, u32[]{:S(2)}, u32[]{:S(2)}) collective-permute-start(bf16[512,128]{1,0:T(8,128)(2,1)S(1)} %get-tuple-element.53), channel_id=1, source_target_pairs={{1,0},{2,1},{3,2},{0,3},{5,4},{6,5},{7,6},{4,7},{9,8},{10,9},{11,1... | collective-permute-start | bytes 393224 | tf_op jit(solution)/shard_map/ppermute | solution.py:403
  57.5 8.7 %collective-permute-start.16 = (bf16[512,128]{1,0:T(8,128)(2,1)S(1)}, bf16[512,128]{1,0:T(8,128)(2,1)S(1)}, u32[]{:S(2)}, u32[]{:S(2)}) collective-permute-start(bf16[512,128]{1,0:T(8,128)(2,1)S(1)} %get-tuple-element.54), channel_id=1, source_target_pairs={{0,1},{1,2},{2,3},{3,0},{4,5},{5,6},{6,7},{7,4},{8,9},{9,10},{10,1... | collective-permute-start | bytes 393224 | tf_op jit(solution)/shard_map/ppermute | solution.py:400

commit v9 on v7

--- a/solution.py
+++ b/solution.py
@@ -60,68 +60,52 @@
     return lax.div(rank, 2), lax.rem(rank, 2), lax.rem(dom, 2), rank, dom
 
 
-def norm_kernel(state_ref, gain_ref, shift_ref, o_ref, x_in, affine, sems):
+def prepare_kernel(
+    state_ref, gain_ref, shift_ref, qkv_ref, out_ref, o_ref, w_ref, x_in, out_in, affine, sems
+):
     sample = my_place()[0]
     s = pl.ds(sample, 1)
+    head = NODE_BLK
     chunks = 4
     step = x_in.shape[0] // chunks
+    parts = qkv_ref.shape[0]
     spans = [pl.ds(k * step, step) for k in range(chunks)]
     jobs = [(state_ref.at[sample, at], x_in.at[at]) for at in spans]
     jobs += [(gain_ref, affine.at[0]), (shift_ref, affine.at[1])]
+    jobs += [(qkv_ref, w_ref.at[pl.ds(0, parts)]), (out_ref, out_in)]
     copies = [pltpu.make_async_copy(a, b, sems.at[k]) for k, (a, b) in enumerate(jobs)]
-    for k in (0, chunks, chunks + 1, *range(1, chunks)):
+    for k in (0, chunks, chunks + 1, *range(1, chunks), *range(chunks + 2, len(jobs))):
         copies[k].start()
-    for c in copies[chunks:]:
+    for c in copies[chunks : chunks + 2]:
         c.wait()
     gain, shift = affine[0, 0, s], affine[1, 0, s]
     for c, at in zip(copies, spans):
         c.wait()
         o_ref[at] = bf(normalise(x_in[at].astype(jnp.float32), gain, shift))
-
-
-def normed_rows(state, gain, shift):
+    for c in copies[chunks + 2 :]:
+        c.wait()
+    for k in range(HEADS):
+        block = slice(k * head, (k + 1) * head)
+        w_ref[parts, block] = out_in[:, block]
+
+
+def prepare(state, gain, shift, qkv, out_w):
     _, rows, width = state.shape
-    return pl.pallas_call(
-        norm_kernel,
-        in_specs=[HBM] * 3,
-        out_specs=VMEM,
-        out_shape=in_vmem((rows, width)),
+    parts, _, head = qkv.shape
+    return pl.pallas_call(
+        prepare_kernel,
+        in_specs=[HBM] * 5,
+        out_specs=[VMEM] * 2,
+        out_shape=[in_vmem((rows, width)), in_vmem((parts + 1, width, head))],
         scratch_shapes=[
             pltpu.VMEM((rows, width), jnp.bfloat16),
+            pltpu.VMEM(out_w.shape, jnp.bfloat16),
             pltpu.VMEM((2, *gain.shape), jnp.float32),
-            pltpu.SemaphoreType.DMA((6,)),
+            pltpu.SemaphoreType.DMA((8,)),
         ],
-        name="norm_rows",
+        name="prepare",
         compiler_params=pltpu.CompilerParams(vmem_limit_bytes=6 * MIB),
-    )(*[kept_in_hbm(v) for v in (state, gain, shift)])
-
-
-def pack_kernel(qkv_ref, out_ref, w_ref, sems):
-    head = NODE_BLK
-    parts = qkv_ref.shape[0]
-    jobs = [(qkv_ref, w_ref.at[pl.ds(0, parts)])]
-    jobs += [
-        (out_ref.at[:, pl.ds(k * head, head)], w_ref.at[parts, pl.ds(k * head, head)])
-        for k in range(HEADS)
-    ]
-    copies = [pltpu.make_async_copy(a, b, sems.at[k]) for k, (a, b) in enumerate(jobs)]
-    for c in copies:
-        c.start()
-    for c in copies:
-        c.wait()
-
-
-def packed(qkv, out_w):
-    parts, width, head = qkv.shape
-    return pl.pallas_call(
-        pack_kernel,
-        in_specs=[HBM] * 2,
-        out_specs=VMEM,
-        out_shape=in_vmem((parts + 1, width, head)),
-        scratch_shapes=[pltpu.SemaphoreType.DMA((1 + HEADS,))],
-        name="pack_weights",
-        compiler_params=pltpu.CompilerParams(vmem_limit_bytes=4 * MIB),
-    )(kept_in_hbm(qkv), kept_in_hbm(out_w))
+    )(*[kept_in_hbm(v) for v in (state, gain, shift, qkv, out_w)])
 
 
 def write_kv(x_ref, wkv_ref, kv_ref, first):
@@ -251,12 +235,13 @@
     return 0.5 * v * (1.0 + jnp.tanh(0.5 * v))
 
 
-def mlp_first_kernel(
-    heads_ref, gain_ref, shift_ref, wo_ref, u0, d0, u1, d1, u2, d2, state_ref,
-    resid_ref, normed_ref,
-    rows_in, hidden_ref, sem,
+def mlp_kernel(
+    heads_ref, gain_ref, shift_ref, wo_ref, u0, d0, u1, d1, u2, d2, u3, d3, state_ref,
+    o0, o1, o2, o3,
+    resid_ref, normed_ref, rows_in, hidden_ref, sem,
 ):
-    sample, share, _, _, _ = my_place()
+    sample, share, _, rank, _ = my_place()
+    head = NODE_BLK
     rows, width = heads_ref.shape
     copy = pltpu.make_async_copy(state_ref.at[sample, aligned(share, rows)], rows_in, sem)
     copy.start()
@@ -265,49 +250,31 @@
     resid_ref[...] = rows_in[...].astype(jnp.float32) + mixed
     s = pl.ds(sample, 1)
     normed_ref[...] = bf(normalise(resid_ref[...], gain_ref[1, s], shift_ref[1, s]))
-    for k, u in enumerate((u0, u1, u2)):
+    for k, u in enumerate((u0, u1, u2, u3)):
         hidden_ref[:, k * width : (k + 1) * width] = bf(silu(matmul(normed_ref[...], u[...])))
-    downs = jnp.concatenate([d0[...], d1[...], d2[...]], axis=0)
+    downs = jnp.concatenate([d0[...], d1[...], d2[...], d3[...]], axis=0)
     resid_ref[...] += matmul(hidden_ref[...], downs)
-
-
-def mlp_first(heads, gain, shift, wo, weights, state):
+    for r, o_ref in enumerate((o0, o1, o2, o3)):
+        o_ref[...] = bf(resid_ref[:, aligned(lax.rem(rank + r, HEADS), head)])
+
+
+def mlp(heads, gain, shift, wo, weights, state):
     rows, width = heads.shape
     return pl.pallas_call(
-        mlp_first_kernel,
+        mlp_kernel,
         in_specs=[VMEM] * (4 + len(weights)) + [HBM],
-        out_specs=[VMEM] * 2,
-        out_shape=[in_vmem((rows, width), jnp.float32), in_vmem((rows, width))],
+        out_specs=[VMEM] * HEADS,
+        out_shape=[in_vmem((rows, width // HEADS))] * HEADS,
         scratch_shapes=[
+            pltpu.VMEM((rows, width), jnp.float32),
             pltpu.VMEM((rows, width), jnp.bfloat16),
-            pltpu.VMEM((rows, 3 * width), jnp.bfloat16),
+            pltpu.VMEM((rows, width), jnp.bfloat16),
+            pltpu.VMEM((rows, HEADS * width), jnp.bfloat16),
             pltpu.SemaphoreType.DMA,
         ],
-        name="mlp_first",
-        compiler_params=pltpu.CompilerParams(vmem_limit_bytes=12 * MIB),
+        name="mlp",
+        compiler_params=pltpu.CompilerParams(vmem_limit_bytes=14 * MIB),
     )(heads, gain, shift, wo, *weights, kept_in_hbm(state))
-
-
-def mlp_second_kernel(resid_ref, normed_ref, u_ref, d_ref, o0, o1, o2, o3, total_ref):
-    rank = my_place()[3]
-    head = NODE_BLK
-    hidden = bf(silu(matmul(normed_ref[...], u_ref[...])))
-    total_ref[...] = resid_ref[...] + matmul(hidden, d_ref[...])
-    for r, o_ref in enumerate((o0, o1, o2, o3)):
-        o_ref[...] = bf(total_ref[:, aligned(lax.rem(rank + r, HEADS), head)])
-
-
-def mlp_second(resid, normed, u, d):
-    rows, width = normed.shape
-    return pl.pallas_call(
-        mlp_second_kernel,
-        in_specs=[VMEM] * 4,
-        out_specs=[VMEM] * HEADS,
-        out_shape=[in_vmem((rows, width // HEADS))] * HEADS,
-        scratch_shapes=[pltpu.VMEM((rows, width), jnp.float32)],
-        name="mlp_second",
-        compiler_params=pltpu.CompilerParams(vmem_limit_bytes=12 * MIB),
-    )(resid, normed, u, d)
 
 
 def place_kernel(own, across, after, before, o_ref):
@@ -339,6 +306,7 @@
     per_dev = row_count // NODE_BLK
     doms = lax.axis_size("dom")
     tps = lax.axis_size("tp")
+
     def hop(v, pairs):
         return lax.ppermute(v, "dom", pairs)
 
@@ -369,36 +337,30 @@
     def across(v):
         return lax.ppermute(v, "tp", [(i, (i + 2) % tps) for i in range(tps)])
 
-    own = normed_rows(state, norm_gain, norm_shift)
+    qkv = jnp.transpose(qkv_weight, (1, 0, 2))
+    own, w0 = prepare(state, norm_gain, norm_shift, qkv, out_weight)
+    w1 = ring(w0)
     partner = swap(own)
     near_rows, far_rows = near(own), far(own)
-
-    qkv, own = lax.optimization_barrier((qkv_weight, own))
-    w0 = packed(jnp.transpose(qkv, (1, 0, 2)), out_weight)
-
-    def gather(own_w, own_up):
-        first = ring(own_w)
-        return first, swap(first), ring(first), ring(own_up)
-
-    def never(own_w, own_up):
-        return own_w, own_w, own_w, own_up
-
-    w1, w2, w3, u1 = lax.cond(lax.axis_index("tp") >= 0, gather, never, w0, up_weight)
+    u1 = ring(after(up_weight, own))
+
+    w1 = after(w1, partner)
+    w2, w3 = swap(w1), ring(w1)
     d1 = ring(after(down_weight, w1))
 
-    kv, query, wkv, wo = kv_first(own, partner, (w0, w1, w2, w3), 5)
-    u1, query = lax.optimization_barrier((u1, query))
-    u3 = ring(u1)
-    near_rows, far_rows, query = lax.optimization_barrier((near_rows, far_rows, query))
+    own_late, u1 = lax.optimization_barrier((own, u1))
+    kv, query, wkv, wo = kv_first(own_late, partner, (w0, w1, w2, w3), 5)
+    u3, d3 = ring(u1), ring(d1)
+    near_rows, far_rows, query, u1, d1 = lax.optimization_barrier(
+        (near_rows, far_rows, query, u1, d1)
+    )
     relay = swap(near_rows)
     kv = kv_second(near_rows, far_rows, wkv, kv)
-    u1, d1, kv = lax.optimization_barrier((u1, d1, kv))
-    u2, d2, d3 = swap(u1), swap(d1), ring(d1)
+    u2, d2 = swap(u1), swap(d1)
 
     heads = attend(neighbours, counts, relay, query, wkv, kv, per_dev, doms)
-    weights = (up_weight, down_weight, u1, d1, u2, d2)
-    resid, normed = mlp_first(heads, norm_gain, norm_shift, wo, weights, state)
-    mine = mlp_second(resid, normed, u3, d3)
+    weights = (up_weight, down_weight, u1, d1, u2, d2, u3, d3)
+    mine = mlp(heads, norm_gain, norm_shift, wo, weights, state)
     out = placed_rows((mine[0], across(mine[2]), down(mine[3]), up(mine[1])))
     return out.reshape(samples, row_count, width // tps)
 

time: 81.4 us -> 68.4 us (0.84)
  starting transfers between devices: 32.6 us -> 24.3 us
  Pallas kernels: 21.6 us -> 17.6 us
    ppermute x7, starting transfers between devices: 19.9 us -> 15 us  [hop(): return lax.ppermute(v, 'dom', pairs)]
    ppermute x6, waiting for transfers between devices: 14.3 us -> 9.7 us  [ring(): return lax.ppermute(v, ('dom', 'tp'), pairs)]
    ppermute x6, starting transfers between devices: 9.37 us -> 5.77 us  [ring(): return lax.ppermute(v, ('dom', 'tp'), pairs)]
    ppermute x7, waiting for transfers between devices: 5.99 us -> 9.45 us  [hop(): return lax.ppermute(v, 'dom', pairs)]
    ppermute x1, waiting for transfers between devices: 0.07 us -> 2.54 us  [up(): return lax.ppermute(v, 'tp', [(i, (i + 1) % tps) for i in range(tps)])]
    pallas_call x4 -> x2, Pallas kernels: 8.49 us -> 6.26 us  [the longest x1 4.22 us: mlp(): pl.pallas_call(mlp_kernel, in_specs=[VMEM] * (4 + len(weights)) + [HBM],...]
    ppermute x1, starting transfers between devices: 0.84 us -> 2.83 us  [down(): return lax.ppermute(v, 'tp', [((i + 1) % tps, i) for i in range(tps)])]
    pallas_call x1, Pallas kernels: 4.48 us -> 2.78 us  [kv_first(): pl.pallas_call(kv_first_kernel, in_specs=[VMEM] * (2 + len(weights)), out...]
  transfers between devices with their start and end apart: 16 -> 16, of which waited for: 8 -> 8; matrix products, arithmetic and copies ran while one was open for 0% -> 0% of each run, Pallas kernels for 22% -> 15%
where the time goes in v9:
time: 68.4 us; the launch traced here: 68.2 us
  waiting for transfers between devices  26.1 us (38%)
  starting transfers between devices  24.3 us (36%)
  Pallas kernels  17.6 us (26%)
    ppermute x7, starting transfers between devices, hop(): return lax.ppermute(v, 'dom', pairs)  15 us
    ppermute x6, waiting for transfers between devices, ring(): return lax.ppermute(v, ('dom', 'tp'), pairs)  9.7 us
    ppermute x7, waiting for transfers between devices, hop(): return lax.ppermute(v, 'dom', pairs)  9.45 us
    ppermute x6, starting transfers between devices, ring(): return lax.ppermute(v, ('dom', 'tp'), pairs)  5.77 us
    pallas_call x1, Pallas kernels, attend(): pl.pallas_call(functools.partial(attend_kernel, doms=doms, per_dev=per_de...  5.43 us
    pallas_call x1, Pallas kernels, mlp(): pl.pallas_call(mlp_kernel, in_specs=[VMEM] * (4 + len(weights)) + [HBM],...  4.22 us
    ppermute x1, starting transfers between devices, down(): return lax.ppermute(v, 'tp', [((i + 1) % tps, i) for i in range(tps)])  2.83 us
    pallas_call x1, Pallas kernels, kv_first(): pl.pallas_call(kv_first_kernel, in_specs=[VMEM] * (2 + len(weights)), out...  2.78 us
  transfers between devices with their start and end apart: 16, of which 8 were waited for; matrix products, arithmetic and copies ran while one was open for 0% of the time, Pallas kernels for 15%

profile of v9, /device:TPU:1, one launch (start us, length us, event | category | flops | bytes accessed | tf_op | source)
XLA Modules:
  0.0 68.2 jit_solution(3591512293078953181)
XLA Ops:
  0.0 2.0 %prepare.1 = (bf16[1024,512]{1,0:T(8,128)(2,1)S(1)}, bf16[4,512,128]{2,1,0:T(8,128)(2,1)S(1)}) custom-call(bf16[2,1024,512]{2,1,0:T(8,128)(2,1)} %state_ref.3, f32[2,2,512]{2,1,0:T(2,128)} %gain_ref.3, f32[2,2,512]{2,1,0:T(2,128)} %shift_ref.3, bf16[3,512,128]{2,1,0:T(8,128)(2,1)} %bitcast.2, bf16[128,512]{1,0:T(8,128)(2,1)} %out_ref.1), custom_call_target="tpu_custom_call" | custom-call | tf_op jit(solution)/shard_map/prepare/pallas_call | solution.py:95
  2.0 3.3 %collective-permute-start.3 = (bf16[1024,512]{1,0:T(8,128)(2,1)S(1)}, bf16[1024,512]{1,0:T(8,128)(2,1)S(1)}, u32[]{:S(2)}, u32[]{:S(2)}) collective-permute-start(bf16[1024,512]{1,0:T(8,128)(2,1)S(1)} %get-tuple-element.28.xa), channel_id=1, source_target_pairs={{4,0},{0,4},{12,8},{8,12},{20,16},{16,20},{28,24},{24,28},{36,32},... | collective-permute-start | bytes 3145736 | tf_op jit(solution)/shard_map/ppermute | solution.py:311
  5.4 1.0 %collective-permute-start.4 = (bf16[4,512,128]{2,1,0:T(8,128)(2,1)S(1)}, bf16[4,512,128]{2,1,0:T(8,128)(2,1)S(1)}, u32[]{:S(2)}, u32[]{:S(2)}) collective-permute-start(bf16[4,512,128]{2,1,0:T(8,128)(2,1)S(1)} %get-tuple-element.29.w0), channel_id=1, source_target_pairs={{3,0},{0,1},{1,2},{2,3},{5,4},{6,5},{7,6},{4,7},{11,8},{8,9},{9,10... | collective-permute-start | bytes 1572872 | tf_op jit(solution)/shard_map/ppermute | solution.py:329
  6.8 1.2 %collective-permute-start = (bf16[1024,512]{1,0:T(8,128)(2,1)S(1)}, bf16[1024,512]{1,0:T(8,128)(2,1)S(1)}, u32[]{:S(2)}, u32[]{:S(2)}) collective-permute-start(bf16[1024,512]{1,0:T(8,128)(2,1)S(1)} %get-tuple-element.28.xa), channel_id=1, source_target_pairs={{8,0},{252,4},{16,8},{4,12},{24,16},{12,20},{32,24},{20,28},{40,32... | collective-permute-start | bytes 3145736 | tf_op jit(solution)/shard_map/ppermute | solution.py:311
  8.0 6.6 %collective-permute-start.1 = (bf16[1024,512]{1,0:T(8,128)(2,1)S(1)}, bf16[1024,512]{1,0:T(8,128)(2,1)S(1)}, u32[]{:S(2)}, u32[]{:S(2)}) collective-permute-start(bf16[1024,512]{1,0:T(8,128)(2,1)S(1)} %get-tuple-element.28.xa), channel_id=1, source_target_pairs={{248,0},{12,4},{0,8},{20,12},{8,16},{28,20},{16,24},{36,28},{24,32... | collective-permute-start | bytes 3145736 | tf_op jit(solution)/shard_map/ppermute | solution.py:311
  14.6 1.2 %collective-permute-start.5 = (bf16[4,512,128]{2,1,0:T(8,128)(2,1)S(1)}, bf16[4,512,128]{2,1,0:T(8,128)(2,1)S(1)}, u32[]{:S(2)}, u32[]{:S(2)}) collective-permute-start(bf16[4,512,128]{2,1,0:T(8,128)(2,1)S(1)} %collective-permute-done.4.w1), channel_id=1, source_target_pairs={{4,0},{0,4},{12,8},{8,12},{20,16},{16,20},{28,24},{24,28},{36,32},... | collective-permute-start | bytes 1572872 | tf_op jit(solution)/shard_map/ppermute | solution.py:311
  16.4 2.9 %collective-permute-done.2.u1 = bf16[512,512]{1,0:T(8,128)(2,1)S(1)} collective-permute-done((bf16[512,512]{1,0:T(8,128)(2,1)}, bf16[512,512]{1,0:T(8,128)(2,1)S(1)}, u32[]{:S(2)}, u32[]{:S(2)}) %collective-permute-start.2) | collective-permute-done | bytes 524320 | tf_op jit(solution)/shard_map/ppermute | solution.py:329
  19.3 1.9 %collective-permute-start.7 = (bf16[512,512]{1,0:T(8,128)(2,1)}, bf16[512,512]{1,0:T(8,128)(2,1)S(1)}, u32[]{:S(2)}, u32[]{:S(2)}) collective-permute-start(bf16[512,512]{1,0:T(8,128)(2,1)} %d0.1), channel_id=1, source_target_pairs={{3,0},{0,1},{1,2},{2,3},{5,4},{6,5},{7,6},{4,7},{11,8},{8,9},{9,10... | collective-permute-start | bytes 1572872 | tf_op jit(solution)/shard_map/ppermute | solution.py:329
  21.2 3.7 %collective-permute-done.6.w3 = bf16[4,512,128]{2,1,0:T(8,128)(2,1)S(1)} collective-permute-done((bf16[4,512,128]{2,1,0:T(8,128)(2,1)S(1)}, bf16[4,512,128]{2,1,0:T(8,128)(2,1)S(1)}, u32[]{:S(2)}, u32[]{:S(2)}) %collective-permute-start.6) | collective-permute-done | bytes 524320 | tf_op jit(solution)/shard_map/ppermute | solution.py:329
  24.9 2.8 %kv_first.1 = (bf16[40,128,1024]{2,1,0:T(8,128)(2,1)S(1)}, bf16[512,512]{1,0:T(8,128)(2,1)S(1)}, bf16[512,1024]{1,0:T(8,128)(2,1)S(1)}, bf16[512,512]{1,0:T(8,128)(2,1)S(1)}) custom-call(bf16[1024,512]{1,0:T(8,128)(2,1)S(1)} %get-tuple-element.28.xa, bf16[1024,512]{1,0:T(8,128)(2,1)S(1)} %collective-permute-done.3.xb, ...), custom_call_target="tpu_custom_call" | custom-call | tf_op jit(solution)/shard_map/kv_first/pallas_call | solution.py:137
  27.7 5.0 %collective-permute-done.xa = bf16[1024,512]{1,0:T(8,128)(2,1)S(1)} collective-permute-done((bf16[1024,512]{1,0:T(8,128)(2,1)S(1)}, bf16[1024,512]{1,0:T(8,128)(2,1)S(1)}, u32[]{:S(2)}, u32[]{:S(2)}) %collective-permute-start) | collective-permute-done | bytes 1048608 | tf_op jit(solution)/shard_map/ppermute | solution.py:311
  32.7 4.5 %collective-permute-done.1.xb = bf16[1024,512]{1,0:T(8,128)(2,1)S(1)} collective-permute-done((bf16[1024,512]{1,0:T(8,128)(2,1)S(1)}, bf16[1024,512]{1,0:T(8,128)(2,1)S(1)}, u32[]{:S(2)}, u32[]{:S(2)}) %collective-permute-start.1) | collective-permute-done | bytes 1048608 | tf_op jit(solution)/shard_map/ppermute | solution.py:311
  37.2 1.6 %collective-permute-start.8 = (bf16[1024,512]{1,0:T(8,128)(2,1)S(1)}, bf16[1024,512]{1,0:T(8,128)(2,1)S(1)}, u32[]{:S(2)}, u32[]{:S(2)}) collective-permute-start(bf16[1024,512]{1,0:T(8,128)(2,1)S(1)} %collective-permute-done.xa), channel_id=1, source_target_pairs={{4,0},{0,4},{12,8},{8,12},{20,16},{16,20},{28,24},{24,28},{36,32},... | collective-permute-start | bytes 3145736 | tf_op jit(solution)/shard_map/ppermute | solution.py:311
  38.9 1.1 %collective-permute-start.10 = (bf16[512,512]{1,0:T(8,128)(2,1)S(1)}, bf16[512,512]{1,0:T(8,128)(2,1)S(1)}, u32[]{:S(2)}, u32[]{:S(2)}) collective-permute-start(bf16[512,512]{1,0:T(8,128)(2,1)S(1)} %collective-permute-done.7.d1), channel_id=1, source_target_pairs={{4,0},{0,4},{12,8},{8,12},{20,16},{16,20},{28,24},{24,28},{36,32},... | collective-permute-start | bytes 1572872 | tf_op jit(solution)/shard_map/ppermute | solution.py:311
  40.0 1.7 %collective-permute-start.12 = (bf16[512,512]{1,0:T(8,128)(2,1)S(1)}, bf16[512,512]{1,0:T(8,128)(2,1)S(1)}, u32[]{:S(2)}, u32[]{:S(2)}) collective-permute-start(bf16[512,512]{1,0:T(8,128)(2,1)S(1)} %collective-permute-done.7.d1), channel_id=1, source_target_pairs={{3,0},{0,1},{1,2},{2,3},{5,4},{6,5},{7,6},{4,7},{11,8},{8,9},{9,10... | collective-permute-start | bytes 1572872 | tf_op jit(solution)/shard_map/ppermute | solution.py:329
  41.7 2.3 %kv_second.1.kv_in = bf16[40,128,1024]{2,1,0:T(8,128)(2,1)S(1)} custom-call(bf16[1024,512]{1,0:T(8,128)(2,1)S(1)} %collective-permute-done.xa, bf16[1024,512]{1,0:T(8,128)(2,1)S(1)} %collective-permute-done.1.xb, bf16[512,1024]{1,0:T(8,128)(2,1)S(1)} %get-tuple-element.36.wkv_ref, ...), custom_call_target="tpu_custom_call", output_to_operand_aliasing={{}: (3, {})} | custom-call | tf_op jit(solution)/shard_map/kv_second/pallas_call | solution.py:161
  44.1 5.4 %attend.1 = (bf16[512,512]{1,0:T(8,128)(2,1)S(1)}, bf16[40,128,1024]{2,1,0:T(8,128)(2,1)S(1)}) custom-call(s32[8,8]{1,0:T(8,128)S(1)} %copy-done.4, s32[8]{0:T(128)S(1)} %copy-done.5, bf16[1024,512]{1,0:T(8,128)(2,1)S(1)} %collective-permute-done.8.relay_ref, bf16[512,512]{1,0:T(8,128)(2,1)S(1)} %get-tuple-element.35.q_ref, ...), custom_call_target="tpu_custom_call", output_to_operand_aliasing={{1}: (5, {})} | custom-call | tf_op jit(solution)/shard_map/attend/pallas_call | solution.py:223
  49.6 3.1 %collective-permute-done.12.d3 = bf16[512,512]{1,0:T(8,128)(2,1)S(1)} collective-permute-done((bf16[512,512]{1,0:T(8,128)(2,1)S(1)}, bf16[512,512]{1,0:T(8,128)(2,1)S(1)}, u32[]{:S(2)}, u32[]{:S(2)}) %collective-permute-start.12) | collective-permute-done | bytes 524320 | tf_op jit(solution)/shard_map/ppermute | solution.py:329
  52.7 4.2 %mlp.1 = (bf16[512,128]{1,0:T(8,128)(2,1)S(1)}, bf16[512,128]{1,0:T(8,128)(2,1)S(1)}, bf16[512,128]{1,0:T(8,128)(2,1)S(1)}, bf16[512,128]{1,0:T(8,128)(2,1)S(1)}) custom-call(bf16[512,512]{1,0:T(8,128)(2,1)S(1)} %get-tuple-element.39.heads_ref, f32[2,2,512]{2,1,0:T(2,128)S(1)} %copy-done.2, f32[2,2,512]{2,1,0:T(2,128)S(1)} %copy-done.3, ...), custom_call_target="tpu_custom_call" | custom-call | tf_op jit(solution)/shard_map/mlp/pallas_call | solution.py:263
  57.6 2.8 %collective-permute-start.14 = (bf16[512,128]{1,0:T(8,128)(2,1)S(1)}, bf16[512,128]{1,0:T(8,128)(2,1)S(1)}, u32[]{:S(2)}, u32[]{:S(2)}) collective-permute-start(bf16[512,128]{1,0:T(8,128)(2,1)S(1)} %get-tuple-element.45), channel_id=1, source_target_pairs={{1,0},{2,1},{3,2},{0,3},{5,4},{6,5},{7,6},{4,7},{9,8},{10,9},{11,1... | collective-permute-start | bytes 393224 | tf_op jit(solution)/shard_map/ppermute | solution.py:335
  60.4 1.9 %collective-permute-done.13.across = bf16[512,128]{1,0:T(8,128)(2,1)S(1)} collective-permute-done((bf16[512,128]{1,0:T(8,128)(2,1)S(1)}, bf16[512,128]{1,0:T(8,128)(2,1)S(1)}, u32[]{:S(2)}, u32[]{:S(2)}) %collective-permute-start.13) | collective-permute-done | bytes 131104 | tf_op jit(solution)/shard_map/ppermute | solution.py:338
  62.3 2.5 %collective-permute-done.14.after = bf16[512,128]{1,0:T(8,128)(2,1)S(1)} collective-permute-done((bf16[512,128]{1,0:T(8,128)(2,1)S(1)}, bf16[512,128]{1,0:T(8,128)(2,1)S(1)}, u32[]{:S(2)}, u32[]{:S(2)}) %collective-permute-start.14) | collective-permute-done | bytes 131104 | tf_op jit(solution)/shard_map/ppermute | solution.py:335
  64.9 2.5 %collective-permute-done.15.before = bf16[512,128]{1,0:T(8,128)(2,1)S(1)} collective-permute-done((bf16[512,128]{1,0:T(8,128)(2,1)S(1)}, bf16[512,128]{1,0:T(8,128)(2,1)S(1)}, u32[]{:S(2)}, u32[]{:S(2)}) %collective-permute-start.15) | collective-permute-done | bytes 131104 | tf_op jit(solution)/shard_map/ppermute | solution.py:332
  67.4 0.8 %place_rows.1 = bf16[4,512,128]{2,1,0:T(8,128)(2,1)} custom-call(bf16[512,128]{1,0:T(8,128)(2,1)S(1)} %get-tuple-element.43.own, bf16[512,128]{1,0:T(8,128)(2,1)S(1)} %collective-permute-done.13.across, bf16[512,128]{1,0:T(8,128)(2,1)S(1)} %collective-permute-done.14.after, bf16[512,128]{1,0:T(8,128)(2,1)S(1)} %collective-permute-done.15.before), custom_call_target="tpu_custom_call" | custom-call | tf_op jit(solution)/shard_map/place_rows/pallas_call | solution.py:288
  (26 shorter events, 1.9 us)
Async XLA Ops:
  2.0 12.6 %collective-permute-start.3 = (bf16[1024,512]{1,0:T(8,128)(2,1)S(1)}, bf16[1024,512]{1,0:T(8,128)(2,1)S(1)}, u32[]{:S(2)}, u32[]{:S(2)}) collective-permute-start(bf16[1024,512]{1,0:T(8,128)(2,1)S(1)} %get-tuple-element.28.xa), channel_id=1, source_target_pairs={{4,0},{0,4},{12,8},{8,12},{20,16},{16,20},{28,24},{24,28},{36,32},... | collective-permute-start | bytes 3145736 | tf_op jit(solution)/shard_map/ppermute | solution.py:311
  5.4 9.2 %collective-permute-start.4 = (bf16[4,512,128]{2,1,0:T(8,128)(2,1)S(1)}, bf16[4,512,128]{2,1,0:T(8,128)(2,1)S(1)}, u32[]{:S(2)}, u32[]{:S(2)}) collective-permute-start(bf16[4,512,128]{2,1,0:T(8,128)(2,1)S(1)} %get-tuple-element.29.w0), channel_id=1, source_target_pairs={{3,0},{0,1},{1,2},{2,3},{5,4},{6,5},{7,6},{4,7},{11,8},{8,9},{9,10... | collective-permute-start | bytes 1572872 | tf_op jit(solution)/shard_map/ppermute | solution.py:329
  6.4 12.9 %collective-permute-start.2 = (bf16[512,512]{1,0:T(8,128)(2,1)}, bf16[512,512]{1,0:T(8,128)(2,1)S(1)}, u32[]{:S(2)}, u32[]{:S(2)}) collective-permute-start(bf16[512,512]{1,0:T(8,128)(2,1)} %u0.1), channel_id=1, source_target_pairs={{3,0},{0,1},{1,2},{2,3},{5,4},{6,5},{7,6},{4,7},{11,8},{8,9},{9,10... | collective-permute-start | bytes 1572872 | tf_op jit(solution)/shard_map/ppermute | solution.py:329
  6.8 25.8 %collective-permute-start = (bf16[1024,512]{1,0:T(8,128)(2,1)S(1)}, bf16[1024,512]{1,0:T(8,128)(2,1)S(1)}, u32[]{:S(2)}, u32[]{:S(2)}) collective-permute-start(bf16[1024,512]{1,0:T(8,128)(2,1)S(1)} %get-tuple-element.28.xa), channel_id=1, source_target_pairs={{8,0},{252,4},{16,8},{4,12},{24,16},{12,20},{32,24},{20,28},{40,32... | collective-permute-start | bytes 3145736 | tf_op jit(solution)/shard_map/ppermute | solution.py:311
  8.0 29.1 %collective-permute-start.1 = (bf16[1024,512]{1,0:T(8,128)(2,1)S(1)}, bf16[1024,512]{1,0:T(8,128)(2,1)S(1)}, u32[]{:S(2)}, u32[]{:S(2)}) collective-permute-start(bf16[1024,512]{1,0:T(8,128)(2,1)S(1)} %get-tuple-element.28.xa), channel_id=1, source_target_pairs={{248,0},{12,4},{0,8},{20,12},{8,16},{28,20},{16,24},{36,28},{24,32... | collective-permute-start | bytes 3145736 | tf_op jit(solution)/shard_map/ppermute | solution.py:311
  14.6 6.6 %collective-permute-start.5 = (bf16[4,512,128]{2,1,0:T(8,128)(2,1)S(1)}, bf16[4,512,128]{2,1,0:T(8,128)(2,1)S(1)}, u32[]{:S(2)}, u32[]{:S(2)}) collective-permute-start(bf16[4,512,128]{2,1,0:T(8,128)(2,1)S(1)} %collective-permute-done.4.w1), channel_id=1, source_target_pairs={{4,0},{0,4},{12,8},{8,12},{20,16},{16,20},{28,24},{24,28},{36,32},... | collective-permute-start | bytes 1572872 | tf_op jit(solution)/shard_map/ppermute | solution.py:311
  15.9 9.1 %collective-permute-start.6 = (bf16[4,512,128]{2,1,0:T(8,128)(2,1)S(1)}, bf16[4,512,128]{2,1,0:T(8,128)(2,1)S(1)}, u32[]{:S(2)}, u32[]{:S(2)}) collective-permute-start(bf16[4,512,128]{2,1,0:T(8,128)(2,1)S(1)} %collective-permute-done.4.w1), channel_id=1, source_target_pairs={{3,0},{0,1},{1,2},{2,3},{5,4},{6,5},{7,6},{4,7},{11,8},{8,9},{9,10... | collective-permute-start | bytes 1572872 | tf_op jit(solution)/shard_map/ppermute | solution.py:329
  19.3 17.8 %collective-permute-start.7 = (bf16[512,512]{1,0:T(8,128)(2,1)}, bf16[512,512]{1,0:T(8,128)(2,1)S(1)}, u32[]{:S(2)}, u32[]{:S(2)}) collective-permute-start(bf16[512,512]{1,0:T(8,128)(2,1)} %d0.1), channel_id=1, source_target_pairs={{3,0},{0,1},{1,2},{2,3},{5,4},{6,5},{7,6},{4,7},{11,8},{8,9},{9,10... | collective-permute-start | bytes 1572872 | tf_op jit(solution)/shard_map/ppermute | solution.py:329
  37.2 6.9 %collective-permute-start.8 = (bf16[1024,512]{1,0:T(8,128)(2,1)S(1)}, bf16[1024,512]{1,0:T(8,128)(2,1)S(1)}, u32[]{:S(2)}, u32[]{:S(2)}) collective-permute-start(bf16[1024,512]{1,0:T(8,128)(2,1)S(1)} %collective-permute-done.xa), channel_id=1, source_target_pairs={{4,0},{0,4},{12,8},{8,12},{20,16},{16,20},{28,24},{24,28},{36,32},... | collective-permute-start | bytes 3145736 | tf_op jit(solution)/shard_map/ppermute | solution.py:311
  38.7 10.8 %collective-permute-start.11 = (bf16[512,512]{1,0:T(8,128)(2,1)S(1)}, bf16[512,512]{1,0:T(8,128)(2,1)S(1)}, u32[]{:S(2)}, u32[]{:S(2)}) collective-permute-start(bf16[512,512]{1,0:T(8,128)(2,1)S(1)} %collective-permute-done.2.u1), channel_id=1, source_target_pairs={{3,0},{0,1},{1,2},{2,3},{5,4},{6,5},{7,6},{4,7},{11,8},{8,9},{9,10... | collective-permute-start | bytes 1572872 | tf_op jit(solution)/shard_map/ppermute | solution.py:329
  38.9 10.7 %collective-permute-start.10 = (bf16[512,512]{1,0:T(8,128)(2,1)S(1)}, bf16[512,512]{1,0:T(8,128)(2,1)S(1)}, u32[]{:S(2)}, u32[]{:S(2)}) collective-permute-start(bf16[512,512]{1,0:T(8,128)(2,1)S(1)} %collective-permute-done.7.d1), channel_id=1, source_target_pairs={{4,0},{0,4},{12,8},{8,12},{20,16},{16,20},{28,24},{24,28},{36,32},... | collective-permute-start | bytes 1572872 | tf_op jit(solution)/shard_map/ppermute | solution.py:311
  40.0 9.6 %collective-permute-start.9 = (bf16[512,512]{1,0:T(8,128)(2,1)S(1)}, bf16[512,512]{1,0:T(8,128)(2,1)S(1)}, u32[]{:S(2)}, u32[]{:S(2)}) collective-permute-start(bf16[512,512]{1,0:T(8,128)(2,1)S(1)} %collective-permute-done.2.u1), channel_id=1, source_target_pairs={{4,0},{0,4},{12,8},{8,12},{20,16},{16,20},{28,24},{24,28},{36,32},... | collective-permute-start | bytes 1572872 | tf_op jit(solution)/shard_map/ppermute | solution.py:311
  40.0 12.7 %collective-permute-start.12 = (bf16[512,512]{1,0:T(8,128)(2,1)S(1)}, bf16[512,512]{1,0:T(8,128)(2,1)S(1)}, u32[]{:S(2)}, u32[]{:S(2)}) collective-permute-start(bf16[512,512]{1,0:T(8,128)(2,1)S(1)} %collective-permute-done.7.d1), channel_id=1, source_target_pairs={{3,0},{0,1},{1,2},{2,3},{5,4},{6,5},{7,6},{4,7},{11,8},{8,9},{9,10... | collective-permute-start | bytes 1572872 | tf_op jit(solution)/shard_map/ppermute | solution.py:329
  41.7 2.4 %copy-start.4 = (s32[8,8]{1,0:T(8,128)S(1)}, s32[8,8]{1,0:T(8,128)}, u32[]{:S(2)}) copy-start(s32[8,8]{1,0:T(8,128)} %list_ref.1) | copy-start | bytes 772
  41.7 2.4 %copy-start.5 = (s32[8]{0:T(128)S(1)}, s32[8]{0:T(128)}, u32[]{:S(2)}) copy-start(s32[8]{0:T(128)} %count_ref.1) | copy-start | bytes 100
  44.0 8.6 %copy-start = (bf16[512,512]{1,0:T(8,128)(2,1)S(1)}, bf16[512,512]{1,0:T(8,128)(2,1)}, u32[]{:S(2)}) copy-start(bf16[512,512]{1,0:T(8,128)(2,1)} %u0.1) | copy-start | bytes 1572868
  44.0 8.6 %copy-start.1 = (bf16[512,512]{1,0:T(8,128)(2,1)S(1)}, bf16[512,512]{1,0:T(8,128)(2,1)}, u32[]{:S(2)}) copy-start(bf16[512,512]{1,0:T(8,128)(2,1)} %d0.1) | copy-start | bytes 1572868
  44.1 8.6 %copy-start.2 = (f32[2,2,512]{2,1,0:T(2,128)S(1)}, f32[2,2,512]{2,1,0:T(2,128)}, u32[]{:S(2)}) copy-start(f32[2,2,512]{2,1,0:T(2,128)} %gain_ref.3) | copy-start | bytes 24580
  44.1 8.6 %copy-start.3 = (f32[2,2,512]{2,1,0:T(2,128)S(1)}, f32[2,2,512]{2,1,0:T(2,128)}, u32[]{:S(2)}) copy-start(f32[2,2,512]{2,1,0:T(2,128)} %shift_ref.3) | copy-start | bytes 24580
  56.9 5.4 %collective-permute-start.13 = (bf16[512,128]{1,0:T(8,128)(2,1)S(1)}, bf16[512,128]{1,0:T(8,128)(2,1)S(1)}, u32[]{:S(2)}, u32[]{:S(2)}) collective-permute-start(bf16[512,128]{1,0:T(8,128)(2,1)S(1)} %get-tuple-element.44), channel_id=1, source_target_pairs={{0,2},{1,3},{2,0},{3,1},{4,6},{5,7},{6,4},{7,5},{8,10},{9,11},{10,... | collective-permute-start | bytes 393224 | tf_op jit(solution)/shard_map/ppermute | solution.py:338
  57.6 7.3 %collective-permute-start.14 = (bf16[512,128]{1,0:T(8,128)(2,1)S(1)}, bf16[512,128]{1,0:T(8,128)(2,1)S(1)}, u32[]{:S(2)}, u32[]{:S(2)}) collective-permute-start(bf16[512,128]{1,0:T(8,128)(2,1)S(1)} %get-tuple-element.45), channel_id=1, source_target_pairs={{1,0},{2,1},{3,2},{0,3},{5,4},{6,5},{7,6},{4,7},{9,8},{10,9},{11,1... | collective-permute-start | bytes 393224 | tf_op jit(solution)/shard_map/ppermute | solution.py:335
  60.4 7.0 %collective-permute-start.15 = (bf16[512,128]{1,0:T(8,128)(2,1)S(1)}, bf16[512,128]{1,0:T(8,128)(2,1)S(1)}, u32[]{:S(2)}, u32[]{:S(2)}) collective-permute-start(bf16[512,128]{1,0:T(8,128)(2,1)S(1)} %get-tuple-element.46), channel_id=1, source_target_pairs={{0,1},{1,2},{2,3},{3,0},{4,5},{5,6},{6,7},{7,4},{8,9},{9,10},{10,1... | collective-permute-start | bytes 393224 | tf_op jit(solution)/shard_map/ppermute | solution.py:332

commit v10 on v6

--- a/solution.py
+++ b/solution.py
@@ -404,7 +404,17 @@
         return lax.ppermute(v, "tp", [((i + 1) % tps, i) for i in range(tps)])
 
     def across(v):
-        return lax.ppermute(v, "tp", [(i, (i + 2) % tps) for i in range(tps)])
+        first = [
+            (i * tps + t, i * tps + (t + 2 if i % 2 == 0 else t - 1) % tps)
+            for i in range(doms)
+            for t in range(tps)
+        ]
+        then = [
+            (i * tps + t, i * tps + (t if i % 2 == 0 else t - 1) % tps)
+            for i in range(doms)
+            for t in range(tps)
+        ]
+        return lax.ppermute(lax.ppermute(v, ("dom", "tp"), first), ("dom", "tp"), then)
 
     qkv = jnp.transpose(qkv_weight, (1, 0, 2))
     own, w0 = prepare(state, norm_gain, norm_shift, qkv, out_weight)

time: 64.8 us -> 66.4 us (1.025)
  starting transfers between devices: 27 us -> 31.7 us
  waiting for transfers between devices: 16.9 us -> 13.8 us
    ppermute x1 -> x2, starting transfers between devices: 0.17 us -> 5.35 us  [the longest x1 4.16 us: across(): lax.ppermute(lax.ppermute(v, ('dom', 'tp'), first), ('dom', 'tp'), then)]
    ppermute x1, starting transfers between devices: 1.97 us -> 0.09 us  [down(): return lax.ppermute(v, 'tp', [((i + 1) % tps, i) for i in range(tps)])]
    ppermute x1, waiting for transfers between devices: 1.53 us -> 0.01 us  [down(): return lax.ppermute(v, 'tp', [((i + 1) % tps, i) for i in range(tps)])]
    ppermute x1, starting transfers between devices: 0.01 us -> 1.38 us  [up(): return lax.ppermute(v, 'tp', [(i, (i + 1) % tps) for i in range(tps)])]
    ppermute x1, waiting for transfers between devices: 1.14 us -> 0.01 us  [up(): return lax.ppermute(v, 'tp', [(i, (i + 1) % tps) for i in range(tps)])]
    ppermute x1 -> x2, waiting for transfers between devices: 4.59 us -> 4.13 us  [the longest x1 2.23 us: across(): lax.ppermute(v, ('dom', 'tp'), first)]
  transfers between devices with their start and end apart: 17 -> 18, of which waited for: 7 -> 6; matrix products, arithmetic and copies ran while one was open for 0% -> 0% of each run, Pallas kernels for 24% -> 24%
where the time goes in v10:
time: 66.4 us; the launch traced here: 66.3 us
  starting transfers between devices  31.7 us (48%)
  Pallas kernels  20.5 us (31%)
  waiting for transfers between devices  13.8 us (21%)
    ppermute x9, starting transfers between devices, hop(): return lax.ppermute(v, 'dom', pairs)  19.1 us
    ppermute x5, waiting for transfers between devices, ring(): return lax.ppermute(v, ('dom', 'tp'), pairs)  6.38 us
    ppermute x5, starting transfers between devices, ring(): return lax.ppermute(v, ('dom', 'tp'), pairs)  5.77 us
    pallas_call x1, Pallas kernels, attend(): pl.pallas_call(functools.partial(attend_kernel, doms=doms, per_dev=per_de...  5.43 us
    pallas_call x1, Pallas kernels, kv_first(): pl.pallas_call(kv_first_kernel, in_specs=[VMEM] * (2 + len(weights)), out...  4.32 us
    ppermute x1, starting transfers between devices, across(): lax.ppermute(lax.ppermute(v, ('dom', 'tp'), first), ('dom', 'tp'), then)  4.16 us
    pallas_call x1, Pallas kernels, mlp_first(): pl.pallas_call(mlp_first_kernel, in_specs=[VMEM] * (4 + len(weights)) + [...  3.49 us
    ppermute x9, waiting for transfers between devices, hop(): return lax.ppermute(v, 'dom', pairs)  3.27 us
  transfers between devices with their start and end apart: 18, of which 6 were waited for; matrix products, arithmetic and copies ran while one was open for 0% of the time, Pallas kernels for 24%

profile of v10, /device:TPU:1, one launch (start us, length us, event | category | flops | bytes accessed | tf_op | source)
XLA Modules:
  0.0 66.3 jit_solution(8558078837081390462)
XLA Ops:
  0.0 3.1 %prepare.1 = (bf16[1024,512]{1,0:T(8,128)(2,1)}, bf16[4,512,128]{2,1,0:T(8,128)(2,1)S(1)}) custom-call(bf16[2,1024,512]{2,1,0:T(8,128)(2,1)} %state_ref.3, f32[2,2,512]{2,1,0:T(2,128)} %gain_ref.3, f32[2,2,512]{2,1,0:T(2,128)} %shift_ref.3, bf16[3,512,128]{2,1,0:T(8,128)(2,1)} %bitcast.2, bf16[128,512]{1,0:T(8,128)(2,1)} %out_ref.1), custom_call_target="tpu_custom_call" | custom-call | tf_op jit(solution)/shard_map/prepare/pallas_call | solution.py:95
  3.1 3.3 %collective-permute-start.3 = (bf16[1024,512]{1,0:T(8,128)(2,1)}, bf16[1024,512]{1,0:T(8,128)(2,1)}, u32[]{:S(2)}, u32[]{:S(2)}) collective-permute-start(bf16[1024,512]{1,0:T(8,128)(2,1)} %get-tuple-element.31.xa), channel_id=1, source_target_pairs={{4,0},{0,4},{12,8},{8,12},{20,16},{16,20},{28,24},{24,28},{36,32},... | collective-permute-start | bytes 3145736 | tf_op jit(solution)/shard_map/ppermute | solution.py:380
  6.4 1.0 %collective-permute-start.4 = (bf16[4,512,128]{2,1,0:T(8,128)(2,1)S(1)}, bf16[4,512,128]{2,1,0:T(8,128)(2,1)S(1)}, u32[]{:S(2)}, u32[]{:S(2)}) collective-permute-start(bf16[4,512,128]{2,1,0:T(8,128)(2,1)S(1)} %get-tuple-element.32.w0), channel_id=1, source_target_pairs={{3,0},{0,1},{1,2},{2,3},{5,4},{6,5},{7,6},{4,7},{11,8},{8,9},{9,10... | collective-permute-start | bytes 1572872 | tf_op jit(solution)/shard_map/ppermute | solution.py:398
  7.4 1.2 %collective-permute-start = (bf16[1024,512]{1,0:T(8,128)(2,1)}, bf16[1024,512]{1,0:T(8,128)(2,1)S(1)}, u32[]{:S(2)}, u32[]{:S(2)}) collective-permute-start(bf16[1024,512]{1,0:T(8,128)(2,1)} %get-tuple-element.31.xa), channel_id=1, source_target_pairs={{8,0},{252,4},{16,8},{4,12},{24,16},{12,20},{32,24},{20,28},{40,32... | collective-permute-start | bytes 3145736 | tf_op jit(solution)/shard_map/ppermute | solution.py:380
  8.6 6.6 %collective-permute-start.1 = (bf16[1024,512]{1,0:T(8,128)(2,1)}, bf16[1024,512]{1,0:T(8,128)(2,1)S(1)}, u32[]{:S(2)}, u32[]{:S(2)}) collective-permute-start(bf16[1024,512]{1,0:T(8,128)(2,1)} %get-tuple-element.31.xa), channel_id=1, source_target_pairs={{248,0},{12,4},{0,8},{20,12},{8,16},{28,20},{16,24},{36,28},{24,32... | collective-permute-start | bytes 3145736 | tf_op jit(solution)/shard_map/ppermute | solution.py:380
  15.2 1.5 %collective-permute-start.6 = (bf16[4,256,128]{2,1,0:T(8,128)(2,1)S(1)}, bf16[4,256,128]{2,1,0:T(8,128)(2,1)S(1)}, u32[]{:S(2)}, u32[]{:S(2)}) collective-permute-start(bf16[4,256,128]{2,1,0:T(8,128)(2,1)S(1)} %constant_dynamic-slice_fusion), channel_id=1, source_target_pairs={{3,0},{0,1},{1,2},{2,3},{5,4},{6,5},{7,6},{4,7},{11,8},{8,9},{9,10... | collective-permute-start | bytes 786440 | tf_op jit(solution)/shard_map/ppermute | solution.py:398
  17.4 3.4 %collective-permute-done.6.w3m = bf16[4,256,128]{2,1,0:T(8,128)(2,1)S(1)} collective-permute-done((bf16[4,256,128]{2,1,0:T(8,128)(2,1)S(1)}, bf16[4,256,128]{2,1,0:T(8,128)(2,1)S(1)}, u32[]{:S(2)}, u32[]{:S(2)}) %collective-permute-start.6) | collective-permute-done | bytes 262176 | tf_op jit(solution)/shard_map/ppermute | solution.py:398
  20.8 2.7 %collective-permute-start.8 = (bf16[512,512]{1,0:T(8,128)(2,1)}, bf16[512,512]{1,0:T(8,128)(2,1)S(1)}, u32[]{:S(2)}, u32[]{:S(2)}) collective-permute-start(bf16[512,512]{1,0:T(8,128)(2,1)} %d0.1), channel_id=1, source_target_pairs={{3,0},{0,1},{1,2},{2,3},{5,4},{6,5},{7,6},{4,7},{11,8},{8,9},{9,10... | collective-permute-start | bytes 1572872 | tf_op jit(solution)/shard_map/ppermute | solution.py:398
  23.5 2.9 %collective-permute-done.2.a_ref.u1 = bf16[512,512]{1,0:T(8,128)(2,1)S(1)} collective-permute-done((bf16[512,512]{1,0:T(8,128)(2,1)}, bf16[512,512]{1,0:T(8,128)(2,1)S(1)}, u32[]{:S(2)}, u32[]{:S(2)}) %collective-permute-start.2) | collective-permute-done | bytes 524320 | tf_op jit(solution)/shard_map/ppermute | solution.py:398
  26.4 3.8 %collective-permute-start.7 = (bf16[4,256,128]{2,1,0:T(8,128)(2,1)S(1)}, bf16[4,256,128]{2,1,0:T(8,128)(2,1)S(1)}, u32[]{:S(2)}, u32[]{:S(2)}) collective-permute-start(bf16[4,256,128]{2,1,0:T(8,128)(2,1)S(1)} %collective-permute-done.6.w3m), channel_id=1, source_target_pairs={{4,0},{0,4},{12,8},{8,12},{20,16},{16,20},{28,24},{24,28},{36,32},... | collective-permute-start | bytes 786440 | tf_op jit(solution)/shard_map/ppermute | solution.py:380
  30.2 1.2 %collective-permute-done.7.w3t = bf16[4,256,128]{2,1,0:T(8,128)(2,1)S(1)} collective-permute-done((bf16[4,256,128]{2,1,0:T(8,128)(2,1)S(1)}, bf16[4,256,128]{2,1,0:T(8,128)(2,1)S(1)}, u32[]{:S(2)}, u32[]{:S(2)}) %collective-permute-start.7) | collective-permute-done | bytes 262176 | tf_op jit(solution)/shard_map/ppermute | solution.py:380
  31.3 4.3 %kv_first.1 = (bf16[40,128,1024]{2,1,0:T(8,128)(2,1)S(1)}, bf16[512,512]{1,0:T(8,128)(2,1)S(1)}, bf16[512,1024]{1,0:T(8,128)(2,1)S(1)}, bf16[512,512]{1,0:T(8,128)(2,1)S(1)}) custom-call(bf16[1024,512]{1,0:T(8,128)(2,1)} %get-tuple-element.31.xa, bf16[1024,512]{1,0:T(8,128)(2,1)} %collective-permute-done.3.xb, ...), custom_call_target="tpu_custom_call" | custom-call | tf_op jit(solution)/shard_map/kv_first/pallas_call | solution.py:172
  35.8 2.1 %collective-permute-done.1.xb = bf16[1024,512]{1,0:T(8,128)(2,1)S(1)} collective-permute-done((bf16[1024,512]{1,0:T(8,128)(2,1)}, bf16[1024,512]{1,0:T(8,128)(2,1)S(1)}, u32[]{:S(2)}, u32[]{:S(2)}) %collective-permute-start.1) | collective-permute-done | bytes 1048608 | tf_op jit(solution)/shard_map/ppermute | solution.py:380
  37.8 1.6 %collective-permute-start.10 = (bf16[1024,512]{1,0:T(8,128)(2,1)S(1)}, bf16[1024,512]{1,0:T(8,128)(2,1)S(1)}, u32[]{:S(2)}, u32[]{:S(2)}) collective-permute-start(bf16[1024,512]{1,0:T(8,128)(2,1)S(1)} %collective-permute-done.xa), channel_id=1, source_target_pairs={{4,0},{0,4},{12,8},{8,12},{20,16},{16,20},{28,24},{24,28},{36,32},... | collective-permute-start | bytes 3145736 | tf_op jit(solution)/shard_map/ppermute | solution.py:380
  40.0 2.3 %kv_second.1.kv_in = bf16[40,128,1024]{2,1,0:T(8,128)(2,1)S(1)} custom-call(bf16[1024,512]{1,0:T(8,128)(2,1)S(1)} %collective-permute-done.xa, bf16[1024,512]{1,0:T(8,128)(2,1)S(1)} %collective-permute-done.1.xb, bf16[512,1024]{1,0:T(8,128)(2,1)S(1)} %get-tuple-element.40.wkv_ref, ...), custom_call_target="tpu_custom_call", output_to_operand_aliasing={{}: (3, {})} | custom-call | tf_op jit(solution)/shard_map/kv_second/pallas_call | solution.py:196
  43.0 5.4 %attend.1 = (bf16[512,512]{1,0:T(8,128)(2,1)S(1)}, bf16[40,128,1024]{2,1,0:T(8,128)(2,1)S(1)}) custom-call(s32[8,8]{1,0:T(8,128)S(1)} %copy-done.4, s32[8]{0:T(128)S(1)} %copy-done.5, bf16[1024,512]{1,0:T(8,128)(2,1)S(1)} %collective-permute-done.10.relay_ref, bf16[512,512]{1,0:T(8,128)(2,1)S(1)} %get-tuple-element.39.q_ref, ...), custom_call_target="tpu_custom_call", output_to_operand_aliasing={{1}: (5, {})} | custom-call | tf_op jit(solution)/shard_map/attend/pallas_call | solution.py:258
  48.4 1.5 %collective-permute-start.13 = (bf16[512,512]{1,0:T(8,128)(2,1)S(1)}, bf16[512,512]{1,0:T(8,128)(2,1)S(1)}, u32[]{:S(2)}, u32[]{:S(2)}) collective-permute-start(bf16[512,512]{1,0:T(8,128)(2,1)S(1)} %collective-permute-done.9.mine), channel_id=1, source_target_pairs={{4,0},{0,4},{12,8},{8,12},{20,16},{16,20},{28,24},{24,28},{36,32},... | collective-permute-start | bytes 1572872 | tf_op jit(solution)/shard_map/ppermute | solution.py:380
  49.9 3.5 %mlp_first.1 = (f32[512,512]{1,0:T(8,128)S(1)}, bf16[512,512]{1,0:T(8,128)(2,1)S(1)}) custom-call(bf16[512,512]{1,0:T(8,128)(2,1)S(1)} %get-tuple-element.44.heads_ref, f32[2,2,512]{2,1,0:T(2,128)S(1)} %copy-done.2, f32[2,2,512]{2,1,0:T(2,128)S(1)} %copy-done.3, bf16[512,512]{1,0:T(8,128)(2,1)S(1)} %get-tuple-element.45.wo_ref, ...), custom_call_target="tpu_custom_call" | custom-call | tf_op jit(solution)/shard_map/mlp_first/pallas_call | solution.py:295
  53.4 1.0 %mlp_second.1 = (bf16[512,128]{1,0:T(8,128)(2,1)S(1)}, bf16[512,128]{1,0:T(8,128)(2,1)S(1)}, bf16[512,128]{1,0:T(8,128)(2,1)S(1)}, bf16[512,128]{1,0:T(8,128)(2,1)S(1)}) custom-call(f32[512,512]{1,0:T(8,128)S(1)} %get-tuple-element.46.resid_ref, bf16[512,512]{1,0:T(8,128)(2,1)S(1)} %get-tuple-element.47.normed_ref, ...), custom_call_target="tpu_custom_call" | custom-call | tf_op jit(solution)/shard_map/mlp_second/pallas_call | solution.py:332
  54.4 1.2 %collective-permute-start.14 = (bf16[512,128]{1,0:T(8,128)(2,1)S(1)}, bf16[512,128]{1,0:T(8,128)(2,1)S(1)}, u32[]{:S(2)}, u32[]{:S(2)}) collective-permute-start(bf16[512,128]{1,0:T(8,128)(2,1)S(1)} %get-tuple-element.50), channel_id=1, source_target_pairs={{0,2},{1,3},{2,0},{3,1},{4,7},{5,4},{6,5},{7,6},{8,10},{9,11},{10,... | collective-permute-start | bytes 393224 | tf_op jit(solution)/shard_map/ppermute | solution.py:417
  55.7 1.4 %collective-permute-start.17 = (bf16[512,128]{1,0:T(8,128)(2,1)S(1)}, bf16[512,128]{1,0:T(8,128)(2,1)S(1)}, u32[]{:S(2)}, u32[]{:S(2)}) collective-permute-start(bf16[512,128]{1,0:T(8,128)(2,1)S(1)} %get-tuple-element.52), channel_id=1, source_target_pairs={{0,1},{1,2},{2,3},{3,0},{4,5},{5,6},{6,7},{7,4},{8,9},{9,10},{10,1... | collective-permute-start | bytes 393224 | tf_op jit(solution)/shard_map/ppermute | solution.py:401
  57.1 2.2 %collective-permute-done.14 = bf16[512,128]{1,0:T(8,128)(2,1)S(1)} collective-permute-done((bf16[512,128]{1,0:T(8,128)(2,1)S(1)}, bf16[512,128]{1,0:T(8,128)(2,1)S(1)}, u32[]{:S(2)}, u32[]{:S(2)}) %collective-permute-start.14) | collective-permute-done | bytes 131104 | tf_op jit(solution)/shard_map/ppermute | solution.py:417
  59.3 4.2 %collective-permute-start.15 = (bf16[512,128]{1,0:T(8,128)(2,1)S(1)}, bf16[512,128]{1,0:T(8,128)(2,1)S(1)}, u32[]{:S(2)}, u32[]{:S(2)}) collective-permute-start(bf16[512,128]{1,0:T(8,128)(2,1)S(1)} %collective-permute-done.14), channel_id=1, source_target_pairs={{0,0},{1,1},{2,2},{3,3},{4,7},{5,4},{6,5},{7,6},{8,8},{9,9},{10,10... | collective-permute-start | bytes 393224 | tf_op jit(solution)/shard_map/ppermute | solution.py:417
  63.5 1.9 %collective-permute-done.15.across = bf16[512,128]{1,0:T(8,128)(2,1)S(1)} collective-permute-done((bf16[512,128]{1,0:T(8,128)(2,1)S(1)}, bf16[512,128]{1,0:T(8,128)(2,1)S(1)}, u32[]{:S(2)}, u32[]{:S(2)}) %collective-permute-start.15) | collective-permute-done | bytes 131104 | tf_op jit(solution)/shard_map/ppermute | solution.py:417
  (33 shorter events, 2.7 us)
Async XLA Ops:
  3.1 12.1 %collective-permute-start.3 = (bf16[1024,512]{1,0:T(8,128)(2,1)}, bf16[1024,512]{1,0:T(8,128)(2,1)}, u32[]{:S(2)}, u32[]{:S(2)}) collective-permute-start(bf16[1024,512]{1,0:T(8,128)(2,1)} %get-tuple-element.31.xa), channel_id=1, source_target_pairs={{4,0},{0,4},{12,8},{8,12},{20,16},{16,20},{28,24},{24,28},{36,32},... | collective-permute-start | bytes 3145736 | tf_op jit(solution)/shard_map/ppermute | solution.py:380
  6.4 8.8 %collective-permute-start.4 = (bf16[4,512,128]{2,1,0:T(8,128)(2,1)S(1)}, bf16[4,512,128]{2,1,0:T(8,128)(2,1)S(1)}, u32[]{:S(2)}, u32[]{:S(2)}) collective-permute-start(bf16[4,512,128]{2,1,0:T(8,128)(2,1)S(1)} %get-tuple-element.32.w0), channel_id=1, source_target_pairs={{3,0},{0,1},{1,2},{2,3},{5,4},{6,5},{7,6},{4,7},{11,8},{8,9},{9,10... | collective-permute-start | bytes 1572872 | tf_op jit(solution)/shard_map/ppermute | solution.py:398
  7.4 28.4 %collective-permute-start = (bf16[1024,512]{1,0:T(8,128)(2,1)}, bf16[1024,512]{1,0:T(8,128)(2,1)S(1)}, u32[]{:S(2)}, u32[]{:S(2)}) collective-permute-start(bf16[1024,512]{1,0:T(8,128)(2,1)} %get-tuple-element.31.xa), channel_id=1, source_target_pairs={{8,0},{252,4},{16,8},{4,12},{24,16},{12,20},{32,24},{20,28},{40,32... | collective-permute-start | bytes 3145736 | tf_op jit(solution)/shard_map/ppermute | solution.py:380
  8.6 29.2 %collective-permute-start.1 = (bf16[1024,512]{1,0:T(8,128)(2,1)}, bf16[1024,512]{1,0:T(8,128)(2,1)S(1)}, u32[]{:S(2)}, u32[]{:S(2)}) collective-permute-start(bf16[1024,512]{1,0:T(8,128)(2,1)} %get-tuple-element.31.xa), channel_id=1, source_target_pairs={{248,0},{12,4},{0,8},{20,12},{8,16},{28,20},{16,24},{36,28},{24,32... | collective-permute-start | bytes 3145736 | tf_op jit(solution)/shard_map/ppermute | solution.py:380
  15.2 5.6 %collective-permute-start.6 = (bf16[4,256,128]{2,1,0:T(8,128)(2,1)S(1)}, bf16[4,256,128]{2,1,0:T(8,128)(2,1)S(1)}, u32[]{:S(2)}, u32[]{:S(2)}) collective-permute-start(bf16[4,256,128]{2,1,0:T(8,128)(2,1)S(1)} %constant_dynamic-slice_fusion), channel_id=1, source_target_pairs={{3,0},{0,1},{1,2},{2,3},{5,4},{6,5},{7,6},{4,7},{11,8},{8,9},{9,10... | collective-permute-start | bytes 786440 | tf_op jit(solution)/shard_map/ppermute | solution.py:398
  16.7 9.7 %collective-permute-start.2 = (bf16[512,512]{1,0:T(8,128)(2,1)}, bf16[512,512]{1,0:T(8,128)(2,1)S(1)}, u32[]{:S(2)}, u32[]{:S(2)}) collective-permute-start(bf16[512,512]{1,0:T(8,128)(2,1)} %u0.1), channel_id=1, source_target_pairs={{3,0},{0,1},{1,2},{2,3},{5,4},{6,5},{7,6},{4,7},{11,8},{8,9},{9,10... | collective-permute-start | bytes 1572872 | tf_op jit(solution)/shard_map/ppermute | solution.py:398
  16.8 13.4 %collective-permute-start.5 = (bf16[4,512,128]{2,1,0:T(8,128)(2,1)S(1)}, bf16[4,512,128]{2,1,0:T(8,128)(2,1)S(1)}, u32[]{:S(2)}, u32[]{:S(2)}) collective-permute-start(bf16[4,512,128]{2,1,0:T(8,128)(2,1)S(1)} %collective-permute-done.4.w1), channel_id=1, source_target_pairs={{4,0},{0,4},{12,8},{8,12},{20,16},{16,20},{28,24},{24,28},{36,32},... | collective-permute-start | bytes 1572872 | tf_op jit(solution)/shard_map/ppermute | solution.py:380
  20.8 14.9 %collective-permute-start.8 = (bf16[512,512]{1,0:T(8,128)(2,1)}, bf16[512,512]{1,0:T(8,128)(2,1)S(1)}, u32[]{:S(2)}, u32[]{:S(2)}) collective-permute-start(bf16[512,512]{1,0:T(8,128)(2,1)} %d0.1), channel_id=1, source_target_pairs={{3,0},{0,1},{1,2},{2,3},{5,4},{6,5},{7,6},{4,7},{11,8},{8,9},{9,10... | collective-permute-start | bytes 1572872 | tf_op jit(solution)/shard_map/ppermute | solution.py:398
  26.4 4.9 %collective-permute-start.7 = (bf16[4,256,128]{2,1,0:T(8,128)(2,1)S(1)}, bf16[4,256,128]{2,1,0:T(8,128)(2,1)S(1)}, u32[]{:S(2)}, u32[]{:S(2)}) collective-permute-start(bf16[4,256,128]{2,1,0:T(8,128)(2,1)S(1)} %collective-permute-done.6.w3m), channel_id=1, source_target_pairs={{4,0},{0,4},{12,8},{8,12},{20,16},{16,20},{28,24},{24,28},{36,32},... | collective-permute-start | bytes 786440 | tf_op jit(solution)/shard_map/ppermute | solution.py:380
  37.8 5.1 %collective-permute-start.10 = (bf16[1024,512]{1,0:T(8,128)(2,1)S(1)}, bf16[1024,512]{1,0:T(8,128)(2,1)S(1)}, u32[]{:S(2)}, u32[]{:S(2)}) collective-permute-start(bf16[1024,512]{1,0:T(8,128)(2,1)S(1)} %collective-permute-done.xa), channel_id=1, source_target_pairs={{4,0},{0,4},{12,8},{8,12},{20,16},{16,20},{28,24},{24,28},{36,32},... | collective-permute-start | bytes 3145736 | tf_op jit(solution)/shard_map/ppermute | solution.py:380
  39.5 8.9 %collective-permute-start.9 = (bf16[512,512]{1,0:T(8,128)(2,1)S(1)}, bf16[512,512]{1,0:T(8,128)(2,1)S(1)}, u32[]{:S(2)}, u32[]{:S(2)}) collective-permute-start(bf16[512,512]{1,0:T(8,128)(2,1)S(1)} %one_to_relay.1), channel_id=1, source_target_pairs={{3,0},{0,1},{1,2},{2,3},{5,4},{6,5},{7,6},{4,7},{11,8},{8,9},{9,10... | collective-permute-start | bytes 1572872 | tf_op jit(solution)/shard_map/ppermute | solution.py:398
  39.9 9.9 %collective-permute-start.11 = (bf16[512,512]{1,0:T(8,128)(2,1)S(1)}, bf16[512,512]{1,0:T(8,128)(2,1)S(1)}, u32[]{:S(2)}, u32[]{:S(2)}) collective-permute-start(bf16[512,512]{1,0:T(8,128)(2,1)S(1)} %collective-permute-done.2.a_ref.u1), channel_id=1, source_target_pairs={{4,0},{0,4},{12,8},{8,12},{20,16},{16,20},{28,24},{24,28},{36,32},... | collective-permute-start | bytes 1572872 | tf_op jit(solution)/shard_map/ppermute | solution.py:380
  39.9 3.0 %copy-start.4 = (s32[8,8]{1,0:T(8,128)S(1)}, s32[8,8]{1,0:T(8,128)}, u32[]{:S(2)}) copy-start(s32[8,8]{1,0:T(8,128)} %list_ref.1) | copy-start | bytes 772
  40.0 3.0 %copy-start.5 = (s32[8]{0:T(128)S(1)}, s32[8]{0:T(128)}, u32[]{:S(2)}) copy-start(s32[8]{0:T(128)} %count_ref.1) | copy-start | bytes 100
  42.3 7.6 %copy-start = (bf16[512,512]{1,0:T(8,128)(2,1)S(1)}, bf16[512,512]{1,0:T(8,128)(2,1)}, u32[]{:S(2)}) copy-start(bf16[512,512]{1,0:T(8,128)(2,1)} %u0.1) | copy-start | bytes 1572868
  42.3 7.6 %copy-start.1 = (bf16[512,512]{1,0:T(8,128)(2,1)S(1)}, bf16[512,512]{1,0:T(8,128)(2,1)}, u32[]{:S(2)}) copy-start(bf16[512,512]{1,0:T(8,128)(2,1)} %d0.1) | copy-start | bytes 1572868
  42.3 7.6 %copy-start.2 = (f32[2,2,512]{2,1,0:T(2,128)S(1)}, f32[2,2,512]{2,1,0:T(2,128)}, u32[]{:S(2)}) copy-start(f32[2,2,512]{2,1,0:T(2,128)} %gain_ref.3) | copy-start | bytes 24580
  42.3 7.6 %copy-start.3 = (f32[2,2,512]{2,1,0:T(2,128)S(1)}, f32[2,2,512]{2,1,0:T(2,128)}, u32[]{:S(2)}) copy-start(f32[2,2,512]{2,1,0:T(2,128)} %shift_ref.3) | copy-start | bytes 24580
  42.4 7.5 %collective-permute-start.12 = (bf16[512,512]{1,0:T(8,128)(2,1)S(1)}, bf16[512,512]{1,0:T(8,128)(2,1)S(1)}, u32[]{:S(2)}, u32[]{:S(2)}) collective-permute-start(bf16[512,512]{1,0:T(8,128)(2,1)S(1)} %collective-permute-done.8.b_ref.d1), channel_id=1, source_target_pairs={{4,0},{0,4},{12,8},{8,12},{20,16},{16,20},{28,24},{24,28},{36,32},... | collective-permute-start | bytes 1572872 | tf_op jit(solution)/shard_map/ppermute | solution.py:380
  48.4 5.0 %collective-permute-start.13 = (bf16[512,512]{1,0:T(8,128)(2,1)S(1)}, bf16[512,512]{1,0:T(8,128)(2,1)S(1)}, u32[]{:S(2)}, u32[]{:S(2)}) collective-permute-start(bf16[512,512]{1,0:T(8,128)(2,1)S(1)} %collective-permute-done.9.mine), channel_id=1, source_target_pairs={{4,0},{0,4},{12,8},{8,12},{20,16},{16,20},{28,24},{24,28},{36,32},... | collective-permute-start | bytes 1572872 | tf_op jit(solution)/shard_map/ppermute | solution.py:380
  54.4 4.9 %collective-permute-start.14 = (bf16[512,128]{1,0:T(8,128)(2,1)S(1)}, bf16[512,128]{1,0:T(8,128)(2,1)S(1)}, u32[]{:S(2)}, u32[]{:S(2)}) collective-permute-start(bf16[512,128]{1,0:T(8,128)(2,1)S(1)} %get-tuple-element.50), channel_id=1, source_target_pairs={{0,2},{1,3},{2,0},{3,1},{4,7},{5,4},{6,5},{7,6},{8,10},{9,11},{10,... | collective-permute-start | bytes 393224 | tf_op jit(solution)/shard_map/ppermute | solution.py:417
  55.6 7.9 %collective-permute-start.16 = (bf16[512,128]{1,0:T(8,128)(2,1)S(1)}, bf16[512,128]{1,0:T(8,128)(2,1)S(1)}, u32[]{:S(2)}, u32[]{:S(2)}) collective-permute-start(bf16[512,128]{1,0:T(8,128)(2,1)S(1)} %get-tuple-element.51), channel_id=1, source_target_pairs={{1,0},{2,1},{3,2},{0,3},{5,4},{6,5},{7,6},{4,7},{9,8},{10,9},{11,1... | collective-permute-start | bytes 393224 | tf_op jit(solution)/shard_map/ppermute | solution.py:404
  55.7 7.8 %collective-permute-start.17 = (bf16[512,128]{1,0:T(8,128)(2,1)S(1)}, bf16[512,128]{1,0:T(8,128)(2,1)S(1)}, u32[]{:S(2)}, u32[]{:S(2)}) collective-permute-start(bf16[512,128]{1,0:T(8,128)(2,1)S(1)} %get-tuple-element.52), channel_id=1, source_target_pairs={{0,1},{1,2},{2,3},{3,0},{4,5},{5,6},{6,7},{7,4},{8,9},{9,10},{10,1... | collective-permute-start | bytes 393224 | tf_op jit(solution)/shard_map/ppermute | solution.py:401
  59.3 6.1 %collective-permute-start.15 = (bf16[512,128]{1,0:T(8,128)(2,1)S(1)}, bf16[512,128]{1,0:T(8,128)(2,1)S(1)}, u32[]{:S(2)}, u32[]{:S(2)}) collective-permute-start(bf16[512,128]{1,0:T(8,128)(2,1)S(1)} %collective-permute-done.14), channel_id=1, source_target_pairs={{0,0},{1,1},{2,2},{3,3},{4,7},{5,4},{6,5},{7,6},{8,8},{9,9},{10,10... | collective-permute-start | bytes 393224 | tf_op jit(solution)/shard_map/ppermute | solution.py:417
